TPU v7x, 32 devices: a whole 2x2x4 slice. The times are simulated.
32 devices in a mesh: dp: 8 (over z, y), group: 4 (over x, core).
Axes of the slice: x: 2, y: 2, z: 4, core: 2. Of those that a mesh axis runs over, the one named last changes fastest.
Arguments:
- gradients: float32 [32, 3, 320, 960], P(('dp', 'group')), may hold values from -0.8 to 0.8
- errors: bfloat16 [32, 3, 320, 960], P(('dp', 'group')), may hold values from -0.59765625 to 0.59765625
- q_init: float32 [3, 960, 32], replicated, may hold values from -0.1875 to 0.1875
- owners: int32 [3], replicated, may hold values from 0 to 31, as said below
- buckets: int32 [3], replicated, may hold values from 0 to 3
- learn_rates: float32 [4], replicated, may hold values from 0.2 to 1
- beta_values: float32 [4], replicated, may hold values from 0.5 to 0.95
- momentum: bfloat16 [64, 320, 960], P(('dp', 'group')), may hold values from -3 to 3
Outputs:
- new_errors: bfloat16 [32, 3, 320, 960], P(('dp', 'group'))
- weight_steps: bfloat16 [32, 3, 320, 960], P(('dp', 'group'))
- new_momentum: bfloat16 [64, 320, 960], P(('dp', 'group'))
Inputs may be any that keep to these rules, and one draw needn't show every extreme that they name: `owners`: no device owns more than 2 matrices, and some device owns exactly 2.
All inputs are finite; a program needn't handle non-finite values.
Results may differ from a plain program's by a relative error of at most 0.001.
Values may be sent and summed in bfloat16 or wider, within the bound.
No kernel may reach another device: no remote copies, remote signals or barrier semaphores. Data moves between devices by JAX's collectives and lax.ppermute only.
A program may use at most 64 MiB of HBM per device.

v0:
```python
import jax
import jax.numpy as jnp
from jax import lax
from jax.sharding import PartitionSpec as P


def from_root(value, axis, source):
    kept = jnp.where(lax.axis_index(axis) == source, value, 0).astype(value.dtype)
    return lax.psum(kept, axis)


def on_device(gradients, errors, q_init, owners, buckets, learn_rates, beta_values, momentum):
    highest = lax.Precision.HIGHEST
    slot_count = momentum.shape[0]
    mat_count = owners.shape[0]
    bucket_count = learn_rates.shape[0]
    my_index = lax.axis_index(("dp", "group"))
    positions = jnp.arange(mat_count, dtype=jnp.int32)
    earlier = (owners[None, :] == owners[:, None]) & (positions[None, :] < positions[:, None])
    slot_list = jnp.sum(earlier.astype(jnp.int32), axis=1)
    bucket_hits = buckets[:, None] == jnp.arange(bucket_count, dtype=jnp.int32)[None, :]
    rate_list = jnp.sum(jnp.where(bucket_hits, learn_rates[None, :], 0.0), axis=1)
    beta_list = jnp.sum(jnp.where(bucket_hits, beta_values[None, :], 0.0), axis=1)
    merged = gradients[0] + errors[0].astype(jnp.float32)
    p_local = jnp.einsum("mkd,mdr->mkr", merged, q_init, precision=highest)
    p_sum = lax.psum(p_local, ("dp", "group"))
    gram_matrix = jnp.einsum("mkr,mks->mrs", p_sum, p_sum, precision=highest)
    lower_factor = jnp.linalg.cholesky(gram_matrix)
    p_hat = lax.linalg.triangular_solve(
        lower_factor, p_sum, left_side=False, lower=True, transpose_a=True
    )
    q_local = jnp.einsum("mkd,mkr->mdr", merged, p_hat, precision=highest)
    q_sum = lax.psum(q_local, ("dp", "group"))
    approx = jnp.einsum("mkr,mdr->mkd", p_hat, q_local, precision=highest)
    new_errors = (merged - approx).astype(jnp.bfloat16)
    update = jnp.einsum("mkr,mdr->mkd", p_hat, q_sum, precision=highest)
    slot_range = jnp.arange(slot_count, dtype=jnp.int32)
    new_slab = jnp.zeros(momentum.shape, jnp.float32)
    step_list = []
    for matrix in range(mat_count):
        old_state = lax.dynamic_index_in_dim(momentum, slot_list[matrix], 0, keepdims=False).astype(
            jnp.float32
        )
        mom_new = beta_list[matrix] * old_state + update[matrix]
        step_value = (-rate_list[matrix] * (update[matrix] + beta_list[matrix] * mom_new)).astype(
            jnp.bfloat16
        )
        step_value = from_root(step_value, ("dp", "group"), owners[matrix])
        step_list.append(step_value)
        selected = (slot_range == slot_list[matrix]) & (owners[matrix] == my_index)
        new_slab = new_slab + jnp.where(selected[:, None, None], mom_new[None], 0.0)
    return (new_errors[None], jnp.stack(step_list)[None], new_slab.astype(jnp.bfloat16))


def solution(mesh):
    placed = (
        P(("dp", "group"), None, None, None),
        P(("dp", "group"), None, None, None),
        P(),
        P(),
        P(),
        P(),
        P(),
        P(("dp", "group"), None, None),
    )
    return jax.shard_map(
        on_device,
        mesh=mesh,
        in_specs=placed,
        out_specs=(
            P(("dp", "group"), None, None, None),
            P(("dp", "group"), None, None, None),
            P(("dp", "group"), None, None),
        ),
        check_vma=False,
    )
```

profile of v0, /device:TPU:0, one launch (start us, length us, event | category | flops | bytes accessed | tf_op | source)
XLA Modules:
  0.0 456.5 jit_solution(16836187007871859211)
XLA Ops:
  7.2 0.0 copy-start
  7.2 0.0 all-reduce.5.cloned.1.call-start
  7.2 0.9 copy-done
  8.2 7.3 %fusion.2 = f32[3,320,32]{1,2,0:T(8,128)} fusion(f32[3,960,32]{1,2,0:T(8,128)S(1)} %copy-done, f32[1,3,320,960]{3,2,1,0:T(8,128)} %param.8, bf16[1,3,320,960]{3,2,1,0:T(8,128)(2,1)} %param.9), kind=kOutput, calls=%fused_computation.3 | convolution fusion | flops 355737600 | bytes 6021120 | tf_op jit(solution)/shard_map/mkd,mdr->mkr/dot_general | solution.py:25
  15.5 0.0 all-reduce.5.cloned.1.call-update
  15.5 0.2 convert_reduce_fusion
  15.7 0.7 fusion.28
  20.2 0.6 fusion.29
  24.7 114.3 %all-reduce.5.cloned.1.call-done = f32[3,320,32]{1,2,0:T(8,128)} async-done(((f32[3,320,32]{1,2,0:T(8,128)}), f32[3,320,32]{1,2,0:T(8,128)}) %all-reduce.5.cloned.1.call-update) | async-done | bytes 122896 | tf_op jit(solution)/shard_map/psum | solution.py:26
  139.0 1.3 fusion.32
  140.3 0.1 copy.13
  140.4 8.8 %custom-call.7 = f32[3,32,32]{2,1,0:T(8,128)S(1)} custom-call(f32[3,32,32]{2,1,0:T(8,128)S(1)} %fusion.26), custom_call_target="Cholesky" | custom-call | tf_op jit(solution)/shard_map/jit(cholesky)/cholesky | solution.py:28
  149.2 0.1 compare_reduce_fusion
  149.3 0.1 select_bitcast_fusion
  149.4 7.4 %custom-call.8 = f32[3,1,32,32]{2,3,1,0:T(8,128)S(1)} custom-call(f32[3,1,32,32]{3,2,1,0:T(8,128)S(1)} %select_bitcast_fusion), custom_call_target="InvertDiagBlocksLowerTriangular" | custom-call | tf_op jit(solution)/shard_map/triangular_solve | solution.py:29
  156.8 1.3 fusion.24
  158.1 4.8 %fusion = f32[3,960,32]{1,2,0:T(8,128)S(1)} fusion(f32[3,320,32]{1,2,0:T(8,128)S(1)} %fusion.24, f32[1,3,320,960]{3,2,1,0:T(8,128)} %param.8, bf16[1,3,320,960]{3,2,1,0:T(8,128)(2,1)S(1)} %copy-done.2), kind=kOutput, calls=%fused_computation.1 | convolution fusion | flops 355737600 | bytes 6021120 | tf_op jit(solution)/shard_map/mkd,mkr->mdr/dot_general | solution.py:32
  162.9 6.3 %fusion.5 = bf16[1,3,320,960]{3,2,1,0:T(8,128)(2,1)} fusion(f32[3,320,32]{1,2,0:T(8,128)S(1)} %fusion.24, f32[3,960,32]{1,2,0:T(8,128)S(1)} %fusion, f32[1,3,320,960]{3,2,1,0:T(8,128)} %param.8, bf16[1,3,320,960]{3,2,1,0:T(8,128)(2,1)S(1)} %copy-done.2), kind=kOutput, calls=%fused_computation.9 | convolution fusion | flops 357580800 | bytes 7864320 | tf_op jit(solution)/shard_map/mkr,mdr->mkd/dot_general | solution.py:34
  169.3 0.7 all-reduce.7.cloned.1.call-update
  170.0 0.2 all-reduce.9.cloned.1.call-start
  170.2 0.2 select_reduce_fusion.2
  170.4 0.7 fusion.30
  174.9 130.5 %all-reduce.7.cloned.1.call-done = f32[3,960,32]{1,2,0:T(8,128)} async-done(((f32[3,960,32]{1,2,0:T(8,128)}), f32[3,960,32]{1,2,0:T(8,128)}) %all-reduce.7.cloned.1.call-update) | async-done | bytes 368656 | tf_op jit(solution)/shard_map/psum | solution.py:33
  305.4 4.3 fusion.33
  309.7 3.9 fusion.19
  313.6 0.0 all-reduce.9.cloned.1.call-update
  313.6 0.6 compare_and_fusion.2
  314.2 1.3 compare_and_fusion
  315.5 4.8 %add_bitcast_fusion.2 = (f32[320,960]{1,0:T(8,128)S(1)}, f32[320,960]{1,0:T(8,128)S(1)}, f32[320,960]{1,0:T(8,128)S(1)}) fusion(f32[3,320,960]{2,1,0:T(8,128)} %copy-done.1, f32[]{:T(128)} %bitcast.8, bf16[2,320,960]{2,1,0:T(8,128)(2,1)S(1)} %copy-done.3, s32[]{:T(128)S(6)} %select_n.55, s32[]{:T(128)S(6)} %select_n.58, f32[]{:T(128)} %bitcast.15, ...), kind=kLoop, calls=%fused_computation.27 | loop fusion | flops 2764800 | bytes 9216024 | tf_op jit(solution)/shard_map/jit(_where)/broadcast_in_dim | solution.py:51
  320.4 1.7 add_convert_fusion
  322.1 125.0 %all-reduce.9.cloned.1.call-done = (bf16[1,320,960]{2,1,0:T(8,128)(2,1)}, bf16[1,320,960]{2,1,0:T(8,128)(2,1)}, bf16[1,320,960]{2,1,0:T(8,128)(2,1)}) async-done(((bf16[1,320,960]{2,1,0:T(8,128)(2,1)}, bf16[1,320,960]{2,1,0:T(8,128)(2,1)}, bf16[1,320,960]{2,1,0:T(8,128)(2,1)}), (bf16[1,320,960]{2,1,0:T(8,128)(2,1)}, bf16[1,320,960]{2,1,0:T(8,128)(2,1)}, ...) | async-done | bytes 1843216 | tf_op jit(solution)/shard_map/psum | solution.py:9
  447.0 3.0 maximum_bitcast_fusion
  (21 shorter events, 0.1 us)
Async XLA Ops:
  7.2 1.0 copy-start
  7.2 8.3 %copy-start.5 = (s32[3]{0:T(128)S(1)}, s32[3]{0:T(128)}, u32[]{:S(2)}) copy-start(s32[3]{0:T(128)} %param.11) | copy-start | bytes 40
  7.2 131.8 %all-reduce.5.cloned.1.call-start = ((), (), s32[]{:S(2)}) async-start(), calls=%async_computation | async-start | bytes 294912 | tf_op jit(solution)/shard_map/psum | solution.py:26
  8.2 149.9 %copy-start.2 = (bf16[1,3,320,960]{3,2,1,0:T(8,128)(2,1)S(1)}, bf16[1,3,320,960]{3,2,1,0:T(8,128)(2,1)}, u32[]{:S(2)}) copy-start(bf16[1,3,320,960]{3,2,1,0:T(8,128)(2,1)} %param.9) | copy-start | bytes 5529604
  162.9 6.4 %copy-start.4 = (f32[3,960,32]{1,2,0:T(8,128)}, f32[3,960,32]{1,2,0:T(8,128)S(1)}, u32[]{:S(2)}) copy-start(f32[3,960,32]{1,2,0:T(8,128)S(1)} %fusion) | copy-start | bytes 1105924
  162.9 7.3 %copy-start.6 = (f32[4]{0:T(128)S(1)}, f32[4]{0:T(128)}, u32[]{:S(2)}) copy-start(f32[4]{0:T(128)} %param.13) | copy-start | bytes 52
  162.9 7.3 %copy-start.7 = (s32[3]{0:T(128)S(1)}, s32[3]{0:T(128)}, u32[]{:S(2)}) copy-start(s32[3]{0:T(128)} %param.12) | copy-start | bytes 40
  162.9 7.3 %copy-start.8 = (f32[4]{0:T(128)S(1)}, f32[4]{0:T(128)}, u32[]{:S(2)}) copy-start(f32[4]{0:T(128)} %param.14) | copy-start | bytes 52
  169.2 136.1 %all-reduce.7.cloned.1.call-start = ((), (), s32[]{:S(2)}) async-start(), calls=%async_computation.1 | async-start | bytes 786432 | tf_op jit(solution)/shard_map/psum | solution.py:33
  170.0 277.0 %all-reduce.9.cloned.1.call-start = ((), (), s32[]{:S(2)}) async-start(), calls=%async_computation.2 | async-start | bytes 3932160 | tf_op jit(solution)/shard_map/psum | solution.py:9
  174.9 134.8 %copy-start.3 = (bf16[2,320,960]{2,1,0:T(8,128)(2,1)S(1)}, bf16[2,320,960]{2,1,0:T(8,128)(2,1)}, u32[]{:S(2)}) copy-start(bf16[2,320,960]{2,1,0:T(8,128)(2,1)} %param.15) | copy-start | bytes 3686404
  309.7 3.9 copy-start.1
Sparse Core Ops, SparseCore 0:
  15.6 123.3 all-reduce.4
  175.9 129.3 all-reduce.6
  313.7 133.2 all-reduce.8
where the time goes:
time: 457 us
  waiting for transfers between devices  371 us (81%)
  other arithmetic  32.1 us (7%)
  between operations  25.4 us (6%)
  matrix products  25.2 us (6%)
    psum x1, waiting for transfers between devices, on_device(): q_sum = lax.psum(q_local, ('dp', 'group'))  131 us
    psum x1, waiting for transfers between devices, from_root(): return lax.psum(kept, axis)  125 us
    psum x1, waiting for transfers between devices, on_device(): p_sum = lax.psum(p_local, ('dp', 'group'))  114 us
  transfers between devices with their start and end apart: 3, of which 3 were waited for; matrix products, arithmetic and copies ran while one was open for 2% of the time, Pallas kernels for 0%

commit v1 on v0

v1 whole, which is shorter than its diff:
```python
import functools

import jax
import jax.numpy as jnp
from jax import lax
from jax.experimental import pallas as pl
from jax.experimental.pallas import tpu as pltpu
from jax.sharding import PartitionSpec as P

AXES = ("dp", "group")
F32 = jnp.float32
BF16 = jnp.bfloat16
SMEM = pl.BlockSpec(memory_space=pltpu.SMEM)


def whole(shape):
    return pl.BlockSpec(shape, lambda i: (0,) * len(shape))


def per_matrix(shape):
    return pl.BlockSpec((1,) + shape, lambda i: (i,) + (0,) * len(shape))


def split(value):
    high = value.astype(BF16)
    return high, (value - high.astype(F32)).astype(BF16)


def dot(left, right, dims):
    return lax.dot_general(left, right, (dims, ((), ())), preferred_element_type=F32)


def params():
    return pltpu.CompilerParams(dimension_semantics=("arbitrary",), vmem_limit_bytes=40 * 1024 * 1024)


def left_kernel(grad_ref, error_ref, q_ref, mine_ref, other_ref, left_ref):
    i = pl.program_id(0)
    mats = left_ref.shape[0]
    me = lax.axis_index(AXES)
    rank = q_ref.shape[1]
    merged = grad_ref[0] + error_ref[0].astype(F32)
    high, low = split(merged)
    q_both = jnp.concatenate(split(q_ref[0]), 0)
    both = dot(q_both, high, ((1,), (1,))) + dot(q_both, low, ((1,), (1,)))
    left_ref[i] = (both[:rank] + both[rank:]).reshape(left_ref.shape[1:])

    @pl.when(i == mats - 1)
    def _():
        bit = me & 1
        rows = grad_ref.shape[1]
        for m in range(mats):
            mine_ref[:, m * rows : (m + 1) * rows] = left_ref[m, bit]
            other_ref[:, m * rows : (m + 1) * rows] = left_ref[m, 1 - bit]


def gather_left(mine_ref, other_ref, left_ref, rows):
    bit = lax.axis_index(AXES) & 1
    for m in range(left_ref.shape[0]):
        left_ref[m, bit] = mine_ref[:, m * rows : (m + 1) * rows]
        left_ref[m, 1 - bit] = other_ref[:, m * rows : (m + 1) * rows]


def right_kernel(mine_ref, other_ref, grad_ref, error_ref, all_ref, k0_ref, k2_ref, s_ref, left_ref, right_ref):
    i = pl.program_id(0)
    low_bits = lax.axis_index(AXES) & 3
    rows = grad_ref.shape[1]

    @pl.when(i == 0)
    def _():
        gather_left(mine_ref, other_ref, left_ref, rows)

    merged = grad_ref[0] + error_ref[0].astype(F32)
    high, low = split(merged)
    left = left_ref[i].reshape(-1, rows)
    rank = left.shape[0]
    l_both = jnp.concatenate(split(left), 0)
    both = dot(l_both, high, ((1,), (0,))) + dot(l_both, low, ((1,), (0,)))
    total = both[:rank] + both[rank:]
    all_ref[0] = total
    right_ref[...] = total.reshape(right_ref.shape)
    k0_ref[0] = right_ref[low_bits]
    k2_ref[0] = right_ref[low_bits ^ 2]
    s_ref[0, 0] = right_ref[low_bits ^ 1]
    s_ref[1, 0] = right_ref[low_bits ^ 3]


def three(left):
    high, low = split(left)
    return jnp.concatenate([high, high, low], 0)


def three_right(right):
    high, low = split(right)
    return jnp.concatenate([high, low, high], 0)


def error_kernel(mine_ref, other_ref, grad_ref, error_ref, all_ref, new_ref, w_ref, left_ref):
    i = pl.program_id(0)
    rows = grad_ref.shape[1]

    @pl.when(i == 0)
    def _():
        gather_left(mine_ref, other_ref, left_ref, rows)

    left = left_ref[i].reshape(-1, rows)
    rank = left.shape[0]
    gram = lax.dot_general(
        left, left, (((1,), (1,)), ((), ())), precision=lax.Precision.HIGHEST, preferred_element_type=F32
    )
    lane = lax.broadcasted_iota(jnp.int32, (rank, rank), 1)
    line = lax.broadcasted_iota(jnp.int32, (rank, 1), 0)

    def eliminate(k, carry):
        gram, solved = carry
        column = jnp.sum(jnp.where(lane == k, gram, 0.0), 1, keepdims=True)
        is_k = line == k
        gram_row = jnp.sum(jnp.where(is_k, gram, 0.0), 0, keepdims=True)
        solved_row = jnp.sum(jnp.where(is_k, solved, 0.0), 0, keepdims=True)
        pivot = jnp.sum(jnp.where(is_k, column, 0.0), 0, keepdims=True)
        gram_row, solved_row = gram_row / pivot, solved_row / pivot
        return (
            jnp.where(is_k, gram_row, gram - column * gram_row),
            jnp.where(is_k, solved_row, solved - column * solved_row),
        )

    _, solved = lax.fori_loop(0, rank, eliminate, (gram, left))
    w = three(solved).T
    w_ref[0] = w
    approx = dot(w, three_right(all_ref[0]), ((1,), (0,)))
    new_ref[0] = (grad_ref[0] + error_ref[0].astype(F32) - approx).astype(BF16)


def slot_of(owners_ref, i):
    slot = jnp.int32(0)
    for j in range(owners_ref.shape[0]):
        slot += jnp.where((j < i) & (owners_ref[j] == owners_ref[i]), 1, 0).astype(jnp.int32)
    return slot


OLD_ORDER = ((0,), (4,), (2, 6), (1, 5, 3, 7))


def old_kernel(owners_ref, mom_ref, k0_ref, k4_ref, k26_ref, odd_ref):
    me = lax.axis_index(AXES)
    outs = (k0_ref, k4_ref, k26_ref, odd_ref)
    for i in range(owners_ref.shape[0]):
        own = owners_ref[i] == me
        slot = slot_of(owners_ref, i)

        @pl.when(own)
        def _():
            for out, order in zip(outs, OLD_ORDER):
                for n, position in enumerate(order):
                    out[n, i] = mom_ref[slot, position ^ (me & 7)]

        @pl.when(jnp.logical_not(own))
        def _():
            for out, order in zip(outs, OLD_ORDER):
                for n in range(len(order)):
                    out[n, i] = jnp.zeros(out.shape[2:], BF16)


def step_kernel(
    owners_ref, buckets_ref, rates_ref, betas_ref,
    r0_ref, r1_ref, r2_ref, r3_ref, w_ref, o0_ref, o4_ref, o2_ref, o6_ref, o1_ref, o5_ref, o3_ref, o7_ref,
    step_ref, mom_ref, right_ref, update_ref,
):
    i = pl.program_id(0)
    me = lax.axis_index(AXES)
    rate = rates_ref[buckets_ref[i]]
    beta = betas_ref[buckets_ref[i]]

    @pl.when(i == 0)
    def _():
        mom_ref[...] = jnp.zeros_like(mom_ref)

    for position, ref in enumerate((r0_ref, r1_ref, r2_ref, r3_ref)):
        right_ref[position ^ (me & 3)] = ref[0]
    right = three_right(right_ref[...].reshape(-1, right_ref.shape[2]))
    update_ref[...] = dot(w_ref[0], right, ((1,), (0,))).reshape(update_ref.shape)
    own = owners_ref[i] == me
    slot = slot_of(owners_ref, i)
    olds = (o0_ref, o1_ref, o2_ref, o3_ref, o4_ref, o5_ref, o6_ref, o7_ref)
    for position, ref in enumerate(olds):
        piece = position ^ (me & 7)
        update = update_ref[piece]
        mom = beta * ref[0, 0].astype(F32) + update
        step_ref[0, piece] = (-rate * (update + beta * mom)).astype(BF16)

        @pl.when(own)
        def _():
            mom_ref[slot, piece] = mom.astype(BF16)


def exchange(value, mask, count):
    return lax.ppermute(value, AXES, [(d, d ^ mask) for d in range(count)])


def total_over(value, bits, count):
    while bits:
        head, bits = bits[:2], bits[2:]
        masks = [1 << head[0]] if len(head) == 1 else [1 << head[0], 1 << head[1], (1 << head[0]) | (1 << head[1])]
        value = functools.reduce(jnp.add, [exchange(value, m, count) for m in masks], value)
    return value


def on_device(count, gradients, errors, q_init, owners, buckets, learn_rates, beta_values, momentum):
    grads, errs = gradients[0], errors[0]
    mats, rows, cols = grads.shape
    rank = q_init.shape[2]
    slots = momentum.shape[0]
    bits = list(range(count.bit_length() - 1))
    q_t = jnp.swapaxes(q_init, 1, 2)
    half, quarter, piece = rank // 2, rank // 4, rows // 8
    grad_spec = per_matrix((rows, cols))
    sds = jax.ShapeDtypeStruct

    mine, other = pl.pallas_call(
        left_kernel,
        grid=(mats,),
        in_specs=[grad_spec, grad_spec, per_matrix((rank, cols))],
        out_specs=[whole((half, mats * rows))] * 2,
        out_shape=[sds((half, mats * rows), F32)] * 2,
        scratch_shapes=[pltpu.VMEM((mats, 2, half, rows), F32)],
        compiler_params=params(),
        name="left",
    )(grads, errs, q_t)

    def old_shape(n):
        return (n, mats, piece, cols)

    sizes = [len(order) for order in OLD_ORDER]
    k0, k4, k26, odd = pl.pallas_call(
        old_kernel,
        grid=(1,),
        in_specs=[SMEM, whole((slots, 8, piece, cols))],
        out_specs=[whole(old_shape(n)) for n in sizes],
        out_shape=[sds(old_shape(n), BF16) for n in sizes],
        compiler_params=params(),
        name="old",
    )(owners, momentum.reshape(slots, 8, piece, cols))

    got = exchange(odd, 1, count)
    got2 = exchange(k26 + got[2:], 2, count)
    k0, k4 = k0 + got[0:1] + got2[0:1], k4 + got[1:2] + got2[1:2]
    v0 = k0 + exchange(k4, 4, count)
    for bit in bits[3:]:
        v0 = v0 + exchange(v0, 1 << bit, count)
    v4 = exchange(v0, 4, count)
    v2 = exchange(v0, 2, count)
    v6 = exchange(v4, 2, count)
    v1, v5, v3, v7 = (exchange(v, 1, count) for v in (v0, v4, v2, v6))

    mine = mine + exchange(other, 1, count)
    mine = total_over(mine, bits[1:], count)
    other = exchange(mine, 1, count)

    right_all, keep, send2, send = pl.pallas_call(
        right_kernel,
        grid=(mats,),
        in_specs=[whole((half, mats * rows))] * 2 + [grad_spec, grad_spec],
        out_specs=[
            per_matrix((rank, cols)),
            per_matrix((quarter, cols)),
            per_matrix((quarter, cols)),
            pl.BlockSpec((2, 1, quarter, cols), lambda i: (0, i, 0, 0)),
        ],
        out_shape=[
            sds((mats, rank, cols), F32),
            sds((mats, quarter, cols), F32),
            sds((mats, quarter, cols), F32),
            sds((2, mats, quarter, cols), F32),
        ],
        scratch_shapes=[pltpu.VMEM((mats, 2, half, rows), F32), pltpu.VMEM((4, quarter, cols), F32)],
        compiler_params=params(),
        name="right",
    )(mine, other, grads, errs)

    new_errors, w = pl.pallas_call(
        error_kernel,
        grid=(mats,),
        in_specs=[whole((half, mats * rows))] * 2 + [grad_spec, grad_spec, per_matrix((rank, cols))],
        out_specs=[grad_spec, per_matrix((rows, 3 * rank))],
        out_shape=[sds((mats, rows, cols), BF16), sds((mats, rows, 3 * rank), BF16)],
        scratch_shapes=[pltpu.VMEM((mats, 2, half, rows), F32)],
        compiler_params=params(),
        name="errors",
    )(mine, other, grads, errs, right_all)

    got = exchange(send, 1, count)
    r0 = keep + got[0] + exchange(send2 + got[1], 2, count)
    r0 = total_over(total_over(r0, bits[2:3], count), bits[3:], count)
    r2 = exchange(r0, 2, count)
    r1 = exchange(r0, 1, count)
    r3 = exchange(r2, 1, count)

    quarter_spec = per_matrix((quarter, cols))
    old_spec = pl.BlockSpec((1, 1, piece, cols), lambda i: (0, i, 0, 0))
    steps, new_mom = pl.pallas_call(
        step_kernel,
        grid=(mats,),
        in_specs=[SMEM] * 4 + [quarter_spec] * 4 + [per_matrix((rows, 3 * rank))] + [old_spec] * 8,
        out_specs=[per_matrix((8, piece, cols)), whole((slots, 8, piece, cols))],
        out_shape=[sds((mats, 8, piece, cols), BF16), sds((slots, 8, piece, cols), BF16)],
        scratch_shapes=[pltpu.VMEM((4, quarter, cols), F32), pltpu.VMEM((8, piece, cols), F32)],
        compiler_params=params(),
        name="step",
    )(owners, buckets, learn_rates, beta_values, r0, r1, r2, r3, w, v0, v4, v2, v6, v1, v5, v3, v7)
    return (new_errors[None], steps.reshape(1, mats, rows, cols), new_mom.reshape(momentum.shape))


def solution(mesh):
    count = mesh.shape["dp"] * mesh.shape["group"]
    rep = P(AXES, None, None, None)
    return jax.shard_map(
        functools.partial(on_device, count),
        mesh=mesh,
        in_specs=(rep, rep, P(), P(), P(), P(), P(), P(AXES, None, None)),
        out_specs=(rep, rep, P(AXES, None, None)),
        check_vma=False,
    )
```

time: 457 us -> 98.6 us (0.22)
  waiting for transfers between devices: 371 us -> 42.8 us
  other arithmetic: 32.1 us -> 0.39 us
  starting transfers between devices: 0.26 us -> 29.2 us
  matrix products: 25.2 us -> 0 us
  between operations: 25.4 us -> 0.82 us
  Pallas kernels: 0 us -> 21 us
    psum x3 -> x0, waiting for transfers between devices: 370 us -> none  [the longest x1 131 us: on_device(): q_sum = lax.psum(q_local, ('dp', 'group'))]
    ppermute x0 -> x29, waiting for transfers between devices: none -> 42.8 us  [exchange(): return lax.ppermute(value, AXES, [(d, d ^ mask) for d in range(count)])]
    ppermute x0 -> x29, starting transfers between devices: none -> 29.2 us  [exchange(): return lax.ppermute(value, AXES, [(d, d ^ mask) for d in range(count)])]
    dot_general x5 -> x0, matrix products: 24 us -> none  [the longest x1 7.29 us: on_device(): p_local = jnp.einsum('mkd,mdr->mkr', merged, q_init, precision=highest)]
    pallas_call x0 -> x5, Pallas kernels: none -> 21 us  [the longest x1 12.7 us: on_device(): pl.pallas_call(error_kernel, grid=(mats,), in_specs=[whole((half, mats *...]
    another operation x8 -> x0, other arithmetic: 20.3 us -> none  [the longest x4 8.96 us: on_device(): lower_factor = jnp.linalg.cholesky(gram_matrix)]
    broadcast_in_dim x2 -> x0, other arithmetic: 7.82 us -> none  [the longest x1 4.84 us: on_device(): new_slab = new_slab + jnp.where(selected[:, None, None], mom_new[None], 0.0)]
  transfers between devices with their start and end apart: 3 -> 29, of which waited for: 3 -> 15; matrix products, arithmetic and copies ran while one was open for 2% -> 0% of each run, Pallas kernels for 0% -> 16%
where the time goes in v1:
time: 98.6 us; the launch traced here: 98.4 us
  waiting for transfers between devices  42.8 us (43%)
  starting transfers between devices  29.2 us (30%)
  Pallas kernels  21 us (21%)
  local copies, waits for them, and re-layouts  4.24 us (4%)
    ppermute x29, waiting for transfers between devices, exchange(): return lax.ppermute(value, AXES, [(d, d ^ mask) for d in range(count)])  42.8 us
    ppermute x29, starting transfers between devices, exchange(): return lax.ppermute(value, AXES, [(d, d ^ mask) for d in range(count)])  29.2 us
    pallas_call x1, Pallas kernels, on_device(): pl.pallas_call(error_kernel, grid=(mats,), in_specs=[whole((half, mats *...  12.7 us
    unnamed x18, local copies, waits for them, and re-layouts  4.24 us
    pallas_call x1, Pallas kernels, on_device(): pl.pallas_call(step_kernel, grid=(mats,), in_specs=[SMEM] * 4 + [quarter_...  4.13 us
  transfers between devices with their start and end apart: 29, of which 15 were waited for; matrix products, arithmetic and copies ran while one was open for 0% of the time, Pallas kernels for 16%

profile of v1, /device:TPU:0, one launch (start us, length us, event | category | flops | bytes accessed | tf_op | source)
XLA Modules:
  0.0 98.4 jit_solution(17997754314513029383)
XLA Ops:
  0.7 1.4 %copy-done.2 = bf16[2,320,960]{2,1,0:T(8,128)(2,1)S(1)} copy-done((bf16[2,320,960]{2,1,0:T(8,128)(2,1)S(1)}, bf16[2,320,960]{2,1,0:T(8,128)(2,1)}, u32[]{:S(2)}) %copy-start.2) | copy-done | bytes 1228824
  4.0 2.2 %collective-permute-done.17 = bf16[4,3,40,960]{3,2,1,0:T(8,128)(2,1)S(1)} collective-permute-done((bf16[4,3,40,960]{3,2,1,0:T(8,128)(2,1)S(1)}, bf16[4,3,40,960]{3,2,1,0:T(8,128)(2,1)S(1)}, u32[]{:S(2)}, u32[]{:S(2)}) %collective-permute-start.17) | collective-permute-done | bytes 921632 | tf_op jit(solution)/shard_map/ppermute | solution.py:197
  6.3 2.9 %collective-permute-start.18 = (bf16[2,3,40,960]{3,2,1,0:T(8,128)(2,1)S(1)}, bf16[2,3,40,960]{3,2,1,0:T(8,128)(2,1)S(1)}, u32[]{:S(2)}, u32[]{:S(2)}) collective-permute-start(bf16[2,3,40,960]{3,2,1,0:T(8,128)(2,1)S(1)} %slice_add_fusion), channel_id=1, source_target_pairs={{0,2},{1,3},{2,0},{3,1},{4,6},{5,7},{6,4},{7,5},{8,10},{9,11},{10,... | collective-permute-start | bytes 1382408 | tf_op jit(solution)/shard_map/ppermute | solution.py:197
  9.2 2.1 %copy-done = f32[1,3,320,960]{3,2,1,0:T(8,128)S(1)} copy-done((f32[1,3,320,960]{3,2,1,0:T(8,128)S(1)}, f32[1,3,320,960]{3,2,1,0:T(8,128)}, u32[]{:S(2)}) %copy-start) | copy-done | bytes 3686424
  11.3 1.7 %left.1 = (f32[16,960]{1,0:T(8,128)S(1)}, f32[16,960]{1,0:T(8,128)S(1)}) custom-call(f32[3,320,960]{2,1,0:T(8,128)S(1)} %bitcast.17, bf16[3,320,960]{2,1,0:T(8,128)(2,1)S(1)} %bitcast.20, f32[3,32,960]{2,1,0:T(8,128)S(1)} %bitcast.24), custom_call_target="tpu_custom_call" | custom-call | tf_op jit(solution)/shard_map/left/pallas_call | solution.py:219
  13.1 1.2 %collective-permute-done = f32[16,960]{1,0:T(8,128)S(1)} collective-permute-done((f32[16,960]{1,0:T(8,128)S(1)}, f32[16,960]{1,0:T(8,128)S(1)}, u32[]{:S(2)}, u32[]{:S(2)}) %collective-permute-start) | collective-permute-done | bytes 61472 | tf_op jit(solution)/shard_map/ppermute | solution.py:197
  14.3 1.6 %collective-permute-start.3 = (f32[16,960]{1,0:T(8,128)S(1)}, f32[16,960]{1,0:T(8,128)S(1)}, u32[]{:S(2)}, u32[]{:S(2)}) collective-permute-start(f32[16,960]{1,0:T(8,128)S(1)} %add.66), channel_id=1, source_target_pairs={{0,6},{1,7},{2,4},{3,5},{4,2},{5,3},{6,0},{7,1},{8,14},{9,15},{10,... | collective-permute-start | bytes 184328 | tf_op jit(solution)/shard_map/ppermute | solution.py:197
  16.0 1.9 %collective-permute-start.1 = (f32[16,960]{1,0:T(8,128)S(1)}, f32[16,960]{1,0:T(8,128)S(1)}, u32[]{:S(2)}, u32[]{:S(2)}) collective-permute-start(f32[16,960]{1,0:T(8,128)S(1)} %add.66), channel_id=1, source_target_pairs={{0,2},{1,3},{2,0},{3,1},{4,6},{5,7},{6,4},{7,5},{8,10},{9,11},{10,... | collective-permute-start | bytes 184328 | tf_op jit(solution)/shard_map/ppermute | solution.py:197
  17.9 6.1 %collective-permute-done.3 = f32[16,960]{1,0:T(8,128)S(1)} collective-permute-done((f32[16,960]{1,0:T(8,128)S(1)}, f32[16,960]{1,0:T(8,128)S(1)}, u32[]{:S(2)}, u32[]{:S(2)}) %collective-permute-start.3) | collective-permute-done | bytes 61472 | tf_op jit(solution)/shard_map/ppermute | solution.py:197
  24.0 3.7 %collective-permute-start.6 = (f32[16,960]{1,0:T(8,128)S(1)}, f32[16,960]{1,0:T(8,128)S(1)}, u32[]{:S(2)}, u32[]{:S(2)}) collective-permute-start(f32[16,960]{1,0:T(8,128)S(1)} %add_add_fusion.2), channel_id=1, source_target_pairs={{0,24},{1,25},{2,26},{3,27},{4,28},{5,29},{6,30},{7,31},{8,16},{9,... | collective-permute-start | bytes 184328 | tf_op jit(solution)/shard_map/ppermute | solution.py:197
  28.5 1.3 %collective-permute-start.19 = (bf16[1,3,40,960]{3,2,1,0:T(8,128)(2,1)S(1)}, bf16[1,3,40,960]{3,2,1,0:T(8,128)(2,1)S(1)}, u32[]{:S(2)}, u32[]{:S(2)}) collective-permute-start(bf16[1,3,40,960]{3,2,1,0:T(8,128)(2,1)S(1)} %slice_add_fusion.1), channel_id=1, source_target_pairs={{0,4},{1,5},{2,6},{3,7},{4,0},{5,1},{6,2},{7,3},{8,12},{9,13},{10,... | collective-permute-start | bytes 691208 | tf_op jit(solution)/shard_map/ppermute | solution.py:197
  30.5 2.6 %collective-permute-done.5 = f32[16,960]{1,0:T(8,128)S(1)} collective-permute-done((f32[16,960]{1,0:T(8,128)S(1)}, f32[16,960]{1,0:T(8,128)S(1)}, u32[]{:S(2)}, u32[]{:S(2)}) %collective-permute-start.5) | collective-permute-done | bytes 61472 | tf_op jit(solution)/shard_map/ppermute | solution.py:197
  33.2 1.6 %collective-permute-done.19 = bf16[1,3,40,960]{3,2,1,0:T(8,128)(2,1)S(1)} collective-permute-done((bf16[1,3,40,960]{3,2,1,0:T(8,128)(2,1)S(1)}, bf16[1,3,40,960]{3,2,1,0:T(8,128)(2,1)S(1)}, u32[]{:S(2)}, u32[]{:S(2)}) %collective-permute-start.19) | collective-permute-done | bytes 230432 | tf_op jit(solution)/shard_map/ppermute | solution.py:197
  34.9 1.5 %collective-permute-start.20 = (bf16[1,3,40,960]{3,2,1,0:T(8,128)(2,1)S(1)}, bf16[1,3,40,960]{3,2,1,0:T(8,128)(2,1)S(1)}, u32[]{:S(2)}, u32[]{:S(2)}) collective-permute-start(bf16[1,3,40,960]{3,2,1,0:T(8,128)(2,1)S(1)} %fusion), channel_id=1, source_target_pairs={{0,8},{1,9},{2,10},{3,11},{4,12},{5,13},{6,14},{7,15},{8,0},{9,1},... | collective-permute-start | bytes 691208 | tf_op jit(solution)/shard_map/ppermute | solution.py:197
  36.3 1.8 %right.1 = (f32[3,32,960]{2,1,0:T(8,128)S(1)}, f32[3,8,960]{2,1,0:T(8,128)S(1)}, f32[3,8,960]{2,1,0:T(8,128)S(1)}, f32[2,3,8,960]{3,2,1,0:T(8,128)S(1)}) custom-call(f32[16,960]{1,0:T(8,128)S(1)} %add_add_fusion.1.mine_ref, f32[16,960]{1,0:T(8,128)S(1)} %collective-permute-done.7.other_ref, f32[3,320,960]{2,1,0:T(8,128)S(1)} %bitcast.18, ...), custom_call_target="tpu_custom_call" | custom-call | tf_op jit(solution)/shard_map/right/pallas_call | solution.py:259
  38.2 3.5 %collective-permute-done.20 = bf16[1,3,40,960]{3,2,1,0:T(8,128)(2,1)S(1)} collective-permute-done((bf16[1,3,40,960]{3,2,1,0:T(8,128)(2,1)S(1)}, bf16[1,3,40,960]{3,2,1,0:T(8,128)(2,1)S(1)}, u32[]{:S(2)}, u32[]{:S(2)}) %collective-permute-start.20) | collective-permute-done | bytes 230432 | tf_op jit(solution)/shard_map/ppermute | solution.py:197
  41.7 2.3 %collective-permute-start.21 = (bf16[1,3,40,960]{3,2,1,0:T(8,128)(2,1)S(1)}, bf16[1,3,40,960]{3,2,1,0:T(8,128)(2,1)S(1)}, u32[]{:S(2)}, u32[]{:S(2)}) collective-permute-start(bf16[1,3,40,960]{3,2,1,0:T(8,128)(2,1)S(1)} %add.86), channel_id=1, source_target_pairs={{0,16},{1,17},{2,18},{3,19},{4,20},{5,21},{6,22},{7,23},{8,24},{9,... | collective-permute-start | bytes 691208 | tf_op jit(solution)/shard_map/ppermute | solution.py:197
  44.0 1.6 %collective-permute-start.9 = (f32[3,8,960]{2,1,0:T(8,128)S(1)}, f32[3,8,960]{2,1,0:T(8,128)S(1)}, u32[]{:S(2)}, u32[]{:S(2)}) collective-permute-start(f32[3,8,960]{2,1,0:T(8,128)S(1)} %fusion.1), channel_id=1, source_target_pairs={{0,2},{1,3},{2,0},{3,1},{4,6},{5,7},{6,4},{7,5},{8,10},{9,11},{10,... | collective-permute-start | bytes 276488 | tf_op jit(solution)/shard_map/ppermute | solution.py:197
  45.6 7.8 %collective-permute-done.21 = bf16[1,3,40,960]{3,2,1,0:T(8,128)(2,1)S(1)} collective-permute-done((bf16[1,3,40,960]{3,2,1,0:T(8,128)(2,1)S(1)}, bf16[1,3,40,960]{3,2,1,0:T(8,128)(2,1)S(1)}, u32[]{:S(2)}, u32[]{:S(2)}) %collective-permute-start.21) | collective-permute-done | bytes 230432 | tf_op jit(solution)/shard_map/ppermute | solution.py:197
  53.5 1.3 %collective-permute-start.22 = (bf16[1,3,40,960]{3,2,1,0:T(8,128)(2,1)S(1)}, bf16[1,3,40,960]{3,2,1,0:T(8,128)(2,1)S(1)}, u32[]{:S(2)}, u32[]{:S(2)}) collective-permute-start(bf16[1,3,40,960]{3,2,1,0:T(8,128)(2,1)S(1)} %add.87.o0_ref), channel_id=1, source_target_pairs={{0,4},{1,5},{2,6},{3,7},{4,0},{5,1},{6,2},{7,3},{8,12},{9,13},{10,... | collective-permute-start | bytes 691208 | tf_op jit(solution)/shard_map/ppermute | solution.py:197
  54.7 0.9 collective-permute-start.10
  55.6 7.1 %collective-permute-done.10 = f32[3,8,960]{2,1,0:T(8,128)S(1)} collective-permute-done((f32[3,8,960]{2,1,0:T(8,128)S(1)}, f32[3,8,960]{2,1,0:T(8,128)S(1)}, u32[]{:S(2)}, u32[]{:S(2)}) %collective-permute-start.10) | collective-permute-done | bytes 92192 | tf_op jit(solution)/shard_map/ppermute | solution.py:197
  63.6 3.7 %collective-permute-start.11 = (f32[3,8,960]{2,1,0:T(8,128)S(1)}, f32[3,8,960]{2,1,0:T(8,128)S(1)}, u32[]{:S(2)}, u32[]{:S(2)}) collective-permute-start(f32[3,8,960]{2,1,0:T(8,128)S(1)} %add.76), channel_id=1, source_target_pairs={{0,8},{1,9},{2,10},{3,11},{4,12},{5,13},{6,14},{7,15},{8,0},{9,1},... | collective-permute-start | bytes 276488 | tf_op jit(solution)/shard_map/ppermute | solution.py:197
  67.3 1.5 %collective-permute-start.23 = (bf16[1,3,40,960]{3,2,1,0:T(8,128)(2,1)S(1)}, bf16[1,3,40,960]{3,2,1,0:T(8,128)(2,1)S(1)}, u32[]{:S(2)}, u32[]{:S(2)}) collective-permute-start(bf16[1,3,40,960]{3,2,1,0:T(8,128)(2,1)S(1)} %add.87.o0_ref), channel_id=1, source_target_pairs={{0,2},{1,3},{2,0},{3,1},{4,6},{5,7},{6,4},{7,5},{8,10},{9,11},{10,... | collective-permute-start | bytes 691208 | tf_op jit(solution)/shard_map/ppermute | solution.py:197
  70.1 1.2 %collective-permute-done.12 = f32[3,8,960]{2,1,0:T(8,128)S(1)} collective-permute-done((f32[3,8,960]{2,1,0:T(8,128)S(1)}, f32[3,8,960]{2,1,0:T(8,128)S(1)}, u32[]{:S(2)}, u32[]{:S(2)}) %collective-permute-start.12) | collective-permute-done | bytes 92192 | tf_op jit(solution)/shard_map/ppermute | solution.py:197
  71.4 1.6 %collective-permute-start.15 = (f32[3,8,960]{2,1,0:T(8,128)S(1)}, f32[3,8,960]{2,1,0:T(8,128)S(1)}, u32[]{:S(2)}, u32[]{:S(2)}) collective-permute-start(f32[3,8,960]{2,1,0:T(8,128)S(1)} %add_add_fusion.r0_ref), channel_id=1, source_target_pairs={{0,2},{1,3},{2,0},{3,1},{4,6},{5,7},{6,4},{7,5},{8,10},{9,11},{10,... | collective-permute-start | bytes 276488 | tf_op jit(solution)/shard_map/ppermute | solution.py:197
  73.4 2.7 %collective-permute-done.23.o2_ref = bf16[1,3,40,960]{3,2,1,0:T(8,128)(2,1)S(1)} collective-permute-done((bf16[1,3,40,960]{3,2,1,0:T(8,128)(2,1)S(1)}, bf16[1,3,40,960]{3,2,1,0:T(8,128)(2,1)S(1)}, u32[]{:S(2)}, u32[]{:S(2)}) %collective-permute-start.23) | collective-permute-done | bytes 230432 | tf_op jit(solution)/shard_map/ppermute | solution.py:197
  76.1 2.8 %collective-permute-done.24.o6_ref = bf16[1,3,40,960]{3,2,1,0:T(8,128)(2,1)S(1)} collective-permute-done((bf16[1,3,40,960]{3,2,1,0:T(8,128)(2,1)S(1)}, bf16[1,3,40,960]{3,2,1,0:T(8,128)(2,1)S(1)}, u32[]{:S(2)}, u32[]{:S(2)}) %collective-permute-start.24) | collective-permute-done | bytes 230432 | tf_op jit(solution)/shard_map/ppermute | solution.py:197
  79.0 1.0 %collective-permute-done.15.r2_ref = f32[3,8,960]{2,1,0:T(8,128)S(1)} collective-permute-done((f32[3,8,960]{2,1,0:T(8,128)S(1)}, f32[3,8,960]{2,1,0:T(8,128)S(1)}, u32[]{:S(2)}, u32[]{:S(2)}) %collective-permute-start.15) | collective-permute-done | bytes 92192 | tf_op jit(solution)/shard_map/ppermute | solution.py:197
  80.0 1.3 %collective-permute-done.14.r1_ref = f32[3,8,960]{2,1,0:T(8,128)S(1)} collective-permute-done((f32[3,8,960]{2,1,0:T(8,128)S(1)}, f32[3,8,960]{2,1,0:T(8,128)S(1)}, u32[]{:S(2)}, u32[]{:S(2)}) %collective-permute-start.14) | collective-permute-done | bytes 92192 | tf_op jit(solution)/shard_map/ppermute | solution.py:197
  81.5 12.7 %errors.1 = (bf16[3,320,960]{2,1,0:T(8,128)(2,1)}, bf16[3,320,96]{2,1,0:T(8,128)(2,1)S(1)}) custom-call(f32[16,960]{1,0:T(8,128)S(1)} %add_add_fusion.1.mine_ref, f32[16,960]{1,0:T(8,128)S(1)} %collective-permute-done.7.other_ref, f32[3,320,960]{2,1,0:T(8,128)S(1)} %bitcast.19, bf16[3,320,960]{2,1,0:T(8,128)(2,1)S(1)} %bitcast.22, ...), custom_call_target="tpu_custom_call" | custom-call | tf_op jit(solution)/shard_map/errors/pallas_call | solution.py:280
  94.3 4.1 %step.1 = (bf16[3,8,40,960]{3,2,1,0:T(8,128)(2,1)}, bf16[2,8,40,960]{3,2,1,0:T(8,128)(2,1)}) custom-call(s32[3]{0:T(128)S(1)} %copy-done.5, s32[3]{0:T(128)S(1)} %copy-done.6, f32[4]{0:T(128)S(1)} %copy-done.7, f32[4]{0:T(128)S(1)} %copy-done.8, f32[3,8,960]{2,1,0:T(8,128)S(1)} %add_add_fusion.r0_ref, f32[3,8,960]{2,1,0:T(8,128)S(1)} %collective-permute-done.14.r1_ref, ...), custom_call_target="tpu_custom_call" | custom-call | tf_op jit(solution)/shard_map/step/pallas_call | solution.py:300
  (61 shorter events, 6.8 us)
Async XLA Ops:
  3.5 2.7 %collective-permute-start.17 = (bf16[4,3,40,960]{3,2,1,0:T(8,128)(2,1)S(1)}, bf16[4,3,40,960]{3,2,1,0:T(8,128)(2,1)S(1)}, u32[]{:S(2)}, u32[]{:S(2)}) collective-permute-start(bf16[4,3,40,960]{3,2,1,0:T(8,128)(2,1)S(1)} %get-tuple-element.26), channel_id=1, source_target_pairs={{0,1},{1,0},{2,3},{3,2},{4,5},{5,4},{6,7},{7,6},{8,9},{9,8},{10,11... | collective-permute-start | bytes 2764808 | tf_op jit(solution)/shard_map/ppermute | solution.py:197
  6.3 22.2 %collective-permute-start.18 = (bf16[2,3,40,960]{3,2,1,0:T(8,128)(2,1)S(1)}, bf16[2,3,40,960]{3,2,1,0:T(8,128)(2,1)S(1)}, u32[]{:S(2)}, u32[]{:S(2)}) collective-permute-start(bf16[2,3,40,960]{3,2,1,0:T(8,128)(2,1)S(1)} %slice_add_fusion), channel_id=1, source_target_pairs={{0,2},{1,3},{2,0},{3,1},{4,6},{5,7},{6,4},{7,5},{8,10},{9,11},{10,... | collective-permute-start | bytes 1382408 | tf_op jit(solution)/shard_map/ppermute | solution.py:197
  13.0 1.3 %collective-permute-start = (f32[16,960]{1,0:T(8,128)S(1)}, f32[16,960]{1,0:T(8,128)S(1)}, u32[]{:S(2)}, u32[]{:S(2)}) collective-permute-start(f32[16,960]{1,0:T(8,128)S(1)} %get-tuple-element.18), channel_id=1, source_target_pairs={{0,1},{1,0},{2,3},{3,2},{4,5},{5,4},{6,7},{7,6},{8,9},{9,8},{10,11... | collective-permute-start | bytes 184328 | tf_op jit(solution)/shard_map/ppermute | solution.py:197
  14.3 9.7 %collective-permute-start.3 = (f32[16,960]{1,0:T(8,128)S(1)}, f32[16,960]{1,0:T(8,128)S(1)}, u32[]{:S(2)}, u32[]{:S(2)}) collective-permute-start(f32[16,960]{1,0:T(8,128)S(1)} %add.66), channel_id=1, source_target_pairs={{0,6},{1,7},{2,4},{3,5},{4,2},{5,3},{6,0},{7,1},{8,14},{9,15},{10,... | collective-permute-start | bytes 184328 | tf_op jit(solution)/shard_map/ppermute | solution.py:197
  15.9 8.1 %collective-permute-start.2 = (f32[16,960]{1,0:T(8,128)S(1)}, f32[16,960]{1,0:T(8,128)S(1)}, u32[]{:S(2)}, u32[]{:S(2)}) collective-permute-start(f32[16,960]{1,0:T(8,128)S(1)} %add.66), channel_id=1, source_target_pairs={{0,4},{1,5},{2,6},{3,7},{4,0},{5,1},{6,2},{7,3},{8,12},{9,13},{10,... | collective-permute-start | bytes 184328 | tf_op jit(solution)/shard_map/ppermute | solution.py:197
  16.0 8.0 %collective-permute-start.1 = (f32[16,960]{1,0:T(8,128)S(1)}, f32[16,960]{1,0:T(8,128)S(1)}, u32[]{:S(2)}, u32[]{:S(2)}) collective-permute-start(f32[16,960]{1,0:T(8,128)S(1)} %add.66), channel_id=1, source_target_pairs={{0,2},{1,3},{2,0},{3,1},{4,6},{5,7},{6,4},{7,5},{8,10},{9,11},{10,... | collective-permute-start | bytes 184328 | tf_op jit(solution)/shard_map/ppermute | solution.py:197
  24.0 6.4 %collective-permute-start.6 = (f32[16,960]{1,0:T(8,128)S(1)}, f32[16,960]{1,0:T(8,128)S(1)}, u32[]{:S(2)}, u32[]{:S(2)}) collective-permute-start(f32[16,960]{1,0:T(8,128)S(1)} %add_add_fusion.2), channel_id=1, source_target_pairs={{0,24},{1,25},{2,26},{3,27},{4,28},{5,29},{6,30},{7,31},{8,16},{9,... | collective-permute-start | bytes 184328 | tf_op jit(solution)/shard_map/ppermute | solution.py:197
  27.7 5.4 %collective-permute-start.5 = (f32[16,960]{1,0:T(8,128)S(1)}, f32[16,960]{1,0:T(8,128)S(1)}, u32[]{:S(2)}, u32[]{:S(2)}) collective-permute-start(f32[16,960]{1,0:T(8,128)S(1)} %add_add_fusion.2), channel_id=1, source_target_pairs={{0,16},{1,17},{2,18},{3,19},{4,20},{5,21},{6,22},{7,23},{8,24},{9,... | collective-permute-start | bytes 184328 | tf_op jit(solution)/shard_map/ppermute | solution.py:197
  27.7 5.4 %collective-permute-start.4 = (f32[16,960]{1,0:T(8,128)S(1)}, f32[16,960]{1,0:T(8,128)S(1)}, u32[]{:S(2)}, u32[]{:S(2)}) collective-permute-start(f32[16,960]{1,0:T(8,128)S(1)} %add_add_fusion.2), channel_id=1, source_target_pairs={{0,8},{1,9},{2,10},{3,11},{4,12},{5,13},{6,14},{7,15},{8,0},{9,1},... | collective-permute-start | bytes 184328 | tf_op jit(solution)/shard_map/ppermute | solution.py:197
  28.5 6.3 %collective-permute-start.19 = (bf16[1,3,40,960]{3,2,1,0:T(8,128)(2,1)S(1)}, bf16[1,3,40,960]{3,2,1,0:T(8,128)(2,1)S(1)}, u32[]{:S(2)}, u32[]{:S(2)}) collective-permute-start(bf16[1,3,40,960]{3,2,1,0:T(8,128)(2,1)S(1)} %slice_add_fusion.1), channel_id=1, source_target_pairs={{0,4},{1,5},{2,6},{3,7},{4,0},{5,1},{6,2},{7,3},{8,12},{9,13},{10,... | collective-permute-start | bytes 691208 | tf_op jit(solution)/shard_map/ppermute | solution.py:197
  33.1 3.2 %collective-permute-start.7 = (f32[16,960]{1,0:T(8,128)S(1)}, f32[16,960]{1,0:T(8,128)S(1)}, u32[]{:S(2)}, u32[]{:S(2)}) collective-permute-start(f32[16,960]{1,0:T(8,128)S(1)} %add_add_fusion.1.mine_ref), channel_id=1, source_target_pairs={{0,1},{1,0},{2,3},{3,2},{4,5},{5,4},{6,7},{7,6},{8,9},{9,8},{10,11... | collective-permute-start | bytes 184328 | tf_op jit(solution)/shard_map/ppermute | solution.py:197
  34.9 6.8 %collective-permute-start.20 = (bf16[1,3,40,960]{3,2,1,0:T(8,128)(2,1)S(1)}, bf16[1,3,40,960]{3,2,1,0:T(8,128)(2,1)S(1)}, u32[]{:S(2)}, u32[]{:S(2)}) collective-permute-start(bf16[1,3,40,960]{3,2,1,0:T(8,128)(2,1)S(1)} %fusion), channel_id=1, source_target_pairs={{0,8},{1,9},{2,10},{3,11},{4,12},{5,13},{6,14},{7,15},{8,0},{9,1},... | collective-permute-start | bytes 691208 | tf_op jit(solution)/shard_map/ppermute | solution.py:197
  38.1 6.0 %collective-permute-start.8 = (f32[2,3,8,960]{3,2,1,0:T(8,128)S(1)}, f32[2,3,8,960]{3,2,1,0:T(8,128)S(1)}, u32[]{:S(2)}, u32[]{:S(2)}) collective-permute-start(f32[2,3,8,960]{3,2,1,0:T(8,128)S(1)} %get-tuple-element.22), channel_id=1, source_target_pairs={{0,1},{1,0},{2,3},{3,2},{4,5},{5,4},{6,7},{7,6},{8,9},{9,8},{10,11... | collective-permute-start | bytes 552968 | tf_op jit(solution)/shard_map/ppermute | solution.py:197
  41.7 11.7 %collective-permute-start.21 = (bf16[1,3,40,960]{3,2,1,0:T(8,128)(2,1)S(1)}, bf16[1,3,40,960]{3,2,1,0:T(8,128)(2,1)S(1)}, u32[]{:S(2)}, u32[]{:S(2)}) collective-permute-start(bf16[1,3,40,960]{3,2,1,0:T(8,128)(2,1)S(1)} %add.86), channel_id=1, source_target_pairs={{0,16},{1,17},{2,18},{3,19},{4,20},{5,21},{6,22},{7,23},{8,24},{9,... | collective-permute-start | bytes 691208 | tf_op jit(solution)/shard_map/ppermute | solution.py:197
  44.0 10.7 %collective-permute-start.9 = (f32[3,8,960]{2,1,0:T(8,128)S(1)}, f32[3,8,960]{2,1,0:T(8,128)S(1)}, u32[]{:S(2)}, u32[]{:S(2)}) collective-permute-start(f32[3,8,960]{2,1,0:T(8,128)S(1)} %fusion.1), channel_id=1, source_target_pairs={{0,2},{1,3},{2,0},{3,1},{4,6},{5,7},{6,4},{7,5},{8,10},{9,11},{10,... | collective-permute-start | bytes 276488 | tf_op jit(solution)/shard_map/ppermute | solution.py:197
  53.5 15.3 %collective-permute-start.22 = (bf16[1,3,40,960]{3,2,1,0:T(8,128)(2,1)S(1)}, bf16[1,3,40,960]{3,2,1,0:T(8,128)(2,1)S(1)}, u32[]{:S(2)}, u32[]{:S(2)}) collective-permute-start(bf16[1,3,40,960]{3,2,1,0:T(8,128)(2,1)S(1)} %add.87.o0_ref), channel_id=1, source_target_pairs={{0,4},{1,5},{2,6},{3,7},{4,0},{5,1},{6,2},{7,3},{8,12},{9,13},{10,... | collective-permute-start | bytes 691208 | tf_op jit(solution)/shard_map/ppermute | solution.py:197
  54.7 8.0 %collective-permute-start.10 = (f32[3,8,960]{2,1,0:T(8,128)S(1)}, f32[3,8,960]{2,1,0:T(8,128)S(1)}, u32[]{:S(2)}, u32[]{:S(2)}) collective-permute-start(f32[3,8,960]{2,1,0:T(8,128)S(1)} %fusion.3), channel_id=1, source_target_pairs={{0,4},{1,5},{2,6},{3,7},{4,0},{5,1},{6,2},{7,3},{8,12},{9,13},{10,... | collective-permute-start | bytes 276488 | tf_op jit(solution)/shard_map/ppermute | solution.py:197
  62.8 7.3 %collective-permute-start.13 = (f32[3,8,960]{2,1,0:T(8,128)S(1)}, f32[3,8,960]{2,1,0:T(8,128)S(1)}, u32[]{:S(2)}, u32[]{:S(2)}) collective-permute-start(f32[3,8,960]{2,1,0:T(8,128)S(1)} %add.76), channel_id=1, source_target_pairs={{0,24},{1,25},{2,26},{3,27},{4,28},{5,29},{6,30},{7,31},{8,16},{9,... | collective-permute-start | bytes 276488 | tf_op jit(solution)/shard_map/ppermute | solution.py:197
  63.6 7.7 %collective-permute-start.12 = (f32[3,8,960]{2,1,0:T(8,128)S(1)}, f32[3,8,960]{2,1,0:T(8,128)S(1)}, u32[]{:S(2)}, u32[]{:S(2)}) collective-permute-start(f32[3,8,960]{2,1,0:T(8,128)S(1)} %add.76), channel_id=1, source_target_pairs={{0,16},{1,17},{2,18},{3,19},{4,20},{5,21},{6,22},{7,23},{8,24},{9,... | collective-permute-start | bytes 276488 | tf_op jit(solution)/shard_map/ppermute | solution.py:197
  63.6 7.7 %collective-permute-start.11 = (f32[3,8,960]{2,1,0:T(8,128)S(1)}, f32[3,8,960]{2,1,0:T(8,128)S(1)}, u32[]{:S(2)}, u32[]{:S(2)}) collective-permute-start(f32[3,8,960]{2,1,0:T(8,128)S(1)} %add.76), channel_id=1, source_target_pairs={{0,8},{1,9},{2,10},{3,11},{4,12},{5,13},{6,14},{7,15},{8,0},{9,1},... | collective-permute-start | bytes 276488 | tf_op jit(solution)/shard_map/ppermute | solution.py:197
  67.3 8.9 %collective-permute-start.23 = (bf16[1,3,40,960]{3,2,1,0:T(8,128)(2,1)S(1)}, bf16[1,3,40,960]{3,2,1,0:T(8,128)(2,1)S(1)}, u32[]{:S(2)}, u32[]{:S(2)}) collective-permute-start(bf16[1,3,40,960]{3,2,1,0:T(8,128)(2,1)S(1)} %add.87.o0_ref), channel_id=1, source_target_pairs={{0,2},{1,3},{2,0},{3,1},{4,6},{5,7},{6,4},{7,5},{8,10},{9,11},{10,... | collective-permute-start | bytes 691208 | tf_op jit(solution)/shard_map/ppermute | solution.py:197
  68.7 10.2 %collective-permute-start.24 = (bf16[1,3,40,960]{3,2,1,0:T(8,128)(2,1)S(1)}, bf16[1,3,40,960]{3,2,1,0:T(8,128)(2,1)S(1)}, u32[]{:S(2)}, u32[]{:S(2)}) collective-permute-start(bf16[1,3,40,960]{3,2,1,0:T(8,128)(2,1)S(1)} %collective-permute-done.22.o4_ref), channel_id=1, source_target_pairs={{0,2},{1,3},{2,0},{3,1},{4,6},{5,7},{6,4},{7,5},{8,10},{9,11},{10,... | collective-permute-start | bytes 691208 | tf_op jit(solution)/shard_map/ppermute | solution.py:197
  71.4 8.7 %collective-permute-start.15 = (f32[3,8,960]{2,1,0:T(8,128)S(1)}, f32[3,8,960]{2,1,0:T(8,128)S(1)}, u32[]{:S(2)}, u32[]{:S(2)}) collective-permute-start(f32[3,8,960]{2,1,0:T(8,128)S(1)} %add_add_fusion.r0_ref), channel_id=1, source_target_pairs={{0,2},{1,3},{2,0},{3,1},{4,6},{5,7},{6,4},{7,5},{8,10},{9,11},{10,... | collective-permute-start | bytes 276488 | tf_op jit(solution)/shard_map/ppermute | solution.py:197
  72.9 21.3 %collective-permute-start.25 = (bf16[1,3,40,960]{3,2,1,0:T(8,128)(2,1)S(1)}, bf16[1,3,40,960]{3,2,1,0:T(8,128)(2,1)S(1)}, u32[]{:S(2)}, u32[]{:S(2)}) collective-permute-start(bf16[1,3,40,960]{3,2,1,0:T(8,128)(2,1)S(1)} %add.87.o0_ref), channel_id=1, source_target_pairs={{0,1},{1,0},{2,3},{3,2},{4,5},{5,4},{6,7},{7,6},{8,9},{9,8},{10,11... | collective-permute-start | bytes 691208 | tf_op jit(solution)/shard_map/ppermute | solution.py:197
  72.9 21.3 %collective-permute-start.26 = (bf16[1,3,40,960]{3,2,1,0:T(8,128)(2,1)S(1)}, bf16[1,3,40,960]{3,2,1,0:T(8,128)(2,1)S(1)}, u32[]{:S(2)}, u32[]{:S(2)}) collective-permute-start(bf16[1,3,40,960]{3,2,1,0:T(8,128)(2,1)S(1)} %collective-permute-done.22.o4_ref), channel_id=1, source_target_pairs={{0,1},{1,0},{2,3},{3,2},{4,5},{5,4},{6,7},{7,6},{8,9},{9,8},{10,11... | collective-permute-start | bytes 691208 | tf_op jit(solution)/shard_map/ppermute | solution.py:197
  76.1 18.1 %collective-permute-start.27 = (bf16[1,3,40,960]{3,2,1,0:T(8,128)(2,1)S(1)}, bf16[1,3,40,960]{3,2,1,0:T(8,128)(2,1)S(1)}, u32[]{:S(2)}, u32[]{:S(2)}) collective-permute-start(bf16[1,3,40,960]{3,2,1,0:T(8,128)(2,1)S(1)} %collective-permute-done.23.o2_ref), channel_id=1, source_target_pairs={{0,1},{1,0},{2,3},{3,2},{4,5},{5,4},{6,7},{7,6},{8,9},{9,8},{10,11... | collective-permute-start | bytes 691208 | tf_op jit(solution)/shard_map/ppermute | solution.py:197
  79.0 15.3 %collective-permute-start.28 = (bf16[1,3,40,960]{3,2,1,0:T(8,128)(2,1)S(1)}, bf16[1,3,40,960]{3,2,1,0:T(8,128)(2,1)S(1)}, u32[]{:S(2)}, u32[]{:S(2)}) collective-permute-start(bf16[1,3,40,960]{3,2,1,0:T(8,128)(2,1)S(1)} %collective-permute-done.24.o6_ref), channel_id=1, source_target_pairs={{0,1},{1,0},{2,3},{3,2},{4,5},{5,4},{6,7},{7,6},{8,9},{9,8},{10,11... | collective-permute-start | bytes 691208 | tf_op jit(solution)/shard_map/ppermute | solution.py:197
  80.0 1.3 %collective-permute-start.14 = (f32[3,8,960]{2,1,0:T(8,128)S(1)}, f32[3,8,960]{2,1,0:T(8,128)S(1)}, u32[]{:S(2)}, u32[]{:S(2)}) collective-permute-start(f32[3,8,960]{2,1,0:T(8,128)S(1)} %add_add_fusion.r0_ref), channel_id=1, source_target_pairs={{0,1},{1,0},{2,3},{3,2},{4,5},{5,4},{6,7},{7,6},{8,9},{9,8},{10,11... | collective-permute-start | bytes 276488 | tf_op jit(solution)/shard_map/ppermute | solution.py:197
  81.3 12.9 %collective-permute-start.16 = (f32[3,8,960]{2,1,0:T(8,128)S(1)}, f32[3,8,960]{2,1,0:T(8,128)S(1)}, u32[]{:S(2)}, u32[]{:S(2)}) collective-permute-start(f32[3,8,960]{2,1,0:T(8,128)S(1)} %collective-permute-done.15.r2_ref), channel_id=1, source_target_pairs={{0,1},{1,0},{2,3},{3,2},{4,5},{5,4},{6,7},{7,6},{8,9},{9,8},{10,11... | collective-permute-start | bytes 276488 | tf_op jit(solution)/shard_map/ppermute | solution.py:197
  81.5 12.8 %copy-start.6 = (s32[3]{0:T(128)S(1)}, s32[3]{0:T(128)}, u32[]{:S(2)}) copy-start(s32[3]{0:T(128)} %buckets_ref.1) | copy-start | bytes 40
  81.5 12.8 %copy-start.7 = (f32[4]{0:T(128)S(1)}, f32[4]{0:T(128)}, u32[]{:S(2)}) copy-start(f32[4]{0:T(128)} %rates_ref.1) | copy-start | bytes 52
  81.5 12.8 %copy-start.8 = (f32[4]{0:T(128)S(1)}, f32[4]{0:T(128)}, u32[]{:S(2)}) copy-start(f32[4]{0:T(128)} %betas_ref.1) | copy-start | bytes 52
  (6 other events, 32.0 us)

commit v2 on v1

--- a/solution.py
+++ b/solution.py
@@ -32,6 +32,14 @@
 
 def params():
     return pltpu.CompilerParams(dimension_semantics=("arbitrary",), vmem_limit_bytes=40 * 1024 * 1024)
+
+
+def cost(mebibytes):
+    return pl.CostEstimate(flops=0, transcendentals=0, bytes_accessed=mebibytes * 1024 * 1024)
+
+
+def after(value, *others):
+    return lax.optimization_barrier((value,) + others)[0]
 
 
 def left_kernel(grad_ref, error_ref, q_ref, mine_ref, other_ref, left_ref):
@@ -95,39 +103,37 @@
     return jnp.concatenate([high, low, high], 0)
 
 
-def error_kernel(mine_ref, other_ref, grad_ref, error_ref, all_ref, new_ref, w_ref, left_ref):
-    i = pl.program_id(0)
-    rows = grad_ref.shape[1]
-
-    @pl.when(i == 0)
-    def _():
-        gather_left(mine_ref, other_ref, left_ref, rows)
-
-    left = left_ref[i].reshape(-1, rows)
-    rank = left.shape[0]
-    gram = lax.dot_general(
-        left, left, (((1,), (1,)), ((), ())), precision=lax.Precision.HIGHEST, preferred_element_type=F32
-    )
-    lane = lax.broadcasted_iota(jnp.int32, (rank, rank), 1)
-    line = lax.broadcasted_iota(jnp.int32, (rank, 1), 0)
-
-    def eliminate(k, carry):
-        gram, solved = carry
-        column = jnp.sum(jnp.where(lane == k, gram, 0.0), 1, keepdims=True)
-        is_k = line == k
-        gram_row = jnp.sum(jnp.where(is_k, gram, 0.0), 0, keepdims=True)
-        solved_row = jnp.sum(jnp.where(is_k, solved, 0.0), 0, keepdims=True)
-        pivot = jnp.sum(jnp.where(is_k, column, 0.0), 0, keepdims=True)
-        gram_row, solved_row = gram_row / pivot, solved_row / pivot
-        return (
-            jnp.where(is_k, gram_row, gram - column * gram_row),
-            jnp.where(is_k, solved_row, solved - column * solved_row),
+def solve_kernel(mine_ref, other_ref, w_ref, left_ref):
+    mats, _, half, rows = left_ref.shape
+    rank = 2 * half
+    gather_left(mine_ref, other_ref, left_ref, rows)
+    left = left_ref[...].reshape(mats, rank, rows)
+
+    def exact(x, y, contract):
+        return jnp.stack(
+            [
+                lax.dot_general(
+                    x[m], y[m], (contract, ((), ())), precision=lax.Precision.HIGHEST, preferred_element_type=F32
+                )
+                for m in range(mats)
+            ]
         )
 
-    _, solved = lax.fori_loop(0, rank, eliminate, (gram, left))
-    w = three(solved).T
-    w_ref[0] = w
-    approx = dot(w, three_right(all_ref[0]), ((1,), (0,)))
+    gram = exact(left, left, ((1,), (1,)))
+    line = lax.broadcasted_iota(jnp.int32, gram.shape, 1)
+    lane = lax.broadcasted_iota(jnp.int32, gram.shape, 2)
+    for k in range(rank):
+        inverse = 1.0 / gram[:, k : k + 1, k : k + 1]
+        row = jnp.where(lane[:, k : k + 1] == k, inverse, gram[:, k : k + 1] * inverse)
+        rest = jnp.where(lane == k, 0.0, gram) - gram[:, :, k : k + 1] * row
+        gram = jnp.where(line == k, row, rest)
+    solved = exact(gram, left, ((1,), (0,)))
+    for m in range(mats):
+        w_ref[m] = three(solved[m]).T
+
+
+def error_kernel(grad_ref, error_ref, w_ref, all_ref, new_ref):
+    approx = dot(w_ref[0], three_right(all_ref[0]), ((1,), (0,)))
     new_ref[0] = (grad_ref[0] + error_ref[0].astype(F32) - approx).astype(BF16)
 
 
@@ -138,12 +144,12 @@
     return slot
 
 
-OLD_ORDER = ((0,), (4,), (2, 6), (1, 5, 3, 7))
-
-
-def old_kernel(owners_ref, mom_ref, k0_ref, k4_ref, k26_ref, odd_ref):
+OLD_ORDER = ((0,), (2,), (4,), (6,), (1, 3, 5, 7))
+
+
+def old_kernel(owners_ref, mom_ref, k0_ref, k2_ref, k4_ref, k6_ref, odd_ref):
     me = lax.axis_index(AXES)
-    outs = (k0_ref, k4_ref, k26_ref, odd_ref)
+    outs = (k0_ref, k2_ref, k4_ref, k6_ref, odd_ref)
     for i in range(owners_ref.shape[0]):
         own = owners_ref[i] == me
         slot = slot_of(owners_ref, i)
@@ -163,7 +169,7 @@
 
 def step_kernel(
     owners_ref, buckets_ref, rates_ref, betas_ref,
-    r0_ref, r1_ref, r2_ref, r3_ref, w_ref, o0_ref, o4_ref, o2_ref, o6_ref, o1_ref, o5_ref, o3_ref, o7_ref,
+    r0_ref, r1_ref, r2_ref, r3_ref, w_ref, o0_ref, o1_ref, o2_ref, o3_ref, o4_ref, o5_ref, o6_ref, o7_ref,
     step_ref, mom_ref, right_ref, update_ref,
 ):
     i = pl.program_id(0)
@@ -231,7 +237,7 @@
         return (n, mats, piece, cols)
 
     sizes = [len(order) for order in OLD_ORDER]
-    k0, k4, k26, odd = pl.pallas_call(
+    *evens, odd = pl.pallas_call(
         old_kernel,
         grid=(1,),
         in_specs=[SMEM, whole((slots, 8, piece, cols))],
@@ -239,22 +245,19 @@
         out_shape=[sds(old_shape(n), BF16) for n in sizes],
         compiler_params=params(),
         name="old",
-    )(owners, momentum.reshape(slots, 8, piece, cols))
-
-    got = exchange(odd, 1, count)
-    got2 = exchange(k26 + got[2:], 2, count)
-    k0, k4 = k0 + got[0:1] + got2[0:1], k4 + got[1:2] + got2[1:2]
-    v0 = k0 + exchange(k4, 4, count)
-    for bit in bits[3:]:
-        v0 = v0 + exchange(v0, 1 << bit, count)
-    v4 = exchange(v0, 4, count)
-    v2 = exchange(v0, 2, count)
-    v6 = exchange(v4, 2, count)
-    v1, v5, v3, v7 = (exchange(v, 1, count) for v in (v0, v4, v2, v6))
-
-    mine = mine + exchange(other, 1, count)
-    mine = total_over(mine, bits[1:], count)
-    other = exchange(mine, 1, count)
+    )(owners, after(momentum.reshape(slots, 8, piece, cols), mine))
+
+    def swap(value, mask):
+        return exchange(value, mask, count)
+
+    got = swap(odd, 1)
+    mine = mine + swap(other, 1)
+    evens = [after(even + got[n : n + 1], mine) for n, even in enumerate(evens)]
+    mine = total_over(mine, bits[1:3], count)
+    old = evens[0] + swap(evens[1], 2) + swap(evens[2], 4) + swap(evens[3], 6)
+    old = after(old, mine)
+    mine = total_over(mine, bits[3:], count)
+    other = swap(mine, 1)
 
     right_all, keep, send2, send = pl.pallas_call(
         right_kernel,
@@ -277,23 +280,45 @@
         name="right",
     )(mine, other, grads, errs)
 
-    new_errors, w = pl.pallas_call(
+    w = pl.pallas_call(
+        solve_kernel,
+        grid=(1,),
+        in_specs=[whole((half, mats * rows))] * 2,
+        out_specs=whole((mats, rows, 3 * rank)),
+        out_shape=sds((mats, rows, 3 * rank), BF16),
+        scratch_shapes=[pltpu.VMEM((mats, 2, half, rows), F32)],
+        compiler_params=params(),
+        cost_estimate=cost(16),
+        name="solve",
+    )(mine, other)
+
+    for bit in bits[3:-1]:
+        old = old + swap(old, 1 << bit)
+    got = swap(send, 1)
+    send2 = send2 + got[1]
+    old = after(old, send2)
+    r0 = keep + got[0] + swap(send2, 2)
+    old = old + swap(old, 1 << bits[-1])
+    r0 = total_over(r0, bits[2:3], count)
+    w = after(w, r0)
+    new_errors = pl.pallas_call(
         error_kernel,
         grid=(mats,),
-        in_specs=[whole((half, mats * rows))] * 2 + [grad_spec, grad_spec, per_matrix((rank, cols))],
-        out_specs=[grad_spec, per_matrix((rows, 3 * rank))],
-        out_shape=[sds((mats, rows, cols), BF16), sds((mats, rows, 3 * rank), BF16)],
-        scratch_shapes=[pltpu.VMEM((mats, 2, half, rows), F32)],
-        compiler_params=params(),
+        in_specs=[grad_spec, grad_spec, per_matrix((rows, 3 * rank)), per_matrix((rank, cols))],
+        out_specs=grad_spec,
+        out_shape=sds((mats, rows, cols), BF16),
+        compiler_params=params(),
+        cost_estimate=cost(12),
         name="errors",
-    )(mine, other, grads, errs, right_all)
-
-    got = exchange(send, 1, count)
-    r0 = keep + got[0] + exchange(send2 + got[1], 2, count)
-    r0 = total_over(total_over(r0, bits[2:3], count), bits[3:], count)
-    r2 = exchange(r0, 2, count)
-    r1 = exchange(r0, 1, count)
-    r3 = exchange(r2, 1, count)
+    )(grads, errs, w, right_all)
+    olds = {0: after(old, r0)}
+    for mask in (2, 4, 6):
+        olds[mask] = swap(olds[0], mask)
+    r0 = total_over(r0, bits[3:], count)
+    r0 = after(r0, new_errors)
+    r1, r2, r3 = (swap(r0, mask) for mask in (1, 2, 3))
+    for mask in (0, 2, 4, 6):
+        olds[mask + 1] = swap(olds[mask], 1)
 
     quarter_spec = per_matrix((quarter, cols))
     old_spec = pl.BlockSpec((1, 1, piece, cols), lambda i: (0, i, 0, 0))
@@ -306,7 +331,7 @@
         scratch_shapes=[pltpu.VMEM((4, quarter, cols), F32), pltpu.VMEM((8, piece, cols), F32)],
         compiler_params=params(),
         name="step",
-    )(owners, buckets, learn_rates, beta_values, r0, r1, r2, r3, w, v0, v4, v2, v6, v1, v5, v3, v7)
+    )(owners, buckets, learn_rates, beta_values, r0, r1, r2, r3, w, *(olds[n] for n in range(8)))
     return (new_errors[None], steps.reshape(1, mats, rows, cols), new_mom.reshape(momentum.shape))
 
 

time: 98.6 us -> 83.3 us (0.84)
  waiting for transfers between devices: 42.8 us -> 33.3 us
  Pallas kernels: 21 us -> 14 us
    ppermute x29 -> x30, waiting for transfers between devices: 42.8 us -> 33.3 us  [exchange(): return lax.ppermute(value, AXES, [(d, d ^ mask) for d in range(count)])]
    pallas_call x1 -> x2, Pallas kernels: 12.7 us -> 5.72 us  [the longest x1 3.38 us: on_device(): pl.pallas_call(solve_kernel, grid=(1,), in_specs=[whole((half, mats * row...]
    ppermute x29 -> x30, starting transfers between devices: 29.2 us -> 29.8 us  [exchange(): return lax.ppermute(value, AXES, [(d, d ^ mask) for d in range(count)])]
  transfers between devices with their start and end apart: 29 -> 30, of which waited for: 15 -> 15; matrix products, arithmetic and copies ran while one was open for 0% -> 0% of each run, Pallas kernels for 16% -> 9%
where the time goes in v2:
time: 83.3 us; the launch traced here: 83.1 us
  waiting for transfers between devices  33.3 us (40%)
  starting transfers between devices  29.8 us (36%)
  Pallas kernels  14 us (17%)
  local copies, waits for them, and re-layouts  4.68 us (6%)
    ppermute x30, waiting for transfers between devices, exchange(): return lax.ppermute(value, AXES, [(d, d ^ mask) for d in range(count)])  33.3 us
    ppermute x30, starting transfers between devices, exchange(): return lax.ppermute(value, AXES, [(d, d ^ mask) for d in range(count)])  29.8 us
    unnamed x18, local copies, waits for them, and re-layouts  4.68 us
    pallas_call x1, Pallas kernels, on_device(): pl.pallas_call(step_kernel, grid=(mats,), in_specs=[SMEM] * 4 + [quarter_...  4.13 us
    pallas_call x1, Pallas kernels, on_device(): pl.pallas_call(solve_kernel, grid=(1,), in_specs=[whole((half, mats * row...  3.38 us
    pallas_call x1, Pallas kernels, on_device(): pl.pallas_call(error_kernel, grid=(mats,), in_specs=[grad_spec, grad_spec...  2.33 us
    pallas_call x1, Pallas kernels, on_device(): pl.pallas_call(right_kernel, grid=(mats,), in_specs=[whole((half, mats *...  1.75 us
    pallas_call x1, Pallas kernels, on_device(): pl.pallas_call(left_kernel, grid=(mats,), in_specs=[grad_spec, grad_spec,...  1.69 us
  transfers between devices with their start and end apart: 30, of which 15 were waited for; matrix products, arithmetic and copies ran while one was open for 0% of the time, Pallas kernels for 9%

profile of v2, /device:TPU:0, one launch (start us, length us, event | category | flops | bytes accessed | tf_op | source)
XLA Modules:
  0.0 83.1 jit_solution(4302524866694539884)
XLA Ops:
  0.6 2.1 %copy-done = f32[1,3,320,960]{3,2,1,0:T(8,128)S(1)} copy-done((f32[1,3,320,960]{3,2,1,0:T(8,128)S(1)}, f32[1,3,320,960]{3,2,1,0:T(8,128)}, u32[]{:S(2)}) %copy-start) | copy-done | bytes 3686424
  2.8 1.5 %copy-done.2 = bf16[1,3,320,960]{3,2,1,0:T(8,128)(2,1)S(1)} copy-done((bf16[1,3,320,960]{3,2,1,0:T(8,128)(2,1)S(1)}, bf16[1,3,320,960]{3,2,1,0:T(8,128)(2,1)}, u32[]{:S(2)}) %copy-start.2) | copy-done | bytes 1843224
  4.3 1.0 %copy-done.4 = f32[3,960,32]{1,2,0:T(8,128)S(1)} copy-done((f32[3,960,32]{1,2,0:T(8,128)S(1)}, f32[3,960,32]{1,2,0:T(8,128)}, u32[]{:S(2)}) %copy-start.4) | copy-done | bytes 368664
  5.3 1.7 %left.1 = (f32[16,960]{1,0:T(8,128)S(1)}, f32[16,960]{1,0:T(8,128)S(1)}) custom-call(f32[3,320,960]{2,1,0:T(8,128)S(1)} %bitcast.17, bf16[3,320,960]{2,1,0:T(8,128)(2,1)S(1)} %bitcast.20, f32[3,32,960]{2,1,0:T(8,128)S(1)} %bitcast.24), custom_call_target="tpu_custom_call" | custom-call | tf_op jit(solution)/shard_map/left/pallas_call | solution.py:225
  8.3 2.2 %collective-permute-done = f32[16,960]{1,0:T(8,128)S(1)} collective-permute-done((f32[16,960]{1,0:T(8,128)S(1)}, f32[16,960]{1,0:T(8,128)S(1)}, u32[]{:S(2)}, u32[]{:S(2)}) %collective-permute-start) | collective-permute-done | bytes 61472 | tf_op jit(solution)/shard_map/ppermute | solution.py:203
  10.5 3.9 %collective-permute-start.3 = (f32[16,960]{1,0:T(8,128)S(1)}, f32[16,960]{1,0:T(8,128)S(1)}, u32[]{:S(2)}, u32[]{:S(2)}) collective-permute-start(f32[16,960]{1,0:T(8,128)S(1)} %add.69), channel_id=1, source_target_pairs={{0,6},{1,7},{2,4},{3,5},{4,2},{5,3},{6,0},{7,1},{8,14},{9,15},{10,... | collective-permute-start | bytes 184328 | tf_op jit(solution)/shard_map/ppermute | solution.py:203
  15.1 1.8 %collective-permute-done.3 = f32[16,960]{1,0:T(8,128)S(1)} collective-permute-done((f32[16,960]{1,0:T(8,128)S(1)}, f32[16,960]{1,0:T(8,128)S(1)}, u32[]{:S(2)}, u32[]{:S(2)}) %collective-permute-start.3) | collective-permute-done | bytes 61472 | tf_op jit(solution)/shard_map/ppermute | solution.py:203
  16.8 1.9 %collective-permute-done.2 = f32[16,960]{1,0:T(8,128)S(1)} collective-permute-done((f32[16,960]{1,0:T(8,128)S(1)}, f32[16,960]{1,0:T(8,128)S(1)}, u32[]{:S(2)}, u32[]{:S(2)}) %collective-permute-start.2) | collective-permute-done | bytes 61472 | tf_op jit(solution)/shard_map/ppermute | solution.py:203
  19.2 3.7 %collective-permute-start.6 = (f32[16,960]{1,0:T(8,128)S(1)}, f32[16,960]{1,0:T(8,128)S(1)}, u32[]{:S(2)}, u32[]{:S(2)}) collective-permute-start(f32[16,960]{1,0:T(8,128)S(1)} %add_add_fusion.3), channel_id=1, source_target_pairs={{0,24},{1,25},{2,26},{3,27},{4,28},{5,29},{6,30},{7,31},{8,16},{9,... | collective-permute-start | bytes 184328 | tf_op jit(solution)/shard_map/ppermute | solution.py:203
  23.8 1.6 %collective-permute-start.19 = (bf16[1,3,40,960]{3,2,1,0:T(8,128)(2,1)S(1)}, bf16[1,3,40,960]{3,2,1,0:T(8,128)(2,1)S(1)}, u32[]{:S(2)}, u32[]{:S(2)}) collective-permute-start(bf16[1,3,40,960]{3,2,1,0:T(8,128)(2,1)S(1)} %get-tuple-element.41), channel_id=1, source_target_pairs={{0,4},{1,5},{2,6},{3,7},{4,0},{5,1},{6,2},{7,3},{8,12},{9,13},{10,... | collective-permute-start | bytes 691208 | tf_op jit(solution)/shard_map/ppermute | solution.py:203
  26.1 1.3 %collective-permute-start.18 = (bf16[1,3,40,960]{3,2,1,0:T(8,128)(2,1)S(1)}, bf16[1,3,40,960]{3,2,1,0:T(8,128)(2,1)S(1)}, u32[]{:S(2)}, u32[]{:S(2)}) collective-permute-start(bf16[1,3,40,960]{3,2,1,0:T(8,128)(2,1)S(1)} %get-tuple-element.39), channel_id=1, source_target_pairs={{0,2},{1,3},{2,0},{3,1},{4,6},{5,7},{6,4},{7,5},{8,10},{9,11},{10,... | collective-permute-start | bytes 691208 | tf_op jit(solution)/shard_map/ppermute | solution.py:203
  28.2 1.2 %collective-permute-done.7.other_ref = f32[16,960]{1,0:T(8,128)S(1)} collective-permute-done((f32[16,960]{1,0:T(8,128)S(1)}, f32[16,960]{1,0:T(8,128)S(1)}, u32[]{:S(2)}, u32[]{:S(2)}) %collective-permute-start.7) | collective-permute-done | bytes 61472 | tf_op jit(solution)/shard_map/ppermute | solution.py:203
  29.4 1.7 %right.1 = (f32[3,32,960]{2,1,0:T(8,128)S(1)}, f32[3,8,960]{2,1,0:T(8,128)S(1)}, f32[3,8,960]{2,1,0:T(8,128)S(1)}, f32[2,3,8,960]{3,2,1,0:T(8,128)S(1)}) custom-call(f32[16,960]{1,0:T(8,128)S(1)} %add_add_fusion.2.mine_ref, f32[16,960]{1,0:T(8,128)S(1)} %collective-permute-done.7.other_ref, f32[3,320,960]{2,1,0:T(8,128)S(1)} %bitcast.18, ...), custom_call_target="tpu_custom_call" | custom-call | tf_op jit(solution)/shard_map/right/pallas_call | solution.py:262
  31.4 3.9 %collective-permute-done.19 = bf16[1,3,40,960]{3,2,1,0:T(8,128)(2,1)S(1)} collective-permute-done((bf16[1,3,40,960]{3,2,1,0:T(8,128)(2,1)S(1)}, bf16[1,3,40,960]{3,2,1,0:T(8,128)(2,1)S(1)}, u32[]{:S(2)}, u32[]{:S(2)}) %collective-permute-start.19) | collective-permute-done | bytes 230432 | tf_op jit(solution)/shard_map/ppermute | solution.py:203
  35.2 1.3 %collective-permute-done.18 = bf16[1,3,40,960]{3,2,1,0:T(8,128)(2,1)S(1)} collective-permute-done((bf16[1,3,40,960]{3,2,1,0:T(8,128)(2,1)S(1)}, bf16[1,3,40,960]{3,2,1,0:T(8,128)(2,1)S(1)}, u32[]{:S(2)}, u32[]{:S(2)}) %collective-permute-start.18) | collective-permute-done | bytes 230432 | tf_op jit(solution)/shard_map/ppermute | solution.py:203
  36.6 1.5 %collective-permute-start.21 = (bf16[1,3,40,960]{3,2,1,0:T(8,128)(2,1)S(1)}, bf16[1,3,40,960]{3,2,1,0:T(8,128)(2,1)S(1)}, u32[]{:S(2)}, u32[]{:S(2)}) collective-permute-start(bf16[1,3,40,960]{3,2,1,0:T(8,128)(2,1)S(1)} %add_add_fusion), channel_id=1, source_target_pairs={{0,8},{1,9},{2,10},{3,11},{4,12},{5,13},{6,14},{7,15},{8,0},{9,1},... | collective-permute-start | bytes 691208 | tf_op jit(solution)/shard_map/ppermute | solution.py:203
  38.1 1.7 %collective-permute-start.9 = (f32[3,8,960]{2,1,0:T(8,128)S(1)}, f32[3,8,960]{2,1,0:T(8,128)S(1)}, u32[]{:S(2)}, u32[]{:S(2)}) collective-permute-start(f32[3,8,960]{2,1,0:T(8,128)S(1)} %fusion), channel_id=1, source_target_pairs={{0,2},{1,3},{2,0},{3,1},{4,6},{5,7},{6,4},{7,5},{8,10},{9,11},{10,... | collective-permute-start | bytes 276488 | tf_op jit(solution)/shard_map/ppermute | solution.py:203
  39.8 4.4 %collective-permute-done.21 = bf16[1,3,40,960]{3,2,1,0:T(8,128)(2,1)S(1)} collective-permute-done((bf16[1,3,40,960]{3,2,1,0:T(8,128)(2,1)S(1)}, bf16[1,3,40,960]{3,2,1,0:T(8,128)(2,1)S(1)}, u32[]{:S(2)}, u32[]{:S(2)}) %collective-permute-start.21) | collective-permute-done | bytes 230432 | tf_op jit(solution)/shard_map/ppermute | solution.py:203
  44.2 2.1 %collective-permute-start.22 = (bf16[1,3,40,960]{3,2,1,0:T(8,128)(2,1)S(1)}, bf16[1,3,40,960]{3,2,1,0:T(8,128)(2,1)S(1)}, u32[]{:S(2)}, u32[]{:S(2)}) collective-permute-start(bf16[1,3,40,960]{3,2,1,0:T(8,128)(2,1)S(1)} %add.90), channel_id=1, source_target_pairs={{0,16},{1,17},{2,18},{3,19},{4,20},{5,21},{6,22},{7,23},{8,24},{9,... | collective-permute-start | bytes 691208 | tf_op jit(solution)/shard_map/ppermute | solution.py:203
  46.3 1.3 %collective-permute-start.10 = (f32[3,8,960]{2,1,0:T(8,128)S(1)}, f32[3,8,960]{2,1,0:T(8,128)S(1)}, u32[]{:S(2)}, u32[]{:S(2)}) collective-permute-start(f32[3,8,960]{2,1,0:T(8,128)S(1)} %fusion.2), channel_id=1, source_target_pairs={{0,4},{1,5},{2,6},{3,7},{4,0},{5,1},{6,2},{7,3},{8,12},{9,13},{10,... | collective-permute-start | bytes 276488 | tf_op jit(solution)/shard_map/ppermute | solution.py:203
  47.6 3.4 %collective-permute-done.10 = f32[3,8,960]{2,1,0:T(8,128)S(1)} collective-permute-done((f32[3,8,960]{2,1,0:T(8,128)S(1)}, f32[3,8,960]{2,1,0:T(8,128)S(1)}, u32[]{:S(2)}, u32[]{:S(2)}) %collective-permute-start.10) | collective-permute-done | bytes 92192 | tf_op jit(solution)/shard_map/ppermute | solution.py:203
  51.7 1.9 %collective-permute-start.12 = (f32[3,8,960]{2,1,0:T(8,128)S(1)}, f32[3,8,960]{2,1,0:T(8,128)S(1)}, u32[]{:S(2)}, u32[]{:S(2)}) collective-permute-start(f32[3,8,960]{2,1,0:T(8,128)S(1)} %add.79), channel_id=1, source_target_pairs={{0,16},{1,17},{2,18},{3,19},{4,20},{5,21},{6,22},{7,23},{8,24},{9,... | collective-permute-start | bytes 276488 | tf_op jit(solution)/shard_map/ppermute | solution.py:203
  53.6 1.9 %collective-permute-start.11 = (f32[3,8,960]{2,1,0:T(8,128)S(1)}, f32[3,8,960]{2,1,0:T(8,128)S(1)}, u32[]{:S(2)}, u32[]{:S(2)}) collective-permute-start(f32[3,8,960]{2,1,0:T(8,128)S(1)} %add.79), channel_id=1, source_target_pairs={{0,8},{1,9},{2,10},{3,11},{4,12},{5,13},{6,14},{7,15},{8,0},{9,1},... | collective-permute-start | bytes 276488 | tf_op jit(solution)/shard_map/ppermute | solution.py:203
  55.5 3.4 %solve.1.w_ref = bf16[3,320,96]{2,1,0:T(8,128)(2,1)S(1)} custom-call(f32[16,960]{1,0:T(8,128)S(1)} %add_add_fusion.2.mine_ref, f32[16,960]{1,0:T(8,128)S(1)} %collective-permute-done.7.other_ref), custom_call_target="tpu_custom_call" | custom-call | bytes 16777216 | tf_op jit(solution)/shard_map/solve/pallas_call | solution.py:283
  58.9 2.3 %errors.1 = bf16[3,320,960]{2,1,0:T(8,128)(2,1)} custom-call(f32[3,320,960]{2,1,0:T(8,128)S(1)} %bitcast.19, bf16[3,320,960]{2,1,0:T(8,128)(2,1)S(1)} %bitcast.22, bf16[3,320,96]{2,1,0:T(8,128)(2,1)S(1)} %solve.1.w_ref, f32[3,32,960]{2,1,0:T(8,128)S(1)} %get-tuple-element.32.all_ref), custom_call_target="tpu_custom_call" | custom-call | bytes 12582912 | tf_op jit(solution)/shard_map/errors/pallas_call | solution.py:304
  61.3 1.6 %collective-permute-start.28 = (bf16[1,3,40,960]{3,2,1,0:T(8,128)(2,1)S(1)}, bf16[1,3,40,960]{3,2,1,0:T(8,128)(2,1)S(1)}, u32[]{:S(2)}, u32[]{:S(2)}) collective-permute-start(bf16[1,3,40,960]{3,2,1,0:T(8,128)(2,1)S(1)} %add.91.o0_ref), channel_id=1, source_target_pairs={{0,6},{1,7},{2,4},{3,5},{4,2},{5,3},{6,0},{7,1},{8,14},{9,15},{10,... | collective-permute-start | bytes 691208 | tf_op jit(solution)/shard_map/ppermute | solution.py:203
  63.6 1.2 %collective-permute-start.24 = (bf16[1,3,40,960]{3,2,1,0:T(8,128)(2,1)S(1)}, bf16[1,3,40,960]{3,2,1,0:T(8,128)(2,1)S(1)}, u32[]{:S(2)}, u32[]{:S(2)}) collective-permute-start(bf16[1,3,40,960]{3,2,1,0:T(8,128)(2,1)S(1)} %add.91.o0_ref), channel_id=1, source_target_pairs={{0,2},{1,3},{2,0},{3,1},{4,6},{5,7},{6,4},{7,5},{8,10},{9,11},{10,... | collective-permute-start | bytes 691208 | tf_op jit(solution)/shard_map/ppermute | solution.py:203
  65.9 2.7 %collective-permute-done.28.o6_ref = bf16[1,3,40,960]{3,2,1,0:T(8,128)(2,1)S(1)} collective-permute-done((bf16[1,3,40,960]{3,2,1,0:T(8,128)(2,1)S(1)}, bf16[1,3,40,960]{3,2,1,0:T(8,128)(2,1)S(1)}, u32[]{:S(2)}, u32[]{:S(2)}) %collective-permute-start.28) | collective-permute-done | bytes 230432 | tf_op jit(solution)/shard_map/ppermute | solution.py:203
  68.6 2.5 %collective-permute-done.26.o4_ref = bf16[1,3,40,960]{3,2,1,0:T(8,128)(2,1)S(1)} collective-permute-done((bf16[1,3,40,960]{3,2,1,0:T(8,128)(2,1)S(1)}, bf16[1,3,40,960]{3,2,1,0:T(8,128)(2,1)S(1)}, u32[]{:S(2)}, u32[]{:S(2)}) %collective-permute-start.26) | collective-permute-done | bytes 230432 | tf_op jit(solution)/shard_map/ppermute | solution.py:203
  72.8 4.7 %collective-permute-done.15.r2_ref = f32[3,8,960]{2,1,0:T(8,128)S(1)} collective-permute-done((f32[3,8,960]{2,1,0:T(8,128)S(1)}, f32[3,8,960]{2,1,0:T(8,128)S(1)}, u32[]{:S(2)}, u32[]{:S(2)}) %collective-permute-start.15) | collective-permute-done | bytes 92192 | tf_op jit(solution)/shard_map/ppermute | solution.py:203
  77.6 1.3 %collective-permute-done.14.r1_ref = f32[3,8,960]{2,1,0:T(8,128)S(1)} collective-permute-done((f32[3,8,960]{2,1,0:T(8,128)S(1)}, f32[3,8,960]{2,1,0:T(8,128)S(1)}, u32[]{:S(2)}, u32[]{:S(2)}) %collective-permute-start.14) | collective-permute-done | bytes 92192 | tf_op jit(solution)/shard_map/ppermute | solution.py:203
  78.9 4.1 %step.1 = (bf16[3,8,40,960]{3,2,1,0:T(8,128)(2,1)}, bf16[2,8,40,960]{3,2,1,0:T(8,128)(2,1)}) custom-call(s32[3]{0:T(128)S(1)} %copy-done.5, s32[3]{0:T(128)S(1)} %copy-done.6, f32[4]{0:T(128)S(1)} %copy-done.7, f32[4]{0:T(128)S(1)} %copy-done.8, f32[3,8,960]{2,1,0:T(8,128)S(1)} %add_add_fusion.1.r0_ref, f32[3,8,960]{2,1,0:T(8,128)S(1)} %collective-permute-done.14.r1_ref, ...), custom_call_target="tpu_custom_call" | custom-call | tf_op jit(solution)/shard_map/step/pallas_call | solution.py:325
  (63 shorter events, 9.5 us)
Async XLA Ops:
  7.0 22.4 %copy-start.1 = (f32[1,3,320,960]{3,2,1,0:T(8,128)S(1)}, f32[1,3,320,960]{3,2,1,0:T(8,128)}, u32[]{:S(2)}) copy-start(f32[1,3,320,960]{3,2,1,0:T(8,128)} %param.8) | copy-start | bytes 11059204
  7.7 15.9 %collective-permute-start.17 = (bf16[4,3,40,960]{3,2,1,0:T(8,128)(2,1)S(1)}, bf16[4,3,40,960]{3,2,1,0:T(8,128)(2,1)S(1)}, u32[]{:S(2)}, u32[]{:S(2)}) collective-permute-start(bf16[4,3,40,960]{3,2,1,0:T(8,128)(2,1)S(1)} %get-tuple-element.36), channel_id=1, source_target_pairs={{0,1},{1,0},{2,3},{3,2},{4,5},{5,4},{6,7},{7,6},{8,9},{9,8},{10,11... | collective-permute-start | bytes 2764808 | tf_op jit(solution)/shard_map/ppermute | solution.py:203
  8.2 2.3 %collective-permute-start = (f32[16,960]{1,0:T(8,128)S(1)}, f32[16,960]{1,0:T(8,128)S(1)}, u32[]{:S(2)}, u32[]{:S(2)}) collective-permute-start(f32[16,960]{1,0:T(8,128)S(1)} %get-tuple-element.27), channel_id=1, source_target_pairs={{0,1},{1,0},{2,3},{3,2},{4,5},{5,4},{6,7},{7,6},{8,9},{9,8},{10,11... | collective-permute-start | bytes 184328 | tf_op jit(solution)/shard_map/ppermute | solution.py:203
  10.5 6.3 %collective-permute-start.3 = (f32[16,960]{1,0:T(8,128)S(1)}, f32[16,960]{1,0:T(8,128)S(1)}, u32[]{:S(2)}, u32[]{:S(2)}) collective-permute-start(f32[16,960]{1,0:T(8,128)S(1)} %add.69), channel_id=1, source_target_pairs={{0,6},{1,7},{2,4},{3,5},{4,2},{5,3},{6,0},{7,1},{8,14},{9,15},{10,... | collective-permute-start | bytes 184328 | tf_op jit(solution)/shard_map/ppermute | solution.py:203
  14.4 4.3 %collective-permute-start.2 = (f32[16,960]{1,0:T(8,128)S(1)}, f32[16,960]{1,0:T(8,128)S(1)}, u32[]{:S(2)}, u32[]{:S(2)}) collective-permute-start(f32[16,960]{1,0:T(8,128)S(1)} %add.69), channel_id=1, source_target_pairs={{0,4},{1,5},{2,6},{3,7},{4,0},{5,1},{6,2},{7,3},{8,12},{9,13},{10,... | collective-permute-start | bytes 184328 | tf_op jit(solution)/shard_map/ppermute | solution.py:203
  14.9 4.3 %collective-permute-start.1 = (f32[16,960]{1,0:T(8,128)S(1)}, f32[16,960]{1,0:T(8,128)S(1)}, u32[]{:S(2)}, u32[]{:S(2)}) collective-permute-start(f32[16,960]{1,0:T(8,128)S(1)} %add.69), channel_id=1, source_target_pairs={{0,2},{1,3},{2,0},{3,1},{4,6},{5,7},{6,4},{7,5},{8,10},{9,11},{10,... | collective-permute-start | bytes 184328 | tf_op jit(solution)/shard_map/ppermute | solution.py:203
  19.2 6.9 %collective-permute-start.6 = (f32[16,960]{1,0:T(8,128)S(1)}, f32[16,960]{1,0:T(8,128)S(1)}, u32[]{:S(2)}, u32[]{:S(2)}) collective-permute-start(f32[16,960]{1,0:T(8,128)S(1)} %add_add_fusion.3), channel_id=1, source_target_pairs={{0,24},{1,25},{2,26},{3,27},{4,28},{5,29},{6,30},{7,31},{8,16},{9,... | collective-permute-start | bytes 184328 | tf_op jit(solution)/shard_map/ppermute | solution.py:203
  22.9 5.2 %collective-permute-start.5 = (f32[16,960]{1,0:T(8,128)S(1)}, f32[16,960]{1,0:T(8,128)S(1)}, u32[]{:S(2)}, u32[]{:S(2)}) collective-permute-start(f32[16,960]{1,0:T(8,128)S(1)} %add_add_fusion.3), channel_id=1, source_target_pairs={{0,16},{1,17},{2,18},{3,19},{4,20},{5,21},{6,22},{7,23},{8,24},{9,... | collective-permute-start | bytes 184328 | tf_op jit(solution)/shard_map/ppermute | solution.py:203
  22.9 5.2 %collective-permute-start.4 = (f32[16,960]{1,0:T(8,128)S(1)}, f32[16,960]{1,0:T(8,128)S(1)}, u32[]{:S(2)}, u32[]{:S(2)}) collective-permute-start(f32[16,960]{1,0:T(8,128)S(1)} %add_add_fusion.3), channel_id=1, source_target_pairs={{0,8},{1,9},{2,10},{3,11},{4,12},{5,13},{6,14},{7,15},{8,0},{9,1},... | collective-permute-start | bytes 184328 | tf_op jit(solution)/shard_map/ppermute | solution.py:203
  23.8 11.4 %collective-permute-start.19 = (bf16[1,3,40,960]{3,2,1,0:T(8,128)(2,1)S(1)}, bf16[1,3,40,960]{3,2,1,0:T(8,128)(2,1)S(1)}, u32[]{:S(2)}, u32[]{:S(2)}) collective-permute-start(bf16[1,3,40,960]{3,2,1,0:T(8,128)(2,1)S(1)} %get-tuple-element.41), channel_id=1, source_target_pairs={{0,4},{1,5},{2,6},{3,7},{4,0},{5,1},{6,2},{7,3},{8,12},{9,13},{10,... | collective-permute-start | bytes 691208 | tf_op jit(solution)/shard_map/ppermute | solution.py:203
  25.4 9.8 %collective-permute-start.20 = (bf16[1,3,40,960]{3,2,1,0:T(8,128)(2,1)S(1)}, bf16[1,3,40,960]{3,2,1,0:T(8,128)(2,1)S(1)}, u32[]{:S(2)}, u32[]{:S(2)}) collective-permute-start(bf16[1,3,40,960]{3,2,1,0:T(8,128)(2,1)S(1)} %get-tuple-element.43), channel_id=1, source_target_pairs={{0,6},{1,7},{2,4},{3,5},{4,2},{5,3},{6,0},{7,1},{8,14},{9,15},{10,... | collective-permute-start | bytes 691208 | tf_op jit(solution)/shard_map/ppermute | solution.py:203
  26.1 10.4 %collective-permute-start.18 = (bf16[1,3,40,960]{3,2,1,0:T(8,128)(2,1)S(1)}, bf16[1,3,40,960]{3,2,1,0:T(8,128)(2,1)S(1)}, u32[]{:S(2)}, u32[]{:S(2)}) collective-permute-start(bf16[1,3,40,960]{3,2,1,0:T(8,128)(2,1)S(1)} %get-tuple-element.39), channel_id=1, source_target_pairs={{0,2},{1,3},{2,0},{3,1},{4,6},{5,7},{6,4},{7,5},{8,10},{9,11},{10,... | collective-permute-start | bytes 691208 | tf_op jit(solution)/shard_map/ppermute | solution.py:203
  28.1 1.3 %collective-permute-start.7 = (f32[16,960]{1,0:T(8,128)S(1)}, f32[16,960]{1,0:T(8,128)S(1)}, u32[]{:S(2)}, u32[]{:S(2)}) collective-permute-start(f32[16,960]{1,0:T(8,128)S(1)} %add_add_fusion.2.mine_ref), channel_id=1, source_target_pairs={{0,1},{1,0},{2,3},{3,2},{4,5},{5,4},{6,7},{7,6},{8,9},{9,8},{10,11... | collective-permute-start | bytes 184328 | tf_op jit(solution)/shard_map/ppermute | solution.py:203
  31.2 6.9 %collective-permute-start.8 = (f32[2,3,8,960]{3,2,1,0:T(8,128)S(1)}, f32[2,3,8,960]{3,2,1,0:T(8,128)S(1)}, u32[]{:S(2)}, u32[]{:S(2)}) collective-permute-start(f32[2,3,8,960]{3,2,1,0:T(8,128)S(1)} %get-tuple-element.29), channel_id=1, source_target_pairs={{0,1},{1,0},{2,3},{3,2},{4,5},{5,4},{6,7},{7,6},{8,9},{9,8},{10,11... | collective-permute-start | bytes 552968 | tf_op jit(solution)/shard_map/ppermute | solution.py:203
  36.6 7.5 %collective-permute-start.21 = (bf16[1,3,40,960]{3,2,1,0:T(8,128)(2,1)S(1)}, bf16[1,3,40,960]{3,2,1,0:T(8,128)(2,1)S(1)}, u32[]{:S(2)}, u32[]{:S(2)}) collective-permute-start(bf16[1,3,40,960]{3,2,1,0:T(8,128)(2,1)S(1)} %add_add_fusion), channel_id=1, source_target_pairs={{0,8},{1,9},{2,10},{3,11},{4,12},{5,13},{6,14},{7,15},{8,0},{9,1},... | collective-permute-start | bytes 691208 | tf_op jit(solution)/shard_map/ppermute | solution.py:203
  38.1 8.2 %collective-permute-start.9 = (f32[3,8,960]{2,1,0:T(8,128)S(1)}, f32[3,8,960]{2,1,0:T(8,128)S(1)}, u32[]{:S(2)}, u32[]{:S(2)}) collective-permute-start(f32[3,8,960]{2,1,0:T(8,128)S(1)} %fusion), channel_id=1, source_target_pairs={{0,2},{1,3},{2,0},{3,1},{4,6},{5,7},{6,4},{7,5},{8,10},{9,11},{10,... | collective-permute-start | bytes 276488 | tf_op jit(solution)/shard_map/ppermute | solution.py:203
  44.2 17.0 %collective-permute-start.22 = (bf16[1,3,40,960]{3,2,1,0:T(8,128)(2,1)S(1)}, bf16[1,3,40,960]{3,2,1,0:T(8,128)(2,1)S(1)}, u32[]{:S(2)}, u32[]{:S(2)}) collective-permute-start(bf16[1,3,40,960]{3,2,1,0:T(8,128)(2,1)S(1)} %add.90), channel_id=1, source_target_pairs={{0,16},{1,17},{2,18},{3,19},{4,20},{5,21},{6,22},{7,23},{8,24},{9,... | collective-permute-start | bytes 691208 | tf_op jit(solution)/shard_map/ppermute | solution.py:203
  46.3 4.7 %collective-permute-start.10 = (f32[3,8,960]{2,1,0:T(8,128)S(1)}, f32[3,8,960]{2,1,0:T(8,128)S(1)}, u32[]{:S(2)}, u32[]{:S(2)}) collective-permute-start(f32[3,8,960]{2,1,0:T(8,128)S(1)} %fusion.2), channel_id=1, source_target_pairs={{0,4},{1,5},{2,6},{3,7},{4,0},{5,1},{6,2},{7,3},{8,12},{9,13},{10,... | collective-permute-start | bytes 276488 | tf_op jit(solution)/shard_map/ppermute | solution.py:203
  51.0 12.6 %collective-permute-start.13 = (f32[3,8,960]{2,1,0:T(8,128)S(1)}, f32[3,8,960]{2,1,0:T(8,128)S(1)}, u32[]{:S(2)}, u32[]{:S(2)}) collective-permute-start(f32[3,8,960]{2,1,0:T(8,128)S(1)} %add.79), channel_id=1, source_target_pairs={{0,24},{1,25},{2,26},{3,27},{4,28},{5,29},{6,30},{7,31},{8,16},{9,... | collective-permute-start | bytes 276488 | tf_op jit(solution)/shard_map/ppermute | solution.py:203
  51.7 13.2 %collective-permute-start.12 = (f32[3,8,960]{2,1,0:T(8,128)S(1)}, f32[3,8,960]{2,1,0:T(8,128)S(1)}, u32[]{:S(2)}, u32[]{:S(2)}) collective-permute-start(f32[3,8,960]{2,1,0:T(8,128)S(1)} %add.79), channel_id=1, source_target_pairs={{0,16},{1,17},{2,18},{3,19},{4,20},{5,21},{6,22},{7,23},{8,24},{9,... | collective-permute-start | bytes 276488 | tf_op jit(solution)/shard_map/ppermute | solution.py:203
  53.6 11.3 %collective-permute-start.11 = (f32[3,8,960]{2,1,0:T(8,128)S(1)}, f32[3,8,960]{2,1,0:T(8,128)S(1)}, u32[]{:S(2)}, u32[]{:S(2)}) collective-permute-start(f32[3,8,960]{2,1,0:T(8,128)S(1)} %add.79), channel_id=1, source_target_pairs={{0,8},{1,9},{2,10},{3,11},{4,12},{5,13},{6,14},{7,15},{8,0},{9,1},... | collective-permute-start | bytes 276488 | tf_op jit(solution)/shard_map/ppermute | solution.py:203
  58.9 20.0 %copy-start.6 = (s32[3]{0:T(128)S(1)}, s32[3]{0:T(128)}, u32[]{:S(2)}) copy-start(s32[3]{0:T(128)} %buckets_ref.1) | copy-start | bytes 40
  61.3 7.3 %collective-permute-start.28 = (bf16[1,3,40,960]{3,2,1,0:T(8,128)(2,1)S(1)}, bf16[1,3,40,960]{3,2,1,0:T(8,128)(2,1)S(1)}, u32[]{:S(2)}, u32[]{:S(2)}) collective-permute-start(bf16[1,3,40,960]{3,2,1,0:T(8,128)(2,1)S(1)} %add.91.o0_ref), channel_id=1, source_target_pairs={{0,6},{1,7},{2,4},{3,5},{4,2},{5,3},{6,0},{7,1},{8,14},{9,15},{10,... | collective-permute-start | bytes 691208 | tf_op jit(solution)/shard_map/ppermute | solution.py:203
  62.9 8.2 %collective-permute-start.26 = (bf16[1,3,40,960]{3,2,1,0:T(8,128)(2,1)S(1)}, bf16[1,3,40,960]{3,2,1,0:T(8,128)(2,1)S(1)}, u32[]{:S(2)}, u32[]{:S(2)}) collective-permute-start(bf16[1,3,40,960]{3,2,1,0:T(8,128)(2,1)S(1)} %add.91.o0_ref), channel_id=1, source_target_pairs={{0,4},{1,5},{2,6},{3,7},{4,0},{5,1},{6,2},{7,3},{8,12},{9,13},{10,... | collective-permute-start | bytes 691208 | tf_op jit(solution)/shard_map/ppermute | solution.py:203
  63.6 8.3 %collective-permute-start.24 = (bf16[1,3,40,960]{3,2,1,0:T(8,128)(2,1)S(1)}, bf16[1,3,40,960]{3,2,1,0:T(8,128)(2,1)S(1)}, u32[]{:S(2)}, u32[]{:S(2)}) collective-permute-start(bf16[1,3,40,960]{3,2,1,0:T(8,128)(2,1)S(1)} %add.91.o0_ref), channel_id=1, source_target_pairs={{0,2},{1,3},{2,0},{3,1},{4,6},{5,7},{6,4},{7,5},{8,10},{9,11},{10,... | collective-permute-start | bytes 691208 | tf_op jit(solution)/shard_map/ppermute | solution.py:203
  64.9 7.1 %collective-permute-start.16 = (f32[3,8,960]{2,1,0:T(8,128)S(1)}, f32[3,8,960]{2,1,0:T(8,128)S(1)}, u32[]{:S(2)}, u32[]{:S(2)}) collective-permute-start(f32[3,8,960]{2,1,0:T(8,128)S(1)} %add_add_fusion.1.r0_ref), channel_id=1, source_target_pairs={{0,3},{1,2},{2,1},{3,0},{4,7},{5,6},{6,5},{7,4},{8,11},{9,10},{10,... | collective-permute-start | bytes 276488 | tf_op jit(solution)/shard_map/ppermute | solution.py:203
  65.0 13.9 %collective-permute-start.23 = (bf16[1,3,40,960]{3,2,1,0:T(8,128)(2,1)S(1)}, bf16[1,3,40,960]{3,2,1,0:T(8,128)(2,1)S(1)}, u32[]{:S(2)}, u32[]{:S(2)}) collective-permute-start(bf16[1,3,40,960]{3,2,1,0:T(8,128)(2,1)S(1)} %add.91.o0_ref), channel_id=1, source_target_pairs={{0,1},{1,0},{2,3},{3,2},{4,5},{5,4},{6,7},{7,6},{8,9},{9,8},{10,11... | collective-permute-start | bytes 691208 | tf_op jit(solution)/shard_map/ppermute | solution.py:203
  68.6 10.3 %collective-permute-start.29 = (bf16[1,3,40,960]{3,2,1,0:T(8,128)(2,1)S(1)}, bf16[1,3,40,960]{3,2,1,0:T(8,128)(2,1)S(1)}, u32[]{:S(2)}, u32[]{:S(2)}) collective-permute-start(bf16[1,3,40,960]{3,2,1,0:T(8,128)(2,1)S(1)} %collective-permute-done.28.o6_ref), channel_id=1, source_target_pairs={{0,1},{1,0},{2,3},{3,2},{4,5},{5,4},{6,7},{7,6},{8,9},{9,8},{10,11... | collective-permute-start | bytes 691208 | tf_op jit(solution)/shard_map/ppermute | solution.py:203
  71.1 7.8 %collective-permute-start.27 = (bf16[1,3,40,960]{3,2,1,0:T(8,128)(2,1)S(1)}, bf16[1,3,40,960]{3,2,1,0:T(8,128)(2,1)S(1)}, u32[]{:S(2)}, u32[]{:S(2)}) collective-permute-start(bf16[1,3,40,960]{3,2,1,0:T(8,128)(2,1)S(1)} %collective-permute-done.26.o4_ref), channel_id=1, source_target_pairs={{0,1},{1,0},{2,3},{3,2},{4,5},{5,4},{6,7},{7,6},{8,9},{9,8},{10,11... | collective-permute-start | bytes 691208 | tf_op jit(solution)/shard_map/ppermute | solution.py:203
  72.0 6.9 %collective-permute-start.25 = (bf16[1,3,40,960]{3,2,1,0:T(8,128)(2,1)S(1)}, bf16[1,3,40,960]{3,2,1,0:T(8,128)(2,1)S(1)}, u32[]{:S(2)}, u32[]{:S(2)}) collective-permute-start(bf16[1,3,40,960]{3,2,1,0:T(8,128)(2,1)S(1)} %collective-permute-done.24.o2_ref), channel_id=1, source_target_pairs={{0,1},{1,0},{2,3},{3,2},{4,5},{5,4},{6,7},{7,6},{8,9},{9,8},{10,11... | collective-permute-start | bytes 691208 | tf_op jit(solution)/shard_map/ppermute | solution.py:203
  72.0 5.6 %collective-permute-start.15 = (f32[3,8,960]{2,1,0:T(8,128)S(1)}, f32[3,8,960]{2,1,0:T(8,128)S(1)}, u32[]{:S(2)}, u32[]{:S(2)}) collective-permute-start(f32[3,8,960]{2,1,0:T(8,128)S(1)} %add_add_fusion.1.r0_ref), channel_id=1, source_target_pairs={{0,2},{1,3},{2,0},{3,1},{4,6},{5,7},{6,4},{7,5},{8,10},{9,11},{10,... | collective-permute-start | bytes 276488 | tf_op jit(solution)/shard_map/ppermute | solution.py:203
  77.6 1.3 %collective-permute-start.14 = (f32[3,8,960]{2,1,0:T(8,128)S(1)}, f32[3,8,960]{2,1,0:T(8,128)S(1)}, u32[]{:S(2)}, u32[]{:S(2)}) collective-permute-start(f32[3,8,960]{2,1,0:T(8,128)S(1)} %add_add_fusion.1.r0_ref), channel_id=1, source_target_pairs={{0,1},{1,0},{2,3},{3,2},{4,5},{5,4},{6,7},{7,6},{8,9},{9,8},{10,11... | collective-permute-start | bytes 276488 | tf_op jit(solution)/shard_map/ppermute | solution.py:203
  (7 other events, 48.1 us)

commit v3 on v2

--- a/solution.py
+++ b/solution.py
@@ -30,8 +30,8 @@
     return lax.dot_general(left, right, (dims, ((), ())), preferred_element_type=F32)
 
 
-def params():
-    return pltpu.CompilerParams(dimension_semantics=("arbitrary",), vmem_limit_bytes=40 * 1024 * 1024)
+def params(mebibytes=40):
+    return pltpu.CompilerParams(dimension_semantics=("arbitrary",), vmem_limit_bytes=mebibytes * 1024 * 1024)
 
 
 def cost(mebibytes):
@@ -169,7 +169,7 @@
 
 def step_kernel(
     owners_ref, buckets_ref, rates_ref, betas_ref,
-    r0_ref, r1_ref, r2_ref, r3_ref, w_ref, o0_ref, o1_ref, o2_ref, o3_ref, o4_ref, o5_ref, o6_ref, o7_ref,
+    r0_ref, r1_ref, r2_ref, r3_ref, w_ref, even_ref, odd_ref,
     step_ref, mom_ref, right_ref, update_ref,
 ):
     i = pl.program_id(0)
@@ -187,11 +187,11 @@
     update_ref[...] = dot(w_ref[0], right, ((1,), (0,))).reshape(update_ref.shape)
     own = owners_ref[i] == me
     slot = slot_of(owners_ref, i)
-    olds = (o0_ref, o1_ref, o2_ref, o3_ref, o4_ref, o5_ref, o6_ref, o7_ref)
-    for position, ref in enumerate(olds):
+    for position in range(8):
+        ref = (even_ref, odd_ref)[position % 2]
         piece = position ^ (me & 7)
         update = update_ref[piece]
-        mom = beta * ref[0, 0].astype(F32) + update
+        mom = beta * ref[position // 2, 0].astype(F32) + update
         step_ref[0, piece] = (-rate * (update + beta * mom)).astype(BF16)
 
         @pl.when(own)
@@ -229,13 +229,17 @@
         out_specs=[whole((half, mats * rows))] * 2,
         out_shape=[sds((half, mats * rows), F32)] * 2,
         scratch_shapes=[pltpu.VMEM((mats, 2, half, rows), F32)],
-        compiler_params=params(),
+        compiler_params=params(61),
         name="left",
     )(grads, errs, q_t)
 
     def old_shape(n):
         return (n, mats, piece, cols)
 
+    def swap(value, mask):
+        return exchange(value, mask, count)
+
+    mine = mine + swap(other, 1)
     sizes = [len(order) for order in OLD_ORDER]
     *evens, odd = pl.pallas_call(
         old_kernel,
@@ -247,17 +251,14 @@
         name="old",
     )(owners, after(momentum.reshape(slots, 8, piece, cols), mine))
 
-    def swap(value, mask):
-        return exchange(value, mask, count)
-
     got = swap(odd, 1)
-    mine = mine + swap(other, 1)
-    evens = [after(even + got[n : n + 1], mine) for n, even in enumerate(evens)]
+    evens = [even + got[n : n + 1] for n, even in enumerate(evens)]
     mine = total_over(mine, bits[1:3], count)
-    old = evens[0] + swap(evens[1], 2) + swap(evens[2], 4) + swap(evens[3], 6)
-    old = after(old, mine)
+    mine = after(mine, *evens)
+    got = [swap(evens[n], 2 * n) for n in (1, 2, 3)]
     mine = total_over(mine, bits[3:], count)
-    other = swap(mine, 1)
+    old = after(evens[0], mine) + got[0] + got[1] + got[2]
+    other = swap(after(mine, old), 1)
 
     right_all, keep, send2, send = pl.pallas_call(
         right_kernel,
@@ -292,15 +293,23 @@
         name="solve",
     )(mine, other)
 
-    for bit in bits[3:-1]:
-        old = old + swap(old, 1 << bit)
     got = swap(send, 1)
     send2 = send2 + got[1]
-    old = after(old, send2)
+    for bit in bits[3:-1]:
+        from_other = swap(old, 1 << bit)
+        old = after(old, send2) + from_other
+    send2 = after(send2, old)
+    from_other = swap(old, 1 << bits[-1])
     r0 = keep + got[0] + swap(send2, 2)
-    old = old + swap(old, 1 << bits[-1])
     r0 = total_over(r0, bits[2:3], count)
-    w = after(w, r0)
+    old = after(old, r0) + from_other
+    r0 = after(r0, old)
+    got = [swap(old, mask) for mask in (2, 4, 6)]
+    r0 = after(total_over(r0, bits[3:], count), w)
+    r1, r2, r3 = (swap(r0, mask) for mask in (1, 2, 3))
+    old = after(old, r0)
+    evens = jnp.concatenate([old] + got)
+    odds = swap(evens, 1)
     new_errors = pl.pallas_call(
         error_kernel,
         grid=(mats,),
@@ -310,28 +319,21 @@
         compiler_params=params(),
         cost_estimate=cost(12),
         name="errors",
-    )(grads, errs, w, right_all)
-    olds = {0: after(old, r0)}
-    for mask in (2, 4, 6):
-        olds[mask] = swap(olds[0], mask)
-    r0 = total_over(r0, bits[3:], count)
-    r0 = after(r0, new_errors)
-    r1, r2, r3 = (swap(r0, mask) for mask in (1, 2, 3))
-    for mask in (0, 2, 4, 6):
-        olds[mask + 1] = swap(olds[mask], 1)
+    )(grads, errs, after(w, evens), right_all)
+    w = after(w, new_errors)
 
     quarter_spec = per_matrix((quarter, cols))
-    old_spec = pl.BlockSpec((1, 1, piece, cols), lambda i: (0, i, 0, 0))
+    old_spec = pl.BlockSpec((4, 1, piece, cols), lambda i: (0, i, 0, 0))
     steps, new_mom = pl.pallas_call(
         step_kernel,
         grid=(mats,),
-        in_specs=[SMEM] * 4 + [quarter_spec] * 4 + [per_matrix((rows, 3 * rank))] + [old_spec] * 8,
+        in_specs=[SMEM] * 4 + [quarter_spec] * 4 + [per_matrix((rows, 3 * rank))] + [old_spec] * 2,
         out_specs=[per_matrix((8, piece, cols)), whole((slots, 8, piece, cols))],
         out_shape=[sds((mats, 8, piece, cols), BF16), sds((slots, 8, piece, cols), BF16)],
         scratch_shapes=[pltpu.VMEM((4, quarter, cols), F32), pltpu.VMEM((8, piece, cols), F32)],
         compiler_params=params(),
         name="step",
-    )(owners, buckets, learn_rates, beta_values, r0, r1, r2, r3, w, *(olds[n] for n in range(8)))
+    )(owners, buckets, learn_rates, beta_values, r0, r1, r2, r3, w, evens, odds)
     return (new_errors[None], steps.reshape(1, mats, rows, cols), new_mom.reshape(momentum.shape))
 
 

time: 83.3 us -> 94.2 us (1.13)
  waiting for transfers between devices: 33.3 us -> 44.4 us
  local copies, waits for them, and re-layouts: 4.68 us -> 0.1 us
  Pallas kernels: 14 us -> 17.3 us
    ppermute x30 -> x27, waiting for transfers between devices: 33.3 us -> 44.4 us  [exchange(): return lax.ppermute(value, AXES, [(d, d ^ mask) for d in range(count)])]
    unnamed x18 -> x17, local copies, waits for them, and re-layouts: 4.68 us -> 0.08 us
    pallas_call x1, Pallas kernels: 1.69 us -> 4.97 us  [on_device(): pl.pallas_call(left_kernel, grid=(mats,), in_specs=[grad_spec, grad_spec,...]
    ppermute x30 -> x27, starting transfers between devices: 29.8 us -> 30.1 us  [exchange(): return lax.ppermute(value, AXES, [(d, d ^ mask) for d in range(count)])]
  transfers between devices with their start and end apart: 30 -> 27, of which waited for: 15 -> 17; matrix products, arithmetic and copies ran while one was open for 0% -> 0% of each run, Pallas kernels for 9% -> 6%
where the time goes in v3:
time: 94.2 us; the launch traced here: 94 us
  waiting for transfers between devices  44.4 us (47%)
  starting transfers between devices  30.1 us (32%)
  Pallas kernels  17.3 us (18%)
  other arithmetic  1.22 us (1%)
    ppermute x27, waiting for transfers between devices, exchange(): return lax.ppermute(value, AXES, [(d, d ^ mask) for d in range(count)])  44.4 us
    ppermute x27, starting transfers between devices, exchange(): return lax.ppermute(value, AXES, [(d, d ^ mask) for d in range(count)])  30.1 us
    pallas_call x1, Pallas kernels, on_device(): pl.pallas_call(left_kernel, grid=(mats,), in_specs=[grad_spec, grad_spec,...  4.97 us
    pallas_call x1, Pallas kernels, on_device(): pl.pallas_call(step_kernel, grid=(mats,), in_specs=[SMEM] * 4 + [quarter_...  4.16 us
    pallas_call x1, Pallas kernels, on_device(): pl.pallas_call(solve_kernel, grid=(1,), in_specs=[whole((half, mats * row...  3.38 us
    pallas_call x1, Pallas kernels, on_device(): pl.pallas_call(error_kernel, grid=(mats,), in_specs=[grad_spec, grad_spec...  2.34 us
  transfers between devices with their start and end apart: 27, of which 17 were waited for; matrix products, arithmetic and copies ran while one was open for 0% of the time, Pallas kernels for 6%

profile of v3, /device:TPU:0, one launch (start us, length us, event | category | flops | bytes accessed | tf_op | source)
XLA Modules:
  0.0 94.0 jit_solution(15715616689315277434)
XLA Ops:
  0.7 5.0 %left.1 = (f32[16,960]{1,0:T(8,128)}, f32[16,960]{1,0:T(8,128)}) custom-call(f32[3,320,960]{2,1,0:T(8,128)} %bitcast.17, bf16[3,320,960]{2,1,0:T(8,128)(2,1)} %bitcast.20, f32[3,32,960]{2,1,0:T(8,128)} %bitcast.25), custom_call_target="tpu_custom_call" | custom-call | tf_op jit(solution)/shard_map/left/pallas_call | solution.py:225
  6.1 1.1 %collective-permute-done = f32[16,960]{1,0:T(8,128)S(1)} collective-permute-done((f32[16,960]{1,0:T(8,128)}, f32[16,960]{1,0:T(8,128)S(1)}, u32[]{:S(2)}, u32[]{:S(2)}) %collective-permute-start) | collective-permute-done | bytes 61472 | tf_op jit(solution)/shard_map/ppermute | solution.py:203
  9.2 3.6 %collective-permute-start.3 = (f32[16,960]{1,0:T(8,128)S(1)}, f32[16,960]{1,0:T(8,128)S(1)}, u32[]{:S(2)}, u32[]{:S(2)}) collective-permute-start(f32[16,960]{1,0:T(8,128)S(1)} %add.69), channel_id=1, source_target_pairs={{0,6},{1,7},{2,4},{3,5},{4,2},{5,3},{6,0},{7,1},{8,14},{9,15},{10,... | collective-permute-start | bytes 184328 | tf_op jit(solution)/shard_map/ppermute | solution.py:203
  13.4 2.0 %collective-permute-done.3 = f32[16,960]{1,0:T(8,128)S(1)} collective-permute-done((f32[16,960]{1,0:T(8,128)S(1)}, f32[16,960]{1,0:T(8,128)S(1)}, u32[]{:S(2)}, u32[]{:S(2)}) %collective-permute-start.3) | collective-permute-done | bytes 61472 | tf_op jit(solution)/shard_map/ppermute | solution.py:203
  15.4 1.7 %collective-permute-done.2 = f32[16,960]{1,0:T(8,128)S(1)} collective-permute-done((f32[16,960]{1,0:T(8,128)S(1)}, f32[16,960]{1,0:T(8,128)S(1)}, u32[]{:S(2)}, u32[]{:S(2)}) %collective-permute-start.2) | collective-permute-done | bytes 61472 | tf_op jit(solution)/shard_map/ppermute | solution.py:203
  17.7 3.7 %collective-permute-start.7 = (f32[16,960]{1,0:T(8,128)S(1)}, f32[16,960]{1,0:T(8,128)S(1)}, u32[]{:S(2)}, u32[]{:S(2)}) collective-permute-start(f32[16,960]{1,0:T(8,128)S(1)} %add_add_fusion.3), channel_id=1, source_target_pairs={{0,24},{1,25},{2,26},{3,27},{4,28},{5,29},{6,30},{7,31},{8,16},{9,... | collective-permute-start | bytes 184328 | tf_op jit(solution)/shard_map/ppermute | solution.py:203
  22.2 1.5 %collective-permute-start.10 = (bf16[1,3,40,960]{3,2,1,0:T(8,128)(2,1)S(1)}, bf16[1,3,40,960]{3,2,1,0:T(8,128)(2,1)S(1)}, u32[]{:S(2)}, u32[]{:S(2)}) collective-permute-start(bf16[1,3,40,960]{3,2,1,0:T(8,128)(2,1)S(1)} %get-tuple-element.53), channel_id=1, source_target_pairs={{0,6},{1,7},{2,4},{3,5},{4,2},{5,3},{6,0},{7,1},{8,14},{9,15},{10,... | collective-permute-start | bytes 691208 | tf_op jit(solution)/shard_map/ppermute | solution.py:203
  23.7 0.9 %collective-permute-start.9 = (bf16[1,3,40,960]{3,2,1,0:T(8,128)(2,1)S(1)}, bf16[1,3,40,960]{3,2,1,0:T(8,128)(2,1)S(1)}, u32[]{:S(2)}, u32[]{:S(2)}) collective-permute-start(bf16[1,3,40,960]{3,2,1,0:T(8,128)(2,1)S(1)} %get-tuple-element.54), channel_id=1, source_target_pairs={{0,4},{1,5},{2,6},{3,7},{4,0},{5,1},{6,2},{7,3},{8,12},{9,13},{10,... | collective-permute-start | bytes 691208 | tf_op jit(solution)/shard_map/ppermute | solution.py:203
  24.6 1.0 %collective-permute-start.8 = (bf16[1,3,40,960]{3,2,1,0:T(8,128)(2,1)S(1)}, bf16[1,3,40,960]{3,2,1,0:T(8,128)(2,1)S(1)}, u32[]{:S(2)}, u32[]{:S(2)}) collective-permute-start(bf16[1,3,40,960]{3,2,1,0:T(8,128)(2,1)S(1)} %get-tuple-element.55), channel_id=1, source_target_pairs={{0,2},{1,3},{2,0},{3,1},{4,6},{5,7},{6,4},{7,5},{8,10},{9,11},{10,... | collective-permute-start | bytes 691208 | tf_op jit(solution)/shard_map/ppermute | solution.py:203
  25.7 1.1 %collective-permute-done.6 = f32[16,960]{1,0:T(8,128)S(1)} collective-permute-done((f32[16,960]{1,0:T(8,128)S(1)}, f32[16,960]{1,0:T(8,128)S(1)}, u32[]{:S(2)}, u32[]{:S(2)}) %collective-permute-start.6) | collective-permute-done | bytes 61472 | tf_op jit(solution)/shard_map/ppermute | solution.py:203
  26.8 5.1 %collective-permute-done.10 = bf16[1,3,40,960]{3,2,1,0:T(8,128)(2,1)S(1)} collective-permute-done((bf16[1,3,40,960]{3,2,1,0:T(8,128)(2,1)S(1)}, bf16[1,3,40,960]{3,2,1,0:T(8,128)(2,1)S(1)}, u32[]{:S(2)}, u32[]{:S(2)}) %collective-permute-start.10) | collective-permute-done | bytes 230432 | tf_op jit(solution)/shard_map/ppermute | solution.py:203
  31.9 2.6 %collective-permute-done.9 = bf16[1,3,40,960]{3,2,1,0:T(8,128)(2,1)S(1)} collective-permute-done((bf16[1,3,40,960]{3,2,1,0:T(8,128)(2,1)S(1)}, bf16[1,3,40,960]{3,2,1,0:T(8,128)(2,1)S(1)}, u32[]{:S(2)}, u32[]{:S(2)}) %collective-permute-start.9) | collective-permute-done | bytes 230432 | tf_op jit(solution)/shard_map/ppermute | solution.py:203
  35.2 1.2 %collective-permute-done.11.other_ref = f32[16,960]{1,0:T(8,128)S(1)} collective-permute-done((f32[16,960]{1,0:T(8,128)S(1)}, f32[16,960]{1,0:T(8,128)S(1)}, u32[]{:S(2)}, u32[]{:S(2)}) %collective-permute-start.11) | collective-permute-done | bytes 61472 | tf_op jit(solution)/shard_map/ppermute | solution.py:203
  36.5 1.7 %right.1 = (f32[3,32,960]{2,1,0:T(8,128)S(1)}, f32[3,8,960]{2,1,0:T(8,128)S(1)}, f32[3,8,960]{2,1,0:T(8,128)S(1)}, f32[2,3,8,960]{3,2,1,0:T(8,128)S(1)}) custom-call(f32[16,960]{1,0:T(8,128)S(1)} %add_add_fusion.2.mine_ref, f32[16,960]{1,0:T(8,128)S(1)} %collective-permute-done.11.other_ref, f32[3,320,960]{2,1,0:T(8,128)S(1)} %bitcast.18, ...), custom_call_target="tpu_custom_call" | custom-call | tf_op jit(solution)/shard_map/right/pallas_call | solution.py:263
  38.4 1.4 %collective-permute-start.13 = (bf16[1,3,40,960]{3,2,1,0:T(8,128)(2,1)S(1)}, bf16[1,3,40,960]{3,2,1,0:T(8,128)(2,1)S(1)}, u32[]{:S(2)}, u32[]{:S(2)}) collective-permute-start(bf16[1,3,40,960]{3,2,1,0:T(8,128)(2,1)S(1)} %add_add_fusion), channel_id=1, source_target_pairs={{0,8},{1,9},{2,10},{3,11},{4,12},{5,13},{6,14},{7,15},{8,0},{9,1},... | collective-permute-start | bytes 691208 | tf_op jit(solution)/shard_map/ppermute | solution.py:203
  39.8 6.8 %collective-permute-done.13 = bf16[1,3,40,960]{3,2,1,0:T(8,128)(2,1)S(1)} collective-permute-done((bf16[1,3,40,960]{3,2,1,0:T(8,128)(2,1)S(1)}, bf16[1,3,40,960]{3,2,1,0:T(8,128)(2,1)S(1)}, u32[]{:S(2)}, u32[]{:S(2)}) %collective-permute-start.13) | collective-permute-done | bytes 230432 | tf_op jit(solution)/shard_map/ppermute | solution.py:203
  46.7 1.5 %collective-permute-start.14 = (f32[3,8,960]{2,1,0:T(8,128)S(1)}, f32[3,8,960]{2,1,0:T(8,128)S(1)}, u32[]{:S(2)}, u32[]{:S(2)}) collective-permute-start(f32[3,8,960]{2,1,0:T(8,128)S(1)} %fusion.2), channel_id=1, source_target_pairs={{0,2},{1,3},{2,0},{3,1},{4,6},{5,7},{6,4},{7,5},{8,10},{9,11},{10,... | collective-permute-start | bytes 276488 | tf_op jit(solution)/shard_map/ppermute | solution.py:203
  48.2 2.3 %collective-permute-start.16 = (bf16[1,3,40,960]{3,2,1,0:T(8,128)(2,1)S(1)}, bf16[1,3,40,960]{3,2,1,0:T(8,128)(2,1)S(1)}, u32[]{:S(2)}, u32[]{:S(2)}) collective-permute-start(bf16[1,3,40,960]{3,2,1,0:T(8,128)(2,1)S(1)} %add.84), channel_id=1, source_target_pairs={{0,16},{1,17},{2,18},{3,19},{4,20},{5,21},{6,22},{7,23},{8,24},{9,... | collective-permute-start | bytes 691208 | tf_op jit(solution)/shard_map/ppermute | solution.py:203
  50.5 0.9 collective-permute-done.14
  51.4 1.5 %collective-permute-start.15 = (f32[3,8,960]{2,1,0:T(8,128)S(1)}, f32[3,8,960]{2,1,0:T(8,128)S(1)}, u32[]{:S(2)}, u32[]{:S(2)}) collective-permute-start(f32[3,8,960]{2,1,0:T(8,128)S(1)} %fusion.1), channel_id=1, source_target_pairs={{0,4},{1,5},{2,6},{3,7},{4,0},{5,1},{6,2},{7,3},{8,12},{9,13},{10,... | collective-permute-start | bytes 276488 | tf_op jit(solution)/shard_map/ppermute | solution.py:203
  52.9 3.2 %collective-permute-done.15 = f32[3,8,960]{2,1,0:T(8,128)S(1)} collective-permute-done((f32[3,8,960]{2,1,0:T(8,128)S(1)}, f32[3,8,960]{2,1,0:T(8,128)S(1)}, u32[]{:S(2)}, u32[]{:S(2)}) %collective-permute-start.15) | collective-permute-done | bytes 92192 | tf_op jit(solution)/shard_map/ppermute | solution.py:203
  56.1 5.4 %collective-permute-done.16 = bf16[1,3,40,960]{3,2,1,0:T(8,128)(2,1)S(1)} collective-permute-done((bf16[1,3,40,960]{3,2,1,0:T(8,128)(2,1)S(1)}, bf16[1,3,40,960]{3,2,1,0:T(8,128)(2,1)S(1)}, u32[]{:S(2)}, u32[]{:S(2)}) %collective-permute-start.16) | collective-permute-done | bytes 230432 | tf_op jit(solution)/shard_map/ppermute | solution.py:203
  61.5 3.3 %collective-permute-start.19 = (f32[3,8,960]{2,1,0:T(8,128)S(1)}, f32[3,8,960]{2,1,0:T(8,128)S(1)}, u32[]{:S(2)}, u32[]{:S(2)}) collective-permute-start(f32[3,8,960]{2,1,0:T(8,128)S(1)} %add.87), channel_id=1, source_target_pairs={{0,24},{1,25},{2,26},{3,27},{4,28},{5,29},{6,30},{7,31},{8,16},{9,... | collective-permute-start | bytes 276488 | tf_op jit(solution)/shard_map/ppermute | solution.py:203
  64.8 1.2 %collective-permute-start.17 = (f32[3,8,960]{2,1,0:T(8,128)S(1)}, f32[3,8,960]{2,1,0:T(8,128)S(1)}, u32[]{:S(2)}, u32[]{:S(2)}) collective-permute-start(f32[3,8,960]{2,1,0:T(8,128)S(1)} %add.87), channel_id=1, source_target_pairs={{0,8},{1,9},{2,10},{3,11},{4,12},{5,13},{6,14},{7,15},{8,0},{9,1},... | collective-permute-start | bytes 276488 | tf_op jit(solution)/shard_map/ppermute | solution.py:203
  66.0 3.4 %solve.1.w_ref = bf16[3,320,96]{2,1,0:T(8,128)(2,1)S(1)} custom-call(f32[16,960]{1,0:T(8,128)S(1)} %add_add_fusion.2.mine_ref, f32[16,960]{1,0:T(8,128)S(1)} %collective-permute-done.11.other_ref), custom_call_target="tpu_custom_call" | custom-call | bytes 16777216 | tf_op jit(solution)/shard_map/solve/pallas_call | solution.py:284
  69.4 1.6 %collective-permute-start.22 = (bf16[1,3,40,960]{3,2,1,0:T(8,128)(2,1)S(1)}, bf16[1,3,40,960]{3,2,1,0:T(8,128)(2,1)S(1)}, u32[]{:S(2)}, u32[]{:S(2)}) collective-permute-start(bf16[1,3,40,960]{3,2,1,0:T(8,128)(2,1)S(1)} %add.88), channel_id=1, source_target_pairs={{0,6},{1,7},{2,4},{3,5},{4,2},{5,3},{6,0},{7,1},{8,14},{9,15},{10,... | collective-permute-start | bytes 691208 | tf_op jit(solution)/shard_map/ppermute | solution.py:203
  71.5 1.4 %collective-permute-start.20 = (bf16[1,3,40,960]{3,2,1,0:T(8,128)(2,1)S(1)}, bf16[1,3,40,960]{3,2,1,0:T(8,128)(2,1)S(1)}, u32[]{:S(2)}, u32[]{:S(2)}) collective-permute-start(bf16[1,3,40,960]{3,2,1,0:T(8,128)(2,1)S(1)} %add.88), channel_id=1, source_target_pairs={{0,2},{1,3},{2,0},{3,1},{4,6},{5,7},{6,4},{7,5},{8,10},{9,11},{10,... | collective-permute-start | bytes 691208 | tf_op jit(solution)/shard_map/ppermute | solution.py:203
  73.0 8.6 %collective-permute-done.20 = bf16[1,3,40,960]{3,2,1,0:T(8,128)(2,1)S(1)} collective-permute-done((bf16[1,3,40,960]{3,2,1,0:T(8,128)(2,1)S(1)}, bf16[1,3,40,960]{3,2,1,0:T(8,128)(2,1)S(1)}, u32[]{:S(2)}, u32[]{:S(2)}) %collective-permute-start.20) | collective-permute-done | bytes 230432 | tf_op jit(solution)/shard_map/ppermute | solution.py:203
  83.3 1.4 %collective-permute-start.24 = (f32[3,8,960]{2,1,0:T(8,128)S(1)}, f32[3,8,960]{2,1,0:T(8,128)S(1)}, u32[]{:S(2)}, u32[]{:S(2)}) collective-permute-start(f32[3,8,960]{2,1,0:T(8,128)S(1)} %add_add_fusion.1.r0_ref), channel_id=1, source_target_pairs={{0,2},{1,3},{2,0},{3,1},{4,6},{5,7},{6,4},{7,5},{8,10},{9,11},{10,... | collective-permute-start | bytes 276488 | tf_op jit(solution)/shard_map/ppermute | solution.py:203
  84.7 2.3 %errors.1 = bf16[3,320,960]{2,1,0:T(8,128)(2,1)} custom-call(f32[3,320,960]{2,1,0:T(8,128)S(1)} %bitcast.19, bf16[3,320,960]{2,1,0:T(8,128)(2,1)S(1)} %bitcast.22, bf16[3,320,96]{2,1,0:T(8,128)(2,1)S(1)} %solve.1.w_ref, f32[3,32,960]{2,1,0:T(8,128)S(1)} %get-tuple-element.49.all_ref), custom_call_target="tpu_custom_call" | custom-call | bytes 12582912 | tf_op jit(solution)/shard_map/errors/pallas_call | solution.py:313
  87.1 2.7 %collective-permute-done.24.r2_ref = f32[3,8,960]{2,1,0:T(8,128)S(1)} collective-permute-done((f32[3,8,960]{2,1,0:T(8,128)S(1)}, f32[3,8,960]{2,1,0:T(8,128)S(1)}, u32[]{:S(2)}, u32[]{:S(2)}) %collective-permute-start.24) | collective-permute-done | bytes 92192 | tf_op jit(solution)/shard_map/ppermute | solution.py:203
  89.8 4.2 %step.1 = (bf16[3,8,40,960]{3,2,1,0:T(8,128)(2,1)}, bf16[2,8,40,960]{3,2,1,0:T(8,128)(2,1)}) custom-call(s32[3]{0:T(128)S(1)} %copy-done.3, s32[3]{0:T(128)S(1)} %copy-done.4, f32[4]{0:T(128)S(1)} %copy-done.5, f32[4]{0:T(128)S(1)} %copy-done.6, f32[3,8,960]{2,1,0:T(8,128)S(1)} %add_add_fusion.1.r0_ref, f32[3,8,960]{2,1,0:T(8,128)S(1)} %collective-permute-done.23.r1_ref, ...), custom_call_target="tpu_custom_call" | custom-call | tf_op jit(solution)/shard_map/step/pallas_call | solution.py:327
  (57 shorter events, 8.1 us)
Async XLA Ops:
  0.6 7.4 %copy-start.2 = (bf16[2,320,960]{2,1,0:T(8,128)(2,1)S(1)}, bf16[2,320,960]{2,1,0:T(8,128)(2,1)}, u32[]{:S(2)}) copy-start(bf16[2,320,960]{2,1,0:T(8,128)(2,1)} %param.15) | copy-start | bytes 3686404
  0.6 7.4 %copy-start.3 = (s32[3]{0:T(128)S(1)}, s32[3]{0:T(128)}, u32[]{:S(2)}) copy-start(s32[3]{0:T(128)} %owners_ref.3) | copy-start | bytes 40
  5.6 1.6 %collective-permute-start = (f32[16,960]{1,0:T(8,128)}, f32[16,960]{1,0:T(8,128)S(1)}, u32[]{:S(2)}, u32[]{:S(2)}) collective-permute-start(f32[16,960]{1,0:T(8,128)} %get-tuple-element.29), channel_id=1, source_target_pairs={{0,1},{1,0},{2,3},{3,2},{4,5},{5,4},{6,7},{7,6},{8,9},{9,8},{10,11... | collective-permute-start | bytes 184328 | tf_op jit(solution)/shard_map/ppermute | solution.py:203
  8.1 28.4 %copy-start.1 = (bf16[1,3,320,960]{3,2,1,0:T(8,128)(2,1)S(1)}, bf16[1,3,320,960]{3,2,1,0:T(8,128)(2,1)}, u32[]{:S(2)}) copy-start(bf16[1,3,320,960]{3,2,1,0:T(8,128)(2,1)} %param.9) | copy-start | bytes 5529604
  8.8 8.8 %collective-permute-start.4 = (bf16[4,3,40,960]{3,2,1,0:T(8,128)(2,1)S(1)}, bf16[4,3,40,960]{3,2,1,0:T(8,128)(2,1)S(1)}, u32[]{:S(2)}, u32[]{:S(2)}) collective-permute-start(bf16[4,3,40,960]{3,2,1,0:T(8,128)(2,1)S(1)} %get-tuple-element.32), channel_id=1, source_target_pairs={{0,1},{1,0},{2,3},{3,2},{4,5},{5,4},{6,7},{7,6},{8,9},{9,8},{10,11... | collective-permute-start | bytes 2764808 | tf_op jit(solution)/shard_map/ppermute | solution.py:203
  9.2 6.2 %collective-permute-start.3 = (f32[16,960]{1,0:T(8,128)S(1)}, f32[16,960]{1,0:T(8,128)S(1)}, u32[]{:S(2)}, u32[]{:S(2)}) collective-permute-start(f32[16,960]{1,0:T(8,128)S(1)} %add.69), channel_id=1, source_target_pairs={{0,6},{1,7},{2,4},{3,5},{4,2},{5,3},{6,0},{7,1},{8,14},{9,15},{10,... | collective-permute-start | bytes 184328 | tf_op jit(solution)/shard_map/ppermute | solution.py:203
  12.8 4.3 %collective-permute-start.2 = (f32[16,960]{1,0:T(8,128)S(1)}, f32[16,960]{1,0:T(8,128)S(1)}, u32[]{:S(2)}, u32[]{:S(2)}) collective-permute-start(f32[16,960]{1,0:T(8,128)S(1)} %add.69), channel_id=1, source_target_pairs={{0,4},{1,5},{2,6},{3,7},{4,0},{5,1},{6,2},{7,3},{8,12},{9,13},{10,... | collective-permute-start | bytes 184328 | tf_op jit(solution)/shard_map/ppermute | solution.py:203
  13.3 4.3 %collective-permute-start.1 = (f32[16,960]{1,0:T(8,128)S(1)}, f32[16,960]{1,0:T(8,128)S(1)}, u32[]{:S(2)}, u32[]{:S(2)}) collective-permute-start(f32[16,960]{1,0:T(8,128)S(1)} %add.69), channel_id=1, source_target_pairs={{0,2},{1,3},{2,0},{3,1},{4,6},{5,7},{6,4},{7,5},{8,10},{9,11},{10,... | collective-permute-start | bytes 184328 | tf_op jit(solution)/shard_map/ppermute | solution.py:203
  17.6 18.8 %copy-start = (f32[1,3,320,960]{3,2,1,0:T(8,128)S(1)}, f32[1,3,320,960]{3,2,1,0:T(8,128)}, u32[]{:S(2)}) copy-start(f32[1,3,320,960]{3,2,1,0:T(8,128)} %param.8) | copy-start | bytes 11059204
  17.7 6.9 %collective-permute-start.7 = (f32[16,960]{1,0:T(8,128)S(1)}, f32[16,960]{1,0:T(8,128)S(1)}, u32[]{:S(2)}, u32[]{:S(2)}) collective-permute-start(f32[16,960]{1,0:T(8,128)S(1)} %add_add_fusion.3), channel_id=1, source_target_pairs={{0,24},{1,25},{2,26},{3,27},{4,28},{5,29},{6,30},{7,31},{8,16},{9,... | collective-permute-start | bytes 184328 | tf_op jit(solution)/shard_map/ppermute | solution.py:203
  21.4 5.4 %collective-permute-start.6 = (f32[16,960]{1,0:T(8,128)S(1)}, f32[16,960]{1,0:T(8,128)S(1)}, u32[]{:S(2)}, u32[]{:S(2)}) collective-permute-start(f32[16,960]{1,0:T(8,128)S(1)} %add_add_fusion.3), channel_id=1, source_target_pairs={{0,16},{1,17},{2,18},{3,19},{4,20},{5,21},{6,22},{7,23},{8,24},{9,... | collective-permute-start | bytes 184328 | tf_op jit(solution)/shard_map/ppermute | solution.py:203
  21.4 5.4 %collective-permute-start.5 = (f32[16,960]{1,0:T(8,128)S(1)}, f32[16,960]{1,0:T(8,128)S(1)}, u32[]{:S(2)}, u32[]{:S(2)}) collective-permute-start(f32[16,960]{1,0:T(8,128)S(1)} %add_add_fusion.3), channel_id=1, source_target_pairs={{0,8},{1,9},{2,10},{3,11},{4,12},{5,13},{6,14},{7,15},{8,0},{9,1},... | collective-permute-start | bytes 184328 | tf_op jit(solution)/shard_map/ppermute | solution.py:203
  22.2 9.7 %collective-permute-start.10 = (bf16[1,3,40,960]{3,2,1,0:T(8,128)(2,1)S(1)}, bf16[1,3,40,960]{3,2,1,0:T(8,128)(2,1)S(1)}, u32[]{:S(2)}, u32[]{:S(2)}) collective-permute-start(bf16[1,3,40,960]{3,2,1,0:T(8,128)(2,1)S(1)} %get-tuple-element.53), channel_id=1, source_target_pairs={{0,6},{1,7},{2,4},{3,5},{4,2},{5,3},{6,0},{7,1},{8,14},{9,15},{10,... | collective-permute-start | bytes 691208 | tf_op jit(solution)/shard_map/ppermute | solution.py:203
  23.7 10.8 %collective-permute-start.9 = (bf16[1,3,40,960]{3,2,1,0:T(8,128)(2,1)S(1)}, bf16[1,3,40,960]{3,2,1,0:T(8,128)(2,1)S(1)}, u32[]{:S(2)}, u32[]{:S(2)}) collective-permute-start(bf16[1,3,40,960]{3,2,1,0:T(8,128)(2,1)S(1)} %get-tuple-element.54), channel_id=1, source_target_pairs={{0,4},{1,5},{2,6},{3,7},{4,0},{5,1},{6,2},{7,3},{8,12},{9,13},{10,... | collective-permute-start | bytes 691208 | tf_op jit(solution)/shard_map/ppermute | solution.py:203
  24.6 10.4 %collective-permute-start.8 = (bf16[1,3,40,960]{3,2,1,0:T(8,128)(2,1)S(1)}, bf16[1,3,40,960]{3,2,1,0:T(8,128)(2,1)S(1)}, u32[]{:S(2)}, u32[]{:S(2)}) collective-permute-start(bf16[1,3,40,960]{3,2,1,0:T(8,128)(2,1)S(1)} %get-tuple-element.55), channel_id=1, source_target_pairs={{0,2},{1,3},{2,0},{3,1},{4,6},{5,7},{6,4},{7,5},{8,10},{9,11},{10,... | collective-permute-start | bytes 691208 | tf_op jit(solution)/shard_map/ppermute | solution.py:203
  35.1 1.3 %collective-permute-start.11 = (f32[16,960]{1,0:T(8,128)S(1)}, f32[16,960]{1,0:T(8,128)S(1)}, u32[]{:S(2)}, u32[]{:S(2)}) collective-permute-start(f32[16,960]{1,0:T(8,128)S(1)} %add_add_fusion.2.mine_ref), channel_id=1, source_target_pairs={{0,1},{1,0},{2,3},{3,2},{4,5},{5,4},{6,7},{7,6},{8,9},{9,8},{10,11... | collective-permute-start | bytes 184328 | tf_op jit(solution)/shard_map/ppermute | solution.py:203
  38.2 1.6 %collective-permute-start.12 = (f32[2,3,8,960]{3,2,1,0:T(8,128)S(1)}, f32[2,3,8,960]{3,2,1,0:T(8,128)S(1)}, u32[]{:S(2)}, u32[]{:S(2)}) collective-permute-start(f32[2,3,8,960]{3,2,1,0:T(8,128)S(1)} %get-tuple-element.40), channel_id=1, source_target_pairs={{0,1},{1,0},{2,3},{3,2},{4,5},{5,4},{6,7},{7,6},{8,9},{9,8},{10,11... | collective-permute-start | bytes 552968 | tf_op jit(solution)/shard_map/ppermute | solution.py:203
  38.4 8.2 %collective-permute-start.13 = (bf16[1,3,40,960]{3,2,1,0:T(8,128)(2,1)S(1)}, bf16[1,3,40,960]{3,2,1,0:T(8,128)(2,1)S(1)}, u32[]{:S(2)}, u32[]{:S(2)}) collective-permute-start(bf16[1,3,40,960]{3,2,1,0:T(8,128)(2,1)S(1)} %add_add_fusion), channel_id=1, source_target_pairs={{0,8},{1,9},{2,10},{3,11},{4,12},{5,13},{6,14},{7,15},{8,0},{9,1},... | collective-permute-start | bytes 691208 | tf_op jit(solution)/shard_map/ppermute | solution.py:203
  46.7 4.7 %collective-permute-start.14 = (f32[3,8,960]{2,1,0:T(8,128)S(1)}, f32[3,8,960]{2,1,0:T(8,128)S(1)}, u32[]{:S(2)}, u32[]{:S(2)}) collective-permute-start(f32[3,8,960]{2,1,0:T(8,128)S(1)} %fusion.2), channel_id=1, source_target_pairs={{0,2},{1,3},{2,0},{3,1},{4,6},{5,7},{6,4},{7,5},{8,10},{9,11},{10,... | collective-permute-start | bytes 276488 | tf_op jit(solution)/shard_map/ppermute | solution.py:203
  48.2 13.3 %collective-permute-start.16 = (bf16[1,3,40,960]{3,2,1,0:T(8,128)(2,1)S(1)}, bf16[1,3,40,960]{3,2,1,0:T(8,128)(2,1)S(1)}, u32[]{:S(2)}, u32[]{:S(2)}) collective-permute-start(bf16[1,3,40,960]{3,2,1,0:T(8,128)(2,1)S(1)} %add.84), channel_id=1, source_target_pairs={{0,16},{1,17},{2,18},{3,19},{4,20},{5,21},{6,22},{7,23},{8,24},{9,... | collective-permute-start | bytes 691208 | tf_op jit(solution)/shard_map/ppermute | solution.py:203
  51.4 4.7 %collective-permute-start.15 = (f32[3,8,960]{2,1,0:T(8,128)S(1)}, f32[3,8,960]{2,1,0:T(8,128)S(1)}, u32[]{:S(2)}, u32[]{:S(2)}) collective-permute-start(f32[3,8,960]{2,1,0:T(8,128)S(1)} %fusion.1), channel_id=1, source_target_pairs={{0,4},{1,5},{2,6},{3,7},{4,0},{5,1},{6,2},{7,3},{8,12},{9,13},{10,... | collective-permute-start | bytes 276488 | tf_op jit(solution)/shard_map/ppermute | solution.py:203
  61.5 10.0 %collective-permute-start.19 = (f32[3,8,960]{2,1,0:T(8,128)S(1)}, f32[3,8,960]{2,1,0:T(8,128)S(1)}, u32[]{:S(2)}, u32[]{:S(2)}) collective-permute-start(f32[3,8,960]{2,1,0:T(8,128)S(1)} %add.87), channel_id=1, source_target_pairs={{0,24},{1,25},{2,26},{3,27},{4,28},{5,29},{6,30},{7,31},{8,16},{9,... | collective-permute-start | bytes 276488 | tf_op jit(solution)/shard_map/ppermute | solution.py:203
  64.8 8.1 %collective-permute-start.18 = (f32[3,8,960]{2,1,0:T(8,128)S(1)}, f32[3,8,960]{2,1,0:T(8,128)S(1)}, u32[]{:S(2)}, u32[]{:S(2)}) collective-permute-start(f32[3,8,960]{2,1,0:T(8,128)S(1)} %add.87), channel_id=1, source_target_pairs={{0,16},{1,17},{2,18},{3,19},{4,20},{5,21},{6,22},{7,23},{8,24},{9,... | collective-permute-start | bytes 276488 | tf_op jit(solution)/shard_map/ppermute | solution.py:203
  64.8 8.1 %collective-permute-start.17 = (f32[3,8,960]{2,1,0:T(8,128)S(1)}, f32[3,8,960]{2,1,0:T(8,128)S(1)}, u32[]{:S(2)}, u32[]{:S(2)}) collective-permute-start(f32[3,8,960]{2,1,0:T(8,128)S(1)} %add.87), channel_id=1, source_target_pairs={{0,8},{1,9},{2,10},{3,11},{4,12},{5,13},{6,14},{7,15},{8,0},{9,1},... | collective-permute-start | bytes 276488 | tf_op jit(solution)/shard_map/ppermute | solution.py:203
  69.4 13.0 %collective-permute-start.22 = (bf16[1,3,40,960]{3,2,1,0:T(8,128)(2,1)S(1)}, bf16[1,3,40,960]{3,2,1,0:T(8,128)(2,1)S(1)}, u32[]{:S(2)}, u32[]{:S(2)}) collective-permute-start(bf16[1,3,40,960]{3,2,1,0:T(8,128)(2,1)S(1)} %add.88), channel_id=1, source_target_pairs={{0,6},{1,7},{2,4},{3,5},{4,2},{5,3},{6,0},{7,1},{8,14},{9,15},{10,... | collective-permute-start | bytes 691208 | tf_op jit(solution)/shard_map/ppermute | solution.py:203
  70.9 11.4 %collective-permute-start.21 = (bf16[1,3,40,960]{3,2,1,0:T(8,128)(2,1)S(1)}, bf16[1,3,40,960]{3,2,1,0:T(8,128)(2,1)S(1)}, u32[]{:S(2)}, u32[]{:S(2)}) collective-permute-start(bf16[1,3,40,960]{3,2,1,0:T(8,128)(2,1)S(1)} %add.88), channel_id=1, source_target_pairs={{0,4},{1,5},{2,6},{3,7},{4,0},{5,1},{6,2},{7,3},{8,12},{9,13},{10,... | collective-permute-start | bytes 691208 | tf_op jit(solution)/shard_map/ppermute | solution.py:203
  71.5 10.0 %collective-permute-start.20 = (bf16[1,3,40,960]{3,2,1,0:T(8,128)(2,1)S(1)}, bf16[1,3,40,960]{3,2,1,0:T(8,128)(2,1)S(1)}, u32[]{:S(2)}, u32[]{:S(2)}) collective-permute-start(bf16[1,3,40,960]{3,2,1,0:T(8,128)(2,1)S(1)} %add.88), channel_id=1, source_target_pairs={{0,2},{1,3},{2,0},{3,1},{4,6},{5,7},{6,4},{7,5},{8,10},{9,11},{10,... | collective-permute-start | bytes 691208 | tf_op jit(solution)/shard_map/ppermute | solution.py:203
  82.4 7.4 %collective-permute-start.26 = (bf16[4,3,40,960]{3,2,1,0:T(8,128)(2,1)S(1)}, bf16[4,3,40,960]{3,2,1,0:T(8,128)(2,1)S(1)}, u32[]{:S(2)}, u32[]{:S(2)}) collective-permute-start(bf16[4,3,40,960]{3,2,1,0:T(8,128)(2,1)S(1)} %constant_dynamic-update-slice_fusion.even_ref), channel_id=1, source_target_pairs={{0,1},{1,0},{2,3},{3,2},{4,5},{5,4},{6,7},{7,6},{8,9},{9,8},{10,11... | collective-permute-start | bytes 2764808 | tf_op jit(solution)/shard_map/ppermute | solution.py:203
  82.5 4.6 %collective-permute-start.25 = (f32[3,8,960]{2,1,0:T(8,128)S(1)}, f32[3,8,960]{2,1,0:T(8,128)S(1)}, u32[]{:S(2)}, u32[]{:S(2)}) collective-permute-start(f32[3,8,960]{2,1,0:T(8,128)S(1)} %add_add_fusion.1.r0_ref), channel_id=1, source_target_pairs={{0,3},{1,2},{2,1},{3,0},{4,7},{5,6},{6,5},{7,4},{8,11},{9,10},{10,... | collective-permute-start | bytes 276488 | tf_op jit(solution)/shard_map/ppermute | solution.py:203
  83.3 6.5 %collective-permute-start.24 = (f32[3,8,960]{2,1,0:T(8,128)S(1)}, f32[3,8,960]{2,1,0:T(8,128)S(1)}, u32[]{:S(2)}, u32[]{:S(2)}) collective-permute-start(f32[3,8,960]{2,1,0:T(8,128)S(1)} %add_add_fusion.1.r0_ref), channel_id=1, source_target_pairs={{0,2},{1,3},{2,0},{3,1},{4,6},{5,7},{6,4},{7,5},{8,10},{9,11},{10,... | collective-permute-start | bytes 276488 | tf_op jit(solution)/shard_map/ppermute | solution.py:203
  84.7 5.1 %collective-permute-start.23 = (f32[3,8,960]{2,1,0:T(8,128)S(1)}, f32[3,8,960]{2,1,0:T(8,128)S(1)}, u32[]{:S(2)}, u32[]{:S(2)}) collective-permute-start(f32[3,8,960]{2,1,0:T(8,128)S(1)} %add_add_fusion.1.r0_ref), channel_id=1, source_target_pairs={{0,1},{1,0},{2,3},{3,2},{4,5},{5,4},{6,7},{7,6},{8,9},{9,8},{10,11... | collective-permute-start | bytes 276488 | tf_op jit(solution)/shard_map/ppermute | solution.py:203
  84.7 5.1 %copy-start.6 = (f32[4]{0:T(128)S(1)}, f32[4]{0:T(128)}, u32[]{:S(2)}) copy-start(f32[4]{0:T(128)} %betas_ref.1) | copy-start | bytes 52
  (2 other events, 10.3 us)

commit v4 on v3

--- a/solution.py
+++ b/solution.py
@@ -42,24 +42,27 @@
     return lax.optimization_barrier((value,) + others)[0]
 
 
-def left_kernel(grad_ref, error_ref, q_ref, mine_ref, other_ref, left_ref):
-    i = pl.program_id(0)
-    mats = left_ref.shape[0]
-    me = lax.axis_index(AXES)
+def left_kernel(grad_hbm, error_hbm, q_hbm, mine_ref, other_ref, grad_ref, error_ref, q_ref, left_ref, sems):
+    mats, rows, _ = grad_ref.shape
     rank = q_ref.shape[1]
-    merged = grad_ref[0] + error_ref[0].astype(F32)
-    high, low = split(merged)
-    q_both = jnp.concatenate(split(q_ref[0]), 0)
-    both = dot(q_both, high, ((1,), (1,))) + dot(q_both, low, ((1,), (1,)))
-    left_ref[i] = (both[:rank] + both[rank:]).reshape(left_ref.shape[1:])
-
-    @pl.when(i == mats - 1)
-    def _():
-        bit = me & 1
-        rows = grad_ref.shape[1]
-        for m in range(mats):
-            mine_ref[:, m * rows : (m + 1) * rows] = left_ref[m, bit]
-            other_ref[:, m * rows : (m + 1) * rows] = left_ref[m, 1 - bit]
+    pairs = ((grad_hbm, grad_ref), (error_hbm, error_ref), (q_hbm, q_ref))
+    copies = [
+        [pltpu.make_async_copy(hbm.at[m], ref.at[m], sems.at[m, n]) for n, (hbm, ref) in enumerate(pairs)]
+        for m in range(mats)
+    ]
+    for per_mat in copies:
+        for copy in per_mat:
+            copy.start()
+    bit = lax.axis_index(AXES) & 1
+    for m in range(mats):
+        for copy in copies[m]:
+            copy.wait()
+        high, low = split(grad_ref[m] + error_ref[m].astype(F32))
+        q_both = jnp.concatenate(split(q_ref[m]), 0)
+        both = dot(q_both, high, ((1,), (1,))) + dot(q_both, low, ((1,), (1,)))
+        left_ref[...] = (both[:rank] + both[rank:]).reshape(left_ref.shape)
+        mine_ref[:, m * rows : (m + 1) * rows] = left_ref[bit]
+        other_ref[:, m * rows : (m + 1) * rows] = left_ref[1 - bit]
 
 
 def gather_left(mine_ref, other_ref, left_ref, rows):
@@ -222,24 +225,12 @@
     grad_spec = per_matrix((rows, cols))
     sds = jax.ShapeDtypeStruct
 
-    mine, other = pl.pallas_call(
-        left_kernel,
-        grid=(mats,),
-        in_specs=[grad_spec, grad_spec, per_matrix((rank, cols))],
-        out_specs=[whole((half, mats * rows))] * 2,
-        out_shape=[sds((half, mats * rows), F32)] * 2,
-        scratch_shapes=[pltpu.VMEM((mats, 2, half, rows), F32)],
-        compiler_params=params(61),
-        name="left",
-    )(grads, errs, q_t)
-
     def old_shape(n):
         return (n, mats, piece, cols)
 
     def swap(value, mask):
         return exchange(value, mask, count)
 
-    mine = mine + swap(other, 1)
     sizes = [len(order) for order in OLD_ORDER]
     *evens, odd = pl.pallas_call(
         old_kernel,
@@ -249,15 +240,34 @@
         out_shape=[sds(old_shape(n), BF16) for n in sizes],
         compiler_params=params(),
         name="old",
-    )(owners, after(momentum.reshape(slots, 8, piece, cols), mine))
+    )(owners, momentum.reshape(slots, 8, piece, cols))
+
+    mine, other = pl.pallas_call(
+        left_kernel,
+        in_specs=[pl.BlockSpec(memory_space=pltpu.HBM)] * 3,
+        out_shape=[sds((half, mats * rows), F32)] * 2,
+        scratch_shapes=[
+            pltpu.VMEM((mats, rows, cols), F32),
+            pltpu.VMEM((mats, rows, cols), BF16),
+            pltpu.VMEM((mats, rank, cols), F32),
+            pltpu.VMEM((2, half, rows), F32),
+            pltpu.SemaphoreType.DMA((mats, 3)),
+        ],
+        compiler_params=pltpu.CompilerParams(vmem_limit_bytes=60 * 1024 * 1024),
+        name="left",
+    )(grads, errs, after(q_t, odd))
 
     got = swap(odd, 1)
-    evens = [even + got[n : n + 1] for n, even in enumerate(evens)]
-    mine = total_over(mine, bits[1:3], count)
-    mine = after(mine, *evens)
+    evens = [after(evens[n], mine) + got[n : n + 1] for n in range(4)]
+    mine = mine + swap(after(other, *evens), 1)
     got = [swap(evens[n], 2 * n) for n in (1, 2, 3)]
+    for bit in bits[1:3]:
+        mine = total_over(mine, [bit], count)
+    old = after(evens[0], mine) + got[0] + got[1] + got[2]
+    mine = after(mine, old)
+    from_other = swap(old, 1 << bits[3])
     mine = total_over(mine, bits[3:], count)
-    old = after(evens[0], mine) + got[0] + got[1] + got[2]
+    old = after(old, mine) + from_other
     other = swap(after(mine, old), 1)
 
     right_all, keep, send2, send = pl.pallas_call(
@@ -294,22 +304,21 @@
     )(mine, other)
 
     got = swap(send, 1)
-    send2 = send2 + got[1]
-    for bit in bits[3:-1]:
-        from_other = swap(old, 1 << bit)
-        old = after(old, send2) + from_other
-    send2 = after(send2, old)
+    r0 = keep + got[0] + swap(send2 + got[1], 2)
+    for bit in bits[4:-1]:
+        old = old + swap(old, 1 << bit)
     from_other = swap(old, 1 << bits[-1])
-    r0 = keep + got[0] + swap(send2, 2)
     r0 = total_over(r0, bits[2:3], count)
     old = after(old, r0) + from_other
     r0 = after(r0, old)
     got = [swap(old, mask) for mask in (2, 4, 6)]
-    r0 = after(total_over(r0, bits[3:], count), w)
+    for bit in bits[3:-1]:
+        r0 = total_over(r0, [bit], count)
+    r0 = total_over(after(r0, w), bits[-1:], count)
+    evens = jnp.concatenate([after(old, r0)] + got)
+    r0 = after(r0, evens)
+    odds = swap(evens, 1)
     r1, r2, r3 = (swap(r0, mask) for mask in (1, 2, 3))
-    old = after(old, r0)
-    evens = jnp.concatenate([old] + got)
-    odds = swap(evens, 1)
     new_errors = pl.pallas_call(
         error_kernel,
         grid=(mats,),

time: 94.2 us -> 97.3 us (1.033)
  waiting for transfers between devices: 44.4 us -> 50.6 us
  starting transfers between devices: 30.1 us -> 24.3 us
  local copies, waits for them, and re-layouts: 0.1 us -> 2.08 us
    ppermute x27 -> x25, waiting for transfers between devices: 44.4 us -> 50.6 us  [exchange(): return lax.ppermute(value, AXES, [(d, d ^ mask) for d in range(count)])]
    ppermute x27 -> x25, starting transfers between devices: 30.1 us -> 24.3 us  [exchange(): return lax.ppermute(value, AXES, [(d, d ^ mask) for d in range(count)])]
    unnamed x17 -> x23, local copies, waits for them, and re-layouts: 0.08 us -> 2.06 us
  transfers between devices with their start and end apart: 27 -> 25, of which waited for: 17 -> 17; matrix products, arithmetic and copies ran while one was open for 0% -> 0% of each run, Pallas kernels for 6% -> 11%
where the time goes in v4:
time: 97.3 us; the launch traced here: 97.2 us
  waiting for transfers between devices  50.6 us (52%)
  starting transfers between devices  24.3 us (25%)
  Pallas kernels  17.4 us (18%)
  local copies, waits for them, and re-layouts  2.08 us (2%)
  other arithmetic  1.83 us (2%)
    ppermute x25, waiting for transfers between devices, exchange(): return lax.ppermute(value, AXES, [(d, d ^ mask) for d in range(count)])  50.6 us
    ppermute x25, starting transfers between devices, exchange(): return lax.ppermute(value, AXES, [(d, d ^ mask) for d in range(count)])  24.3 us
    pallas_call x1, Pallas kernels, on_device(): pl.pallas_call(left_kernel, in_specs=[pl.BlockSpec(memory_space=pltpu.HBM...  5.04 us
    pallas_call x1, Pallas kernels, on_device(): pl.pallas_call(step_kernel, grid=(mats,), in_specs=[SMEM] * 4 + [quarter_...  4.19 us
    pallas_call x1, Pallas kernels, on_device(): pl.pallas_call(solve_kernel, grid=(1,), in_specs=[whole((half, mats * row...  3.38 us
    pallas_call x1, Pallas kernels, on_device(): pl.pallas_call(error_kernel, grid=(mats,), in_specs=[grad_spec, grad_spec...  2.34 us
    unnamed x23, local copies, waits for them, and re-layouts  2.06 us
  transfers between devices with their start and end apart: 25, of which 17 were waited for; matrix products, arithmetic and copies ran while one was open for 0% of the time, Pallas kernels for 11%

profile of v4, /device:TPU:0, one launch (start us, length us, event | category | flops | bytes accessed | tf_op | source)
XLA Modules:
  0.0 97.2 jit_solution(10421747081729407217)
XLA Ops:
  0.6 1.3 %copy-done.2 = bf16[2,320,960]{2,1,0:T(8,128)(2,1)S(1)} copy-done((bf16[2,320,960]{2,1,0:T(8,128)(2,1)S(1)}, bf16[2,320,960]{2,1,0:T(8,128)(2,1)}, u32[]{:S(2)}) %copy-start.2) | copy-done | bytes 1228824
  3.8 5.0 %left.1 = (f32[16,960]{1,0:T(8,128)}, f32[16,960]{1,0:T(8,128)}) custom-call(f32[3,320,960]{2,1,0:T(8,128)} %bitcast.17, bf16[3,320,960]{2,1,0:T(8,128)(2,1)} %bitcast.20, f32[3,32,960]{2,1,0:T(8,128)} %bitcast.25), custom_call_target="tpu_custom_call" | custom-call | tf_op jit(solution)/shard_map/left/pallas_call | solution.py:245
  8.9 1.6 %slice_add_fusion = (bf16[1,3,40,960]{3,2,1,0:T(8,128)(2,1)S(1)}, bf16[1,3,40,960]{3,2,1,0:T(8,128)(2,1)S(1)}, bf16[1,3,40,960]{3,2,1,0:T(8,128)(2,1)S(1)}, bf16[1,3,40,960]{3,2,1,0:T(8,128)(2,1)S(1)}) fusion(bf16[1,3,40,960]{3,2,1,0:T(8,128)(2,1)S(1)} %get-tuple-element.44, bf16[4,3,40,960]{3,2,1,0:T(8,128)(2,1)} %collective-permute-done, ...), kind=kLoop, calls=%fused_computation | loop fusion | flops 460800 | bytes 2764800 | tf_op jit(solution)/shard_map/add | solution.py:261
  10.5 3.5 %collective-permute-start.6 = (bf16[1,3,40,960]{3,2,1,0:T(8,128)(2,1)S(1)}, bf16[1,3,40,960]{3,2,1,0:T(8,128)(2,1)S(1)}, u32[]{:S(2)}, u32[]{:S(2)}) collective-permute-start(bf16[1,3,40,960]{3,2,1,0:T(8,128)(2,1)S(1)} %get-tuple-element.63), channel_id=1, source_target_pairs={{0,6},{1,7},{2,4},{3,5},{4,2},{5,3},{6,0},{7,1},{8,14},{9,15},{10,... | collective-permute-start | bytes 691208 | tf_op jit(solution)/shard_map/ppermute | solution.py:206
  14.7 1.3 %collective-permute-done.1 = f32[16,960]{1,0:T(8,128)S(1)} collective-permute-done((f32[16,960]{1,0:T(8,128)S(1)}, f32[16,960]{1,0:T(8,128)S(1)}, u32[]{:S(2)}, u32[]{:S(2)}) %collective-permute-start.1) | collective-permute-done | bytes 61472 | tf_op jit(solution)/shard_map/ppermute | solution.py:206
  15.9 2.0 %collective-permute-start.2 = (f32[16,960]{1,0:T(8,128)S(1)}, f32[16,960]{1,0:T(8,128)S(1)}, u32[]{:S(2)}, u32[]{:S(2)}) collective-permute-start(f32[16,960]{1,0:T(8,128)S(1)} %add.67), channel_id=1, source_target_pairs={{0,2},{1,3},{2,0},{3,1},{4,6},{5,7},{6,4},{7,5},{8,10},{9,11},{10,... | collective-permute-start | bytes 184328 | tf_op jit(solution)/shard_map/ppermute | solution.py:206
  17.9 9.7 %collective-permute-done.2 = f32[16,960]{1,0:T(8,128)S(1)} collective-permute-done((f32[16,960]{1,0:T(8,128)S(1)}, f32[16,960]{1,0:T(8,128)S(1)}, u32[]{:S(2)}, u32[]{:S(2)}) %collective-permute-start.2) | collective-permute-done | bytes 61472 | tf_op jit(solution)/shard_map/ppermute | solution.py:206
  28.0 3.9 %collective-permute-done.3 = f32[16,960]{1,0:T(8,128)S(1)} collective-permute-done((f32[16,960]{1,0:T(8,128)S(1)}, f32[16,960]{1,0:T(8,128)S(1)}, u32[]{:S(2)}, u32[]{:S(2)}) %collective-permute-start.3) | collective-permute-done | bytes 61472 | tf_op jit(solution)/shard_map/ppermute | solution.py:206
  32.0 3.7 %collective-permute-start.9 = (f32[16,960]{1,0:T(8,128)S(1)}, f32[16,960]{1,0:T(8,128)S(1)}, u32[]{:S(2)}, u32[]{:S(2)}) collective-permute-start(f32[16,960]{1,0:T(8,128)S(1)} %add.69), channel_id=1, source_target_pairs={{0,24},{1,25},{2,26},{3,27},{4,28},{5,29},{6,30},{7,31},{8,16},{9,... | collective-permute-start | bytes 184328 | tf_op jit(solution)/shard_map/ppermute | solution.py:206
  35.7 0.8 collective-permute-start.7
  36.5 1.2 %collective-permute-start.10 = (bf16[1,3,40,960]{3,2,1,0:T(8,128)(2,1)S(1)}, bf16[1,3,40,960]{3,2,1,0:T(8,128)(2,1)S(1)}, u32[]{:S(2)}, u32[]{:S(2)}) collective-permute-start(bf16[1,3,40,960]{3,2,1,0:T(8,128)(2,1)S(1)} %add_add_fusion), channel_id=1, source_target_pairs={{0,8},{1,9},{2,10},{3,11},{4,12},{5,13},{6,14},{7,15},{8,0},{9,1},... | collective-permute-start | bytes 691208 | tf_op jit(solution)/shard_map/ppermute | solution.py:206
  38.3 2.9 %collective-permute-done.8 = f32[16,960]{1,0:T(8,128)S(1)} collective-permute-done((f32[16,960]{1,0:T(8,128)S(1)}, f32[16,960]{1,0:T(8,128)S(1)}, u32[]{:S(2)}, u32[]{:S(2)}) %collective-permute-start.8) | collective-permute-done | bytes 61472 | tf_op jit(solution)/shard_map/ppermute | solution.py:206
  41.5 3.9 %collective-permute-done.10 = bf16[1,3,40,960]{3,2,1,0:T(8,128)(2,1)S(1)} collective-permute-done((bf16[1,3,40,960]{3,2,1,0:T(8,128)(2,1)S(1)}, bf16[1,3,40,960]{3,2,1,0:T(8,128)(2,1)S(1)}, u32[]{:S(2)}, u32[]{:S(2)}) %collective-permute-start.10) | collective-permute-done | bytes 230432 | tf_op jit(solution)/shard_map/ppermute | solution.py:206
  45.5 1.2 %collective-permute-done.11.other_ref = f32[16,960]{1,0:T(8,128)S(1)} collective-permute-done((f32[16,960]{1,0:T(8,128)S(1)}, f32[16,960]{1,0:T(8,128)S(1)}, u32[]{:S(2)}, u32[]{:S(2)}) %collective-permute-start.11) | collective-permute-done | bytes 61472 | tf_op jit(solution)/shard_map/ppermute | solution.py:206
  46.7 1.8 %right.1 = (f32[3,32,960]{2,1,0:T(8,128)S(1)}, f32[3,8,960]{2,1,0:T(8,128)S(1)}, f32[3,8,960]{2,1,0:T(8,128)S(1)}, f32[2,3,8,960]{3,2,1,0:T(8,128)S(1)}) custom-call(f32[16,960]{1,0:T(8,128)S(1)} %add_add_fusion.1.mine_ref, f32[16,960]{1,0:T(8,128)S(1)} %collective-permute-done.11.other_ref, f32[3,320,960]{2,1,0:T(8,128)S(1)} %bitcast.18, ...), custom_call_target="tpu_custom_call" | custom-call | tf_op jit(solution)/shard_map/right/pallas_call | solution.py:273
  48.7 1.3 %collective-permute-done.12 = f32[2,3,8,960]{3,2,1,0:T(8,128)S(1)} collective-permute-done((f32[2,3,8,960]{3,2,1,0:T(8,128)S(1)}, f32[2,3,8,960]{3,2,1,0:T(8,128)S(1)}, u32[]{:S(2)}, u32[]{:S(2)}) %collective-permute-start.12) | collective-permute-done | bytes 184352 | tf_op jit(solution)/shard_map/ppermute | solution.py:206
  50.0 1.6 %collective-permute-start.13 = (f32[3,8,960]{2,1,0:T(8,128)S(1)}, f32[3,8,960]{2,1,0:T(8,128)S(1)}, u32[]{:S(2)}, u32[]{:S(2)}) collective-permute-start(f32[3,8,960]{2,1,0:T(8,128)S(1)} %fusion), channel_id=1, source_target_pairs={{0,2},{1,3},{2,0},{3,1},{4,6},{5,7},{6,4},{7,5},{8,10},{9,11},{10,... | collective-permute-start | bytes 276488 | tf_op jit(solution)/shard_map/ppermute | solution.py:206
  51.6 1.2 %collective-permute-start.15 = (bf16[1,3,40,960]{3,2,1,0:T(8,128)(2,1)S(1)}, bf16[1,3,40,960]{3,2,1,0:T(8,128)(2,1)S(1)}, u32[]{:S(2)}, u32[]{:S(2)}) collective-permute-start(bf16[1,3,40,960]{3,2,1,0:T(8,128)(2,1)S(1)} %add.76), channel_id=1, source_target_pairs={{0,16},{1,17},{2,18},{3,19},{4,20},{5,21},{6,22},{7,23},{8,24},{9,... | collective-permute-start | bytes 691208 | tf_op jit(solution)/shard_map/ppermute | solution.py:206
  52.8 2.1 %collective-permute-done.13 = f32[3,8,960]{2,1,0:T(8,128)S(1)} collective-permute-done((f32[3,8,960]{2,1,0:T(8,128)S(1)}, f32[3,8,960]{2,1,0:T(8,128)S(1)}, u32[]{:S(2)}, u32[]{:S(2)}) %collective-permute-start.13) | collective-permute-done | bytes 92192 | tf_op jit(solution)/shard_map/ppermute | solution.py:206
  55.5 4.1 %collective-permute-done.14 = f32[3,8,960]{2,1,0:T(8,128)S(1)} collective-permute-done((f32[3,8,960]{2,1,0:T(8,128)S(1)}, f32[3,8,960]{2,1,0:T(8,128)S(1)}, u32[]{:S(2)}, u32[]{:S(2)}) %collective-permute-start.14) | collective-permute-done | bytes 92192 | tf_op jit(solution)/shard_map/ppermute | solution.py:206
  59.7 5.8 %collective-permute-done.15 = bf16[1,3,40,960]{3,2,1,0:T(8,128)(2,1)S(1)} collective-permute-done((bf16[1,3,40,960]{3,2,1,0:T(8,128)(2,1)S(1)}, bf16[1,3,40,960]{3,2,1,0:T(8,128)(2,1)S(1)}, u32[]{:S(2)}, u32[]{:S(2)}) %collective-permute-start.15) | collective-permute-done | bytes 230432 | tf_op jit(solution)/shard_map/ppermute | solution.py:206
  66.2 3.4 %solve.1.w_ref = bf16[3,320,96]{2,1,0:T(8,128)(2,1)S(1)} custom-call(f32[16,960]{1,0:T(8,128)S(1)} %add_add_fusion.1.mine_ref, f32[16,960]{1,0:T(8,128)S(1)} %collective-permute-done.11.other_ref), custom_call_target="tpu_custom_call" | custom-call | bytes 16777216 | tf_op jit(solution)/shard_map/solve/pallas_call | solution.py:294
  70.3 2.1 %collective-permute-start.17 = (f32[3,8,960]{2,1,0:T(8,128)S(1)}, f32[3,8,960]{2,1,0:T(8,128)S(1)}, u32[]{:S(2)}, u32[]{:S(2)}) collective-permute-start(f32[3,8,960]{2,1,0:T(8,128)S(1)} %add.82), channel_id=1, source_target_pairs={{0,16},{1,17},{2,18},{3,19},{4,20},{5,21},{6,22},{7,23},{8,24},{9,... | collective-permute-start | bytes 276488 | tf_op jit(solution)/shard_map/ppermute | solution.py:206
  72.3 1.4 %collective-permute-start.20 = (bf16[1,3,40,960]{3,2,1,0:T(8,128)(2,1)S(1)}, bf16[1,3,40,960]{3,2,1,0:T(8,128)(2,1)S(1)}, u32[]{:S(2)}, u32[]{:S(2)}) collective-permute-start(bf16[1,3,40,960]{3,2,1,0:T(8,128)(2,1)S(1)} %add.81), channel_id=1, source_target_pairs={{0,6},{1,7},{2,4},{3,5},{4,2},{5,3},{6,0},{7,1},{8,14},{9,15},{10,... | collective-permute-start | bytes 691208 | tf_op jit(solution)/shard_map/ppermute | solution.py:206
  73.8 1.5 %collective-permute-start.19 = (bf16[1,3,40,960]{3,2,1,0:T(8,128)(2,1)S(1)}, bf16[1,3,40,960]{3,2,1,0:T(8,128)(2,1)S(1)}, u32[]{:S(2)}, u32[]{:S(2)}) collective-permute-start(bf16[1,3,40,960]{3,2,1,0:T(8,128)(2,1)S(1)} %add.81), channel_id=1, source_target_pairs={{0,4},{1,5},{2,6},{3,7},{4,0},{5,1},{6,2},{7,3},{8,12},{9,13},{10,... | collective-permute-start | bytes 691208 | tf_op jit(solution)/shard_map/ppermute | solution.py:206
  75.3 1.6 %collective-permute-done.17 = f32[3,8,960]{2,1,0:T(8,128)S(1)} collective-permute-done((f32[3,8,960]{2,1,0:T(8,128)S(1)}, f32[3,8,960]{2,1,0:T(8,128)S(1)}, u32[]{:S(2)}, u32[]{:S(2)}) %collective-permute-start.17) | collective-permute-done | bytes 92192 | tf_op jit(solution)/shard_map/ppermute | solution.py:206
  77.0 8.6 %collective-permute-done.19 = bf16[1,3,40,960]{3,2,1,0:T(8,128)(2,1)S(1)} collective-permute-done((bf16[1,3,40,960]{3,2,1,0:T(8,128)(2,1)S(1)}, bf16[1,3,40,960]{3,2,1,0:T(8,128)(2,1)S(1)}, u32[]{:S(2)}, u32[]{:S(2)}) %collective-permute-start.19) | collective-permute-done | bytes 230432 | tf_op jit(solution)/shard_map/ppermute | solution.py:206
  85.7 0.9 collective-permute-start.23
  86.6 1.2 %collective-permute-start.22 = (f32[3,8,960]{2,1,0:T(8,128)S(1)}, f32[3,8,960]{2,1,0:T(8,128)S(1)}, u32[]{:S(2)}, u32[]{:S(2)}) collective-permute-start(f32[3,8,960]{2,1,0:T(8,128)S(1)} %add.83.r0_ref), channel_id=1, source_target_pairs={{0,2},{1,3},{2,0},{3,1},{4,6},{5,7},{6,4},{7,5},{8,10},{9,11},{10,... | collective-permute-start | bytes 276488 | tf_op jit(solution)/shard_map/ppermute | solution.py:206
  87.8 2.3 %errors.1 = bf16[3,320,960]{2,1,0:T(8,128)(2,1)} custom-call(f32[3,320,960]{2,1,0:T(8,128)S(1)} %bitcast.19, bf16[3,320,960]{2,1,0:T(8,128)(2,1)S(1)} %bitcast.22, bf16[3,320,96]{2,1,0:T(8,128)(2,1)S(1)} %solve.1.w_ref, f32[3,32,960]{2,1,0:T(8,128)S(1)} %get-tuple-element.58.all_ref), custom_call_target="tpu_custom_call" | custom-call | bytes 12582912 | tf_op jit(solution)/shard_map/errors/pallas_call | solution.py:322
  90.3 2.7 %collective-permute-done.22.r2_ref = f32[3,8,960]{2,1,0:T(8,128)S(1)} collective-permute-done((f32[3,8,960]{2,1,0:T(8,128)S(1)}, f32[3,8,960]{2,1,0:T(8,128)S(1)}, u32[]{:S(2)}, u32[]{:S(2)}) %collective-permute-start.22) | collective-permute-done | bytes 92192 | tf_op jit(solution)/shard_map/ppermute | solution.py:206
  93.0 4.2 %step.1 = (bf16[3,8,40,960]{3,2,1,0:T(8,128)(2,1)}, bf16[2,8,40,960]{3,2,1,0:T(8,128)(2,1)}) custom-call(s32[3]{0:T(128)S(1)} %copy-done.4, s32[3]{0:T(128)S(1)} %copy-done.5, f32[4]{0:T(128)S(1)} %copy-done.6, f32[4]{0:T(128)S(1)} %copy-done.7, f32[3,8,960]{2,1,0:T(8,128)S(1)} %add.83.r0_ref, f32[3,8,960]{2,1,0:T(8,128)S(1)} %collective-permute-done.21.r1_ref, ...), custom_call_target="tpu_custom_call" | custom-call | tf_op jit(solution)/shard_map/step/pallas_call | solution.py:336
  (61 shorter events, 6.5 us)
Async XLA Ops:
  3.3 5.6 %collective-permute-start = (bf16[4,3,40,960]{3,2,1,0:T(8,128)(2,1)S(1)}, bf16[4,3,40,960]{3,2,1,0:T(8,128)(2,1)}, u32[]{:S(2)}, u32[]{:S(2)}) collective-permute-start(bf16[4,3,40,960]{3,2,1,0:T(8,128)(2,1)S(1)} %get-tuple-element.33), channel_id=1, source_target_pairs={{0,1},{1,0},{2,3},{3,2},{4,5},{5,4},{6,7},{7,6},{8,9},{9,8},{10,11... | collective-permute-start | bytes 2764808 | tf_op jit(solution)/shard_map/ppermute | solution.py:206
  3.8 42.9 %copy-start.1 = (bf16[1,3,320,960]{3,2,1,0:T(8,128)(2,1)S(1)}, bf16[1,3,320,960]{3,2,1,0:T(8,128)(2,1)}, u32[]{:S(2)}) copy-start(bf16[1,3,320,960]{3,2,1,0:T(8,128)(2,1)} %param.9) | copy-start | bytes 5529604
  8.9 5.8 %copy-start.9 = (f32[16,960]{1,0:T(8,128)S(1)}, f32[16,960]{1,0:T(8,128)}, u32[]{:S(2)}) copy-start(f32[16,960]{1,0:T(8,128)} %get-tuple-element.45) | copy-start | bytes 184324
  8.9 7.0 %copy-start.8 = (f32[16,960]{1,0:T(8,128)S(1)}, f32[16,960]{1,0:T(8,128)}, u32[]{:S(2)}) copy-start(f32[16,960]{1,0:T(8,128)} %get-tuple-element.35) | copy-start | bytes 184324
  8.9 37.8 %copy-start = (f32[1,3,320,960]{3,2,1,0:T(8,128)S(1)}, f32[1,3,320,960]{3,2,1,0:T(8,128)}, u32[]{:S(2)}) copy-start(f32[1,3,320,960]{3,2,1,0:T(8,128)} %param.8) | copy-start | bytes 11059204
  10.5 21.5 %collective-permute-start.6 = (bf16[1,3,40,960]{3,2,1,0:T(8,128)(2,1)S(1)}, bf16[1,3,40,960]{3,2,1,0:T(8,128)(2,1)S(1)}, u32[]{:S(2)}, u32[]{:S(2)}) collective-permute-start(bf16[1,3,40,960]{3,2,1,0:T(8,128)(2,1)S(1)} %get-tuple-element.63), channel_id=1, source_target_pairs={{0,6},{1,7},{2,4},{3,5},{4,2},{5,3},{6,0},{7,1},{8,14},{9,15},{10,... | collective-permute-start | bytes 691208 | tf_op jit(solution)/shard_map/ppermute | solution.py:206
  14.0 17.9 %collective-permute-start.5 = (bf16[1,3,40,960]{3,2,1,0:T(8,128)(2,1)S(1)}, bf16[1,3,40,960]{3,2,1,0:T(8,128)(2,1)S(1)}, u32[]{:S(2)}, u32[]{:S(2)}) collective-permute-start(bf16[1,3,40,960]{3,2,1,0:T(8,128)(2,1)S(1)} %get-tuple-element.64), channel_id=1, source_target_pairs={{0,4},{1,5},{2,6},{3,7},{4,0},{5,1},{6,2},{7,3},{8,12},{9,13},{10,... | collective-permute-start | bytes 691208 | tf_op jit(solution)/shard_map/ppermute | solution.py:206
  14.5 17.4 %collective-permute-start.4 = (bf16[1,3,40,960]{3,2,1,0:T(8,128)(2,1)S(1)}, bf16[1,3,40,960]{3,2,1,0:T(8,128)(2,1)S(1)}, u32[]{:S(2)}, u32[]{:S(2)}) collective-permute-start(bf16[1,3,40,960]{3,2,1,0:T(8,128)(2,1)S(1)} %get-tuple-element.65), channel_id=1, source_target_pairs={{0,2},{1,3},{2,0},{3,1},{4,6},{5,7},{6,4},{7,5},{8,10},{9,11},{10,... | collective-permute-start | bytes 691208 | tf_op jit(solution)/shard_map/ppermute | solution.py:206
  14.7 1.3 %collective-permute-start.1 = (f32[16,960]{1,0:T(8,128)S(1)}, f32[16,960]{1,0:T(8,128)S(1)}, u32[]{:S(2)}, u32[]{:S(2)}) collective-permute-start(f32[16,960]{1,0:T(8,128)S(1)} %copy-done.9), channel_id=1, source_target_pairs={{0,1},{1,0},{2,3},{3,2},{4,5},{5,4},{6,7},{7,6},{8,9},{9,8},{10,11... | collective-permute-start | bytes 184328 | tf_op jit(solution)/shard_map/ppermute | solution.py:206
  15.9 11.6 %collective-permute-start.2 = (f32[16,960]{1,0:T(8,128)S(1)}, f32[16,960]{1,0:T(8,128)S(1)}, u32[]{:S(2)}, u32[]{:S(2)}) collective-permute-start(f32[16,960]{1,0:T(8,128)S(1)} %add.67), channel_id=1, source_target_pairs={{0,2},{1,3},{2,0},{3,1},{4,6},{5,7},{6,4},{7,5},{8,10},{9,11},{10,... | collective-permute-start | bytes 184328 | tf_op jit(solution)/shard_map/ppermute | solution.py:206
  27.6 4.3 %collective-permute-start.3 = (f32[16,960]{1,0:T(8,128)S(1)}, f32[16,960]{1,0:T(8,128)S(1)}, u32[]{:S(2)}, u32[]{:S(2)}) collective-permute-start(f32[16,960]{1,0:T(8,128)S(1)} %add.68), channel_id=1, source_target_pairs={{0,4},{1,5},{2,6},{3,7},{4,0},{5,1},{6,2},{7,3},{8,12},{9,13},{10,... | collective-permute-start | bytes 184328 | tf_op jit(solution)/shard_map/ppermute | solution.py:206
  32.0 6.2 %collective-permute-start.9 = (f32[16,960]{1,0:T(8,128)S(1)}, f32[16,960]{1,0:T(8,128)S(1)}, u32[]{:S(2)}, u32[]{:S(2)}) collective-permute-start(f32[16,960]{1,0:T(8,128)S(1)} %add.69), channel_id=1, source_target_pairs={{0,24},{1,25},{2,26},{3,27},{4,28},{5,29},{6,30},{7,31},{8,16},{9,... | collective-permute-start | bytes 184328 | tf_op jit(solution)/shard_map/ppermute | solution.py:206
  35.7 5.4 %collective-permute-start.8 = (f32[16,960]{1,0:T(8,128)S(1)}, f32[16,960]{1,0:T(8,128)S(1)}, u32[]{:S(2)}, u32[]{:S(2)}) collective-permute-start(f32[16,960]{1,0:T(8,128)S(1)} %add.69), channel_id=1, source_target_pairs={{0,16},{1,17},{2,18},{3,19},{4,20},{5,21},{6,22},{7,23},{8,24},{9,... | collective-permute-start | bytes 184328 | tf_op jit(solution)/shard_map/ppermute | solution.py:206
  35.7 5.8 %collective-permute-start.7 = (f32[16,960]{1,0:T(8,128)S(1)}, f32[16,960]{1,0:T(8,128)S(1)}, u32[]{:S(2)}, u32[]{:S(2)}) collective-permute-start(f32[16,960]{1,0:T(8,128)S(1)} %add.69), channel_id=1, source_target_pairs={{0,8},{1,9},{2,10},{3,11},{4,12},{5,13},{6,14},{7,15},{8,0},{9,1},... | collective-permute-start | bytes 184328 | tf_op jit(solution)/shard_map/ppermute | solution.py:206
  36.5 8.9 %collective-permute-start.10 = (bf16[1,3,40,960]{3,2,1,0:T(8,128)(2,1)S(1)}, bf16[1,3,40,960]{3,2,1,0:T(8,128)(2,1)S(1)}, u32[]{:S(2)}, u32[]{:S(2)}) collective-permute-start(bf16[1,3,40,960]{3,2,1,0:T(8,128)(2,1)S(1)} %add_add_fusion), channel_id=1, source_target_pairs={{0,8},{1,9},{2,10},{3,11},{4,12},{5,13},{6,14},{7,15},{8,0},{9,1},... | collective-permute-start | bytes 691208 | tf_op jit(solution)/shard_map/ppermute | solution.py:206
  45.4 1.3 %collective-permute-start.11 = (f32[16,960]{1,0:T(8,128)S(1)}, f32[16,960]{1,0:T(8,128)S(1)}, u32[]{:S(2)}, u32[]{:S(2)}) collective-permute-start(f32[16,960]{1,0:T(8,128)S(1)} %add_add_fusion.1.mine_ref), channel_id=1, source_target_pairs={{0,1},{1,0},{2,3},{3,2},{4,5},{5,4},{6,7},{7,6},{8,9},{9,8},{10,11... | collective-permute-start | bytes 184328 | tf_op jit(solution)/shard_map/ppermute | solution.py:206
  48.5 1.5 %collective-permute-start.12 = (f32[2,3,8,960]{3,2,1,0:T(8,128)S(1)}, f32[2,3,8,960]{3,2,1,0:T(8,128)S(1)}, u32[]{:S(2)}, u32[]{:S(2)}) collective-permute-start(f32[2,3,8,960]{3,2,1,0:T(8,128)S(1)} %get-tuple-element.51), channel_id=1, source_target_pairs={{0,1},{1,0},{2,3},{3,2},{4,5},{5,4},{6,7},{7,6},{8,9},{9,8},{10,11... | collective-permute-start | bytes 552968 | tf_op jit(solution)/shard_map/ppermute | solution.py:206
  50.0 4.9 %collective-permute-start.13 = (f32[3,8,960]{2,1,0:T(8,128)S(1)}, f32[3,8,960]{2,1,0:T(8,128)S(1)}, u32[]{:S(2)}, u32[]{:S(2)}) collective-permute-start(f32[3,8,960]{2,1,0:T(8,128)S(1)} %fusion), channel_id=1, source_target_pairs={{0,2},{1,3},{2,0},{3,1},{4,6},{5,7},{6,4},{7,5},{8,10},{9,11},{10,... | collective-permute-start | bytes 276488 | tf_op jit(solution)/shard_map/ppermute | solution.py:206
  51.6 13.9 %collective-permute-start.15 = (bf16[1,3,40,960]{3,2,1,0:T(8,128)(2,1)S(1)}, bf16[1,3,40,960]{3,2,1,0:T(8,128)(2,1)S(1)}, u32[]{:S(2)}, u32[]{:S(2)}) collective-permute-start(bf16[1,3,40,960]{3,2,1,0:T(8,128)(2,1)S(1)} %add.76), channel_id=1, source_target_pairs={{0,16},{1,17},{2,18},{3,19},{4,20},{5,21},{6,22},{7,23},{8,24},{9,... | collective-permute-start | bytes 691208 | tf_op jit(solution)/shard_map/ppermute | solution.py:206
  55.0 4.7 %collective-permute-start.14 = (f32[3,8,960]{2,1,0:T(8,128)S(1)}, f32[3,8,960]{2,1,0:T(8,128)S(1)}, u32[]{:S(2)}, u32[]{:S(2)}) collective-permute-start(f32[3,8,960]{2,1,0:T(8,128)S(1)} %fusion.2), channel_id=1, source_target_pairs={{0,4},{1,5},{2,6},{3,7},{4,0},{5,1},{6,2},{7,3},{8,12},{9,13},{10,... | collective-permute-start | bytes 276488 | tf_op jit(solution)/shard_map/ppermute | solution.py:206
  65.6 4.7 %collective-permute-start.16 = (f32[3,8,960]{2,1,0:T(8,128)S(1)}, f32[3,8,960]{2,1,0:T(8,128)S(1)}, u32[]{:S(2)}, u32[]{:S(2)}) collective-permute-start(f32[3,8,960]{2,1,0:T(8,128)S(1)} %add.80), channel_id=1, source_target_pairs={{0,8},{1,9},{2,10},{3,11},{4,12},{5,13},{6,14},{7,15},{8,0},{9,1},... | collective-permute-start | bytes 276488 | tf_op jit(solution)/shard_map/ppermute | solution.py:206
  65.6 11.3 %collective-permute-start.18 = (bf16[1,3,40,960]{3,2,1,0:T(8,128)(2,1)S(1)}, bf16[1,3,40,960]{3,2,1,0:T(8,128)(2,1)S(1)}, u32[]{:S(2)}, u32[]{:S(2)}) collective-permute-start(bf16[1,3,40,960]{3,2,1,0:T(8,128)(2,1)S(1)} %add.81), channel_id=1, source_target_pairs={{0,2},{1,3},{2,0},{3,1},{4,6},{5,7},{6,4},{7,5},{8,10},{9,11},{10,... | collective-permute-start | bytes 691208 | tf_op jit(solution)/shard_map/ppermute | solution.py:206
  70.3 6.6 %collective-permute-start.17 = (f32[3,8,960]{2,1,0:T(8,128)S(1)}, f32[3,8,960]{2,1,0:T(8,128)S(1)}, u32[]{:S(2)}, u32[]{:S(2)}) collective-permute-start(f32[3,8,960]{2,1,0:T(8,128)S(1)} %add.82), channel_id=1, source_target_pairs={{0,16},{1,17},{2,18},{3,19},{4,20},{5,21},{6,22},{7,23},{8,24},{9,... | collective-permute-start | bytes 276488 | tf_op jit(solution)/shard_map/ppermute | solution.py:206
  72.3 13.2 %collective-permute-start.20 = (bf16[1,3,40,960]{3,2,1,0:T(8,128)(2,1)S(1)}, bf16[1,3,40,960]{3,2,1,0:T(8,128)(2,1)S(1)}, u32[]{:S(2)}, u32[]{:S(2)}) collective-permute-start(bf16[1,3,40,960]{3,2,1,0:T(8,128)(2,1)S(1)} %add.81), channel_id=1, source_target_pairs={{0,6},{1,7},{2,4},{3,5},{4,2},{5,3},{6,0},{7,1},{8,14},{9,15},{10,... | collective-permute-start | bytes 691208 | tf_op jit(solution)/shard_map/ppermute | solution.py:206
  73.8 11.8 %collective-permute-start.19 = (bf16[1,3,40,960]{3,2,1,0:T(8,128)(2,1)S(1)}, bf16[1,3,40,960]{3,2,1,0:T(8,128)(2,1)S(1)}, u32[]{:S(2)}, u32[]{:S(2)}) collective-permute-start(bf16[1,3,40,960]{3,2,1,0:T(8,128)(2,1)S(1)} %add.81), channel_id=1, source_target_pairs={{0,4},{1,5},{2,6},{3,7},{4,0},{5,1},{6,2},{7,3},{8,12},{9,13},{10,... | collective-permute-start | bytes 691208 | tf_op jit(solution)/shard_map/ppermute | solution.py:206
  85.6 7.4 %collective-permute-start.24 = (bf16[4,3,40,960]{3,2,1,0:T(8,128)(2,1)S(1)}, bf16[4,3,40,960]{3,2,1,0:T(8,128)(2,1)S(1)}, u32[]{:S(2)}, u32[]{:S(2)}) collective-permute-start(bf16[4,3,40,960]{3,2,1,0:T(8,128)(2,1)S(1)} %constant_dynamic-update-slice_fusion.even_ref), channel_id=1, source_target_pairs={{0,1},{1,0},{2,3},{3,2},{4,5},{5,4},{6,7},{7,6},{8,9},{9,8},{10,11... | collective-permute-start | bytes 2764808 | tf_op jit(solution)/shard_map/ppermute | solution.py:206
  85.7 4.6 %collective-permute-start.23 = (f32[3,8,960]{2,1,0:T(8,128)S(1)}, f32[3,8,960]{2,1,0:T(8,128)S(1)}, u32[]{:S(2)}, u32[]{:S(2)}) collective-permute-start(f32[3,8,960]{2,1,0:T(8,128)S(1)} %add.83.r0_ref), channel_id=1, source_target_pairs={{0,3},{1,2},{2,1},{3,0},{4,7},{5,6},{6,5},{7,4},{8,11},{9,10},{10,... | collective-permute-start | bytes 276488 | tf_op jit(solution)/shard_map/ppermute | solution.py:206
  86.6 6.4 %collective-permute-start.22 = (f32[3,8,960]{2,1,0:T(8,128)S(1)}, f32[3,8,960]{2,1,0:T(8,128)S(1)}, u32[]{:S(2)}, u32[]{:S(2)}) collective-permute-start(f32[3,8,960]{2,1,0:T(8,128)S(1)} %add.83.r0_ref), channel_id=1, source_target_pairs={{0,2},{1,3},{2,0},{3,1},{4,6},{5,7},{6,4},{7,5},{8,10},{9,11},{10,... | collective-permute-start | bytes 276488 | tf_op jit(solution)/shard_map/ppermute | solution.py:206
  87.8 5.1 %collective-permute-start.21 = (f32[3,8,960]{2,1,0:T(8,128)S(1)}, f32[3,8,960]{2,1,0:T(8,128)S(1)}, u32[]{:S(2)}, u32[]{:S(2)}) collective-permute-start(f32[3,8,960]{2,1,0:T(8,128)S(1)} %add.83.r0_ref), channel_id=1, source_target_pairs={{0,1},{1,0},{2,3},{3,2},{4,5},{5,4},{6,7},{7,6},{8,9},{9,8},{10,11... | collective-permute-start | bytes 276488 | tf_op jit(solution)/shard_map/ppermute | solution.py:206
  87.8 5.1 %copy-start.5 = (s32[3]{0:T(128)S(1)}, s32[3]{0:T(128)}, u32[]{:S(2)}) copy-start(s32[3]{0:T(128)} %buckets_ref.1) | copy-start | bytes 40
  87.8 5.1 %copy-start.6 = (f32[4]{0:T(128)S(1)}, f32[4]{0:T(128)}, u32[]{:S(2)}) copy-start(f32[4]{0:T(128)} %rates_ref.1) | copy-start | bytes 52
  87.8 5.1 %copy-start.7 = (f32[4]{0:T(128)S(1)}, f32[4]{0:T(128)}, u32[]{:S(2)}) copy-start(f32[4]{0:T(128)} %betas_ref.1) | copy-start | bytes 52
  (3 other events, 7.1 us)

commit v5 on v4

--- a/solution.py
+++ b/solution.py
@@ -261,14 +261,14 @@
     evens = [after(evens[n], mine) + got[n : n + 1] for n in range(4)]
     mine = mine + swap(after(other, *evens), 1)
     got = [swap(evens[n], 2 * n) for n in (1, 2, 3)]
-    for bit in bits[1:3]:
+    for bit in bits[3:]:
         mine = total_over(mine, [bit], count)
     old = after(evens[0], mine) + got[0] + got[1] + got[2]
     mine = after(mine, old)
     from_other = swap(old, 1 << bits[3])
-    mine = total_over(mine, bits[3:], count)
+    mine = total_over(mine, bits[1:3], count)
     old = after(old, mine) + from_other
-    other = swap(after(mine, old), 1)
+    other = swap(mine, 1)
 
     right_all, keep, send2, send = pl.pallas_call(
         right_kernel,
@@ -303,18 +303,17 @@
         name="solve",
     )(mine, other)
 
-    got = swap(send, 1)
+    got = swap(after(send, old), 1)
     r0 = keep + got[0] + swap(send2 + got[1], 2)
     for bit in bits[4:-1]:
         old = old + swap(old, 1 << bit)
     from_other = swap(old, 1 << bits[-1])
     r0 = total_over(r0, bits[2:3], count)
     old = after(old, r0) + from_other
-    r0 = after(r0, old)
+    r0 = after(r0, old, w)
     got = [swap(old, mask) for mask in (2, 4, 6)]
-    for bit in bits[3:-1]:
+    for bit in bits[3:]:
         r0 = total_over(r0, [bit], count)
-    r0 = total_over(after(r0, w), bits[-1:], count)
     evens = jnp.concatenate([after(old, r0)] + got)
     r0 = after(r0, evens)
     odds = swap(evens, 1)

time: 97.3 us -> 86 us (0.88)
  waiting for transfers between devices: 50.6 us -> 34.7 us
  starting transfers between devices: 24.3 us -> 29 us
    ppermute x25, waiting for transfers between devices: 50.6 us -> 34.7 us  [exchange(): return lax.ppermute(value, AXES, [(d, d ^ mask) for d in range(count)])]
    ppermute x25, starting transfers between devices: 24.3 us -> 29 us  [exchange(): return lax.ppermute(value, AXES, [(d, d ^ mask) for d in range(count)])]
  transfers between devices with their start and end apart: 25 -> 25, of which waited for: 17 -> 16; matrix products, arithmetic and copies ran while one was open for 0% -> 0% of each run, Pallas kernels for 11% -> 15%
where the time goes in v5:
time: 86 us; the launch traced here: 85.9 us
  waiting for transfers between devices  34.7 us (40%)
  starting transfers between devices  29 us (34%)
  Pallas kernels  17.4 us (20%)
  local copies, waits for them, and re-layouts  2.08 us (2%)
  other arithmetic  1.84 us (2%)
  between operations  0.9 us (1%)
    ppermute x25, waiting for transfers between devices, exchange(): return lax.ppermute(value, AXES, [(d, d ^ mask) for d in range(count)])  34.7 us
    ppermute x25, starting transfers between devices, exchange(): return lax.ppermute(value, AXES, [(d, d ^ mask) for d in range(count)])  29 us
    pallas_call x1, Pallas kernels, on_device(): pl.pallas_call(left_kernel, in_specs=[pl.BlockSpec(memory_space=pltpu.HBM...  5.04 us
    pallas_call x1, Pallas kernels, on_device(): pl.pallas_call(step_kernel, grid=(mats,), in_specs=[SMEM] * 4 + [quarter_...  4.16 us
    pallas_call x1, Pallas kernels, on_device(): pl.pallas_call(solve_kernel, grid=(1,), in_specs=[whole((half, mats * row...  3.38 us
    pallas_call x1, Pallas kernels, on_device(): pl.pallas_call(error_kernel, grid=(mats,), in_specs=[grad_spec, grad_spec...  2.33 us
    unnamed x23, local copies, waits for them, and re-layouts  2.06 us
    pallas_call x1, Pallas kernels, on_device(): pl.pallas_call(right_kernel, grid=(mats,), in_specs=[whole((half, mats *...  1.75 us
  transfers between devices with their start and end apart: 25, of which 16 were waited for; matrix products, arithmetic and copies ran while one was open for 0% of the time, Pallas kernels for 15%

profile of v5, /device:TPU:0, one launch (start us, length us, event | category | flops | bytes accessed | tf_op | source)
XLA Modules:
  0.0 85.9 jit_solution(17686470357493380423)
XLA Ops:
  0.6 1.3 %copy-done.2 = bf16[2,320,960]{2,1,0:T(8,128)(2,1)S(1)} copy-done((bf16[2,320,960]{2,1,0:T(8,128)(2,1)S(1)}, bf16[2,320,960]{2,1,0:T(8,128)(2,1)}, u32[]{:S(2)}) %copy-start.2) | copy-done | bytes 1228824
  2.6 0.7 old.1
  3.8 5.0 %left.1 = (f32[16,960]{1,0:T(8,128)}, f32[16,960]{1,0:T(8,128)}) custom-call(f32[3,320,960]{2,1,0:T(8,128)} %bitcast.17, bf16[3,320,960]{2,1,0:T(8,128)(2,1)} %bitcast.20, f32[3,32,960]{2,1,0:T(8,128)} %bitcast.25), custom_call_target="tpu_custom_call" | custom-call | tf_op jit(solution)/shard_map/left/pallas_call | solution.py:245
  8.9 1.6 %slice_add_fusion = (bf16[1,3,40,960]{3,2,1,0:T(8,128)(2,1)S(1)}, bf16[1,3,40,960]{3,2,1,0:T(8,128)(2,1)S(1)}, bf16[1,3,40,960]{3,2,1,0:T(8,128)(2,1)S(1)}, bf16[1,3,40,960]{3,2,1,0:T(8,128)(2,1)S(1)}) fusion(bf16[1,3,40,960]{3,2,1,0:T(8,128)(2,1)S(1)} %get-tuple-element.43, bf16[4,3,40,960]{3,2,1,0:T(8,128)(2,1)} %collective-permute-done, ...), kind=kLoop, calls=%fused_computation | loop fusion | flops 460800 | bytes 2764800 | tf_op jit(solution)/shard_map/add | solution.py:261
  10.5 3.5 %collective-permute-start.6 = (bf16[1,3,40,960]{3,2,1,0:T(8,128)(2,1)S(1)}, bf16[1,3,40,960]{3,2,1,0:T(8,128)(2,1)S(1)}, u32[]{:S(2)}, u32[]{:S(2)}) collective-permute-start(bf16[1,3,40,960]{3,2,1,0:T(8,128)(2,1)S(1)} %get-tuple-element.61), channel_id=1, source_target_pairs={{0,6},{1,7},{2,4},{3,5},{4,2},{5,3},{6,0},{7,1},{8,14},{9,15},{10,... | collective-permute-start | bytes 691208 | tf_op jit(solution)/shard_map/ppermute | solution.py:206
  14.7 1.3 %collective-permute-done.1 = f32[16,960]{1,0:T(8,128)S(1)} collective-permute-done((f32[16,960]{1,0:T(8,128)S(1)}, f32[16,960]{1,0:T(8,128)S(1)}, u32[]{:S(2)}, u32[]{:S(2)}) %collective-permute-start.1) | collective-permute-done | bytes 61472 | tf_op jit(solution)/shard_map/ppermute | solution.py:206
  15.9 2.0 %collective-permute-start.2 = (f32[16,960]{1,0:T(8,128)S(1)}, f32[16,960]{1,0:T(8,128)S(1)}, u32[]{:S(2)}, u32[]{:S(2)}) collective-permute-start(f32[16,960]{1,0:T(8,128)S(1)} %add.67), channel_id=1, source_target_pairs={{0,8},{1,9},{2,10},{3,11},{4,12},{5,13},{6,14},{7,15},{8,0},{9,1},... | collective-permute-start | bytes 184328 | tf_op jit(solution)/shard_map/ppermute | solution.py:206
  18.0 2.4 %collective-permute-done.2 = f32[16,960]{1,0:T(8,128)S(1)} collective-permute-done((f32[16,960]{1,0:T(8,128)S(1)}, f32[16,960]{1,0:T(8,128)S(1)}, u32[]{:S(2)}, u32[]{:S(2)}) %collective-permute-start.2) | collective-permute-done | bytes 61472 | tf_op jit(solution)/shard_map/ppermute | solution.py:206
  20.4 2.9 %collective-permute-start.3 = (f32[16,960]{1,0:T(8,128)S(1)}, f32[16,960]{1,0:T(8,128)S(1)}, u32[]{:S(2)}, u32[]{:S(2)}) collective-permute-start(f32[16,960]{1,0:T(8,128)S(1)} %add.68), channel_id=1, source_target_pairs={{0,16},{1,17},{2,18},{3,19},{4,20},{5,21},{6,22},{7,23},{8,24},{9,... | collective-permute-start | bytes 184328 | tf_op jit(solution)/shard_map/ppermute | solution.py:206
  23.3 2.6 %collective-permute-done.3 = f32[16,960]{1,0:T(8,128)S(1)} collective-permute-done((f32[16,960]{1,0:T(8,128)S(1)}, f32[16,960]{1,0:T(8,128)S(1)}, u32[]{:S(2)}, u32[]{:S(2)}) %collective-permute-start.3) | collective-permute-done | bytes 61472 | tf_op jit(solution)/shard_map/ppermute | solution.py:206
  26.2 2.3 %collective-permute-start.9 = (f32[16,960]{1,0:T(8,128)S(1)}, f32[16,960]{1,0:T(8,128)S(1)}, u32[]{:S(2)}, u32[]{:S(2)}) collective-permute-start(f32[16,960]{1,0:T(8,128)S(1)} %add.69), channel_id=1, source_target_pairs={{0,6},{1,7},{2,4},{3,5},{4,2},{5,3},{6,0},{7,1},{8,14},{9,15},{10,... | collective-permute-start | bytes 184328 | tf_op jit(solution)/shard_map/ppermute | solution.py:206
  28.6 0.7 collective-permute-start.8
  29.8 1.6 %collective-permute-start.11 = (bf16[1,3,40,960]{3,2,1,0:T(8,128)(2,1)S(1)}, bf16[1,3,40,960]{3,2,1,0:T(8,128)(2,1)S(1)}, u32[]{:S(2)}, u32[]{:S(2)}) collective-permute-start(bf16[1,3,40,960]{3,2,1,0:T(8,128)(2,1)S(1)} %add_add_fusion), channel_id=1, source_target_pairs={{0,8},{1,9},{2,10},{3,11},{4,12},{5,13},{6,14},{7,15},{8,0},{9,1},... | collective-permute-start | bytes 691208 | tf_op jit(solution)/shard_map/ppermute | solution.py:206
  31.9 0.9 %collective-permute-done.8 = f32[16,960]{1,0:T(8,128)S(1)} collective-permute-done((f32[16,960]{1,0:T(8,128)S(1)}, f32[16,960]{1,0:T(8,128)S(1)}, u32[]{:S(2)}, u32[]{:S(2)}) %collective-permute-start.8) | collective-permute-done | bytes 61472 | tf_op jit(solution)/shard_map/ppermute | solution.py:206
  33.6 1.2 %collective-permute-done.10.other_ref = f32[16,960]{1,0:T(8,128)S(1)} collective-permute-done((f32[16,960]{1,0:T(8,128)S(1)}, f32[16,960]{1,0:T(8,128)S(1)}, u32[]{:S(2)}, u32[]{:S(2)}) %collective-permute-start.10) | collective-permute-done | bytes 61472 | tf_op jit(solution)/shard_map/ppermute | solution.py:206
  34.9 1.8 %right.1 = (f32[3,32,960]{2,1,0:T(8,128)S(1)}, f32[3,8,960]{2,1,0:T(8,128)S(1)}, f32[3,8,960]{2,1,0:T(8,128)S(1)}, f32[2,3,8,960]{3,2,1,0:T(8,128)S(1)}) custom-call(f32[16,960]{1,0:T(8,128)S(1)} %add_add_fusion.1.mine_ref, f32[16,960]{1,0:T(8,128)S(1)} %collective-permute-done.10.other_ref, f32[3,320,960]{2,1,0:T(8,128)S(1)} %bitcast.18, ...), custom_call_target="tpu_custom_call" | custom-call | tf_op jit(solution)/shard_map/right/pallas_call | solution.py:273
  36.9 1.3 %collective-permute-done.12 = f32[2,3,8,960]{3,2,1,0:T(8,128)S(1)} collective-permute-done((f32[2,3,8,960]{3,2,1,0:T(8,128)S(1)}, f32[2,3,8,960]{3,2,1,0:T(8,128)S(1)}, u32[]{:S(2)}, u32[]{:S(2)}) %collective-permute-start.12) | collective-permute-done | bytes 184352 | tf_op jit(solution)/shard_map/ppermute | solution.py:206
  38.2 1.7 %collective-permute-start.13 = (f32[3,8,960]{2,1,0:T(8,128)S(1)}, f32[3,8,960]{2,1,0:T(8,128)S(1)}, u32[]{:S(2)}, u32[]{:S(2)}) collective-permute-start(f32[3,8,960]{2,1,0:T(8,128)S(1)} %fusion), channel_id=1, source_target_pairs={{0,2},{1,3},{2,0},{3,1},{4,6},{5,7},{6,4},{7,5},{8,10},{9,11},{10,... | collective-permute-start | bytes 276488 | tf_op jit(solution)/shard_map/ppermute | solution.py:206
  39.9 2.6 %collective-permute-start.15 = (bf16[1,3,40,960]{3,2,1,0:T(8,128)(2,1)S(1)}, bf16[1,3,40,960]{3,2,1,0:T(8,128)(2,1)S(1)}, u32[]{:S(2)}, u32[]{:S(2)}) collective-permute-start(bf16[1,3,40,960]{3,2,1,0:T(8,128)(2,1)S(1)} %add.76), channel_id=1, source_target_pairs={{0,16},{1,17},{2,18},{3,19},{4,20},{5,21},{6,22},{7,23},{8,24},{9,... | collective-permute-start | bytes 691208 | tf_op jit(solution)/shard_map/ppermute | solution.py:206
  43.2 1.7 %collective-permute-start.14 = (f32[3,8,960]{2,1,0:T(8,128)S(1)}, f32[3,8,960]{2,1,0:T(8,128)S(1)}, u32[]{:S(2)}, u32[]{:S(2)}) collective-permute-start(f32[3,8,960]{2,1,0:T(8,128)S(1)} %fusion.2), channel_id=1, source_target_pairs={{0,4},{1,5},{2,6},{3,7},{4,0},{5,1},{6,2},{7,3},{8,12},{9,13},{10,... | collective-permute-start | bytes 276488 | tf_op jit(solution)/shard_map/ppermute | solution.py:206
  44.9 3.4 %solve.1.w_ref = bf16[3,320,96]{2,1,0:T(8,128)(2,1)S(1)} custom-call(f32[16,960]{1,0:T(8,128)S(1)} %add_add_fusion.1.mine_ref, f32[16,960]{1,0:T(8,128)S(1)} %collective-permute-done.10.other_ref), custom_call_target="tpu_custom_call" | custom-call | bytes 16777216 | tf_op jit(solution)/shard_map/solve/pallas_call | solution.py:294
  48.3 5.5 %collective-permute-done.15 = bf16[1,3,40,960]{3,2,1,0:T(8,128)(2,1)S(1)} collective-permute-done((bf16[1,3,40,960]{3,2,1,0:T(8,128)(2,1)S(1)}, bf16[1,3,40,960]{3,2,1,0:T(8,128)(2,1)S(1)}, u32[]{:S(2)}, u32[]{:S(2)}) %collective-permute-start.15) | collective-permute-done | bytes 230432 | tf_op jit(solution)/shard_map/ppermute | solution.py:206
  53.8 0.7 collective-permute-start.16
  55.1 3.4 %collective-permute-done.16 = f32[3,8,960]{2,1,0:T(8,128)S(1)} collective-permute-done((f32[3,8,960]{2,1,0:T(8,128)S(1)}, f32[3,8,960]{2,1,0:T(8,128)S(1)}, u32[]{:S(2)}, u32[]{:S(2)}) %collective-permute-start.16) | collective-permute-done | bytes 92192 | tf_op jit(solution)/shard_map/ppermute | solution.py:206
  58.5 2.5 %collective-permute-start.17 = (f32[3,8,960]{2,1,0:T(8,128)S(1)}, f32[3,8,960]{2,1,0:T(8,128)S(1)}, u32[]{:S(2)}, u32[]{:S(2)}) collective-permute-start(f32[3,8,960]{2,1,0:T(8,128)S(1)} %add.82), channel_id=1, source_target_pairs={{0,16},{1,17},{2,18},{3,19},{4,20},{5,21},{6,22},{7,23},{8,24},{9,... | collective-permute-start | bytes 276488 | tf_op jit(solution)/shard_map/ppermute | solution.py:206
  61.0 1.5 %collective-permute-start.20 = (bf16[1,3,40,960]{3,2,1,0:T(8,128)(2,1)S(1)}, bf16[1,3,40,960]{3,2,1,0:T(8,128)(2,1)S(1)}, u32[]{:S(2)}, u32[]{:S(2)}) collective-permute-start(bf16[1,3,40,960]{3,2,1,0:T(8,128)(2,1)S(1)} %add.81), channel_id=1, source_target_pairs={{0,6},{1,7},{2,4},{3,5},{4,2},{5,3},{6,0},{7,1},{8,14},{9,15},{10,... | collective-permute-start | bytes 691208 | tf_op jit(solution)/shard_map/ppermute | solution.py:206
  63.0 2.6 %collective-permute-done.17 = f32[3,8,960]{2,1,0:T(8,128)S(1)} collective-permute-done((f32[3,8,960]{2,1,0:T(8,128)S(1)}, f32[3,8,960]{2,1,0:T(8,128)S(1)}, u32[]{:S(2)}, u32[]{:S(2)}) %collective-permute-start.17) | collective-permute-done | bytes 92192 | tf_op jit(solution)/shard_map/ppermute | solution.py:206
  65.7 8.6 %collective-permute-done.19 = bf16[1,3,40,960]{3,2,1,0:T(8,128)(2,1)S(1)} collective-permute-done((bf16[1,3,40,960]{3,2,1,0:T(8,128)(2,1)S(1)}, bf16[1,3,40,960]{3,2,1,0:T(8,128)(2,1)S(1)}, u32[]{:S(2)}, u32[]{:S(2)}) %collective-permute-start.19) | collective-permute-done | bytes 230432 | tf_op jit(solution)/shard_map/ppermute | solution.py:206
  75.1 1.5 %collective-permute-start.22 = (f32[3,8,960]{2,1,0:T(8,128)S(1)}, f32[3,8,960]{2,1,0:T(8,128)S(1)}, u32[]{:S(2)}, u32[]{:S(2)}) collective-permute-start(f32[3,8,960]{2,1,0:T(8,128)S(1)} %add.83.r0_ref), channel_id=1, source_target_pairs={{0,2},{1,3},{2,0},{3,1},{4,6},{5,7},{6,4},{7,5},{8,10},{9,11},{10,... | collective-permute-start | bytes 276488 | tf_op jit(solution)/shard_map/ppermute | solution.py:206
  76.6 2.3 %errors.1 = bf16[3,320,960]{2,1,0:T(8,128)(2,1)} custom-call(f32[3,320,960]{2,1,0:T(8,128)S(1)} %bitcast.19, bf16[3,320,960]{2,1,0:T(8,128)(2,1)S(1)} %bitcast.22, bf16[3,320,96]{2,1,0:T(8,128)(2,1)S(1)} %solve.1.w_ref, f32[3,32,960]{2,1,0:T(8,128)S(1)} %get-tuple-element.56.all_ref), custom_call_target="tpu_custom_call" | custom-call | bytes 12582912 | tf_op jit(solution)/shard_map/errors/pallas_call | solution.py:321
  79.0 2.7 %collective-permute-done.22.r2_ref = f32[3,8,960]{2,1,0:T(8,128)S(1)} collective-permute-done((f32[3,8,960]{2,1,0:T(8,128)S(1)}, f32[3,8,960]{2,1,0:T(8,128)S(1)}, u32[]{:S(2)}, u32[]{:S(2)}) %collective-permute-start.22) | collective-permute-done | bytes 92192 | tf_op jit(solution)/shard_map/ppermute | solution.py:206
  81.7 4.2 %step.1 = (bf16[3,8,40,960]{3,2,1,0:T(8,128)(2,1)}, bf16[2,8,40,960]{3,2,1,0:T(8,128)(2,1)}) custom-call(s32[3]{0:T(128)S(1)} %copy-done.4, s32[3]{0:T(128)S(1)} %copy-done.5, f32[4]{0:T(128)S(1)} %copy-done.6, f32[4]{0:T(128)S(1)} %copy-done.7, f32[3,8,960]{2,1,0:T(8,128)S(1)} %add.83.r0_ref, f32[3,8,960]{2,1,0:T(8,128)S(1)} %collective-permute-done.21.r1_ref, ...), custom_call_target="tpu_custom_call" | custom-call | tf_op jit(solution)/shard_map/step/pallas_call | solution.py:335
  (61 shorter events, 7.0 us)
Async XLA Ops:
  3.3 5.6 %collective-permute-start = (bf16[4,3,40,960]{3,2,1,0:T(8,128)(2,1)S(1)}, bf16[4,3,40,960]{3,2,1,0:T(8,128)(2,1)}, u32[]{:S(2)}, u32[]{:S(2)}) collective-permute-start(bf16[4,3,40,960]{3,2,1,0:T(8,128)(2,1)S(1)} %get-tuple-element.32), channel_id=1, source_target_pairs={{0,1},{1,0},{2,3},{3,2},{4,5},{5,4},{6,7},{7,6},{8,9},{9,8},{10,11... | collective-permute-start | bytes 2764808 | tf_op jit(solution)/shard_map/ppermute | solution.py:206
  3.8 31.0 %copy-start.1 = (bf16[1,3,320,960]{3,2,1,0:T(8,128)(2,1)S(1)}, bf16[1,3,320,960]{3,2,1,0:T(8,128)(2,1)}, u32[]{:S(2)}) copy-start(bf16[1,3,320,960]{3,2,1,0:T(8,128)(2,1)} %param.9) | copy-start | bytes 5529604
  8.9 5.8 %copy-start.9 = (f32[16,960]{1,0:T(8,128)S(1)}, f32[16,960]{1,0:T(8,128)}, u32[]{:S(2)}) copy-start(f32[16,960]{1,0:T(8,128)} %get-tuple-element.44) | copy-start | bytes 184324
  8.9 7.0 %copy-start.8 = (f32[16,960]{1,0:T(8,128)S(1)}, f32[16,960]{1,0:T(8,128)}, u32[]{:S(2)}) copy-start(f32[16,960]{1,0:T(8,128)} %get-tuple-element.34) | copy-start | bytes 184324
  8.9 26.0 %copy-start = (f32[1,3,320,960]{3,2,1,0:T(8,128)S(1)}, f32[1,3,320,960]{3,2,1,0:T(8,128)}, u32[]{:S(2)}) copy-start(f32[1,3,320,960]{3,2,1,0:T(8,128)} %param.8) | copy-start | bytes 11059204
  10.5 15.5 %collective-permute-start.6 = (bf16[1,3,40,960]{3,2,1,0:T(8,128)(2,1)S(1)}, bf16[1,3,40,960]{3,2,1,0:T(8,128)(2,1)S(1)}, u32[]{:S(2)}, u32[]{:S(2)}) collective-permute-start(bf16[1,3,40,960]{3,2,1,0:T(8,128)(2,1)S(1)} %get-tuple-element.61), channel_id=1, source_target_pairs={{0,6},{1,7},{2,4},{3,5},{4,2},{5,3},{6,0},{7,1},{8,14},{9,15},{10,... | collective-permute-start | bytes 691208 | tf_op jit(solution)/shard_map/ppermute | solution.py:206
  14.0 12.0 %collective-permute-start.5 = (bf16[1,3,40,960]{3,2,1,0:T(8,128)(2,1)S(1)}, bf16[1,3,40,960]{3,2,1,0:T(8,128)(2,1)S(1)}, u32[]{:S(2)}, u32[]{:S(2)}) collective-permute-start(bf16[1,3,40,960]{3,2,1,0:T(8,128)(2,1)S(1)} %get-tuple-element.62), channel_id=1, source_target_pairs={{0,4},{1,5},{2,6},{3,7},{4,0},{5,1},{6,2},{7,3},{8,12},{9,13},{10,... | collective-permute-start | bytes 691208 | tf_op jit(solution)/shard_map/ppermute | solution.py:206
  14.5 11.7 %collective-permute-start.4 = (bf16[1,3,40,960]{3,2,1,0:T(8,128)(2,1)S(1)}, bf16[1,3,40,960]{3,2,1,0:T(8,128)(2,1)S(1)}, u32[]{:S(2)}, u32[]{:S(2)}) collective-permute-start(bf16[1,3,40,960]{3,2,1,0:T(8,128)(2,1)S(1)} %get-tuple-element.63), channel_id=1, source_target_pairs={{0,2},{1,3},{2,0},{3,1},{4,6},{5,7},{6,4},{7,5},{8,10},{9,11},{10,... | collective-permute-start | bytes 691208 | tf_op jit(solution)/shard_map/ppermute | solution.py:206
  14.7 1.3 %collective-permute-start.1 = (f32[16,960]{1,0:T(8,128)S(1)}, f32[16,960]{1,0:T(8,128)S(1)}, u32[]{:S(2)}, u32[]{:S(2)}) collective-permute-start(f32[16,960]{1,0:T(8,128)S(1)} %copy-done.9), channel_id=1, source_target_pairs={{0,1},{1,0},{2,3},{3,2},{4,5},{5,4},{6,7},{7,6},{8,9},{9,8},{10,11... | collective-permute-start | bytes 184328 | tf_op jit(solution)/shard_map/ppermute | solution.py:206
  15.9 4.5 %collective-permute-start.2 = (f32[16,960]{1,0:T(8,128)S(1)}, f32[16,960]{1,0:T(8,128)S(1)}, u32[]{:S(2)}, u32[]{:S(2)}) collective-permute-start(f32[16,960]{1,0:T(8,128)S(1)} %add.67), channel_id=1, source_target_pairs={{0,8},{1,9},{2,10},{3,11},{4,12},{5,13},{6,14},{7,15},{8,0},{9,1},... | collective-permute-start | bytes 184328 | tf_op jit(solution)/shard_map/ppermute | solution.py:206
  20.4 5.6 %collective-permute-start.3 = (f32[16,960]{1,0:T(8,128)S(1)}, f32[16,960]{1,0:T(8,128)S(1)}, u32[]{:S(2)}, u32[]{:S(2)}) collective-permute-start(f32[16,960]{1,0:T(8,128)S(1)} %add.68), channel_id=1, source_target_pairs={{0,16},{1,17},{2,18},{3,19},{4,20},{5,21},{6,22},{7,23},{8,24},{9,... | collective-permute-start | bytes 184328 | tf_op jit(solution)/shard_map/ppermute | solution.py:206
  26.2 5.7 %collective-permute-start.9 = (f32[16,960]{1,0:T(8,128)S(1)}, f32[16,960]{1,0:T(8,128)S(1)}, u32[]{:S(2)}, u32[]{:S(2)}) collective-permute-start(f32[16,960]{1,0:T(8,128)S(1)} %add.69), channel_id=1, source_target_pairs={{0,6},{1,7},{2,4},{3,5},{4,2},{5,3},{6,0},{7,1},{8,14},{9,15},{10,... | collective-permute-start | bytes 184328 | tf_op jit(solution)/shard_map/ppermute | solution.py:206
  28.6 4.3 %collective-permute-start.8 = (f32[16,960]{1,0:T(8,128)S(1)}, f32[16,960]{1,0:T(8,128)S(1)}, u32[]{:S(2)}, u32[]{:S(2)}) collective-permute-start(f32[16,960]{1,0:T(8,128)S(1)} %add.69), channel_id=1, source_target_pairs={{0,4},{1,5},{2,6},{3,7},{4,0},{5,1},{6,2},{7,3},{8,12},{9,13},{10,... | collective-permute-start | bytes 184328 | tf_op jit(solution)/shard_map/ppermute | solution.py:206
  29.3 4.3 %collective-permute-start.7 = (f32[16,960]{1,0:T(8,128)S(1)}, f32[16,960]{1,0:T(8,128)S(1)}, u32[]{:S(2)}, u32[]{:S(2)}) collective-permute-start(f32[16,960]{1,0:T(8,128)S(1)} %add.69), channel_id=1, source_target_pairs={{0,2},{1,3},{2,0},{3,1},{4,6},{5,7},{6,4},{7,5},{8,10},{9,11},{10,... | collective-permute-start | bytes 184328 | tf_op jit(solution)/shard_map/ppermute | solution.py:206
  29.8 6.8 %collective-permute-start.11 = (bf16[1,3,40,960]{3,2,1,0:T(8,128)(2,1)S(1)}, bf16[1,3,40,960]{3,2,1,0:T(8,128)(2,1)S(1)}, u32[]{:S(2)}, u32[]{:S(2)}) collective-permute-start(bf16[1,3,40,960]{3,2,1,0:T(8,128)(2,1)S(1)} %add_add_fusion), channel_id=1, source_target_pairs={{0,8},{1,9},{2,10},{3,11},{4,12},{5,13},{6,14},{7,15},{8,0},{9,1},... | collective-permute-start | bytes 691208 | tf_op jit(solution)/shard_map/ppermute | solution.py:206
  33.5 1.3 %collective-permute-start.10 = (f32[16,960]{1,0:T(8,128)S(1)}, f32[16,960]{1,0:T(8,128)S(1)}, u32[]{:S(2)}, u32[]{:S(2)}) collective-permute-start(f32[16,960]{1,0:T(8,128)S(1)} %add_add_fusion.1.mine_ref), channel_id=1, source_target_pairs={{0,1},{1,0},{2,3},{3,2},{4,5},{5,4},{6,7},{7,6},{8,9},{9,8},{10,11... | collective-permute-start | bytes 184328 | tf_op jit(solution)/shard_map/ppermute | solution.py:206
  36.7 1.5 %collective-permute-start.12 = (f32[2,3,8,960]{3,2,1,0:T(8,128)S(1)}, f32[2,3,8,960]{3,2,1,0:T(8,128)S(1)}, u32[]{:S(2)}, u32[]{:S(2)}) collective-permute-start(f32[2,3,8,960]{3,2,1,0:T(8,128)S(1)} %get-tuple-element.50), channel_id=1, source_target_pairs={{0,1},{1,0},{2,3},{3,2},{4,5},{5,4},{6,7},{7,6},{8,9},{9,8},{10,11... | collective-permute-start | bytes 552968 | tf_op jit(solution)/shard_map/ppermute | solution.py:206
  38.2 4.9 %collective-permute-start.13 = (f32[3,8,960]{2,1,0:T(8,128)S(1)}, f32[3,8,960]{2,1,0:T(8,128)S(1)}, u32[]{:S(2)}, u32[]{:S(2)}) collective-permute-start(f32[3,8,960]{2,1,0:T(8,128)S(1)} %fusion), channel_id=1, source_target_pairs={{0,2},{1,3},{2,0},{3,1},{4,6},{5,7},{6,4},{7,5},{8,10},{9,11},{10,... | collective-permute-start | bytes 276488 | tf_op jit(solution)/shard_map/ppermute | solution.py:206
  39.9 13.9 %collective-permute-start.15 = (bf16[1,3,40,960]{3,2,1,0:T(8,128)(2,1)S(1)}, bf16[1,3,40,960]{3,2,1,0:T(8,128)(2,1)S(1)}, u32[]{:S(2)}, u32[]{:S(2)}) collective-permute-start(bf16[1,3,40,960]{3,2,1,0:T(8,128)(2,1)S(1)} %add.76), channel_id=1, source_target_pairs={{0,16},{1,17},{2,18},{3,19},{4,20},{5,21},{6,22},{7,23},{8,24},{9,... | collective-permute-start | bytes 691208 | tf_op jit(solution)/shard_map/ppermute | solution.py:206
  43.2 5.1 %collective-permute-start.14 = (f32[3,8,960]{2,1,0:T(8,128)S(1)}, f32[3,8,960]{2,1,0:T(8,128)S(1)}, u32[]{:S(2)}, u32[]{:S(2)}) collective-permute-start(f32[3,8,960]{2,1,0:T(8,128)S(1)} %fusion.2), channel_id=1, source_target_pairs={{0,4},{1,5},{2,6},{3,7},{4,0},{5,1},{6,2},{7,3},{8,12},{9,13},{10,... | collective-permute-start | bytes 276488 | tf_op jit(solution)/shard_map/ppermute | solution.py:206
  53.8 4.7 %collective-permute-start.16 = (f32[3,8,960]{2,1,0:T(8,128)S(1)}, f32[3,8,960]{2,1,0:T(8,128)S(1)}, u32[]{:S(2)}, u32[]{:S(2)}) collective-permute-start(f32[3,8,960]{2,1,0:T(8,128)S(1)} %add.80), channel_id=1, source_target_pairs={{0,8},{1,9},{2,10},{3,11},{4,12},{5,13},{6,14},{7,15},{8,0},{9,1},... | collective-permute-start | bytes 276488 | tf_op jit(solution)/shard_map/ppermute | solution.py:206
  54.6 11.0 %collective-permute-start.18 = (bf16[1,3,40,960]{3,2,1,0:T(8,128)(2,1)S(1)}, bf16[1,3,40,960]{3,2,1,0:T(8,128)(2,1)S(1)}, u32[]{:S(2)}, u32[]{:S(2)}) collective-permute-start(bf16[1,3,40,960]{3,2,1,0:T(8,128)(2,1)S(1)} %add.81), channel_id=1, source_target_pairs={{0,2},{1,3},{2,0},{3,1},{4,6},{5,7},{6,4},{7,5},{8,10},{9,11},{10,... | collective-permute-start | bytes 691208 | tf_op jit(solution)/shard_map/ppermute | solution.py:206
  58.5 7.0 %collective-permute-start.17 = (f32[3,8,960]{2,1,0:T(8,128)S(1)}, f32[3,8,960]{2,1,0:T(8,128)S(1)}, u32[]{:S(2)}, u32[]{:S(2)}) collective-permute-start(f32[3,8,960]{2,1,0:T(8,128)S(1)} %add.82), channel_id=1, source_target_pairs={{0,16},{1,17},{2,18},{3,19},{4,20},{5,21},{6,22},{7,23},{8,24},{9,... | collective-permute-start | bytes 276488 | tf_op jit(solution)/shard_map/ppermute | solution.py:206
  61.0 13.3 %collective-permute-start.20 = (bf16[1,3,40,960]{3,2,1,0:T(8,128)(2,1)S(1)}, bf16[1,3,40,960]{3,2,1,0:T(8,128)(2,1)S(1)}, u32[]{:S(2)}, u32[]{:S(2)}) collective-permute-start(bf16[1,3,40,960]{3,2,1,0:T(8,128)(2,1)S(1)} %add.81), channel_id=1, source_target_pairs={{0,6},{1,7},{2,4},{3,5},{4,2},{5,3},{6,0},{7,1},{8,14},{9,15},{10,... | collective-permute-start | bytes 691208 | tf_op jit(solution)/shard_map/ppermute | solution.py:206
  62.5 11.7 %collective-permute-start.19 = (bf16[1,3,40,960]{3,2,1,0:T(8,128)(2,1)S(1)}, bf16[1,3,40,960]{3,2,1,0:T(8,128)(2,1)S(1)}, u32[]{:S(2)}, u32[]{:S(2)}) collective-permute-start(bf16[1,3,40,960]{3,2,1,0:T(8,128)(2,1)S(1)} %add.81), channel_id=1, source_target_pairs={{0,4},{1,5},{2,6},{3,7},{4,0},{5,1},{6,2},{7,3},{8,12},{9,13},{10,... | collective-permute-start | bytes 691208 | tf_op jit(solution)/shard_map/ppermute | solution.py:206
  74.3 7.4 %collective-permute-start.24 = (bf16[4,3,40,960]{3,2,1,0:T(8,128)(2,1)S(1)}, bf16[4,3,40,960]{3,2,1,0:T(8,128)(2,1)S(1)}, u32[]{:S(2)}, u32[]{:S(2)}) collective-permute-start(bf16[4,3,40,960]{3,2,1,0:T(8,128)(2,1)S(1)} %constant_dynamic-update-slice_fusion.even_ref), channel_id=1, source_target_pairs={{0,1},{1,0},{2,3},{3,2},{4,5},{5,4},{6,7},{7,6},{8,9},{9,8},{10,11... | collective-permute-start | bytes 2764808 | tf_op jit(solution)/shard_map/ppermute | solution.py:206
  74.4 4.6 %collective-permute-start.23 = (f32[3,8,960]{2,1,0:T(8,128)S(1)}, f32[3,8,960]{2,1,0:T(8,128)S(1)}, u32[]{:S(2)}, u32[]{:S(2)}) collective-permute-start(f32[3,8,960]{2,1,0:T(8,128)S(1)} %add.83.r0_ref), channel_id=1, source_target_pairs={{0,3},{1,2},{2,1},{3,0},{4,7},{5,6},{6,5},{7,4},{8,11},{9,10},{10,... | collective-permute-start | bytes 276488 | tf_op jit(solution)/shard_map/ppermute | solution.py:206
  75.1 6.6 %collective-permute-start.22 = (f32[3,8,960]{2,1,0:T(8,128)S(1)}, f32[3,8,960]{2,1,0:T(8,128)S(1)}, u32[]{:S(2)}, u32[]{:S(2)}) collective-permute-start(f32[3,8,960]{2,1,0:T(8,128)S(1)} %add.83.r0_ref), channel_id=1, source_target_pairs={{0,2},{1,3},{2,0},{3,1},{4,6},{5,7},{6,4},{7,5},{8,10},{9,11},{10,... | collective-permute-start | bytes 276488 | tf_op jit(solution)/shard_map/ppermute | solution.py:206
  76.5 5.1 %collective-permute-start.21 = (f32[3,8,960]{2,1,0:T(8,128)S(1)}, f32[3,8,960]{2,1,0:T(8,128)S(1)}, u32[]{:S(2)}, u32[]{:S(2)}) collective-permute-start(f32[3,8,960]{2,1,0:T(8,128)S(1)} %add.83.r0_ref), channel_id=1, source_target_pairs={{0,1},{1,0},{2,3},{3,2},{4,5},{5,4},{6,7},{7,6},{8,9},{9,8},{10,11... | collective-permute-start | bytes 276488 | tf_op jit(solution)/shard_map/ppermute | solution.py:206
  76.5 5.1 %copy-start.5 = (s32[3]{0:T(128)S(1)}, s32[3]{0:T(128)}, u32[]{:S(2)}) copy-start(s32[3]{0:T(128)} %buckets_ref.1) | copy-start | bytes 40
  76.5 5.1 %copy-start.6 = (f32[4]{0:T(128)S(1)}, f32[4]{0:T(128)}, u32[]{:S(2)}) copy-start(f32[4]{0:T(128)} %rates_ref.1) | copy-start | bytes 52
  76.6 5.1 %copy-start.7 = (f32[4]{0:T(128)S(1)}, f32[4]{0:T(128)}, u32[]{:S(2)}) copy-start(f32[4]{0:T(128)} %betas_ref.1) | copy-start | bytes 52
  (3 other events, 7.1 us)

commit v6 on v5

--- a/solution.py
+++ b/solution.py
@@ -11,6 +11,7 @@
 F32 = jnp.float32
 BF16 = jnp.bfloat16
 SMEM = pl.BlockSpec(memory_space=pltpu.SMEM)
+LIMIT = 53
 
 
 def whole(shape):
@@ -40,29 +41,6 @@
 
 def after(value, *others):
     return lax.optimization_barrier((value,) + others)[0]
-
-
-def left_kernel(grad_hbm, error_hbm, q_hbm, mine_ref, other_ref, grad_ref, error_ref, q_ref, left_ref, sems):
-    mats, rows, _ = grad_ref.shape
-    rank = q_ref.shape[1]
-    pairs = ((grad_hbm, grad_ref), (error_hbm, error_ref), (q_hbm, q_ref))
-    copies = [
-        [pltpu.make_async_copy(hbm.at[m], ref.at[m], sems.at[m, n]) for n, (hbm, ref) in enumerate(pairs)]
-        for m in range(mats)
-    ]
-    for per_mat in copies:
-        for copy in per_mat:
-            copy.start()
-    bit = lax.axis_index(AXES) & 1
-    for m in range(mats):
-        for copy in copies[m]:
-            copy.wait()
-        high, low = split(grad_ref[m] + error_ref[m].astype(F32))
-        q_both = jnp.concatenate(split(q_ref[m]), 0)
-        both = dot(q_both, high, ((1,), (1,))) + dot(q_both, low, ((1,), (1,)))
-        left_ref[...] = (both[:rank] + both[rank:]).reshape(left_ref.shape)
-        mine_ref[:, m * rows : (m + 1) * rows] = left_ref[bit]
-        other_ref[:, m * rows : (m + 1) * rows] = left_ref[1 - bit]
 
 
 def gather_left(mine_ref, other_ref, left_ref, rows):
@@ -150,24 +128,49 @@
 OLD_ORDER = ((0,), (2,), (4,), (6,), (1, 3, 5, 7))
 
 
-def old_kernel(owners_ref, mom_ref, k0_ref, k2_ref, k4_ref, k6_ref, odd_ref):
+def first_kernel(
+    owners_ref, grad_hbm, error_hbm, q_hbm, mom_hbm,
+    mine_ref, other_ref, k0_ref, k2_ref, k4_ref, k6_ref, odd_ref,
+    grad_ref, error_ref, q_ref, mom_ref, left_ref, sems, mom_sem,
+):
+    mats, rows, _ = grad_ref.shape
+    rank = q_ref.shape[1]
     me = lax.axis_index(AXES)
+    pairs = ((grad_hbm, grad_ref), (error_hbm, error_ref), (q_hbm, q_ref))
+    copies = [
+        [pltpu.make_async_copy(hbm.at[m], ref.at[m], sems.at[m, n]) for n, (hbm, ref) in enumerate(pairs)]
+        for m in range(mats)
+    ]
+    mom_copy = pltpu.make_async_copy(mom_hbm, mom_ref, mom_sem)
+    for copy in copies[0]:
+        copy.start()
+    mom_copy.start()
+
     outs = (k0_ref, k2_ref, k4_ref, k6_ref, odd_ref)
-    for i in range(owners_ref.shape[0]):
-        own = owners_ref[i] == me
-        slot = slot_of(owners_ref, i)
-
-        @pl.when(own)
-        def _():
-            for out, order in zip(outs, OLD_ORDER):
-                for n, position in enumerate(order):
-                    out[n, i] = mom_ref[slot, position ^ (me & 7)]
-
-        @pl.when(jnp.logical_not(own))
-        def _():
-            for out, order in zip(outs, OLD_ORDER):
-                for n in range(len(order)):
-                    out[n, i] = jnp.zeros(out.shape[2:], BF16)
+    for out in outs:
+        out[...] = jnp.zeros(out.shape, BF16)
+    for m in range(mats):
+        if m + 1 < mats:
+            for copy in copies[m + 1]:
+                copy.start()
+        for copy in copies[m]:
+            copy.wait()
+        high, low = split(grad_ref[m] + error_ref[m].astype(F32))
+        q_both = jnp.concatenate(split(q_ref[m]), 0)
+        both = dot(q_both, high, ((1,), (1,))) + dot(q_both, low, ((1,), (1,)))
+        left_ref[...] = (both[:rank] + both[rank:]).reshape(left_ref.shape)
+        mine_ref[:, m * rows : (m + 1) * rows] = left_ref[me & 1]
+        other_ref[:, m * rows : (m + 1) * rows] = left_ref[1 - (me & 1)]
+        if m == 0:
+            mom_copy.wait()
+            for i in range(mats):
+                slot = slot_of(owners_ref, i)
+
+                @pl.when(owners_ref[i] == me)
+                def _():
+                    for out, order in zip(outs, OLD_ORDER):
+                        for n, position in enumerate(order):
+                            out[n, i] = mom_ref[slot, position ^ (me & 7)]
 
 
 def step_kernel(
@@ -179,6 +182,7 @@
     me = lax.axis_index(AXES)
     rate = rates_ref[buckets_ref[i]]
     beta = betas_ref[buckets_ref[i]]
+    of_update, of_old = -rate * (1.0 + beta), -rate * beta * beta
 
     @pl.when(i == 0)
     def _():
@@ -194,12 +198,12 @@
         ref = (even_ref, odd_ref)[position % 2]
         piece = position ^ (me & 7)
         update = update_ref[piece]
-        mom = beta * ref[position // 2, 0].astype(F32) + update
-        step_ref[0, piece] = (-rate * (update + beta * mom)).astype(BF16)
+        old = ref[position // 2, 0].astype(F32)
+        step_ref[0, piece] = (of_update * update + of_old * old).astype(BF16)
 
         @pl.when(own)
         def _():
-            mom_ref[slot, piece] = mom.astype(BF16)
+            mom_ref[slot, piece] = (beta * old + update).astype(BF16)
 
 
 def exchange(value, mask, count):
@@ -232,36 +236,30 @@
         return exchange(value, mask, count)
 
     sizes = [len(order) for order in OLD_ORDER]
-    *evens, odd = pl.pallas_call(
-        old_kernel,
-        grid=(1,),
-        in_specs=[SMEM, whole((slots, 8, piece, cols))],
-        out_specs=[whole(old_shape(n)) for n in sizes],
-        out_shape=[sds(old_shape(n), BF16) for n in sizes],
-        compiler_params=params(),
-        name="old",
-    )(owners, momentum.reshape(slots, 8, piece, cols))
-
-    mine, other = pl.pallas_call(
-        left_kernel,
-        in_specs=[pl.BlockSpec(memory_space=pltpu.HBM)] * 3,
-        out_shape=[sds((half, mats * rows), F32)] * 2,
+    mine, other, *evens, odd = pl.pallas_call(
+        first_kernel,
+        in_specs=[SMEM] + [pl.BlockSpec(memory_space=pltpu.HBM)] * 4,
+        out_shape=[sds((half, mats * rows), F32)] * 2 + [sds(old_shape(n), BF16) for n in sizes],
         scratch_shapes=[
             pltpu.VMEM((mats, rows, cols), F32),
             pltpu.VMEM((mats, rows, cols), BF16),
             pltpu.VMEM((mats, rank, cols), F32),
+            pltpu.VMEM((slots, 8, piece, cols), BF16),
             pltpu.VMEM((2, half, rows), F32),
             pltpu.SemaphoreType.DMA((mats, 3)),
+            pltpu.SemaphoreType.DMA,
         ],
-        compiler_params=pltpu.CompilerParams(vmem_limit_bytes=60 * 1024 * 1024),
-        name="left",
-    )(grads, errs, after(q_t, odd))
+        compiler_params=pltpu.CompilerParams(vmem_limit_bytes=LIMIT * 1024 * 1024),
+        name="first",
+    )(owners, grads, errs, q_t, momentum.reshape(slots, 8, piece, cols))
 
     got = swap(odd, 1)
-    evens = [after(evens[n], mine) + got[n : n + 1] for n in range(4)]
-    mine = mine + swap(after(other, *evens), 1)
+    mine = mine + swap(other, 1)
+    evens = [after(even, mine) + got[n : n + 1] for n, even in enumerate(evens)]
     got = [swap(evens[n], 2 * n) for n in (1, 2, 3)]
-    for bit in bits[3:]:
+    mine = total_over(mine, bits[3:4], count)
+    mine = after(mine, *evens)
+    for bit in bits[4:]:
         mine = total_over(mine, [bit], count)
     old = after(evens[0], mine) + got[0] + got[1] + got[2]
     mine = after(mine, old)
@@ -304,17 +302,21 @@
     )(mine, other)
 
     got = swap(after(send, old), 1)
-    r0 = keep + got[0] + swap(send2 + got[1], 2)
     for bit in bits[4:-1]:
         old = old + swap(old, 1 << bit)
     from_other = swap(old, 1 << bits[-1])
+    r0 = keep + got[0] + swap(send2 + got[1], 2)
     r0 = total_over(r0, bits[2:3], count)
     old = after(old, r0) + from_other
     r0 = after(r0, old, w)
-    got = [swap(old, mask) for mask in (2, 4, 6)]
-    for bit in bits[3:]:
+    near = [swap(old, 2), swap(old, 4)]
+    for n, bit in enumerate(bits[3:]):
         r0 = total_over(r0, [bit], count)
-    evens = jnp.concatenate([after(old, r0)] + got)
+        if n == 0:
+            near = [after(value, r0) for value in near]
+            r0 = after(r0, *near)
+    far = swap(near[0], 4)
+    evens = jnp.concatenate([after(old, r0)] + near + [far])
     r0 = after(r0, evens)
     odds = swap(evens, 1)
     r1, r2, r3 = (swap(r0, mask) for mask in (1, 2, 3))

time: 86 us -> 84.8 us (0.986)
  local copies, waits for them, and re-layouts: 2.08 us -> 0.74 us
    unnamed x23 -> x15, local copies, waits for them, and re-layouts: 2.06 us -> 0.72 us
    pallas_call x2 -> x1, Pallas kernels: 5.74 us -> 5.73 us  [on_device(): pl.pallas_call(first_kernel, in_specs=[SMEM] + [pl.BlockSpec(memory_space...]
  transfers between devices with their start and end apart: 25 -> 25, of which waited for: 16 -> 18; matrix products, arithmetic and copies ran while one was open for 0% -> 0% of each run, Pallas kernels for 15% -> 9%
where the time goes in v6:
time: 84.8 us; the launch traced here: 84.6 us
  waiting for transfers between devices  34.9 us (41%)
  starting transfers between devices  29.2 us (34%)
  Pallas kernels  17.3 us (20%)
  other arithmetic  1.57 us (2%)
    ppermute x25, waiting for transfers between devices, exchange(): return lax.ppermute(value, AXES, [(d, d ^ mask) for d in range(count)])  34.9 us
    ppermute x25, starting transfers between devices, exchange(): return lax.ppermute(value, AXES, [(d, d ^ mask) for d in range(count)])  29.2 us
    pallas_call x1, Pallas kernels, on_device(): pl.pallas_call(first_kernel, in_specs=[SMEM] + [pl.BlockSpec(memory_space...  5.73 us
    pallas_call x1, Pallas kernels, on_device(): pl.pallas_call(step_kernel, grid=(mats,), in_specs=[SMEM] * 4 + [quarter_...  3.99 us
    pallas_call x1, Pallas kernels, on_device(): pl.pallas_call(solve_kernel, grid=(1,), in_specs=[whole((half, mats * row...  3.38 us
    pallas_call x1, Pallas kernels, on_device(): pl.pallas_call(error_kernel, grid=(mats,), in_specs=[grad_spec, grad_spec...  2.4 us
    pallas_call x1, Pallas kernels, on_device(): pl.pallas_call(right_kernel, grid=(mats,), in_specs=[whole((half, mats *...  1.79 us
  transfers between devices with their start and end apart: 25, of which 18 were waited for; matrix products, arithmetic and copies ran while one was open for 0% of the time, Pallas kernels for 9%

profile of v6, /device:TPU:0, one launch (start us, length us, event | category | flops | bytes accessed | tf_op | source)
XLA Modules:
  0.0 84.6 jit_solution(3933024460376836700)
XLA Ops:
  1.3 5.7 %first.1 = (f32[16,960]{1,0:T(8,128)S(1)}, f32[16,960]{1,0:T(8,128)S(1)}, bf16[1,3,40,960]{3,2,1,0:T(8,128)(2,1)S(1)}, bf16[1,3,40,960]{3,2,1,0:T(8,128)(2,1)S(1...) custom-call(s32[3]{0:T(128)S(1)} %copy-done.2, ...), custom_call_target="tpu_custom_call" | custom-call | tf_op jit(solution)/shard_map/first/pallas_call | solution.py:239
  7.6 2.1 %collective-permute-done = f32[16,960]{1,0:T(8,128)S(1)} collective-permute-done((f32[16,960]{1,0:T(8,128)S(1)}, f32[16,960]{1,0:T(8,128)S(1)}, u32[]{:S(2)}, u32[]{:S(2)}) %collective-permute-start) | collective-permute-done | bytes 61472 | tf_op jit(solution)/shard_map/ppermute | solution.py:210
  10.0 1.3 %slice_add_fusion = (bf16[1,3,40,960]{3,2,1,0:T(8,128)(2,1)S(1)}, bf16[1,3,40,960]{3,2,1,0:T(8,128)(2,1)S(1)}, bf16[1,3,40,960]{3,2,1,0:T(8,128)(2,1)S(1)}, bf16[1,3,40,960]{3,2,1,0:T(8,128)(2,1)S(1)}) fusion(bf16[1,3,40,960]{3,2,1,0:T(8,128)(2,1)} %get-tuple-element.44, bf16[4,3,40,960]{3,2,1,0:T(8,128)(2,1)S(1)} %collective-permute-done.2, ...), kind=kLoop, calls=%fused_computation | loop fusion | flops 460800 | bytes 2764800 | tf_op jit(solution)/shard_map/add | solution.py:258
  11.3 4.0 %collective-permute-start.6 = (bf16[1,3,40,960]{3,2,1,0:T(8,128)(2,1)S(1)}, bf16[1,3,40,960]{3,2,1,0:T(8,128)(2,1)S(1)}, u32[]{:S(2)}, u32[]{:S(2)}) collective-permute-start(bf16[1,3,40,960]{3,2,1,0:T(8,128)(2,1)S(1)} %get-tuple-element.65), channel_id=1, source_target_pairs={{0,6},{1,7},{2,4},{3,5},{4,2},{5,3},{6,0},{7,1},{8,14},{9,15},{10,... | collective-permute-start | bytes 691208 | tf_op jit(solution)/shard_map/ppermute | solution.py:210
  16.0 2.0 %collective-permute-start.1 = (f32[16,960]{1,0:T(8,128)S(1)}, f32[16,960]{1,0:T(8,128)S(1)}, u32[]{:S(2)}, u32[]{:S(2)}) collective-permute-start(f32[16,960]{1,0:T(8,128)S(1)} %add.63), channel_id=1, source_target_pairs={{0,8},{1,9},{2,10},{3,11},{4,12},{5,13},{6,14},{7,15},{8,0},{9,1},... | collective-permute-start | bytes 184328 | tf_op jit(solution)/shard_map/ppermute | solution.py:210
  17.9 2.3 %collective-permute-done.1 = f32[16,960]{1,0:T(8,128)S(1)} collective-permute-done((f32[16,960]{1,0:T(8,128)S(1)}, f32[16,960]{1,0:T(8,128)S(1)}, u32[]{:S(2)}, u32[]{:S(2)}) %collective-permute-start.1) | collective-permute-done | bytes 61472 | tf_op jit(solution)/shard_map/ppermute | solution.py:210
  20.2 3.1 %collective-permute-start.3 = (f32[16,960]{1,0:T(8,128)S(1)}, f32[16,960]{1,0:T(8,128)S(1)}, u32[]{:S(2)}, u32[]{:S(2)}) collective-permute-start(f32[16,960]{1,0:T(8,128)S(1)} %add.64), channel_id=1, source_target_pairs={{0,16},{1,17},{2,18},{3,19},{4,20},{5,21},{6,22},{7,23},{8,24},{9,... | collective-permute-start | bytes 184328 | tf_op jit(solution)/shard_map/ppermute | solution.py:210
  23.3 2.2 %collective-permute-done.3 = f32[16,960]{1,0:T(8,128)S(1)} collective-permute-done((f32[16,960]{1,0:T(8,128)S(1)}, f32[16,960]{1,0:T(8,128)S(1)}, u32[]{:S(2)}, u32[]{:S(2)}) %collective-permute-start.3) | collective-permute-done | bytes 61472 | tf_op jit(solution)/shard_map/ppermute | solution.py:210
  25.6 1.2 %collective-permute-done.5 = bf16[1,3,40,960]{3,2,1,0:T(8,128)(2,1)S(1)} collective-permute-done((bf16[1,3,40,960]{3,2,1,0:T(8,128)(2,1)S(1)}, bf16[1,3,40,960]{3,2,1,0:T(8,128)(2,1)S(1)}, u32[]{:S(2)}, u32[]{:S(2)}) %collective-permute-start.5) | collective-permute-done | bytes 230432 | tf_op jit(solution)/shard_map/ppermute | solution.py:210
  27.1 1.6 %collective-permute-start.9 = (f32[16,960]{1,0:T(8,128)S(1)}, f32[16,960]{1,0:T(8,128)S(1)}, u32[]{:S(2)}, u32[]{:S(2)}) collective-permute-start(f32[16,960]{1,0:T(8,128)S(1)} %add.69), channel_id=1, source_target_pairs={{0,6},{1,7},{2,4},{3,5},{4,2},{5,3},{6,0},{7,1},{8,14},{9,15},{10,... | collective-permute-start | bytes 184328 | tf_op jit(solution)/shard_map/ppermute | solution.py:210
  28.7 1.4 %collective-permute-start.8 = (f32[16,960]{1,0:T(8,128)S(1)}, f32[16,960]{1,0:T(8,128)S(1)}, u32[]{:S(2)}, u32[]{:S(2)}) collective-permute-start(f32[16,960]{1,0:T(8,128)S(1)} %add.69), channel_id=1, source_target_pairs={{0,4},{1,5},{2,6},{3,7},{4,0},{5,1},{6,2},{7,3},{8,12},{9,13},{10,... | collective-permute-start | bytes 184328 | tf_op jit(solution)/shard_map/ppermute | solution.py:210
  30.6 1.6 %collective-permute-start.11 = (bf16[1,3,40,960]{3,2,1,0:T(8,128)(2,1)S(1)}, bf16[1,3,40,960]{3,2,1,0:T(8,128)(2,1)S(1)}, u32[]{:S(2)}, u32[]{:S(2)}) collective-permute-start(bf16[1,3,40,960]{3,2,1,0:T(8,128)(2,1)S(1)} %add_add_fusion), channel_id=1, source_target_pairs={{0,8},{1,9},{2,10},{3,11},{4,12},{5,13},{6,14},{7,15},{8,0},{9,1},... | collective-permute-start | bytes 691208 | tf_op jit(solution)/shard_map/ppermute | solution.py:210
  33.2 1.1 %collective-permute-done.7 = f32[16,960]{1,0:T(8,128)S(1)} collective-permute-done((f32[16,960]{1,0:T(8,128)S(1)}, f32[16,960]{1,0:T(8,128)S(1)}, u32[]{:S(2)}, u32[]{:S(2)}) %collective-permute-start.7) | collective-permute-done | bytes 61472 | tf_op jit(solution)/shard_map/ppermute | solution.py:210
  34.5 1.2 %collective-permute-done.10.other_ref = f32[16,960]{1,0:T(8,128)S(1)} collective-permute-done((f32[16,960]{1,0:T(8,128)S(1)}, f32[16,960]{1,0:T(8,128)S(1)}, u32[]{:S(2)}, u32[]{:S(2)}) %collective-permute-start.10) | collective-permute-done | bytes 61472 | tf_op jit(solution)/shard_map/ppermute | solution.py:210
  35.7 1.8 %right.1 = (f32[3,32,960]{2,1,0:T(8,128)S(1)}, f32[3,8,960]{2,1,0:T(8,128)S(1)}, f32[3,8,960]{2,1,0:T(8,128)S(1)}, f32[2,3,8,960]{3,2,1,0:T(8,128)S(1)}) custom-call(f32[16,960]{1,0:T(8,128)S(1)} %add_add_fusion.1.mine_ref, f32[16,960]{1,0:T(8,128)S(1)} %collective-permute-done.10.other_ref, f32[3,320,960]{2,1,0:T(8,128)S(1)} %bitcast.18, ...), custom_call_target="tpu_custom_call" | custom-call | tf_op jit(solution)/shard_map/right/pallas_call | solution.py:271
  37.8 1.3 %collective-permute-done.12 = f32[2,3,8,960]{3,2,1,0:T(8,128)S(1)} collective-permute-done((f32[2,3,8,960]{3,2,1,0:T(8,128)S(1)}, f32[2,3,8,960]{3,2,1,0:T(8,128)S(1)}, u32[]{:S(2)}, u32[]{:S(2)}) %collective-permute-start.12) | collective-permute-done | bytes 184352 | tf_op jit(solution)/shard_map/ppermute | solution.py:210
  39.1 1.6 %collective-permute-start.13 = (f32[3,8,960]{2,1,0:T(8,128)S(1)}, f32[3,8,960]{2,1,0:T(8,128)S(1)}, u32[]{:S(2)}, u32[]{:S(2)}) collective-permute-start(f32[3,8,960]{2,1,0:T(8,128)S(1)} %fusion), channel_id=1, source_target_pairs={{0,2},{1,3},{2,0},{3,1},{4,6},{5,7},{6,4},{7,5},{8,10},{9,11},{10,... | collective-permute-start | bytes 276488 | tf_op jit(solution)/shard_map/ppermute | solution.py:210
  40.7 2.7 %collective-permute-start.15 = (bf16[1,3,40,960]{3,2,1,0:T(8,128)(2,1)S(1)}, bf16[1,3,40,960]{3,2,1,0:T(8,128)(2,1)S(1)}, u32[]{:S(2)}, u32[]{:S(2)}) collective-permute-start(bf16[1,3,40,960]{3,2,1,0:T(8,128)(2,1)S(1)} %add.76), channel_id=1, source_target_pairs={{0,16},{1,17},{2,18},{3,19},{4,20},{5,21},{6,22},{7,23},{8,24},{9,... | collective-permute-start | bytes 691208 | tf_op jit(solution)/shard_map/ppermute | solution.py:210
  44.1 1.6 %collective-permute-start.14 = (f32[3,8,960]{2,1,0:T(8,128)S(1)}, f32[3,8,960]{2,1,0:T(8,128)S(1)}, u32[]{:S(2)}, u32[]{:S(2)}) collective-permute-start(f32[3,8,960]{2,1,0:T(8,128)S(1)} %fusion.2), channel_id=1, source_target_pairs={{0,4},{1,5},{2,6},{3,7},{4,0},{5,1},{6,2},{7,3},{8,12},{9,13},{10,... | collective-permute-start | bytes 276488 | tf_op jit(solution)/shard_map/ppermute | solution.py:210
  45.7 3.1 %collective-permute-done.14 = f32[3,8,960]{2,1,0:T(8,128)S(1)} collective-permute-done((f32[3,8,960]{2,1,0:T(8,128)S(1)}, f32[3,8,960]{2,1,0:T(8,128)S(1)}, u32[]{:S(2)}, u32[]{:S(2)}) %collective-permute-start.14) | collective-permute-done | bytes 92192 | tf_op jit(solution)/shard_map/ppermute | solution.py:210
  48.8 5.9 %collective-permute-done.15 = bf16[1,3,40,960]{3,2,1,0:T(8,128)(2,1)S(1)} collective-permute-done((bf16[1,3,40,960]{3,2,1,0:T(8,128)(2,1)S(1)}, bf16[1,3,40,960]{3,2,1,0:T(8,128)(2,1)S(1)}, u32[]{:S(2)}, u32[]{:S(2)}) %collective-permute-start.15) | collective-permute-done | bytes 230432 | tf_op jit(solution)/shard_map/ppermute | solution.py:210
  55.2 1.6 %collective-permute-start.17 = (bf16[1,3,40,960]{3,2,1,0:T(8,128)(2,1)S(1)}, bf16[1,3,40,960]{3,2,1,0:T(8,128)(2,1)S(1)}, u32[]{:S(2)}, u32[]{:S(2)}) collective-permute-start(bf16[1,3,40,960]{3,2,1,0:T(8,128)(2,1)S(1)} %add.81), channel_id=1, source_target_pairs={{0,2},{1,3},{2,0},{3,1},{4,6},{5,7},{6,4},{7,5},{8,10},{9,11},{10,... | collective-permute-start | bytes 691208 | tf_op jit(solution)/shard_map/ppermute | solution.py:210
  56.8 3.4 %solve.1.w_ref = bf16[3,320,96]{2,1,0:T(8,128)(2,1)S(1)} custom-call(f32[16,960]{1,0:T(8,128)S(1)} %add_add_fusion.1.mine_ref, f32[16,960]{1,0:T(8,128)S(1)} %collective-permute-done.10.other_ref), custom_call_target="tpu_custom_call" | custom-call | bytes 16777216 | tf_op jit(solution)/shard_map/solve/pallas_call | solution.py:292
  60.2 0.7 collective-permute-start.16
  60.9 3.9 %collective-permute-done.16 = f32[3,8,960]{2,1,0:T(8,128)S(1)} collective-permute-done((f32[3,8,960]{2,1,0:T(8,128)S(1)}, f32[3,8,960]{2,1,0:T(8,128)S(1)}, u32[]{:S(2)}, u32[]{:S(2)}) %collective-permute-start.16) | collective-permute-done | bytes 92192 | tf_op jit(solution)/shard_map/ppermute | solution.py:210
  64.9 2.1 %collective-permute-start.19 = (f32[3,8,960]{2,1,0:T(8,128)S(1)}, f32[3,8,960]{2,1,0:T(8,128)S(1)}, u32[]{:S(2)}, u32[]{:S(2)}) collective-permute-start(f32[3,8,960]{2,1,0:T(8,128)S(1)} %add.82), channel_id=1, source_target_pairs={{0,16},{1,17},{2,18},{3,19},{4,20},{5,21},{6,22},{7,23},{8,24},{9,... | collective-permute-start | bytes 276488 | tf_op jit(solution)/shard_map/ppermute | solution.py:210
  67.5 4.0 %collective-permute-done.19 = f32[3,8,960]{2,1,0:T(8,128)S(1)} collective-permute-done((f32[3,8,960]{2,1,0:T(8,128)S(1)}, f32[3,8,960]{2,1,0:T(8,128)S(1)}, u32[]{:S(2)}, u32[]{:S(2)}) %collective-permute-start.19) | collective-permute-done | bytes 92192 | tf_op jit(solution)/shard_map/ppermute | solution.py:210
  71.6 1.6 %collective-permute-done.20 = bf16[1,3,40,960]{3,2,1,0:T(8,128)(2,1)S(1)} collective-permute-done((bf16[1,3,40,960]{3,2,1,0:T(8,128)(2,1)S(1)}, bf16[1,3,40,960]{3,2,1,0:T(8,128)(2,1)S(1)}, u32[]{:S(2)}, u32[]{:S(2)}) %collective-permute-start.20) | collective-permute-done | bytes 230432 | tf_op jit(solution)/shard_map/ppermute | solution.py:210
  73.8 1.6 %collective-permute-start.22 = (f32[3,8,960]{2,1,0:T(8,128)S(1)}, f32[3,8,960]{2,1,0:T(8,128)S(1)}, u32[]{:S(2)}, u32[]{:S(2)}) collective-permute-start(f32[3,8,960]{2,1,0:T(8,128)S(1)} %add.83.r0_ref), channel_id=1, source_target_pairs={{0,2},{1,3},{2,0},{3,1},{4,6},{5,7},{6,4},{7,5},{8,10},{9,11},{10,... | collective-permute-start | bytes 276488 | tf_op jit(solution)/shard_map/ppermute | solution.py:210
  75.5 2.4 %errors.1 = bf16[3,320,960]{2,1,0:T(8,128)(2,1)} custom-call(f32[3,320,960]{2,1,0:T(8,128)S(1)} %bitcast.19, bf16[3,320,960]{2,1,0:T(8,128)(2,1)S(1)} %bitcast.22, bf16[3,320,96]{2,1,0:T(8,128)(2,1)S(1)} %solve.1.w_ref, f32[3,32,960]{2,1,0:T(8,128)S(1)} %get-tuple-element.60.all_ref), custom_call_target="tpu_custom_call" | custom-call | bytes 12582912 | tf_op jit(solution)/shard_map/errors/pallas_call | solution.py:323
  77.9 2.7 %collective-permute-done.22.r2_ref = f32[3,8,960]{2,1,0:T(8,128)S(1)} collective-permute-done((f32[3,8,960]{2,1,0:T(8,128)S(1)}, f32[3,8,960]{2,1,0:T(8,128)S(1)}, u32[]{:S(2)}, u32[]{:S(2)}) %collective-permute-start.22) | collective-permute-done | bytes 92192 | tf_op jit(solution)/shard_map/ppermute | solution.py:210
  80.6 4.0 %step.1 = (bf16[3,8,40,960]{3,2,1,0:T(8,128)(2,1)}, bf16[2,8,40,960]{3,2,1,0:T(8,128)(2,1)}) custom-call(s32[3]{0:T(128)S(1)} %copy-done.2, s32[3]{0:T(128)S(1)} %copy-done.3, f32[4]{0:T(128)S(1)} %copy-done.4, f32[4]{0:T(128)S(1)} %copy-done.5, f32[3,8,960]{2,1,0:T(8,128)S(1)} %add.83.r0_ref, f32[3,8,960]{2,1,0:T(8,128)S(1)} %collective-permute-done.21.r1_ref, ...), custom_call_target="tpu_custom_call" | custom-call | tf_op jit(solution)/shard_map/step/pallas_call | solution.py:337
  (52 shorter events, 7.0 us)
Async XLA Ops:
  0.6 0.7 copy-start.2
  1.3 34.4 %copy-start.1 = (bf16[1,3,320,960]{3,2,1,0:T(8,128)(2,1)S(1)}, bf16[1,3,320,960]{3,2,1,0:T(8,128)(2,1)}, u32[]{:S(2)}) copy-start(bf16[1,3,320,960]{3,2,1,0:T(8,128)(2,1)} %param.9) | copy-start | bytes 5529604
  7.0 3.0 %collective-permute-start.2 = (bf16[4,3,40,960]{3,2,1,0:T(8,128)(2,1)}, bf16[4,3,40,960]{3,2,1,0:T(8,128)(2,1)S(1)}, u32[]{:S(2)}, u32[]{:S(2)}) collective-permute-start(bf16[4,3,40,960]{3,2,1,0:T(8,128)(2,1)} %get-tuple-element.38), channel_id=1, source_target_pairs={{0,1},{1,0},{2,3},{3,2},{4,5},{5,4},{6,7},{7,6},{8,9},{9,8},{10,11... | collective-permute-start | bytes 2764808 | tf_op jit(solution)/shard_map/ppermute | solution.py:210
  7.5 2.2 %collective-permute-start = (f32[16,960]{1,0:T(8,128)S(1)}, f32[16,960]{1,0:T(8,128)S(1)}, u32[]{:S(2)}, u32[]{:S(2)}) collective-permute-start(f32[16,960]{1,0:T(8,128)S(1)} %get-tuple-element.35), channel_id=1, source_target_pairs={{0,1},{1,0},{2,3},{3,2},{4,5},{5,4},{6,7},{7,6},{8,9},{9,8},{10,11... | collective-permute-start | bytes 184328 | tf_op jit(solution)/shard_map/ppermute | solution.py:210
  9.8 25.9 %copy-start = (f32[1,3,320,960]{3,2,1,0:T(8,128)S(1)}, f32[1,3,320,960]{3,2,1,0:T(8,128)}, u32[]{:S(2)}) copy-start(f32[1,3,320,960]{3,2,1,0:T(8,128)} %param.8) | copy-start | bytes 11059204
  11.3 14.2 %collective-permute-start.6 = (bf16[1,3,40,960]{3,2,1,0:T(8,128)(2,1)S(1)}, bf16[1,3,40,960]{3,2,1,0:T(8,128)(2,1)S(1)}, u32[]{:S(2)}, u32[]{:S(2)}) collective-permute-start(bf16[1,3,40,960]{3,2,1,0:T(8,128)(2,1)S(1)} %get-tuple-element.65), channel_id=1, source_target_pairs={{0,6},{1,7},{2,4},{3,5},{4,2},{5,3},{6,0},{7,1},{8,14},{9,15},{10,... | collective-permute-start | bytes 691208 | tf_op jit(solution)/shard_map/ppermute | solution.py:210
  15.3 11.4 %collective-permute-start.5 = (bf16[1,3,40,960]{3,2,1,0:T(8,128)(2,1)S(1)}, bf16[1,3,40,960]{3,2,1,0:T(8,128)(2,1)S(1)}, u32[]{:S(2)}, u32[]{:S(2)}) collective-permute-start(bf16[1,3,40,960]{3,2,1,0:T(8,128)(2,1)S(1)} %get-tuple-element.66), channel_id=1, source_target_pairs={{0,4},{1,5},{2,6},{3,7},{4,0},{5,1},{6,2},{7,3},{8,12},{9,13},{10,... | collective-permute-start | bytes 691208 | tf_op jit(solution)/shard_map/ppermute | solution.py:210
  15.8 11.2 %collective-permute-start.4 = (bf16[1,3,40,960]{3,2,1,0:T(8,128)(2,1)S(1)}, bf16[1,3,40,960]{3,2,1,0:T(8,128)(2,1)S(1)}, u32[]{:S(2)}, u32[]{:S(2)}) collective-permute-start(bf16[1,3,40,960]{3,2,1,0:T(8,128)(2,1)S(1)} %get-tuple-element.67), channel_id=1, source_target_pairs={{0,2},{1,3},{2,0},{3,1},{4,6},{5,7},{6,4},{7,5},{8,10},{9,11},{10,... | collective-permute-start | bytes 691208 | tf_op jit(solution)/shard_map/ppermute | solution.py:210
  16.0 4.3 %collective-permute-start.1 = (f32[16,960]{1,0:T(8,128)S(1)}, f32[16,960]{1,0:T(8,128)S(1)}, u32[]{:S(2)}, u32[]{:S(2)}) collective-permute-start(f32[16,960]{1,0:T(8,128)S(1)} %add.63), channel_id=1, source_target_pairs={{0,8},{1,9},{2,10},{3,11},{4,12},{5,13},{6,14},{7,15},{8,0},{9,1},... | collective-permute-start | bytes 184328 | tf_op jit(solution)/shard_map/ppermute | solution.py:210
  20.2 5.3 %collective-permute-start.3 = (f32[16,960]{1,0:T(8,128)S(1)}, f32[16,960]{1,0:T(8,128)S(1)}, u32[]{:S(2)}, u32[]{:S(2)}) collective-permute-start(f32[16,960]{1,0:T(8,128)S(1)} %add.64), channel_id=1, source_target_pairs={{0,16},{1,17},{2,18},{3,19},{4,20},{5,21},{6,22},{7,23},{8,24},{9,... | collective-permute-start | bytes 184328 | tf_op jit(solution)/shard_map/ppermute | solution.py:210
  27.1 5.7 %collective-permute-start.9 = (f32[16,960]{1,0:T(8,128)S(1)}, f32[16,960]{1,0:T(8,128)S(1)}, u32[]{:S(2)}, u32[]{:S(2)}) collective-permute-start(f32[16,960]{1,0:T(8,128)S(1)} %add.69), channel_id=1, source_target_pairs={{0,6},{1,7},{2,4},{3,5},{4,2},{5,3},{6,0},{7,1},{8,14},{9,15},{10,... | collective-permute-start | bytes 184328 | tf_op jit(solution)/shard_map/ppermute | solution.py:210
  28.7 4.6 %collective-permute-start.8 = (f32[16,960]{1,0:T(8,128)S(1)}, f32[16,960]{1,0:T(8,128)S(1)}, u32[]{:S(2)}, u32[]{:S(2)}) collective-permute-start(f32[16,960]{1,0:T(8,128)S(1)} %add.69), channel_id=1, source_target_pairs={{0,4},{1,5},{2,6},{3,7},{4,0},{5,1},{6,2},{7,3},{8,12},{9,13},{10,... | collective-permute-start | bytes 184328 | tf_op jit(solution)/shard_map/ppermute | solution.py:210
  30.1 4.3 %collective-permute-start.7 = (f32[16,960]{1,0:T(8,128)S(1)}, f32[16,960]{1,0:T(8,128)S(1)}, u32[]{:S(2)}, u32[]{:S(2)}) collective-permute-start(f32[16,960]{1,0:T(8,128)S(1)} %add.69), channel_id=1, source_target_pairs={{0,2},{1,3},{2,0},{3,1},{4,6},{5,7},{6,4},{7,5},{8,10},{9,11},{10,... | collective-permute-start | bytes 184328 | tf_op jit(solution)/shard_map/ppermute | solution.py:210
  30.6 6.9 %collective-permute-start.11 = (bf16[1,3,40,960]{3,2,1,0:T(8,128)(2,1)S(1)}, bf16[1,3,40,960]{3,2,1,0:T(8,128)(2,1)S(1)}, u32[]{:S(2)}, u32[]{:S(2)}) collective-permute-start(bf16[1,3,40,960]{3,2,1,0:T(8,128)(2,1)S(1)} %add_add_fusion), channel_id=1, source_target_pairs={{0,8},{1,9},{2,10},{3,11},{4,12},{5,13},{6,14},{7,15},{8,0},{9,1},... | collective-permute-start | bytes 691208 | tf_op jit(solution)/shard_map/ppermute | solution.py:210
  34.4 1.3 %collective-permute-start.10 = (f32[16,960]{1,0:T(8,128)S(1)}, f32[16,960]{1,0:T(8,128)S(1)}, u32[]{:S(2)}, u32[]{:S(2)}) collective-permute-start(f32[16,960]{1,0:T(8,128)S(1)} %add_add_fusion.1.mine_ref), channel_id=1, source_target_pairs={{0,1},{1,0},{2,3},{3,2},{4,5},{5,4},{6,7},{7,6},{8,9},{9,8},{10,11... | collective-permute-start | bytes 184328 | tf_op jit(solution)/shard_map/ppermute | solution.py:210
  37.6 1.5 %collective-permute-start.12 = (f32[2,3,8,960]{3,2,1,0:T(8,128)S(1)}, f32[2,3,8,960]{3,2,1,0:T(8,128)S(1)}, u32[]{:S(2)}, u32[]{:S(2)}) collective-permute-start(f32[2,3,8,960]{3,2,1,0:T(8,128)S(1)} %get-tuple-element.51), channel_id=1, source_target_pairs={{0,1},{1,0},{2,3},{3,2},{4,5},{5,4},{6,7},{7,6},{8,9},{9,8},{10,11... | collective-permute-start | bytes 552968 | tf_op jit(solution)/shard_map/ppermute | solution.py:210
  39.1 4.9 %collective-permute-start.13 = (f32[3,8,960]{2,1,0:T(8,128)S(1)}, f32[3,8,960]{2,1,0:T(8,128)S(1)}, u32[]{:S(2)}, u32[]{:S(2)}) collective-permute-start(f32[3,8,960]{2,1,0:T(8,128)S(1)} %fusion), channel_id=1, source_target_pairs={{0,2},{1,3},{2,0},{3,1},{4,6},{5,7},{6,4},{7,5},{8,10},{9,11},{10,... | collective-permute-start | bytes 276488 | tf_op jit(solution)/shard_map/ppermute | solution.py:210
  40.7 13.9 %collective-permute-start.15 = (bf16[1,3,40,960]{3,2,1,0:T(8,128)(2,1)S(1)}, bf16[1,3,40,960]{3,2,1,0:T(8,128)(2,1)S(1)}, u32[]{:S(2)}, u32[]{:S(2)}) collective-permute-start(bf16[1,3,40,960]{3,2,1,0:T(8,128)(2,1)S(1)} %add.76), channel_id=1, source_target_pairs={{0,16},{1,17},{2,18},{3,19},{4,20},{5,21},{6,22},{7,23},{8,24},{9,... | collective-permute-start | bytes 691208 | tf_op jit(solution)/shard_map/ppermute | solution.py:210
  44.1 4.7 %collective-permute-start.14 = (f32[3,8,960]{2,1,0:T(8,128)S(1)}, f32[3,8,960]{2,1,0:T(8,128)S(1)}, u32[]{:S(2)}, u32[]{:S(2)}) collective-permute-start(f32[3,8,960]{2,1,0:T(8,128)S(1)} %fusion.2), channel_id=1, source_target_pairs={{0,4},{1,5},{2,6},{3,7},{4,0},{5,1},{6,2},{7,3},{8,12},{9,13},{10,... | collective-permute-start | bytes 276488 | tf_op jit(solution)/shard_map/ppermute | solution.py:210
  54.7 10.2 %collective-permute-start.18 = (bf16[1,3,40,960]{3,2,1,0:T(8,128)(2,1)S(1)}, bf16[1,3,40,960]{3,2,1,0:T(8,128)(2,1)S(1)}, u32[]{:S(2)}, u32[]{:S(2)}) collective-permute-start(bf16[1,3,40,960]{3,2,1,0:T(8,128)(2,1)S(1)} %add.81), channel_id=1, source_target_pairs={{0,4},{1,5},{2,6},{3,7},{4,0},{5,1},{6,2},{7,3},{8,12},{9,13},{10,... | collective-permute-start | bytes 691208 | tf_op jit(solution)/shard_map/ppermute | solution.py:210
  55.2 9.7 %collective-permute-start.17 = (bf16[1,3,40,960]{3,2,1,0:T(8,128)(2,1)S(1)}, bf16[1,3,40,960]{3,2,1,0:T(8,128)(2,1)S(1)}, u32[]{:S(2)}, u32[]{:S(2)}) collective-permute-start(bf16[1,3,40,960]{3,2,1,0:T(8,128)(2,1)S(1)} %add.81), channel_id=1, source_target_pairs={{0,2},{1,3},{2,0},{3,1},{4,6},{5,7},{6,4},{7,5},{8,10},{9,11},{10,... | collective-permute-start | bytes 691208 | tf_op jit(solution)/shard_map/ppermute | solution.py:210
  60.2 4.7 %collective-permute-start.16 = (f32[3,8,960]{2,1,0:T(8,128)S(1)}, f32[3,8,960]{2,1,0:T(8,128)S(1)}, u32[]{:S(2)}, u32[]{:S(2)}) collective-permute-start(f32[3,8,960]{2,1,0:T(8,128)S(1)} %add.80), channel_id=1, source_target_pairs={{0,8},{1,9},{2,10},{3,11},{4,12},{5,13},{6,14},{7,15},{8,0},{9,1},... | collective-permute-start | bytes 276488 | tf_op jit(solution)/shard_map/ppermute | solution.py:210
  64.9 6.6 %collective-permute-start.19 = (f32[3,8,960]{2,1,0:T(8,128)S(1)}, f32[3,8,960]{2,1,0:T(8,128)S(1)}, u32[]{:S(2)}, u32[]{:S(2)}) collective-permute-start(f32[3,8,960]{2,1,0:T(8,128)S(1)} %add.82), channel_id=1, source_target_pairs={{0,16},{1,17},{2,18},{3,19},{4,20},{5,21},{6,22},{7,23},{8,24},{9,... | collective-permute-start | bytes 276488 | tf_op jit(solution)/shard_map/ppermute | solution.py:210
  67.0 6.2 %collective-permute-start.20 = (bf16[1,3,40,960]{3,2,1,0:T(8,128)(2,1)S(1)}, bf16[1,3,40,960]{3,2,1,0:T(8,128)(2,1)S(1)}, u32[]{:S(2)}, u32[]{:S(2)}) collective-permute-start(bf16[1,3,40,960]{3,2,1,0:T(8,128)(2,1)S(1)} %collective-permute-done.17), channel_id=1, source_target_pairs={{0,4},{1,5},{2,6},{3,7},{4,0},{5,1},{6,2},{7,3},{8,12},{9,13},{10,... | collective-permute-start | bytes 691208 | tf_op jit(solution)/shard_map/ppermute | solution.py:210
  73.2 7.4 %collective-permute-start.24 = (bf16[4,3,40,960]{3,2,1,0:T(8,128)(2,1)S(1)}, bf16[4,3,40,960]{3,2,1,0:T(8,128)(2,1)S(1)}, u32[]{:S(2)}, u32[]{:S(2)}) collective-permute-start(bf16[4,3,40,960]{3,2,1,0:T(8,128)(2,1)S(1)} %constant_dynamic-update-slice_fusion.even_ref), channel_id=1, source_target_pairs={{0,1},{1,0},{2,3},{3,2},{4,5},{5,4},{6,7},{7,6},{8,9},{9,8},{10,11... | collective-permute-start | bytes 2764808 | tf_op jit(solution)/shard_map/ppermute | solution.py:210
  73.3 4.6 %collective-permute-start.23 = (f32[3,8,960]{2,1,0:T(8,128)S(1)}, f32[3,8,960]{2,1,0:T(8,128)S(1)}, u32[]{:S(2)}, u32[]{:S(2)}) collective-permute-start(f32[3,8,960]{2,1,0:T(8,128)S(1)} %add.83.r0_ref), channel_id=1, source_target_pairs={{0,3},{1,2},{2,1},{3,0},{4,7},{5,6},{6,5},{7,4},{8,11},{9,10},{10,... | collective-permute-start | bytes 276488 | tf_op jit(solution)/shard_map/ppermute | solution.py:210
  73.8 6.7 %collective-permute-start.22 = (f32[3,8,960]{2,1,0:T(8,128)S(1)}, f32[3,8,960]{2,1,0:T(8,128)S(1)}, u32[]{:S(2)}, u32[]{:S(2)}) collective-permute-start(f32[3,8,960]{2,1,0:T(8,128)S(1)} %add.83.r0_ref), channel_id=1, source_target_pairs={{0,2},{1,3},{2,0},{3,1},{4,6},{5,7},{6,4},{7,5},{8,10},{9,11},{10,... | collective-permute-start | bytes 276488 | tf_op jit(solution)/shard_map/ppermute | solution.py:210
  75.4 5.1 %collective-permute-start.21 = (f32[3,8,960]{2,1,0:T(8,128)S(1)}, f32[3,8,960]{2,1,0:T(8,128)S(1)}, u32[]{:S(2)}, u32[]{:S(2)}) collective-permute-start(f32[3,8,960]{2,1,0:T(8,128)S(1)} %add.83.r0_ref), channel_id=1, source_target_pairs={{0,1},{1,0},{2,3},{3,2},{4,5},{5,4},{6,7},{7,6},{8,9},{9,8},{10,11... | collective-permute-start | bytes 276488 | tf_op jit(solution)/shard_map/ppermute | solution.py:210
  75.5 5.1 %copy-start.3 = (s32[3]{0:T(128)S(1)}, s32[3]{0:T(128)}, u32[]{:S(2)}) copy-start(s32[3]{0:T(128)} %buckets_ref.1) | copy-start | bytes 40
  75.5 5.1 %copy-start.4 = (f32[4]{0:T(128)S(1)}, f32[4]{0:T(128)}, u32[]{:S(2)}) copy-start(f32[4]{0:T(128)} %rates_ref.1) | copy-start | bytes 52
  75.5 5.1 %copy-start.5 = (f32[4]{0:T(128)S(1)}, f32[4]{0:T(128)}, u32[]{:S(2)}) copy-start(f32[4]{0:T(128)} %betas_ref.1) | copy-start | bytes 52

commit v7 on v6

--- a/solution.py
+++ b/solution.py
@@ -11,7 +11,6 @@
 F32 = jnp.float32
 BF16 = jnp.bfloat16
 SMEM = pl.BlockSpec(memory_space=pltpu.SMEM)
-LIMIT = 53
 
 
 def whole(shape):
@@ -125,13 +124,10 @@
     return slot
 
 
-OLD_ORDER = ((0,), (2,), (4,), (6,), (1, 3, 5, 7))
-
-
 def first_kernel(
-    owners_ref, grad_hbm, error_hbm, q_hbm, mom_hbm,
-    mine_ref, other_ref, k0_ref, k2_ref, k4_ref, k6_ref, odd_ref,
-    grad_ref, error_ref, q_ref, mom_ref, left_ref, sems, mom_sem,
+    owners_hbm, grad_hbm, error_hbm, q_hbm, mom_hbm,
+    mine_ref, other_ref, odd_ref,
+    owners_ref, grad_ref, error_ref, q_ref, mom_ref, left_ref, sems, mom_sems,
 ):
     mats, rows, _ = grad_ref.shape
     rank = q_ref.shape[1]
@@ -141,14 +137,14 @@
         [pltpu.make_async_copy(hbm.at[m], ref.at[m], sems.at[m, n]) for n, (hbm, ref) in enumerate(pairs)]
         for m in range(mats)
     ]
-    mom_copy = pltpu.make_async_copy(mom_hbm, mom_ref, mom_sem)
-    for copy in copies[0]:
+    mom_copies = [
+        pltpu.make_async_copy(mom_hbm, mom_ref, mom_sems.at[0]),
+        pltpu.make_async_copy(owners_hbm, owners_ref, mom_sems.at[1]),
+    ]
+    for copy in copies[0] + mom_copies:
         copy.start()
-    mom_copy.start()
-
-    outs = (k0_ref, k2_ref, k4_ref, k6_ref, odd_ref)
-    for out in outs:
-        out[...] = jnp.zeros(out.shape, BF16)
+
+    odd_ref[...] = jnp.zeros(odd_ref.shape, BF16)
     for m in range(mats):
         if m + 1 < mats:
             for copy in copies[m + 1]:
@@ -162,15 +158,28 @@
         mine_ref[:, m * rows : (m + 1) * rows] = left_ref[me & 1]
         other_ref[:, m * rows : (m + 1) * rows] = left_ref[1 - (me & 1)]
         if m == 0:
-            mom_copy.wait()
+            for copy in mom_copies:
+                copy.wait()
             for i in range(mats):
                 slot = slot_of(owners_ref, i)
 
                 @pl.when(owners_ref[i] == me)
                 def _():
-                    for out, order in zip(outs, OLD_ORDER):
-                        for n, position in enumerate(order):
-                            out[n, i] = mom_ref[slot, position ^ (me & 7)]
+                    for n in range(4):
+                        odd_ref[n, i] = mom_ref[slot, (2 * n + 1) ^ (me & 7)]
+
+
+def even_kernel(owners_ref, mom_ref, got_ref, *outs):
+    me = lax.axis_index(AXES)
+    for n, out in enumerate(outs):
+        out[0] = got_ref[n]
+    for i in range(owners_ref.shape[0]):
+        slot = slot_of(owners_ref, i)
+
+        @pl.when(owners_ref[i] == me)
+        def _():
+            for n, out in enumerate(outs):
+                out[0, i] = mom_ref[slot, (2 * n) ^ (me & 7)]
 
 
 def step_kernel(
@@ -235,27 +244,36 @@
     def swap(value, mask):
         return exchange(value, mask, count)
 
-    sizes = [len(order) for order in OLD_ORDER]
-    mine, other, *evens, odd = pl.pallas_call(
+    momentum = momentum.reshape(slots, 8, piece, cols)
+    mine, other, odd = pl.pallas_call(
         first_kernel,
-        in_specs=[SMEM] + [pl.BlockSpec(memory_space=pltpu.HBM)] * 4,
-        out_shape=[sds((half, mats * rows), F32)] * 2 + [sds(old_shape(n), BF16) for n in sizes],
+        in_specs=[pl.BlockSpec(memory_space=pltpu.HBM)] * 5,
+        out_shape=[sds((half, mats * rows), F32)] * 2 + [sds(old_shape(4), BF16)],
         scratch_shapes=[
+            pltpu.SMEM((mats,), jnp.int32),
             pltpu.VMEM((mats, rows, cols), F32),
             pltpu.VMEM((mats, rows, cols), BF16),
             pltpu.VMEM((mats, rank, cols), F32),
             pltpu.VMEM((slots, 8, piece, cols), BF16),
             pltpu.VMEM((2, half, rows), F32),
             pltpu.SemaphoreType.DMA((mats, 3)),
-            pltpu.SemaphoreType.DMA,
+            pltpu.SemaphoreType.DMA((2,)),
         ],
-        compiler_params=pltpu.CompilerParams(vmem_limit_bytes=LIMIT * 1024 * 1024),
+        compiler_params=pltpu.CompilerParams(vmem_limit_bytes=40 * 1024 * 1024),
         name="first",
-    )(owners, grads, errs, q_t, momentum.reshape(slots, 8, piece, cols))
+    )(*(pltpu.with_memory_space_constraint(v, pltpu.HBM) for v in (owners, grads, errs, q_t, momentum)))
 
     got = swap(odd, 1)
     mine = mine + swap(other, 1)
-    evens = [after(even, mine) + got[n : n + 1] for n, even in enumerate(evens)]
+    evens = pl.pallas_call(
+        even_kernel,
+        grid=(1,),
+        in_specs=[SMEM, whole((slots, 8, piece, cols)), whole(old_shape(4))],
+        out_specs=[whole(old_shape(1))] * 4,
+        out_shape=[sds(old_shape(1), BF16)] * 4,
+        compiler_params=params(),
+        name="even",
+    )(owners, momentum, after(got, mine))
     got = [swap(evens[n], 2 * n) for n in (1, 2, 3)]
     mine = total_over(mine, bits[3:4], count)
     mine = after(mine, *evens)
@@ -307,8 +325,8 @@
     from_other = swap(old, 1 << bits[-1])
     r0 = keep + got[0] + swap(send2 + got[1], 2)
     r0 = total_over(r0, bits[2:3], count)
-    old = after(old, r0) + from_other
-    r0 = after(r0, old, w)
+    old = after(old, r0, w) + from_other
+    r0 = after(r0, old)
     near = [swap(old, 2), swap(old, 4)]
     for n, bit in enumerate(bits[3:]):
         r0 = total_over(r0, [bit], count)
@@ -317,7 +335,6 @@
             r0 = after(r0, *near)
     far = swap(near[0], 4)
     evens = jnp.concatenate([after(old, r0)] + near + [far])
-    r0 = after(r0, evens)
     odds = swap(evens, 1)
     r1, r2, r3 = (swap(r0, mask) for mask in (1, 2, 3))
     new_errors = pl.pallas_call(
@@ -344,7 +361,7 @@
         compiler_params=params(),
         name="step",
     )(owners, buckets, learn_rates, beta_values, r0, r1, r2, r3, w, evens, odds)
-    return (new_errors[None], steps.reshape(1, mats, rows, cols), new_mom.reshape(momentum.shape))
+    return (new_errors[None], steps.reshape(1, mats, rows, cols), new_mom.reshape(slots, rows, cols))
 
 
 def solution(mesh):

time: 84.8 us -> 80 us (0.943); the launches traced: 84.6 us -> 78.8 us
  waiting for transfers between devices: 34.9 us -> 33 us
  starting transfers between devices: 29.2 us -> 27.4 us
  other arithmetic: 1.57 us -> 0.3 us
    ppermute x25, waiting for transfers between devices: 34.9 us -> 33 us  [exchange(): return lax.ppermute(value, AXES, [(d, d ^ mask) for d in range(count)])]
    ppermute x25, starting transfers between devices: 29.2 us -> 27.4 us  [exchange(): return lax.ppermute(value, AXES, [(d, d ^ mask) for d in range(count)])]
    add x2 -> x1, other arithmetic: 1.33 us -> 0.06 us  [on_device(): old = after(old, r0, w) + from_other]
    pallas_call x1 -> x2, Pallas kernels: 5.73 us -> 5.74 us  [the longest x1 5.11 us: on_device(): pl.pallas_call(first_kernel, in_specs=[pl.BlockSpec(memory_space=pltpu.HB...]
where the time goes in v7:
time: 80 us; the launch traced here: 78.8 us
  waiting for transfers between devices  33 us (41%)
  starting transfers between devices  27.4 us (34%)
  Pallas kernels  17.2 us (22%)
  between operations  0.88 us (1%)
    ppermute x25, waiting for transfers between devices, exchange(): return lax.ppermute(value, AXES, [(d, d ^ mask) for d in range(count)])  33 us
    ppermute x25, starting transfers between devices, exchange(): return lax.ppermute(value, AXES, [(d, d ^ mask) for d in range(count)])  27.4 us
    pallas_call x1, Pallas kernels, on_device(): pl.pallas_call(first_kernel, in_specs=[pl.BlockSpec(memory_space=pltpu.HB...  5.11 us
    pallas_call x1, Pallas kernels, on_device(): pl.pallas_call(step_kernel, grid=(mats,), in_specs=[SMEM] * 4 + [quarter_...  3.99 us
    pallas_call x1, Pallas kernels, on_device(): pl.pallas_call(solve_kernel, grid=(1,), in_specs=[whole((half, mats * row...  3.38 us
    pallas_call x1, Pallas kernels, on_device(): pl.pallas_call(error_kernel, grid=(mats,), in_specs=[grad_spec, grad_spec...  2.33 us
    pallas_call x1, Pallas kernels, on_device(): pl.pallas_call(right_kernel, grid=(mats,), in_specs=[whole((half, mats *...  1.75 us
  transfers between devices with their start and end apart: 25, of which 18 were waited for; matrix products, arithmetic and copies ran while one was open for 0% of the time, Pallas kernels for 9%

profile of v7, /device:TPU:0, one launch (start us, length us, event | category | flops | bytes accessed | tf_op | source)
XLA Modules:
  0.0 78.8 jit_solution(9514875978140285542)
XLA Ops:
  0.7 5.1 %first.1 = (f32[16,960]{1,0:T(8,128)S(1)}, f32[16,960]{1,0:T(8,128)S(1)}, bf16[4,3,40,960]{3,2,1,0:T(8,128)(2,1)S(1)}) custom-call(s32[3]{0:T(128)} %owners_ref.3, f32[3,320,960]{2,1,0:T(8,128)} %bitcast.17, bf16[3,320,960]{2,1,0:T(8,128)(2,1)} %bitcast.20, f32[3,32,960]{2,1,0:T(8,128)} %bitcast.26, bf16[2,8,40,960]{3,2,1,0:T(8,128)(2,1)} %bitcast.23), custom_call_target="tpu_custom_call" | custom-call | tf_op jit(solution)/shard_map/first/pallas_call | solution.py:248
  6.4 2.2 %collective-permute-done = f32[16,960]{1,0:T(8,128)S(1)} collective-permute-done((f32[16,960]{1,0:T(8,128)S(1)}, f32[16,960]{1,0:T(8,128)S(1)}, u32[]{:S(2)}, u32[]{:S(2)}) %collective-permute-start) | collective-permute-done | bytes 61472 | tf_op jit(solution)/shard_map/ppermute | solution.py:219
  9.3 2.9 %collective-permute-start.4 = (bf16[1,3,40,960]{3,2,1,0:T(8,128)(2,1)S(1)}, bf16[1,3,40,960]{3,2,1,0:T(8,128)(2,1)S(1)}, u32[]{:S(2)}, u32[]{:S(2)}) collective-permute-start(bf16[1,3,40,960]{3,2,1,0:T(8,128)(2,1)S(1)} %get-tuple-element.35), channel_id=1, source_target_pairs={{0,2},{1,3},{2,0},{3,1},{4,6},{5,7},{6,4},{7,5},{8,10},{9,11},{10,... | collective-permute-start | bytes 691208 | tf_op jit(solution)/shard_map/ppermute | solution.py:219
  12.2 1.5 %collective-permute-start.5 = (bf16[1,3,40,960]{3,2,1,0:T(8,128)(2,1)S(1)}, bf16[1,3,40,960]{3,2,1,0:T(8,128)(2,1)S(1)}, u32[]{:S(2)}, u32[]{:S(2)}) collective-permute-start(bf16[1,3,40,960]{3,2,1,0:T(8,128)(2,1)S(1)} %get-tuple-element.36), channel_id=1, source_target_pairs={{0,4},{1,5},{2,6},{3,7},{4,0},{5,1},{6,2},{7,3},{8,12},{9,13},{10,... | collective-permute-start | bytes 691208 | tf_op jit(solution)/shard_map/ppermute | solution.py:219
  13.7 2.0 %collective-permute-start.1 = (f32[16,960]{1,0:T(8,128)S(1)}, f32[16,960]{1,0:T(8,128)S(1)}, u32[]{:S(2)}, u32[]{:S(2)}) collective-permute-start(f32[16,960]{1,0:T(8,128)S(1)} %add.51), channel_id=1, source_target_pairs={{0,8},{1,9},{2,10},{3,11},{4,12},{5,13},{6,14},{7,15},{8,0},{9,1},... | collective-permute-start | bytes 184328 | tf_op jit(solution)/shard_map/ppermute | solution.py:219
  15.8 2.2 %collective-permute-done.1 = f32[16,960]{1,0:T(8,128)S(1)} collective-permute-done((f32[16,960]{1,0:T(8,128)S(1)}, f32[16,960]{1,0:T(8,128)S(1)}, u32[]{:S(2)}, u32[]{:S(2)}) %collective-permute-start.1) | collective-permute-done | bytes 61472 | tf_op jit(solution)/shard_map/ppermute | solution.py:219
  18.0 3.1 %collective-permute-start.3 = (f32[16,960]{1,0:T(8,128)S(1)}, f32[16,960]{1,0:T(8,128)S(1)}, u32[]{:S(2)}, u32[]{:S(2)}) collective-permute-start(f32[16,960]{1,0:T(8,128)S(1)} %add.52), channel_id=1, source_target_pairs={{0,16},{1,17},{2,18},{3,19},{4,20},{5,21},{6,22},{7,23},{8,24},{9,... | collective-permute-start | bytes 184328 | tf_op jit(solution)/shard_map/ppermute | solution.py:219
  21.1 2.2 %collective-permute-done.3 = f32[16,960]{1,0:T(8,128)S(1)} collective-permute-done((f32[16,960]{1,0:T(8,128)S(1)}, f32[16,960]{1,0:T(8,128)S(1)}, u32[]{:S(2)}, u32[]{:S(2)}) %collective-permute-start.3) | collective-permute-done | bytes 61472 | tf_op jit(solution)/shard_map/ppermute | solution.py:219
  23.4 1.8 %collective-permute-done.5 = bf16[1,3,40,960]{3,2,1,0:T(8,128)(2,1)S(1)} collective-permute-done((bf16[1,3,40,960]{3,2,1,0:T(8,128)(2,1)S(1)}, bf16[1,3,40,960]{3,2,1,0:T(8,128)(2,1)S(1)}, u32[]{:S(2)}, u32[]{:S(2)}) %collective-permute-start.5) | collective-permute-done | bytes 230432 | tf_op jit(solution)/shard_map/ppermute | solution.py:219
  25.2 1.6 %collective-permute-start.9 = (f32[16,960]{1,0:T(8,128)S(1)}, f32[16,960]{1,0:T(8,128)S(1)}, u32[]{:S(2)}, u32[]{:S(2)}) collective-permute-start(f32[16,960]{1,0:T(8,128)S(1)} %add.53), channel_id=1, source_target_pairs={{0,6},{1,7},{2,4},{3,5},{4,2},{5,3},{6,0},{7,1},{8,14},{9,15},{10,... | collective-permute-start | bytes 184328 | tf_op jit(solution)/shard_map/ppermute | solution.py:219
  26.8 1.2 %collective-permute-start.8 = (f32[16,960]{1,0:T(8,128)S(1)}, f32[16,960]{1,0:T(8,128)S(1)}, u32[]{:S(2)}, u32[]{:S(2)}) collective-permute-start(f32[16,960]{1,0:T(8,128)S(1)} %add.53), channel_id=1, source_target_pairs={{0,4},{1,5},{2,6},{3,7},{4,0},{5,1},{6,2},{7,3},{8,12},{9,13},{10,... | collective-permute-start | bytes 184328 | tf_op jit(solution)/shard_map/ppermute | solution.py:219
  28.8 1.6 %collective-permute-start.11 = (bf16[1,3,40,960]{3,2,1,0:T(8,128)(2,1)S(1)}, bf16[1,3,40,960]{3,2,1,0:T(8,128)(2,1)S(1)}, u32[]{:S(2)}, u32[]{:S(2)}) collective-permute-start(bf16[1,3,40,960]{3,2,1,0:T(8,128)(2,1)S(1)} %add_add_fusion), channel_id=1, source_target_pairs={{0,8},{1,9},{2,10},{3,11},{4,12},{5,13},{6,14},{7,15},{8,0},{9,1},... | collective-permute-start | bytes 691208 | tf_op jit(solution)/shard_map/ppermute | solution.py:219
  32.4 1.2 %collective-permute-done.10.other_ref = f32[16,960]{1,0:T(8,128)S(1)} collective-permute-done((f32[16,960]{1,0:T(8,128)S(1)}, f32[16,960]{1,0:T(8,128)S(1)}, u32[]{:S(2)}, u32[]{:S(2)}) %collective-permute-start.10) | collective-permute-done | bytes 61472 | tf_op jit(solution)/shard_map/ppermute | solution.py:219
  33.6 1.8 %right.1 = (f32[3,32,960]{2,1,0:T(8,128)S(1)}, f32[3,8,960]{2,1,0:T(8,128)S(1)}, f32[3,8,960]{2,1,0:T(8,128)S(1)}, f32[2,3,8,960]{3,2,1,0:T(8,128)S(1)}) custom-call(f32[16,960]{1,0:T(8,128)S(1)} %add_add_fusion.1.mine_ref, f32[16,960]{1,0:T(8,128)S(1)} %collective-permute-done.10.other_ref, f32[3,320,960]{2,1,0:T(8,128)S(1)} %bitcast.18, ...), custom_call_target="tpu_custom_call" | custom-call | tf_op jit(solution)/shard_map/right/pallas_call | solution.py:289
  35.7 1.3 %collective-permute-done.12 = f32[2,3,8,960]{3,2,1,0:T(8,128)S(1)} collective-permute-done((f32[2,3,8,960]{3,2,1,0:T(8,128)S(1)}, f32[2,3,8,960]{3,2,1,0:T(8,128)S(1)}, u32[]{:S(2)}, u32[]{:S(2)}) %collective-permute-start.12) | collective-permute-done | bytes 184352 | tf_op jit(solution)/shard_map/ppermute | solution.py:219
  37.0 1.0 %collective-permute-start.13 = (f32[3,8,960]{2,1,0:T(8,128)S(1)}, f32[3,8,960]{2,1,0:T(8,128)S(1)}, u32[]{:S(2)}, u32[]{:S(2)}) collective-permute-start(f32[3,8,960]{2,1,0:T(8,128)S(1)} %fusion), channel_id=1, source_target_pairs={{0,2},{1,3},{2,0},{3,1},{4,6},{5,7},{6,4},{7,5},{8,10},{9,11},{10,... | collective-permute-start | bytes 276488 | tf_op jit(solution)/shard_map/ppermute | solution.py:219
  38.0 2.6 %collective-permute-start.15 = (bf16[1,3,40,960]{3,2,1,0:T(8,128)(2,1)S(1)}, bf16[1,3,40,960]{3,2,1,0:T(8,128)(2,1)S(1)}, u32[]{:S(2)}, u32[]{:S(2)}) collective-permute-start(bf16[1,3,40,960]{3,2,1,0:T(8,128)(2,1)S(1)} %add.60), channel_id=1, source_target_pairs={{0,16},{1,17},{2,18},{3,19},{4,20},{5,21},{6,22},{7,23},{8,24},{9,... | collective-permute-start | bytes 691208 | tf_op jit(solution)/shard_map/ppermute | solution.py:219
  40.6 1.3 %collective-permute-done.13 = f32[3,8,960]{2,1,0:T(8,128)S(1)} collective-permute-done((f32[3,8,960]{2,1,0:T(8,128)S(1)}, f32[3,8,960]{2,1,0:T(8,128)S(1)}, u32[]{:S(2)}, u32[]{:S(2)}) %collective-permute-start.13) | collective-permute-done | bytes 92192 | tf_op jit(solution)/shard_map/ppermute | solution.py:219
  41.9 1.2 %collective-permute-start.14 = (f32[3,8,960]{2,1,0:T(8,128)S(1)}, f32[3,8,960]{2,1,0:T(8,128)S(1)}, u32[]{:S(2)}, u32[]{:S(2)}) collective-permute-start(f32[3,8,960]{2,1,0:T(8,128)S(1)} %fusion.2), channel_id=1, source_target_pairs={{0,4},{1,5},{2,6},{3,7},{4,0},{5,1},{6,2},{7,3},{8,12},{9,13},{10,... | collective-permute-start | bytes 276488 | tf_op jit(solution)/shard_map/ppermute | solution.py:219
  43.1 3.4 %solve.1.w_ref = bf16[3,320,96]{2,1,0:T(8,128)(2,1)S(1)} custom-call(f32[16,960]{1,0:T(8,128)S(1)} %add_add_fusion.1.mine_ref, f32[16,960]{1,0:T(8,128)S(1)} %collective-permute-done.10.other_ref), custom_call_target="tpu_custom_call" | custom-call | bytes 16777216 | tf_op jit(solution)/shard_map/solve/pallas_call | solution.py:310
  46.6 5.3 %collective-permute-done.15 = bf16[1,3,40,960]{3,2,1,0:T(8,128)(2,1)S(1)} collective-permute-done((bf16[1,3,40,960]{3,2,1,0:T(8,128)(2,1)S(1)}, bf16[1,3,40,960]{3,2,1,0:T(8,128)(2,1)S(1)}, u32[]{:S(2)}, u32[]{:S(2)}) %collective-permute-start.15) | collective-permute-done | bytes 230432 | tf_op jit(solution)/shard_map/ppermute | solution.py:219
  52.0 1.4 %collective-permute-start.18 = (bf16[1,3,40,960]{3,2,1,0:T(8,128)(2,1)S(1)}, bf16[1,3,40,960]{3,2,1,0:T(8,128)(2,1)S(1)}, u32[]{:S(2)}, u32[]{:S(2)}) collective-permute-start(bf16[1,3,40,960]{3,2,1,0:T(8,128)(2,1)S(1)} %add.65), channel_id=1, source_target_pairs={{0,4},{1,5},{2,6},{3,7},{4,0},{5,1},{6,2},{7,3},{8,12},{9,13},{10,... | collective-permute-start | bytes 691208 | tf_op jit(solution)/shard_map/ppermute | solution.py:219
  54.9 4.0 %collective-permute-done.16 = f32[3,8,960]{2,1,0:T(8,128)S(1)} collective-permute-done((f32[3,8,960]{2,1,0:T(8,128)S(1)}, f32[3,8,960]{2,1,0:T(8,128)S(1)}, u32[]{:S(2)}, u32[]{:S(2)}) %collective-permute-start.16) | collective-permute-done | bytes 92192 | tf_op jit(solution)/shard_map/ppermute | solution.py:219
  58.9 1.1 %collective-permute-done.17 = bf16[1,3,40,960]{3,2,1,0:T(8,128)(2,1)S(1)} collective-permute-done((bf16[1,3,40,960]{3,2,1,0:T(8,128)(2,1)S(1)}, bf16[1,3,40,960]{3,2,1,0:T(8,128)(2,1)S(1)}, u32[]{:S(2)}, u32[]{:S(2)}) %collective-permute-start.17) | collective-permute-done | bytes 230432 | tf_op jit(solution)/shard_map/ppermute | solution.py:219
  60.0 0.9 %collective-permute-start.19 = (f32[3,8,960]{2,1,0:T(8,128)S(1)}, f32[3,8,960]{2,1,0:T(8,128)S(1)}, u32[]{:S(2)}, u32[]{:S(2)}) collective-permute-start(f32[3,8,960]{2,1,0:T(8,128)S(1)} %add.66), channel_id=1, source_target_pairs={{0,16},{1,17},{2,18},{3,19},{4,20},{5,21},{6,22},{7,23},{8,24},{9,... | collective-permute-start | bytes 276488 | tf_op jit(solution)/shard_map/ppermute | solution.py:219
  61.0 0.9 %collective-permute-start.20 = (bf16[1,3,40,960]{3,2,1,0:T(8,128)(2,1)S(1)}, bf16[1,3,40,960]{3,2,1,0:T(8,128)(2,1)S(1)}, u32[]{:S(2)}, u32[]{:S(2)}) collective-permute-start(bf16[1,3,40,960]{3,2,1,0:T(8,128)(2,1)S(1)} %collective-permute-done.17), channel_id=1, source_target_pairs={{0,4},{1,5},{2,6},{3,7},{4,0},{5,1},{6,2},{7,3},{8,12},{9,13},{10,... | collective-permute-start | bytes 691208 | tf_op jit(solution)/shard_map/ppermute | solution.py:219
  61.9 5.5 %collective-permute-done.19 = f32[3,8,960]{2,1,0:T(8,128)S(1)} collective-permute-done((f32[3,8,960]{2,1,0:T(8,128)S(1)}, f32[3,8,960]{2,1,0:T(8,128)S(1)}, u32[]{:S(2)}, u32[]{:S(2)}) %collective-permute-start.19) | collective-permute-done | bytes 92192 | tf_op jit(solution)/shard_map/ppermute | solution.py:219
  67.5 1.0 %collective-permute-start.23 = (f32[3,8,960]{2,1,0:T(8,128)S(1)}, f32[3,8,960]{2,1,0:T(8,128)S(1)}, u32[]{:S(2)}, u32[]{:S(2)}) collective-permute-start(f32[3,8,960]{2,1,0:T(8,128)S(1)} %add.67.r0_ref), channel_id=1, source_target_pairs={{0,3},{1,2},{2,1},{3,0},{4,7},{5,6},{6,5},{7,4},{8,11},{9,10},{10,... | collective-permute-start | bytes 276488 | tf_op jit(solution)/shard_map/ppermute | solution.py:219
  68.6 1.1 %collective-permute-start.22 = (f32[3,8,960]{2,1,0:T(8,128)S(1)}, f32[3,8,960]{2,1,0:T(8,128)S(1)}, u32[]{:S(2)}, u32[]{:S(2)}) collective-permute-start(f32[3,8,960]{2,1,0:T(8,128)S(1)} %add.67.r0_ref), channel_id=1, source_target_pairs={{0,2},{1,3},{2,0},{3,1},{4,6},{5,7},{6,4},{7,5},{8,10},{9,11},{10,... | collective-permute-start | bytes 276488 | tf_op jit(solution)/shard_map/ppermute | solution.py:219
  69.7 2.3 %errors.1 = bf16[3,320,960]{2,1,0:T(8,128)(2,1)} custom-call(f32[3,320,960]{2,1,0:T(8,128)S(1)} %bitcast.19, bf16[3,320,960]{2,1,0:T(8,128)(2,1)S(1)} %bitcast.22, bf16[3,320,96]{2,1,0:T(8,128)(2,1)S(1)} %solve.1.w_ref, f32[3,32,960]{2,1,0:T(8,128)S(1)} %get-tuple-element.53.all_ref), custom_call_target="tpu_custom_call" | custom-call | bytes 12582912 | tf_op jit(solution)/shard_map/errors/pallas_call | solution.py:340
  72.1 2.7 %collective-permute-done.22.r2_ref = f32[3,8,960]{2,1,0:T(8,128)S(1)} collective-permute-done((f32[3,8,960]{2,1,0:T(8,128)S(1)}, f32[3,8,960]{2,1,0:T(8,128)S(1)}, u32[]{:S(2)}, u32[]{:S(2)}) %collective-permute-start.22) | collective-permute-done | bytes 92192 | tf_op jit(solution)/shard_map/ppermute | solution.py:219
  74.8 4.0 %step.1 = (bf16[3,8,40,960]{3,2,1,0:T(8,128)(2,1)}, bf16[2,8,40,960]{3,2,1,0:T(8,128)(2,1)}) custom-call(s32[3]{0:T(128)S(1)} %copy-done.3, s32[3]{0:T(128)S(1)} %copy-done.4, f32[4]{0:T(128)S(1)} %copy-done.5, f32[4]{0:T(128)S(1)} %copy-done.6, f32[3,8,960]{2,1,0:T(8,128)S(1)} %add.67.r0_ref, f32[3,8,960]{2,1,0:T(8,128)S(1)} %collective-permute-done.21.r1_ref, ...), custom_call_target="tpu_custom_call" | custom-call | tf_op jit(solution)/shard_map/step/pallas_call | solution.py:354
  (54 shorter events, 6.5 us)
Async XLA Ops:
  0.6 8.0 %copy-start.2 = (bf16[2,320,960]{2,1,0:T(8,128)(2,1)S(1)}, bf16[2,320,960]{2,1,0:T(8,128)(2,1)}, u32[]{:S(2)}) copy-start(bf16[2,320,960]{2,1,0:T(8,128)(2,1)} %param.15) | copy-start | bytes 3686404
  0.6 8.0 %copy-start.3 = (s32[3]{0:T(128)S(1)}, s32[3]{0:T(128)}, u32[]{:S(2)}) copy-start(s32[3]{0:T(128)} %owners_ref.3) | copy-start | bytes 40
  0.7 33.0 %copy-start.1 = (bf16[1,3,320,960]{3,2,1,0:T(8,128)(2,1)S(1)}, bf16[1,3,320,960]{3,2,1,0:T(8,128)(2,1)}, u32[]{:S(2)}) copy-start(bf16[1,3,320,960]{3,2,1,0:T(8,128)(2,1)} %param.9) | copy-start | bytes 5529604
  5.8 2.8 %collective-permute-start.2 = (bf16[4,3,40,960]{3,2,1,0:T(8,128)(2,1)S(1)}, bf16[4,3,40,960]{3,2,1,0:T(8,128)(2,1)S(1)}, u32[]{:S(2)}, u32[]{:S(2)}) collective-permute-start(bf16[4,3,40,960]{3,2,1,0:T(8,128)(2,1)S(1)} %get-tuple-element.32), channel_id=1, source_target_pairs={{0,1},{1,0},{2,3},{3,2},{4,5},{5,4},{6,7},{7,6},{8,9},{9,8},{10,11... | collective-permute-start | bytes 2764808 | tf_op jit(solution)/shard_map/ppermute | solution.py:219
  6.3 2.3 %collective-permute-start = (f32[16,960]{1,0:T(8,128)S(1)}, f32[16,960]{1,0:T(8,128)S(1)}, u32[]{:S(2)}, u32[]{:S(2)}) collective-permute-start(f32[16,960]{1,0:T(8,128)S(1)} %get-tuple-element.31), channel_id=1, source_target_pairs={{0,1},{1,0},{2,3},{3,2},{4,5},{5,4},{6,7},{7,6},{8,9},{9,8},{10,11... | collective-permute-start | bytes 184328 | tf_op jit(solution)/shard_map/ppermute | solution.py:219
  8.6 25.0 %copy-start = (f32[1,3,320,960]{3,2,1,0:T(8,128)S(1)}, f32[1,3,320,960]{3,2,1,0:T(8,128)}, u32[]{:S(2)}) copy-start(f32[1,3,320,960]{3,2,1,0:T(8,128)} %param.8) | copy-start | bytes 11059204
  9.3 14.1 %collective-permute-start.4 = (bf16[1,3,40,960]{3,2,1,0:T(8,128)(2,1)S(1)}, bf16[1,3,40,960]{3,2,1,0:T(8,128)(2,1)S(1)}, u32[]{:S(2)}, u32[]{:S(2)}) collective-permute-start(bf16[1,3,40,960]{3,2,1,0:T(8,128)(2,1)S(1)} %get-tuple-element.35), channel_id=1, source_target_pairs={{0,2},{1,3},{2,0},{3,1},{4,6},{5,7},{6,4},{7,5},{8,10},{9,11},{10,... | collective-permute-start | bytes 691208 | tf_op jit(solution)/shard_map/ppermute | solution.py:219
  12.2 13.0 %collective-permute-start.5 = (bf16[1,3,40,960]{3,2,1,0:T(8,128)(2,1)S(1)}, bf16[1,3,40,960]{3,2,1,0:T(8,128)(2,1)S(1)}, u32[]{:S(2)}, u32[]{:S(2)}) collective-permute-start(bf16[1,3,40,960]{3,2,1,0:T(8,128)(2,1)S(1)} %get-tuple-element.36), channel_id=1, source_target_pairs={{0,4},{1,5},{2,6},{3,7},{4,0},{5,1},{6,2},{7,3},{8,12},{9,13},{10,... | collective-permute-start | bytes 691208 | tf_op jit(solution)/shard_map/ppermute | solution.py:219
  13.7 11.5 %collective-permute-start.6 = (bf16[1,3,40,960]{3,2,1,0:T(8,128)(2,1)S(1)}, bf16[1,3,40,960]{3,2,1,0:T(8,128)(2,1)S(1)}, u32[]{:S(2)}, u32[]{:S(2)}) collective-permute-start(bf16[1,3,40,960]{3,2,1,0:T(8,128)(2,1)S(1)} %get-tuple-element.37), channel_id=1, source_target_pairs={{0,6},{1,7},{2,4},{3,5},{4,2},{5,3},{6,0},{7,1},{8,14},{9,15},{10,... | collective-permute-start | bytes 691208 | tf_op jit(solution)/shard_map/ppermute | solution.py:219
  13.7 4.3 %collective-permute-start.1 = (f32[16,960]{1,0:T(8,128)S(1)}, f32[16,960]{1,0:T(8,128)S(1)}, u32[]{:S(2)}, u32[]{:S(2)}) collective-permute-start(f32[16,960]{1,0:T(8,128)S(1)} %add.51), channel_id=1, source_target_pairs={{0,8},{1,9},{2,10},{3,11},{4,12},{5,13},{6,14},{7,15},{8,0},{9,1},... | collective-permute-start | bytes 184328 | tf_op jit(solution)/shard_map/ppermute | solution.py:219
  18.0 5.3 %collective-permute-start.3 = (f32[16,960]{1,0:T(8,128)S(1)}, f32[16,960]{1,0:T(8,128)S(1)}, u32[]{:S(2)}, u32[]{:S(2)}) collective-permute-start(f32[16,960]{1,0:T(8,128)S(1)} %add.52), channel_id=1, source_target_pairs={{0,16},{1,17},{2,18},{3,19},{4,20},{5,21},{6,22},{7,23},{8,24},{9,... | collective-permute-start | bytes 184328 | tf_op jit(solution)/shard_map/ppermute | solution.py:219
  25.2 5.6 %collective-permute-start.9 = (f32[16,960]{1,0:T(8,128)S(1)}, f32[16,960]{1,0:T(8,128)S(1)}, u32[]{:S(2)}, u32[]{:S(2)}) collective-permute-start(f32[16,960]{1,0:T(8,128)S(1)} %add.53), channel_id=1, source_target_pairs={{0,6},{1,7},{2,4},{3,5},{4,2},{5,3},{6,0},{7,1},{8,14},{9,15},{10,... | collective-permute-start | bytes 184328 | tf_op jit(solution)/shard_map/ppermute | solution.py:219
  26.8 4.6 %collective-permute-start.8 = (f32[16,960]{1,0:T(8,128)S(1)}, f32[16,960]{1,0:T(8,128)S(1)}, u32[]{:S(2)}, u32[]{:S(2)}) collective-permute-start(f32[16,960]{1,0:T(8,128)S(1)} %add.53), channel_id=1, source_target_pairs={{0,4},{1,5},{2,6},{3,7},{4,0},{5,1},{6,2},{7,3},{8,12},{9,13},{10,... | collective-permute-start | bytes 184328 | tf_op jit(solution)/shard_map/ppermute | solution.py:219
  28.0 4.3 %collective-permute-start.7 = (f32[16,960]{1,0:T(8,128)S(1)}, f32[16,960]{1,0:T(8,128)S(1)}, u32[]{:S(2)}, u32[]{:S(2)}) collective-permute-start(f32[16,960]{1,0:T(8,128)S(1)} %add.53), channel_id=1, source_target_pairs={{0,2},{1,3},{2,0},{3,1},{4,6},{5,7},{6,4},{7,5},{8,10},{9,11},{10,... | collective-permute-start | bytes 184328 | tf_op jit(solution)/shard_map/ppermute | solution.py:219
  28.8 6.6 %collective-permute-start.11 = (bf16[1,3,40,960]{3,2,1,0:T(8,128)(2,1)S(1)}, bf16[1,3,40,960]{3,2,1,0:T(8,128)(2,1)S(1)}, u32[]{:S(2)}, u32[]{:S(2)}) collective-permute-start(bf16[1,3,40,960]{3,2,1,0:T(8,128)(2,1)S(1)} %add_add_fusion), channel_id=1, source_target_pairs={{0,8},{1,9},{2,10},{3,11},{4,12},{5,13},{6,14},{7,15},{8,0},{9,1},... | collective-permute-start | bytes 691208 | tf_op jit(solution)/shard_map/ppermute | solution.py:219
  32.3 1.3 %collective-permute-start.10 = (f32[16,960]{1,0:T(8,128)S(1)}, f32[16,960]{1,0:T(8,128)S(1)}, u32[]{:S(2)}, u32[]{:S(2)}) collective-permute-start(f32[16,960]{1,0:T(8,128)S(1)} %add_add_fusion.1.mine_ref), channel_id=1, source_target_pairs={{0,1},{1,0},{2,3},{3,2},{4,5},{5,4},{6,7},{7,6},{8,9},{9,8},{10,11... | collective-permute-start | bytes 184328 | tf_op jit(solution)/shard_map/ppermute | solution.py:219
  35.5 1.5 %collective-permute-start.12 = (f32[2,3,8,960]{3,2,1,0:T(8,128)S(1)}, f32[2,3,8,960]{3,2,1,0:T(8,128)S(1)}, u32[]{:S(2)}, u32[]{:S(2)}) collective-permute-start(f32[2,3,8,960]{3,2,1,0:T(8,128)S(1)} %get-tuple-element.44), channel_id=1, source_target_pairs={{0,1},{1,0},{2,3},{3,2},{4,5},{5,4},{6,7},{7,6},{8,9},{9,8},{10,11... | collective-permute-start | bytes 552968 | tf_op jit(solution)/shard_map/ppermute | solution.py:219
  37.0 4.9 %collective-permute-start.13 = (f32[3,8,960]{2,1,0:T(8,128)S(1)}, f32[3,8,960]{2,1,0:T(8,128)S(1)}, u32[]{:S(2)}, u32[]{:S(2)}) collective-permute-start(f32[3,8,960]{2,1,0:T(8,128)S(1)} %fusion), channel_id=1, source_target_pairs={{0,2},{1,3},{2,0},{3,1},{4,6},{5,7},{6,4},{7,5},{8,10},{9,11},{10,... | collective-permute-start | bytes 276488 | tf_op jit(solution)/shard_map/ppermute | solution.py:219
  38.0 13.9 %collective-permute-start.15 = (bf16[1,3,40,960]{3,2,1,0:T(8,128)(2,1)S(1)}, bf16[1,3,40,960]{3,2,1,0:T(8,128)(2,1)S(1)}, u32[]{:S(2)}, u32[]{:S(2)}) collective-permute-start(bf16[1,3,40,960]{3,2,1,0:T(8,128)(2,1)S(1)} %add.60), channel_id=1, source_target_pairs={{0,16},{1,17},{2,18},{3,19},{4,20},{5,21},{6,22},{7,23},{8,24},{9,... | collective-permute-start | bytes 691208 | tf_op jit(solution)/shard_map/ppermute | solution.py:219
  41.9 4.7 %collective-permute-start.14 = (f32[3,8,960]{2,1,0:T(8,128)S(1)}, f32[3,8,960]{2,1,0:T(8,128)S(1)}, u32[]{:S(2)}, u32[]{:S(2)}) collective-permute-start(f32[3,8,960]{2,1,0:T(8,128)S(1)} %fusion.2), channel_id=1, source_target_pairs={{0,4},{1,5},{2,6},{3,7},{4,0},{5,1},{6,2},{7,3},{8,12},{9,13},{10,... | collective-permute-start | bytes 276488 | tf_op jit(solution)/shard_map/ppermute | solution.py:219
  52.0 7.0 %collective-permute-start.18 = (bf16[1,3,40,960]{3,2,1,0:T(8,128)(2,1)S(1)}, bf16[1,3,40,960]{3,2,1,0:T(8,128)(2,1)S(1)}, u32[]{:S(2)}, u32[]{:S(2)}) collective-permute-start(bf16[1,3,40,960]{3,2,1,0:T(8,128)(2,1)S(1)} %add.65), channel_id=1, source_target_pairs={{0,4},{1,5},{2,6},{3,7},{4,0},{5,1},{6,2},{7,3},{8,12},{9,13},{10,... | collective-permute-start | bytes 691208 | tf_op jit(solution)/shard_map/ppermute | solution.py:219
  53.4 6.6 %collective-permute-start.17 = (bf16[1,3,40,960]{3,2,1,0:T(8,128)(2,1)S(1)}, bf16[1,3,40,960]{3,2,1,0:T(8,128)(2,1)S(1)}, u32[]{:S(2)}, u32[]{:S(2)}) collective-permute-start(bf16[1,3,40,960]{3,2,1,0:T(8,128)(2,1)S(1)} %add.65), channel_id=1, source_target_pairs={{0,2},{1,3},{2,0},{3,1},{4,6},{5,7},{6,4},{7,5},{8,10},{9,11},{10,... | collective-permute-start | bytes 691208 | tf_op jit(solution)/shard_map/ppermute | solution.py:219
  54.2 4.6 %collective-permute-start.16 = (f32[3,8,960]{2,1,0:T(8,128)S(1)}, f32[3,8,960]{2,1,0:T(8,128)S(1)}, u32[]{:S(2)}, u32[]{:S(2)}) collective-permute-start(f32[3,8,960]{2,1,0:T(8,128)S(1)} %add.64), channel_id=1, source_target_pairs={{0,8},{1,9},{2,10},{3,11},{4,12},{5,13},{6,14},{7,15},{8,0},{9,1},... | collective-permute-start | bytes 276488 | tf_op jit(solution)/shard_map/ppermute | solution.py:219
  60.0 7.3 %collective-permute-start.19 = (f32[3,8,960]{2,1,0:T(8,128)S(1)}, f32[3,8,960]{2,1,0:T(8,128)S(1)}, u32[]{:S(2)}, u32[]{:S(2)}) collective-permute-start(f32[3,8,960]{2,1,0:T(8,128)S(1)} %add.66), channel_id=1, source_target_pairs={{0,16},{1,17},{2,18},{3,19},{4,20},{5,21},{6,22},{7,23},{8,24},{9,... | collective-permute-start | bytes 276488 | tf_op jit(solution)/shard_map/ppermute | solution.py:219
  61.0 6.5 %collective-permute-start.20 = (bf16[1,3,40,960]{3,2,1,0:T(8,128)(2,1)S(1)}, bf16[1,3,40,960]{3,2,1,0:T(8,128)(2,1)S(1)}, u32[]{:S(2)}, u32[]{:S(2)}) collective-permute-start(bf16[1,3,40,960]{3,2,1,0:T(8,128)(2,1)S(1)} %collective-permute-done.17), channel_id=1, source_target_pairs={{0,4},{1,5},{2,6},{3,7},{4,0},{5,1},{6,2},{7,3},{8,12},{9,13},{10,... | collective-permute-start | bytes 691208 | tf_op jit(solution)/shard_map/ppermute | solution.py:219
  67.5 7.4 %collective-permute-start.24 = (bf16[4,3,40,960]{3,2,1,0:T(8,128)(2,1)S(1)}, bf16[4,3,40,960]{3,2,1,0:T(8,128)(2,1)S(1)}, u32[]{:S(2)}, u32[]{:S(2)}) collective-permute-start(bf16[4,3,40,960]{3,2,1,0:T(8,128)(2,1)S(1)} %constant_dynamic-update-slice_fusion.even_ref), channel_id=1, source_target_pairs={{0,1},{1,0},{2,3},{3,2},{4,5},{5,4},{6,7},{7,6},{8,9},{9,8},{10,11... | collective-permute-start | bytes 2764808 | tf_op jit(solution)/shard_map/ppermute | solution.py:219
  67.5 4.6 %collective-permute-start.23 = (f32[3,8,960]{2,1,0:T(8,128)S(1)}, f32[3,8,960]{2,1,0:T(8,128)S(1)}, u32[]{:S(2)}, u32[]{:S(2)}) collective-permute-start(f32[3,8,960]{2,1,0:T(8,128)S(1)} %add.67.r0_ref), channel_id=1, source_target_pairs={{0,3},{1,2},{2,1},{3,0},{4,7},{5,6},{6,5},{7,4},{8,11},{9,10},{10,... | collective-permute-start | bytes 276488 | tf_op jit(solution)/shard_map/ppermute | solution.py:219
  68.6 6.2 %collective-permute-start.22 = (f32[3,8,960]{2,1,0:T(8,128)S(1)}, f32[3,8,960]{2,1,0:T(8,128)S(1)}, u32[]{:S(2)}, u32[]{:S(2)}) collective-permute-start(f32[3,8,960]{2,1,0:T(8,128)S(1)} %add.67.r0_ref), channel_id=1, source_target_pairs={{0,2},{1,3},{2,0},{3,1},{4,6},{5,7},{6,4},{7,5},{8,10},{9,11},{10,... | collective-permute-start | bytes 276488 | tf_op jit(solution)/shard_map/ppermute | solution.py:219
  69.7 5.1 %collective-permute-start.21 = (f32[3,8,960]{2,1,0:T(8,128)S(1)}, f32[3,8,960]{2,1,0:T(8,128)S(1)}, u32[]{:S(2)}, u32[]{:S(2)}) collective-permute-start(f32[3,8,960]{2,1,0:T(8,128)S(1)} %add.67.r0_ref), channel_id=1, source_target_pairs={{0,1},{1,0},{2,3},{3,2},{4,5},{5,4},{6,7},{7,6},{8,9},{9,8},{10,11... | collective-permute-start | bytes 276488 | tf_op jit(solution)/shard_map/ppermute | solution.py:219
  69.7 5.1 %copy-start.4 = (s32[3]{0:T(128)S(1)}, s32[3]{0:T(128)}, u32[]{:S(2)}) copy-start(s32[3]{0:T(128)} %buckets_ref.1) | copy-start | bytes 40
  69.7 5.1 %copy-start.5 = (f32[4]{0:T(128)S(1)}, f32[4]{0:T(128)}, u32[]{:S(2)}) copy-start(f32[4]{0:T(128)} %rates_ref.1) | copy-start | bytes 52
  69.7 5.1 %copy-start.6 = (f32[4]{0:T(128)S(1)}, f32[4]{0:T(128)}, u32[]{:S(2)}) copy-start(f32[4]{0:T(128)} %betas_ref.1) | copy-start | bytes 52

commit v8 on v7

--- a/solution.py
+++ b/solution.py
@@ -49,7 +49,7 @@
         left_ref[m, 1 - bit] = other_ref[:, m * rows : (m + 1) * rows]
 
 
-def right_kernel(mine_ref, other_ref, grad_ref, error_ref, all_ref, k0_ref, k2_ref, s_ref, left_ref, right_ref):
+def right_kernel(mine_ref, other_ref, grad_ref, error_ref, all_ref, k0_ref, k2_ref, s1_ref, s3_ref, left_ref, right_ref):
     i = pl.program_id(0)
     low_bits = lax.axis_index(AXES) & 3
     rows = grad_ref.shape[1]
@@ -69,8 +69,8 @@
     right_ref[...] = total.reshape(right_ref.shape)
     k0_ref[0] = right_ref[low_bits]
     k2_ref[0] = right_ref[low_bits ^ 2]
-    s_ref[0, 0] = right_ref[low_bits ^ 1]
-    s_ref[1, 0] = right_ref[low_bits ^ 3]
+    s1_ref[0] = right_ref[low_bits ^ 1]
+    s3_ref[0] = right_ref[low_bits ^ 3]
 
 
 def three(left):
@@ -281,27 +281,17 @@
         mine = total_over(mine, [bit], count)
     old = after(evens[0], mine) + got[0] + got[1] + got[2]
     mine = after(mine, old)
-    from_other = swap(old, 1 << bits[3])
-    mine = total_over(mine, bits[1:3], count)
-    old = after(old, mine) + from_other
+    from_other = swap(old, 1 << bits[-1])
+    for bit in bits[1:3]:
+        mine = total_over(mine, [bit], count)
     other = swap(mine, 1)
 
-    right_all, keep, send2, send = pl.pallas_call(
+    right_all, keep, send2, send1, send3 = pl.pallas_call(
         right_kernel,
         grid=(mats,),
         in_specs=[whole((half, mats * rows))] * 2 + [grad_spec, grad_spec],
-        out_specs=[
-            per_matrix((rank, cols)),
-            per_matrix((quarter, cols)),
-            per_matrix((quarter, cols)),
-            pl.BlockSpec((2, 1, quarter, cols), lambda i: (0, i, 0, 0)),
-        ],
-        out_shape=[
-            sds((mats, rank, cols), F32),
-            sds((mats, quarter, cols), F32),
-            sds((mats, quarter, cols), F32),
-            sds((2, mats, quarter, cols), F32),
-        ],
+        out_specs=[per_matrix((rank, cols))] + [per_matrix((quarter, cols))] * 4,
+        out_shape=[sds((mats, rank, cols), F32)] + [sds((mats, quarter, cols), F32)] * 4,
         scratch_shapes=[pltpu.VMEM((mats, 2, half, rows), F32), pltpu.VMEM((4, quarter, cols), F32)],
         compiler_params=params(),
         name="right",
@@ -315,15 +305,18 @@
         out_shape=sds((mats, rows, 3 * rank), BF16),
         scratch_shapes=[pltpu.VMEM((mats, 2, half, rows), F32)],
         compiler_params=params(),
-        cost_estimate=cost(16),
+        cost_estimate=cost(1),
         name="solve",
     )(mine, other)
 
-    got = swap(after(send, old), 1)
-    for bit in bits[4:-1]:
+    got = swap(send1, 1), swap(send3, 1)
+    r0, send2 = keep + got[0], send2 + got[1]
+    old = after(old, r0, send2) + from_other
+    for bit in reversed(bits[4:-1]):
         old = old + swap(old, 1 << bit)
-    from_other = swap(old, 1 << bits[-1])
-    r0 = keep + got[0] + swap(send2 + got[1], 2)
+    send2 = after(send2, old)
+    from_other = swap(old, 1 << bits[3])
+    r0 = r0 + swap(send2, 2)
     r0 = total_over(r0, bits[2:3], count)
     old = after(old, r0, w) + from_other
     r0 = after(r0, old)
@@ -336,7 +329,8 @@
     far = swap(near[0], 4)
     evens = jnp.concatenate([after(old, r0)] + near + [far])
     odds = swap(evens, 1)
-    r1, r2, r3 = (swap(r0, mask) for mask in (1, 2, 3))
+    r1, r2 = swap(r0, 1), swap(r0, 2)
+    r3 = swap(r2, 1)
     new_errors = pl.pallas_call(
         error_kernel,
         grid=(mats,),

time: 80 us -> 78.8 us (0.985); the launches traced: 78.8 us -> 78.6 us
  transfers between devices with their start and end apart: 25 -> 25, of which waited for: 18 -> 17; matrix products, arithmetic and copies ran while one was open for 0% -> 0% of each run, Pallas kernels for 9% -> 9%
where the time goes in v8:
time: 78.8 us; the launch traced here: 78.6 us
  waiting for transfers between devices  32.2 us (41%)
  starting transfers between devices  28 us (36%)
  Pallas kernels  17.2 us (22%)
  between operations  0.89 us (1%)
    ppermute x25, waiting for transfers between devices, exchange(): return lax.ppermute(value, AXES, [(d, d ^ mask) for d in range(count)])  32.2 us
    ppermute x25, starting transfers between devices, exchange(): return lax.ppermute(value, AXES, [(d, d ^ mask) for d in range(count)])  28 us
    pallas_call x1, Pallas kernels, on_device(): pl.pallas_call(first_kernel, in_specs=[pl.BlockSpec(memory_space=pltpu.HB...  5.11 us
    pallas_call x1, Pallas kernels, on_device(): pl.pallas_call(step_kernel, grid=(mats,), in_specs=[SMEM] * 4 + [quarter_...  3.99 us
    pallas_call x1, Pallas kernels, on_device(): pl.pallas_call(solve_kernel, grid=(1,), in_specs=[whole((half, mats * row...  3.38 us
    pallas_call x1, Pallas kernels, on_device(): pl.pallas_call(error_kernel, grid=(mats,), in_specs=[grad_spec, grad_spec...  2.34 us
    pallas_call x1, Pallas kernels, on_device(): pl.pallas_call(right_kernel, grid=(mats,), in_specs=[whole((half, mats *...  1.71 us
  transfers between devices with their start and end apart: 25, of which 17 were waited for; matrix products, arithmetic and copies ran while one was open for 0% of the time, Pallas kernels for 9%

profile of v8, /device:TPU:0, one launch (start us, length us, event | category | flops | bytes accessed | tf_op | source)
XLA Modules:
  0.0 78.6 jit_solution(9148382356723553926)
XLA Ops:
  0.7 5.1 %first.1 = (f32[16,960]{1,0:T(8,128)S(1)}, f32[16,960]{1,0:T(8,128)S(1)}, bf16[4,3,40,960]{3,2,1,0:T(8,128)(2,1)S(1)}) custom-call(s32[3]{0:T(128)} %owners_ref.3, f32[3,320,960]{2,1,0:T(8,128)} %bitcast.7, bf16[3,320,960]{2,1,0:T(8,128)(2,1)} %bitcast.10, f32[3,32,960]{2,1,0:T(8,128)} %bitcast.16, bf16[2,8,40,960]{3,2,1,0:T(8,128)(2,1)} %bitcast.13), custom_call_target="tpu_custom_call" | custom-call | tf_op jit(solution)/shard_map/first/pallas_call | solution.py:248
  6.4 2.2 %collective-permute-done = f32[16,960]{1,0:T(8,128)S(1)} collective-permute-done((f32[16,960]{1,0:T(8,128)S(1)}, f32[16,960]{1,0:T(8,128)S(1)}, u32[]{:S(2)}, u32[]{:S(2)}) %collective-permute-start) | collective-permute-done | bytes 61472 | tf_op jit(solution)/shard_map/ppermute | solution.py:219
  9.3 2.9 %collective-permute-start.4 = (bf16[1,3,40,960]{3,2,1,0:T(8,128)(2,1)S(1)}, bf16[1,3,40,960]{3,2,1,0:T(8,128)(2,1)S(1)}, u32[]{:S(2)}, u32[]{:S(2)}) collective-permute-start(bf16[1,3,40,960]{3,2,1,0:T(8,128)(2,1)S(1)} %get-tuple-element.36), channel_id=1, source_target_pairs={{0,2},{1,3},{2,0},{3,1},{4,6},{5,7},{6,4},{7,5},{8,10},{9,11},{10,... | collective-permute-start | bytes 691208 | tf_op jit(solution)/shard_map/ppermute | solution.py:219
  12.2 1.5 %collective-permute-start.5 = (bf16[1,3,40,960]{3,2,1,0:T(8,128)(2,1)S(1)}, bf16[1,3,40,960]{3,2,1,0:T(8,128)(2,1)S(1)}, u32[]{:S(2)}, u32[]{:S(2)}) collective-permute-start(bf16[1,3,40,960]{3,2,1,0:T(8,128)(2,1)S(1)} %get-tuple-element.37), channel_id=1, source_target_pairs={{0,4},{1,5},{2,6},{3,7},{4,0},{5,1},{6,2},{7,3},{8,12},{9,13},{10,... | collective-permute-start | bytes 691208 | tf_op jit(solution)/shard_map/ppermute | solution.py:219
  13.8 2.0 %collective-permute-start.1 = (f32[16,960]{1,0:T(8,128)S(1)}, f32[16,960]{1,0:T(8,128)S(1)}, u32[]{:S(2)}, u32[]{:S(2)}) collective-permute-start(f32[16,960]{1,0:T(8,128)S(1)} %add.48), channel_id=1, source_target_pairs={{0,8},{1,9},{2,10},{3,11},{4,12},{5,13},{6,14},{7,15},{8,0},{9,1},... | collective-permute-start | bytes 184328 | tf_op jit(solution)/shard_map/ppermute | solution.py:219
  15.8 2.2 %collective-permute-done.1 = f32[16,960]{1,0:T(8,128)S(1)} collective-permute-done((f32[16,960]{1,0:T(8,128)S(1)}, f32[16,960]{1,0:T(8,128)S(1)}, u32[]{:S(2)}, u32[]{:S(2)}) %collective-permute-start.1) | collective-permute-done | bytes 61472 | tf_op jit(solution)/shard_map/ppermute | solution.py:219
  18.0 3.1 %collective-permute-start.3 = (f32[16,960]{1,0:T(8,128)S(1)}, f32[16,960]{1,0:T(8,128)S(1)}, u32[]{:S(2)}, u32[]{:S(2)}) collective-permute-start(f32[16,960]{1,0:T(8,128)S(1)} %add.49), channel_id=1, source_target_pairs={{0,16},{1,17},{2,18},{3,19},{4,20},{5,21},{6,22},{7,23},{8,24},{9,... | collective-permute-start | bytes 184328 | tf_op jit(solution)/shard_map/ppermute | solution.py:219
  21.1 2.2 %collective-permute-done.3 = f32[16,960]{1,0:T(8,128)S(1)} collective-permute-done((f32[16,960]{1,0:T(8,128)S(1)}, f32[16,960]{1,0:T(8,128)S(1)}, u32[]{:S(2)}, u32[]{:S(2)}) %collective-permute-start.3) | collective-permute-done | bytes 61472 | tf_op jit(solution)/shard_map/ppermute | solution.py:219
  23.4 1.8 %collective-permute-done.5 = bf16[1,3,40,960]{3,2,1,0:T(8,128)(2,1)S(1)} collective-permute-done((bf16[1,3,40,960]{3,2,1,0:T(8,128)(2,1)S(1)}, bf16[1,3,40,960]{3,2,1,0:T(8,128)(2,1)S(1)}, u32[]{:S(2)}, u32[]{:S(2)}) %collective-permute-start.5) | collective-permute-done | bytes 230432 | tf_op jit(solution)/shard_map/ppermute | solution.py:219
  25.2 1.3 %collective-permute-start.7 = (f32[16,960]{1,0:T(8,128)S(1)}, f32[16,960]{1,0:T(8,128)S(1)}, u32[]{:S(2)}, u32[]{:S(2)}) collective-permute-start(f32[16,960]{1,0:T(8,128)S(1)} %add.50), channel_id=1, source_target_pairs={{0,2},{1,3},{2,0},{3,1},{4,6},{5,7},{6,4},{7,5},{8,10},{9,11},{10,... | collective-permute-start | bytes 184328 | tf_op jit(solution)/shard_map/ppermute | solution.py:219
  26.5 2.6 %collective-permute-start.12 = (bf16[1,3,40,960]{3,2,1,0:T(8,128)(2,1)S(1)}, bf16[1,3,40,960]{3,2,1,0:T(8,128)(2,1)S(1)}, u32[]{:S(2)}, u32[]{:S(2)}) collective-permute-start(bf16[1,3,40,960]{3,2,1,0:T(8,128)(2,1)S(1)} %add_add_fusion), channel_id=1, source_target_pairs={{0,16},{1,17},{2,18},{3,19},{4,20},{5,21},{6,22},{7,23},{8,24},{9,... | collective-permute-start | bytes 691208 | tf_op jit(solution)/shard_map/ppermute | solution.py:219
  29.6 1.6 %collective-permute-start.8 = (f32[16,960]{1,0:T(8,128)S(1)}, f32[16,960]{1,0:T(8,128)S(1)}, u32[]{:S(2)}, u32[]{:S(2)}) collective-permute-start(f32[16,960]{1,0:T(8,128)S(1)} %add.54), channel_id=1, source_target_pairs={{0,4},{1,5},{2,6},{3,7},{4,0},{5,1},{6,2},{7,3},{8,12},{9,13},{10,... | collective-permute-start | bytes 184328 | tf_op jit(solution)/shard_map/ppermute | solution.py:219
  31.2 2.8 %collective-permute-done.8 = f32[16,960]{1,0:T(8,128)S(1)} collective-permute-done((f32[16,960]{1,0:T(8,128)S(1)}, f32[16,960]{1,0:T(8,128)S(1)}, u32[]{:S(2)}, u32[]{:S(2)}) %collective-permute-start.8) | collective-permute-done | bytes 61472 | tf_op jit(solution)/shard_map/ppermute | solution.py:219
  34.0 1.2 %collective-permute-done.9.other_ref = f32[16,960]{1,0:T(8,128)S(1)} collective-permute-done((f32[16,960]{1,0:T(8,128)S(1)}, f32[16,960]{1,0:T(8,128)S(1)}, u32[]{:S(2)}, u32[]{:S(2)}) %collective-permute-start.9) | collective-permute-done | bytes 61472 | tf_op jit(solution)/shard_map/ppermute | solution.py:219
  35.3 1.7 %right.1 = (f32[3,32,960]{2,1,0:T(8,128)S(1)}, f32[3,8,960]{2,1,0:T(8,128)S(1)}, f32[3,8,960]{2,1,0:T(8,128)S(1)}, f32[3,8,960]{2,1,0:T(8,128)S(1)}, f32[3,8,960]{2,1,0:T(8,128)S(1)}) custom-call(f32[16,960]{1,0:T(8,128)S(1)} %add.55.mine_ref, f32[16,960]{1,0:T(8,128)S(1)} %collective-permute-done.9.other_ref, f32[3,320,960]{2,1,0:T(8,128)S(1)} %bitcast.8, ...), custom_call_target="tpu_custom_call" | custom-call | tf_op jit(solution)/shard_map/right/pallas_call | solution.py:289
  37.5 0.8 %collective-permute-done.10 = f32[3,8,960]{2,1,0:T(8,128)S(1)} collective-permute-done((f32[3,8,960]{2,1,0:T(8,128)S(1)}, f32[3,8,960]{2,1,0:T(8,128)S(1)}, u32[]{:S(2)}, u32[]{:S(2)}) %collective-permute-start.10) | collective-permute-done | bytes 92192 | tf_op jit(solution)/shard_map/ppermute | solution.py:219
  38.5 1.0 %collective-permute-done.12 = bf16[1,3,40,960]{3,2,1,0:T(8,128)(2,1)S(1)} collective-permute-done((bf16[1,3,40,960]{3,2,1,0:T(8,128)(2,1)S(1)}, bf16[1,3,40,960]{3,2,1,0:T(8,128)(2,1)S(1)}, u32[]{:S(2)}, u32[]{:S(2)}) %collective-permute-start.12) | collective-permute-done | bytes 230432 | tf_op jit(solution)/shard_map/ppermute | solution.py:219
  39.6 0.8 %collective-permute-start.15 = (bf16[1,3,40,960]{3,2,1,0:T(8,128)(2,1)S(1)}, bf16[1,3,40,960]{3,2,1,0:T(8,128)(2,1)S(1)}, u32[]{:S(2)}, u32[]{:S(2)}) collective-permute-start(bf16[1,3,40,960]{3,2,1,0:T(8,128)(2,1)S(1)} %add.58), channel_id=1, source_target_pairs={{0,8},{1,9},{2,10},{3,11},{4,12},{5,13},{6,14},{7,15},{8,0},{9,1},... | collective-permute-start | bytes 691208 | tf_op jit(solution)/shard_map/ppermute | solution.py:219
  40.4 1.1 %collective-permute-start.13 = (f32[3,8,960]{2,1,0:T(8,128)S(1)}, f32[3,8,960]{2,1,0:T(8,128)S(1)}, u32[]{:S(2)}, u32[]{:S(2)}) collective-permute-start(f32[3,8,960]{2,1,0:T(8,128)S(1)} %add.57), channel_id=1, source_target_pairs={{0,2},{1,3},{2,0},{3,1},{4,6},{5,7},{6,4},{7,5},{8,10},{9,11},{10,... | collective-permute-start | bytes 276488 | tf_op jit(solution)/shard_map/ppermute | solution.py:219
  41.5 3.5 %collective-permute-done.13 = f32[3,8,960]{2,1,0:T(8,128)S(1)} collective-permute-done((f32[3,8,960]{2,1,0:T(8,128)S(1)}, f32[3,8,960]{2,1,0:T(8,128)S(1)}, u32[]{:S(2)}, u32[]{:S(2)}) %collective-permute-start.13) | collective-permute-done | bytes 92192 | tf_op jit(solution)/shard_map/ppermute | solution.py:219
  45.0 1.6 %collective-permute-start.14 = (f32[3,8,960]{2,1,0:T(8,128)S(1)}, f32[3,8,960]{2,1,0:T(8,128)S(1)}, u32[]{:S(2)}, u32[]{:S(2)}) collective-permute-start(f32[3,8,960]{2,1,0:T(8,128)S(1)} %add.59), channel_id=1, source_target_pairs={{0,4},{1,5},{2,6},{3,7},{4,0},{5,1},{6,2},{7,3},{8,12},{9,13},{10,... | collective-permute-start | bytes 276488 | tf_op jit(solution)/shard_map/ppermute | solution.py:219
  46.6 3.4 %solve.1.w_ref = bf16[3,320,96]{2,1,0:T(8,128)(2,1)S(1)} custom-call(f32[16,960]{1,0:T(8,128)S(1)} %add.55.mine_ref, f32[16,960]{1,0:T(8,128)S(1)} %collective-permute-done.9.other_ref), custom_call_target="tpu_custom_call" | custom-call | bytes 1048576 | tf_op jit(solution)/shard_map/solve/pallas_call | solution.py:300
  50.1 1.3 %collective-permute-start.18 = (bf16[1,3,40,960]{3,2,1,0:T(8,128)(2,1)S(1)}, bf16[1,3,40,960]{3,2,1,0:T(8,128)(2,1)S(1)}, u32[]{:S(2)}, u32[]{:S(2)}) collective-permute-start(bf16[1,3,40,960]{3,2,1,0:T(8,128)(2,1)S(1)} %add.61), channel_id=1, source_target_pairs={{0,4},{1,5},{2,6},{3,7},{4,0},{5,1},{6,2},{7,3},{8,12},{9,13},{10,... | collective-permute-start | bytes 691208 | tf_op jit(solution)/shard_map/ppermute | solution.py:219
  51.9 1.2 %collective-permute-start.16 = (f32[3,8,960]{2,1,0:T(8,128)S(1)}, f32[3,8,960]{2,1,0:T(8,128)S(1)}, u32[]{:S(2)}, u32[]{:S(2)}) collective-permute-start(f32[3,8,960]{2,1,0:T(8,128)S(1)} %add.60), channel_id=1, source_target_pairs={{0,8},{1,9},{2,10},{3,11},{4,12},{5,13},{6,14},{7,15},{8,0},{9,1},... | collective-permute-start | bytes 276488 | tf_op jit(solution)/shard_map/ppermute | solution.py:219
  53.2 3.4 %collective-permute-done.16 = f32[3,8,960]{2,1,0:T(8,128)S(1)} collective-permute-done((f32[3,8,960]{2,1,0:T(8,128)S(1)}, f32[3,8,960]{2,1,0:T(8,128)S(1)}, u32[]{:S(2)}, u32[]{:S(2)}) %collective-permute-start.16) | collective-permute-done | bytes 92192 | tf_op jit(solution)/shard_map/ppermute | solution.py:219
  57.6 3.2 %collective-permute-start.19 = (f32[3,8,960]{2,1,0:T(8,128)S(1)}, f32[3,8,960]{2,1,0:T(8,128)S(1)}, u32[]{:S(2)}, u32[]{:S(2)}) collective-permute-start(f32[3,8,960]{2,1,0:T(8,128)S(1)} %add.62), channel_id=1, source_target_pairs={{0,16},{1,17},{2,18},{3,19},{4,20},{5,21},{6,22},{7,23},{8,24},{9,... | collective-permute-start | bytes 276488 | tf_op jit(solution)/shard_map/ppermute | solution.py:219
  61.5 2.7 %collective-permute-done.19 = f32[3,8,960]{2,1,0:T(8,128)S(1)} collective-permute-done((f32[3,8,960]{2,1,0:T(8,128)S(1)}, f32[3,8,960]{2,1,0:T(8,128)S(1)}, u32[]{:S(2)}, u32[]{:S(2)}) %collective-permute-start.19) | collective-permute-done | bytes 92192 | tf_op jit(solution)/shard_map/ppermute | solution.py:219
  64.3 2.7 %collective-permute-done.20 = bf16[1,3,40,960]{3,2,1,0:T(8,128)(2,1)S(1)} collective-permute-done((bf16[1,3,40,960]{3,2,1,0:T(8,128)(2,1)S(1)}, bf16[1,3,40,960]{3,2,1,0:T(8,128)(2,1)S(1)}, u32[]{:S(2)}, u32[]{:S(2)}) %collective-permute-start.20) | collective-permute-done | bytes 230432 | tf_op jit(solution)/shard_map/ppermute | solution.py:219
  67.0 1.0 %collective-permute-start.22 = (f32[3,8,960]{2,1,0:T(8,128)S(1)}, f32[3,8,960]{2,1,0:T(8,128)S(1)}, u32[]{:S(2)}, u32[]{:S(2)}) collective-permute-start(f32[3,8,960]{2,1,0:T(8,128)S(1)} %add.63.r0_ref), channel_id=1, source_target_pairs={{0,2},{1,3},{2,0},{3,1},{4,6},{5,7},{6,4},{7,5},{8,10},{9,11},{10,... | collective-permute-start | bytes 276488 | tf_op jit(solution)/shard_map/ppermute | solution.py:219
  68.2 4.0 %collective-permute-done.22.r2_ref = f32[3,8,960]{2,1,0:T(8,128)S(1)} collective-permute-done((f32[3,8,960]{2,1,0:T(8,128)S(1)}, f32[3,8,960]{2,1,0:T(8,128)S(1)}, u32[]{:S(2)}, u32[]{:S(2)}) %collective-permute-start.22) | collective-permute-done | bytes 92192 | tf_op jit(solution)/shard_map/ppermute | solution.py:219
  72.3 2.3 %errors.1 = bf16[3,320,960]{2,1,0:T(8,128)(2,1)} custom-call(f32[3,320,960]{2,1,0:T(8,128)S(1)} %bitcast.9, bf16[3,320,960]{2,1,0:T(8,128)(2,1)S(1)} %bitcast.12, bf16[3,320,96]{2,1,0:T(8,128)(2,1)S(1)} %solve.1.w_ref, f32[3,32,960]{2,1,0:T(8,128)S(1)} %get-tuple-element.55.all_ref), custom_call_target="tpu_custom_call" | custom-call | bytes 12582912 | tf_op jit(solution)/shard_map/errors/pallas_call | solution.py:334
  74.6 4.0 %step.1 = (bf16[3,8,40,960]{3,2,1,0:T(8,128)(2,1)}, bf16[2,8,40,960]{3,2,1,0:T(8,128)(2,1)}) custom-call(s32[3]{0:T(128)S(1)} %copy-done.3, s32[3]{0:T(128)S(1)} %copy-done.4, f32[4]{0:T(128)S(1)} %copy-done.5, f32[4]{0:T(128)S(1)} %copy-done.6, f32[3,8,960]{2,1,0:T(8,128)S(1)} %add.63.r0_ref, f32[3,8,960]{2,1,0:T(8,128)S(1)} %collective-permute-done.21.r1_ref, ...), custom_call_target="tpu_custom_call" | custom-call | tf_op jit(solution)/shard_map/step/pallas_call | solution.py:348
  (56 shorter events, 5.4 us)
Async XLA Ops:
  0.6 8.0 %copy-start.2 = (bf16[2,320,960]{2,1,0:T(8,128)(2,1)S(1)}, bf16[2,320,960]{2,1,0:T(8,128)(2,1)}, u32[]{:S(2)}) copy-start(bf16[2,320,960]{2,1,0:T(8,128)(2,1)} %param.15) | copy-start | bytes 3686404
  0.6 8.0 %copy-start.3 = (s32[3]{0:T(128)S(1)}, s32[3]{0:T(128)}, u32[]{:S(2)}) copy-start(s32[3]{0:T(128)} %owners_ref.3) | copy-start | bytes 40
  0.7 34.6 %copy-start.1 = (bf16[1,3,320,960]{3,2,1,0:T(8,128)(2,1)S(1)}, bf16[1,3,320,960]{3,2,1,0:T(8,128)(2,1)}, u32[]{:S(2)}) copy-start(bf16[1,3,320,960]{3,2,1,0:T(8,128)(2,1)} %param.9) | copy-start | bytes 5529604
  5.8 2.8 %collective-permute-start.2 = (bf16[4,3,40,960]{3,2,1,0:T(8,128)(2,1)S(1)}, bf16[4,3,40,960]{3,2,1,0:T(8,128)(2,1)S(1)}, u32[]{:S(2)}, u32[]{:S(2)}) collective-permute-start(bf16[4,3,40,960]{3,2,1,0:T(8,128)(2,1)S(1)} %get-tuple-element.33), channel_id=1, source_target_pairs={{0,1},{1,0},{2,3},{3,2},{4,5},{5,4},{6,7},{7,6},{8,9},{9,8},{10,11... | collective-permute-start | bytes 2764808 | tf_op jit(solution)/shard_map/ppermute | solution.py:219
  6.3 2.3 %collective-permute-start = (f32[16,960]{1,0:T(8,128)S(1)}, f32[16,960]{1,0:T(8,128)S(1)}, u32[]{:S(2)}, u32[]{:S(2)}) collective-permute-start(f32[16,960]{1,0:T(8,128)S(1)} %get-tuple-element.32), channel_id=1, source_target_pairs={{0,1},{1,0},{2,3},{3,2},{4,5},{5,4},{6,7},{7,6},{8,9},{9,8},{10,11... | collective-permute-start | bytes 184328 | tf_op jit(solution)/shard_map/ppermute | solution.py:219
  8.6 26.6 %copy-start = (f32[1,3,320,960]{3,2,1,0:T(8,128)S(1)}, f32[1,3,320,960]{3,2,1,0:T(8,128)}, u32[]{:S(2)}) copy-start(f32[1,3,320,960]{3,2,1,0:T(8,128)} %param.8) | copy-start | bytes 11059204
  9.3 14.1 %collective-permute-start.4 = (bf16[1,3,40,960]{3,2,1,0:T(8,128)(2,1)S(1)}, bf16[1,3,40,960]{3,2,1,0:T(8,128)(2,1)S(1)}, u32[]{:S(2)}, u32[]{:S(2)}) collective-permute-start(bf16[1,3,40,960]{3,2,1,0:T(8,128)(2,1)S(1)} %get-tuple-element.36), channel_id=1, source_target_pairs={{0,2},{1,3},{2,0},{3,1},{4,6},{5,7},{6,4},{7,5},{8,10},{9,11},{10,... | collective-permute-start | bytes 691208 | tf_op jit(solution)/shard_map/ppermute | solution.py:219
  12.2 13.0 %collective-permute-start.5 = (bf16[1,3,40,960]{3,2,1,0:T(8,128)(2,1)S(1)}, bf16[1,3,40,960]{3,2,1,0:T(8,128)(2,1)S(1)}, u32[]{:S(2)}, u32[]{:S(2)}) collective-permute-start(bf16[1,3,40,960]{3,2,1,0:T(8,128)(2,1)S(1)} %get-tuple-element.37), channel_id=1, source_target_pairs={{0,4},{1,5},{2,6},{3,7},{4,0},{5,1},{6,2},{7,3},{8,12},{9,13},{10,... | collective-permute-start | bytes 691208 | tf_op jit(solution)/shard_map/ppermute | solution.py:219
  13.8 11.4 %collective-permute-start.6 = (bf16[1,3,40,960]{3,2,1,0:T(8,128)(2,1)S(1)}, bf16[1,3,40,960]{3,2,1,0:T(8,128)(2,1)S(1)}, u32[]{:S(2)}, u32[]{:S(2)}) collective-permute-start(bf16[1,3,40,960]{3,2,1,0:T(8,128)(2,1)S(1)} %get-tuple-element.38), channel_id=1, source_target_pairs={{0,6},{1,7},{2,4},{3,5},{4,2},{5,3},{6,0},{7,1},{8,14},{9,15},{10,... | collective-permute-start | bytes 691208 | tf_op jit(solution)/shard_map/ppermute | solution.py:219
  13.8 4.3 %collective-permute-start.1 = (f32[16,960]{1,0:T(8,128)S(1)}, f32[16,960]{1,0:T(8,128)S(1)}, u32[]{:S(2)}, u32[]{:S(2)}) collective-permute-start(f32[16,960]{1,0:T(8,128)S(1)} %add.48), channel_id=1, source_target_pairs={{0,8},{1,9},{2,10},{3,11},{4,12},{5,13},{6,14},{7,15},{8,0},{9,1},... | collective-permute-start | bytes 184328 | tf_op jit(solution)/shard_map/ppermute | solution.py:219
  18.0 5.3 %collective-permute-start.3 = (f32[16,960]{1,0:T(8,128)S(1)}, f32[16,960]{1,0:T(8,128)S(1)}, u32[]{:S(2)}, u32[]{:S(2)}) collective-permute-start(f32[16,960]{1,0:T(8,128)S(1)} %add.49), channel_id=1, source_target_pairs={{0,16},{1,17},{2,18},{3,19},{4,20},{5,21},{6,22},{7,23},{8,24},{9,... | collective-permute-start | bytes 184328 | tf_op jit(solution)/shard_map/ppermute | solution.py:219
  25.2 4.3 %collective-permute-start.7 = (f32[16,960]{1,0:T(8,128)S(1)}, f32[16,960]{1,0:T(8,128)S(1)}, u32[]{:S(2)}, u32[]{:S(2)}) collective-permute-start(f32[16,960]{1,0:T(8,128)S(1)} %add.50), channel_id=1, source_target_pairs={{0,2},{1,3},{2,0},{3,1},{4,6},{5,7},{6,4},{7,5},{8,10},{9,11},{10,... | collective-permute-start | bytes 184328 | tf_op jit(solution)/shard_map/ppermute | solution.py:219
  26.5 13.0 %collective-permute-start.12 = (bf16[1,3,40,960]{3,2,1,0:T(8,128)(2,1)S(1)}, bf16[1,3,40,960]{3,2,1,0:T(8,128)(2,1)S(1)}, u32[]{:S(2)}, u32[]{:S(2)}) collective-permute-start(bf16[1,3,40,960]{3,2,1,0:T(8,128)(2,1)S(1)} %add_add_fusion), channel_id=1, source_target_pairs={{0,16},{1,17},{2,18},{3,19},{4,20},{5,21},{6,22},{7,23},{8,24},{9,... | collective-permute-start | bytes 691208 | tf_op jit(solution)/shard_map/ppermute | solution.py:219
  29.6 4.3 %collective-permute-start.8 = (f32[16,960]{1,0:T(8,128)S(1)}, f32[16,960]{1,0:T(8,128)S(1)}, u32[]{:S(2)}, u32[]{:S(2)}) collective-permute-start(f32[16,960]{1,0:T(8,128)S(1)} %add.54), channel_id=1, source_target_pairs={{0,4},{1,5},{2,6},{3,7},{4,0},{5,1},{6,2},{7,3},{8,12},{9,13},{10,... | collective-permute-start | bytes 184328 | tf_op jit(solution)/shard_map/ppermute | solution.py:219
  33.9 1.3 %collective-permute-start.9 = (f32[16,960]{1,0:T(8,128)S(1)}, f32[16,960]{1,0:T(8,128)S(1)}, u32[]{:S(2)}, u32[]{:S(2)}) collective-permute-start(f32[16,960]{1,0:T(8,128)S(1)} %add.55.mine_ref), channel_id=1, source_target_pairs={{0,1},{1,0},{2,3},{3,2},{4,5},{5,4},{6,7},{7,6},{8,9},{9,8},{10,11... | collective-permute-start | bytes 184328 | tf_op jit(solution)/shard_map/ppermute | solution.py:219
  37.0 1.4 %collective-permute-start.10 = (f32[3,8,960]{2,1,0:T(8,128)S(1)}, f32[3,8,960]{2,1,0:T(8,128)S(1)}, u32[]{:S(2)}, u32[]{:S(2)}) collective-permute-start(f32[3,8,960]{2,1,0:T(8,128)S(1)} %get-tuple-element.43), channel_id=1, source_target_pairs={{0,1},{1,0},{2,3},{3,2},{4,5},{5,4},{6,7},{7,6},{8,9},{9,8},{10,11... | collective-permute-start | bytes 276488 | tf_op jit(solution)/shard_map/ppermute | solution.py:219
  37.2 1.3 %collective-permute-start.11 = (f32[3,8,960]{2,1,0:T(8,128)S(1)}, f32[3,8,960]{2,1,0:T(8,128)S(1)}, u32[]{:S(2)}, u32[]{:S(2)}) collective-permute-start(f32[3,8,960]{2,1,0:T(8,128)S(1)} %get-tuple-element.45), channel_id=1, source_target_pairs={{0,1},{1,0},{2,3},{3,2},{4,5},{5,4},{6,7},{7,6},{8,9},{9,8},{10,11... | collective-permute-start | bytes 276488 | tf_op jit(solution)/shard_map/ppermute | solution.py:219
  39.6 10.4 %collective-permute-start.15 = (bf16[1,3,40,960]{3,2,1,0:T(8,128)(2,1)S(1)}, bf16[1,3,40,960]{3,2,1,0:T(8,128)(2,1)S(1)}, u32[]{:S(2)}, u32[]{:S(2)}) collective-permute-start(bf16[1,3,40,960]{3,2,1,0:T(8,128)(2,1)S(1)} %add.58), channel_id=1, source_target_pairs={{0,8},{1,9},{2,10},{3,11},{4,12},{5,13},{6,14},{7,15},{8,0},{9,1},... | collective-permute-start | bytes 691208 | tf_op jit(solution)/shard_map/ppermute | solution.py:219
  40.4 4.6 %collective-permute-start.13 = (f32[3,8,960]{2,1,0:T(8,128)S(1)}, f32[3,8,960]{2,1,0:T(8,128)S(1)}, u32[]{:S(2)}, u32[]{:S(2)}) collective-permute-start(f32[3,8,960]{2,1,0:T(8,128)S(1)} %add.57), channel_id=1, source_target_pairs={{0,2},{1,3},{2,0},{3,1},{4,6},{5,7},{6,4},{7,5},{8,10},{9,11},{10,... | collective-permute-start | bytes 276488 | tf_op jit(solution)/shard_map/ppermute | solution.py:219
  45.0 5.0 %collective-permute-start.14 = (f32[3,8,960]{2,1,0:T(8,128)S(1)}, f32[3,8,960]{2,1,0:T(8,128)S(1)}, u32[]{:S(2)}, u32[]{:S(2)}) collective-permute-start(f32[3,8,960]{2,1,0:T(8,128)S(1)} %add.59), channel_id=1, source_target_pairs={{0,4},{1,5},{2,6},{3,7},{4,0},{5,1},{6,2},{7,3},{8,12},{9,13},{10,... | collective-permute-start | bytes 276488 | tf_op jit(solution)/shard_map/ppermute | solution.py:219
  50.1 6.9 %collective-permute-start.18 = (bf16[1,3,40,960]{3,2,1,0:T(8,128)(2,1)S(1)}, bf16[1,3,40,960]{3,2,1,0:T(8,128)(2,1)S(1)}, u32[]{:S(2)}, u32[]{:S(2)}) collective-permute-start(bf16[1,3,40,960]{3,2,1,0:T(8,128)(2,1)S(1)} %add.61), channel_id=1, source_target_pairs={{0,4},{1,5},{2,6},{3,7},{4,0},{5,1},{6,2},{7,3},{8,12},{9,13},{10,... | collective-permute-start | bytes 691208 | tf_op jit(solution)/shard_map/ppermute | solution.py:219
  51.4 6.2 %collective-permute-start.17 = (bf16[1,3,40,960]{3,2,1,0:T(8,128)(2,1)S(1)}, bf16[1,3,40,960]{3,2,1,0:T(8,128)(2,1)S(1)}, u32[]{:S(2)}, u32[]{:S(2)}) collective-permute-start(bf16[1,3,40,960]{3,2,1,0:T(8,128)(2,1)S(1)} %add.61), channel_id=1, source_target_pairs={{0,2},{1,3},{2,0},{3,1},{4,6},{5,7},{6,4},{7,5},{8,10},{9,11},{10,... | collective-permute-start | bytes 691208 | tf_op jit(solution)/shard_map/ppermute | solution.py:219
  51.9 4.6 %collective-permute-start.16 = (f32[3,8,960]{2,1,0:T(8,128)S(1)}, f32[3,8,960]{2,1,0:T(8,128)S(1)}, u32[]{:S(2)}, u32[]{:S(2)}) collective-permute-start(f32[3,8,960]{2,1,0:T(8,128)S(1)} %add.60), channel_id=1, source_target_pairs={{0,8},{1,9},{2,10},{3,11},{4,12},{5,13},{6,14},{7,15},{8,0},{9,1},... | collective-permute-start | bytes 276488 | tf_op jit(solution)/shard_map/ppermute | solution.py:219
  57.6 6.6 %collective-permute-start.19 = (f32[3,8,960]{2,1,0:T(8,128)S(1)}, f32[3,8,960]{2,1,0:T(8,128)S(1)}, u32[]{:S(2)}, u32[]{:S(2)}) collective-permute-start(f32[3,8,960]{2,1,0:T(8,128)S(1)} %add.62), channel_id=1, source_target_pairs={{0,16},{1,17},{2,18},{3,19},{4,20},{5,21},{6,22},{7,23},{8,24},{9,... | collective-permute-start | bytes 276488 | tf_op jit(solution)/shard_map/ppermute | solution.py:219
  60.7 6.2 %collective-permute-start.20 = (bf16[1,3,40,960]{3,2,1,0:T(8,128)(2,1)S(1)}, bf16[1,3,40,960]{3,2,1,0:T(8,128)(2,1)S(1)}, u32[]{:S(2)}, u32[]{:S(2)}) collective-permute-start(bf16[1,3,40,960]{3,2,1,0:T(8,128)(2,1)S(1)} %collective-permute-done.17), channel_id=1, source_target_pairs={{0,4},{1,5},{2,6},{3,7},{4,0},{5,1},{6,2},{7,3},{8,12},{9,13},{10,... | collective-permute-start | bytes 691208 | tf_op jit(solution)/shard_map/ppermute | solution.py:219
  67.0 7.7 %collective-permute-start.24 = (bf16[4,3,40,960]{3,2,1,0:T(8,128)(2,1)S(1)}, bf16[4,3,40,960]{3,2,1,0:T(8,128)(2,1)S(1)}, u32[]{:S(2)}, u32[]{:S(2)}) collective-permute-start(bf16[4,3,40,960]{3,2,1,0:T(8,128)(2,1)S(1)} %constant_dynamic-update-slice_fusion.even_ref), channel_id=1, source_target_pairs={{0,1},{1,0},{2,3},{3,2},{4,5},{5,4},{6,7},{7,6},{8,9},{9,8},{10,11... | collective-permute-start | bytes 2764808 | tf_op jit(solution)/shard_map/ppermute | solution.py:219
  67.0 5.2 %collective-permute-start.22 = (f32[3,8,960]{2,1,0:T(8,128)S(1)}, f32[3,8,960]{2,1,0:T(8,128)S(1)}, u32[]{:S(2)}, u32[]{:S(2)}) collective-permute-start(f32[3,8,960]{2,1,0:T(8,128)S(1)} %add.63.r0_ref), channel_id=1, source_target_pairs={{0,2},{1,3},{2,0},{3,1},{4,6},{5,7},{6,4},{7,5},{8,10},{9,11},{10,... | collective-permute-start | bytes 276488 | tf_op jit(solution)/shard_map/ppermute | solution.py:219
  68.1 6.5 %collective-permute-start.21 = (f32[3,8,960]{2,1,0:T(8,128)S(1)}, f32[3,8,960]{2,1,0:T(8,128)S(1)}, u32[]{:S(2)}, u32[]{:S(2)}) collective-permute-start(f32[3,8,960]{2,1,0:T(8,128)S(1)} %add.63.r0_ref), channel_id=1, source_target_pairs={{0,1},{1,0},{2,3},{3,2},{4,5},{5,4},{6,7},{7,6},{8,9},{9,8},{10,11... | collective-permute-start | bytes 276488 | tf_op jit(solution)/shard_map/ppermute | solution.py:219
  72.3 2.4 %collective-permute-start.23 = (f32[3,8,960]{2,1,0:T(8,128)S(1)}, f32[3,8,960]{2,1,0:T(8,128)S(1)}, u32[]{:S(2)}, u32[]{:S(2)}) collective-permute-start(f32[3,8,960]{2,1,0:T(8,128)S(1)} %collective-permute-done.22.r2_ref), channel_id=1, source_target_pairs={{0,1},{1,0},{2,3},{3,2},{4,5},{5,4},{6,7},{7,6},{8,9},{9,8},{10,11... | collective-permute-start | bytes 276488 | tf_op jit(solution)/shard_map/ppermute | solution.py:219
  72.3 2.4 %copy-start.4 = (s32[3]{0:T(128)S(1)}, s32[3]{0:T(128)}, u32[]{:S(2)}) copy-start(s32[3]{0:T(128)} %buckets_ref.1) | copy-start | bytes 40
  72.3 2.4 %copy-start.5 = (f32[4]{0:T(128)S(1)}, f32[4]{0:T(128)}, u32[]{:S(2)}) copy-start(f32[4]{0:T(128)} %rates_ref.1) | copy-start | bytes 52
  72.3 2.4 %copy-start.6 = (f32[4]{0:T(128)S(1)}, f32[4]{0:T(128)}, u32[]{:S(2)}) copy-start(f32[4]{0:T(128)} %betas_ref.1) | copy-start | bytes 52

commit v9 on v8

--- a/solution.py
+++ b/solution.py
@@ -184,7 +184,7 @@
 
 def step_kernel(
     owners_ref, buckets_ref, rates_ref, betas_ref,
-    r0_ref, r1_ref, r2_ref, r3_ref, w_ref, even_ref, odd_ref,
+    r0_ref, r1_ref, r2_ref, r3_ref, w_ref, even_ref, odd_ref, far_ref, odd_far_ref,
     step_ref, mom_ref, right_ref, update_ref,
 ):
     i = pl.program_id(0)
@@ -204,10 +204,10 @@
     own = owners_ref[i] == me
     slot = slot_of(owners_ref, i)
     for position in range(8):
-        ref = (even_ref, odd_ref)[position % 2]
+        near, far = ((even_ref, far_ref), (odd_ref, odd_far_ref))[position % 2]
         piece = position ^ (me & 7)
         update = update_ref[piece]
-        old = ref[position // 2, 0].astype(F32)
+        old = (near[position // 2, 0] if position < 6 else far[0, 0]).astype(F32)
         step_ref[0, piece] = (of_update * update + of_old * old).astype(BF16)
 
         @pl.when(own)
@@ -327,10 +327,6 @@
             near = [after(value, r0) for value in near]
             r0 = after(r0, *near)
     far = swap(near[0], 4)
-    evens = jnp.concatenate([after(old, r0)] + near + [far])
-    odds = swap(evens, 1)
-    r1, r2 = swap(r0, 1), swap(r0, 2)
-    r3 = swap(r2, 1)
     new_errors = pl.pallas_call(
         error_kernel,
         grid=(mats,),
@@ -340,21 +336,27 @@
         compiler_params=params(),
         cost_estimate=cost(12),
         name="errors",
-    )(grads, errs, after(w, evens), right_all)
-    w = after(w, new_errors)
+    )(grads, errs, after(w, *near), right_all)
+    r0 = after(r0, new_errors)
+    r1, r2 = swap(r0, 1), swap(r0, 2)
+    evens = jnp.concatenate([old] + near)
+    odds = swap(evens, 1)
+    r3 = swap(r2, 1)
+    far = after(far, r0)
+    odd_far = swap(far, 1)
 
     quarter_spec = per_matrix((quarter, cols))
-    old_spec = pl.BlockSpec((4, 1, piece, cols), lambda i: (0, i, 0, 0))
+    old_specs = [pl.BlockSpec((n, 1, piece, cols), lambda i: (0, i, 0, 0)) for n in (3, 3, 1, 1)]
     steps, new_mom = pl.pallas_call(
         step_kernel,
         grid=(mats,),
-        in_specs=[SMEM] * 4 + [quarter_spec] * 4 + [per_matrix((rows, 3 * rank))] + [old_spec] * 2,
+        in_specs=[SMEM] * 4 + [quarter_spec] * 4 + [per_matrix((rows, 3 * rank))] + old_specs,
         out_specs=[per_matrix((8, piece, cols)), whole((slots, 8, piece, cols))],
         out_shape=[sds((mats, 8, piece, cols), BF16), sds((slots, 8, piece, cols), BF16)],
         scratch_shapes=[pltpu.VMEM((4, quarter, cols), F32), pltpu.VMEM((8, piece, cols), F32)],
         compiler_params=params(),
         name="step",
-    )(owners, buckets, learn_rates, beta_values, r0, r1, r2, r3, w, evens, odds)
+    )(owners, buckets, learn_rates, beta_values, r0, r1, r2, r3, w, evens, odds, far, odd_far)
     return (new_errors[None], steps.reshape(1, mats, rows, cols), new_mom.reshape(slots, rows, cols))
 
 

time: 78.8 us -> 77.7 us (0.986)
  waiting for transfers between devices: 32.2 us -> 31.2 us
    ppermute x25 -> x26, waiting for transfers between devices: 32.2 us -> 31.2 us  [exchange(): return lax.ppermute(value, AXES, [(d, d ^ mask) for d in range(count)])]
    ppermute x25 -> x26, starting transfers between devices: 28 us -> 27.9 us  [exchange(): return lax.ppermute(value, AXES, [(d, d ^ mask) for d in range(count)])]
  transfers between devices with their start and end apart: 25 -> 26, of which waited for: 17 -> 17; matrix products, arithmetic and copies ran while one was open for 0% -> 0% of each run, Pallas kernels for 9% -> 10%
where the time goes in v9:
time: 77.7 us; the launch traced here: 77.6 us
  waiting for transfers between devices  31.2 us (40%)
  starting transfers between devices  27.9 us (36%)
  Pallas kernels  17.1 us (22%)
  between operations  0.87 us (1%)
    ppermute x26, waiting for transfers between devices, exchange(): return lax.ppermute(value, AXES, [(d, d ^ mask) for d in range(count)])  31.2 us
    ppermute x26, starting transfers between devices, exchange(): return lax.ppermute(value, AXES, [(d, d ^ mask) for d in range(count)])  27.9 us
    pallas_call x1, Pallas kernels, on_device(): pl.pallas_call(first_kernel, in_specs=[pl.BlockSpec(memory_space=pltpu.HB...  5.11 us
    pallas_call x1, Pallas kernels, on_device(): pl.pallas_call(step_kernel, grid=(mats,), in_specs=[SMEM] * 4 + [quarter_...  3.98 us
    pallas_call x1, Pallas kernels, on_device(): pl.pallas_call(solve_kernel, grid=(1,), in_specs=[whole((half, mats * row...  3.38 us
    pallas_call x1, Pallas kernels, on_device(): pl.pallas_call(error_kernel, grid=(mats,), in_specs=[grad_spec, grad_spec...  2.31 us
    pallas_call x1, Pallas kernels, on_device(): pl.pallas_call(right_kernel, grid=(mats,), in_specs=[whole((half, mats *...  1.71 us
  transfers between devices with their start and end apart: 26, of which 17 were waited for; matrix products, arithmetic and copies ran while one was open for 0% of the time, Pallas kernels for 10%

profile of v9, /device:TPU:0, one launch (start us, length us, event | category | flops | bytes accessed | tf_op | source)
XLA Modules:
  0.0 77.6 jit_solution(2285696641805143565)
XLA Ops:
  0.7 5.1 %first.1 = (f32[16,960]{1,0:T(8,128)S(1)}, f32[16,960]{1,0:T(8,128)S(1)}, bf16[4,3,40,960]{3,2,1,0:T(8,128)(2,1)S(1)}) custom-call(s32[3]{0:T(128)} %owners_ref.3, f32[3,320,960]{2,1,0:T(8,128)} %bitcast.7, bf16[3,320,960]{2,1,0:T(8,128)(2,1)} %bitcast.10, f32[3,32,960]{2,1,0:T(8,128)} %bitcast.16, bf16[2,8,40,960]{3,2,1,0:T(8,128)(2,1)} %bitcast.13), custom_call_target="tpu_custom_call" | custom-call | tf_op jit(solution)/shard_map/first/pallas_call | solution.py:248
  6.4 2.2 %collective-permute-done = f32[16,960]{1,0:T(8,128)S(1)} collective-permute-done((f32[16,960]{1,0:T(8,128)S(1)}, f32[16,960]{1,0:T(8,128)S(1)}, u32[]{:S(2)}, u32[]{:S(2)}) %collective-permute-start) | collective-permute-done | bytes 61472 | tf_op jit(solution)/shard_map/ppermute | solution.py:219
  9.3 2.9 %collective-permute-start.4 = (bf16[1,3,40,960]{3,2,1,0:T(8,128)(2,1)S(1)}, bf16[1,3,40,960]{3,2,1,0:T(8,128)(2,1)S(1)}, u32[]{:S(2)}, u32[]{:S(2)}) collective-permute-start(bf16[1,3,40,960]{3,2,1,0:T(8,128)(2,1)S(1)} %get-tuple-element.36), channel_id=1, source_target_pairs={{0,2},{1,3},{2,0},{3,1},{4,6},{5,7},{6,4},{7,5},{8,10},{9,11},{10,... | collective-permute-start | bytes 691208 | tf_op jit(solution)/shard_map/ppermute | solution.py:219
  12.2 1.5 %collective-permute-start.5 = (bf16[1,3,40,960]{3,2,1,0:T(8,128)(2,1)S(1)}, bf16[1,3,40,960]{3,2,1,0:T(8,128)(2,1)S(1)}, u32[]{:S(2)}, u32[]{:S(2)}) collective-permute-start(bf16[1,3,40,960]{3,2,1,0:T(8,128)(2,1)S(1)} %get-tuple-element.37), channel_id=1, source_target_pairs={{0,4},{1,5},{2,6},{3,7},{4,0},{5,1},{6,2},{7,3},{8,12},{9,13},{10,... | collective-permute-start | bytes 691208 | tf_op jit(solution)/shard_map/ppermute | solution.py:219
  13.7 2.0 %collective-permute-start.1 = (f32[16,960]{1,0:T(8,128)S(1)}, f32[16,960]{1,0:T(8,128)S(1)}, u32[]{:S(2)}, u32[]{:S(2)}) collective-permute-start(f32[16,960]{1,0:T(8,128)S(1)} %add.48), channel_id=1, source_target_pairs={{0,8},{1,9},{2,10},{3,11},{4,12},{5,13},{6,14},{7,15},{8,0},{9,1},... | collective-permute-start | bytes 184328 | tf_op jit(solution)/shard_map/ppermute | solution.py:219
  15.8 2.2 %collective-permute-done.1 = f32[16,960]{1,0:T(8,128)S(1)} collective-permute-done((f32[16,960]{1,0:T(8,128)S(1)}, f32[16,960]{1,0:T(8,128)S(1)}, u32[]{:S(2)}, u32[]{:S(2)}) %collective-permute-start.1) | collective-permute-done | bytes 61472 | tf_op jit(solution)/shard_map/ppermute | solution.py:219
  18.0 3.1 %collective-permute-start.3 = (f32[16,960]{1,0:T(8,128)S(1)}, f32[16,960]{1,0:T(8,128)S(1)}, u32[]{:S(2)}, u32[]{:S(2)}) collective-permute-start(f32[16,960]{1,0:T(8,128)S(1)} %add.49), channel_id=1, source_target_pairs={{0,16},{1,17},{2,18},{3,19},{4,20},{5,21},{6,22},{7,23},{8,24},{9,... | collective-permute-start | bytes 184328 | tf_op jit(solution)/shard_map/ppermute | solution.py:219
  21.1 2.2 %collective-permute-done.3 = f32[16,960]{1,0:T(8,128)S(1)} collective-permute-done((f32[16,960]{1,0:T(8,128)S(1)}, f32[16,960]{1,0:T(8,128)S(1)}, u32[]{:S(2)}, u32[]{:S(2)}) %collective-permute-start.3) | collective-permute-done | bytes 61472 | tf_op jit(solution)/shard_map/ppermute | solution.py:219
  23.4 1.8 %collective-permute-done.5 = bf16[1,3,40,960]{3,2,1,0:T(8,128)(2,1)S(1)} collective-permute-done((bf16[1,3,40,960]{3,2,1,0:T(8,128)(2,1)S(1)}, bf16[1,3,40,960]{3,2,1,0:T(8,128)(2,1)S(1)}, u32[]{:S(2)}, u32[]{:S(2)}) %collective-permute-start.5) | collective-permute-done | bytes 230432 | tf_op jit(solution)/shard_map/ppermute | solution.py:219
  25.2 1.3 %collective-permute-start.7 = (f32[16,960]{1,0:T(8,128)S(1)}, f32[16,960]{1,0:T(8,128)S(1)}, u32[]{:S(2)}, u32[]{:S(2)}) collective-permute-start(f32[16,960]{1,0:T(8,128)S(1)} %add.50), channel_id=1, source_target_pairs={{0,2},{1,3},{2,0},{3,1},{4,6},{5,7},{6,4},{7,5},{8,10},{9,11},{10,... | collective-permute-start | bytes 184328 | tf_op jit(solution)/shard_map/ppermute | solution.py:219
  26.5 2.6 %collective-permute-start.12 = (bf16[1,3,40,960]{3,2,1,0:T(8,128)(2,1)S(1)}, bf16[1,3,40,960]{3,2,1,0:T(8,128)(2,1)S(1)}, u32[]{:S(2)}, u32[]{:S(2)}) collective-permute-start(bf16[1,3,40,960]{3,2,1,0:T(8,128)(2,1)S(1)} %add_add_fusion), channel_id=1, source_target_pairs={{0,16},{1,17},{2,18},{3,19},{4,20},{5,21},{6,22},{7,23},{8,24},{9,... | collective-permute-start | bytes 691208 | tf_op jit(solution)/shard_map/ppermute | solution.py:219
  29.6 1.6 %collective-permute-start.8 = (f32[16,960]{1,0:T(8,128)S(1)}, f32[16,960]{1,0:T(8,128)S(1)}, u32[]{:S(2)}, u32[]{:S(2)}) collective-permute-start(f32[16,960]{1,0:T(8,128)S(1)} %add.54), channel_id=1, source_target_pairs={{0,4},{1,5},{2,6},{3,7},{4,0},{5,1},{6,2},{7,3},{8,12},{9,13},{10,... | collective-permute-start | bytes 184328 | tf_op jit(solution)/shard_map/ppermute | solution.py:219
  31.2 2.7 %collective-permute-done.8 = f32[16,960]{1,0:T(8,128)S(1)} collective-permute-done((f32[16,960]{1,0:T(8,128)S(1)}, f32[16,960]{1,0:T(8,128)S(1)}, u32[]{:S(2)}, u32[]{:S(2)}) %collective-permute-start.8) | collective-permute-done | bytes 61472 | tf_op jit(solution)/shard_map/ppermute | solution.py:219
  34.0 1.2 %collective-permute-done.9.other_ref = f32[16,960]{1,0:T(8,128)S(1)} collective-permute-done((f32[16,960]{1,0:T(8,128)S(1)}, f32[16,960]{1,0:T(8,128)S(1)}, u32[]{:S(2)}, u32[]{:S(2)}) %collective-permute-start.9) | collective-permute-done | bytes 61472 | tf_op jit(solution)/shard_map/ppermute | solution.py:219
  35.3 1.7 %right.1 = (f32[3,32,960]{2,1,0:T(8,128)S(1)}, f32[3,8,960]{2,1,0:T(8,128)S(1)}, f32[3,8,960]{2,1,0:T(8,128)S(1)}, f32[3,8,960]{2,1,0:T(8,128)S(1)}, f32[3,8,960]{2,1,0:T(8,128)S(1)}) custom-call(f32[16,960]{1,0:T(8,128)S(1)} %add.55.mine_ref, f32[16,960]{1,0:T(8,128)S(1)} %collective-permute-done.9.other_ref, f32[3,320,960]{2,1,0:T(8,128)S(1)} %bitcast.8, ...), custom_call_target="tpu_custom_call" | custom-call | tf_op jit(solution)/shard_map/right/pallas_call | solution.py:289
  37.6 0.8 %collective-permute-done.10 = f32[3,8,960]{2,1,0:T(8,128)S(1)} collective-permute-done((f32[3,8,960]{2,1,0:T(8,128)S(1)}, f32[3,8,960]{2,1,0:T(8,128)S(1)}, u32[]{:S(2)}, u32[]{:S(2)}) %collective-permute-start.10) | collective-permute-done | bytes 92192 | tf_op jit(solution)/shard_map/ppermute | solution.py:219
  38.5 1.1 %collective-permute-done.12 = bf16[1,3,40,960]{3,2,1,0:T(8,128)(2,1)S(1)} collective-permute-done((bf16[1,3,40,960]{3,2,1,0:T(8,128)(2,1)S(1)}, bf16[1,3,40,960]{3,2,1,0:T(8,128)(2,1)S(1)}, u32[]{:S(2)}, u32[]{:S(2)}) %collective-permute-start.12) | collective-permute-done | bytes 230432 | tf_op jit(solution)/shard_map/ppermute | solution.py:219
  40.4 1.1 %collective-permute-start.13 = (f32[3,8,960]{2,1,0:T(8,128)S(1)}, f32[3,8,960]{2,1,0:T(8,128)S(1)}, u32[]{:S(2)}, u32[]{:S(2)}) collective-permute-start(f32[3,8,960]{2,1,0:T(8,128)S(1)} %add.57), channel_id=1, source_target_pairs={{0,2},{1,3},{2,0},{3,1},{4,6},{5,7},{6,4},{7,5},{8,10},{9,11},{10,... | collective-permute-start | bytes 276488 | tf_op jit(solution)/shard_map/ppermute | solution.py:219
  41.5 3.5 %collective-permute-done.13 = f32[3,8,960]{2,1,0:T(8,128)S(1)} collective-permute-done((f32[3,8,960]{2,1,0:T(8,128)S(1)}, f32[3,8,960]{2,1,0:T(8,128)S(1)}, u32[]{:S(2)}, u32[]{:S(2)}) %collective-permute-start.13) | collective-permute-done | bytes 92192 | tf_op jit(solution)/shard_map/ppermute | solution.py:219
  45.0 1.6 %collective-permute-start.14 = (f32[3,8,960]{2,1,0:T(8,128)S(1)}, f32[3,8,960]{2,1,0:T(8,128)S(1)}, u32[]{:S(2)}, u32[]{:S(2)}) collective-permute-start(f32[3,8,960]{2,1,0:T(8,128)S(1)} %add.59), channel_id=1, source_target_pairs={{0,4},{1,5},{2,6},{3,7},{4,0},{5,1},{6,2},{7,3},{8,12},{9,13},{10,... | collective-permute-start | bytes 276488 | tf_op jit(solution)/shard_map/ppermute | solution.py:219
  46.6 3.4 %solve.1.w_ref = bf16[3,320,96]{2,1,0:T(8,128)(2,1)S(1)} custom-call(f32[16,960]{1,0:T(8,128)S(1)} %add.55.mine_ref, f32[16,960]{1,0:T(8,128)S(1)} %collective-permute-done.9.other_ref), custom_call_target="tpu_custom_call" | custom-call | bytes 1048576 | tf_op jit(solution)/shard_map/solve/pallas_call | solution.py:300
  50.1 1.3 %collective-permute-start.18 = (bf16[1,3,40,960]{3,2,1,0:T(8,128)(2,1)S(1)}, bf16[1,3,40,960]{3,2,1,0:T(8,128)(2,1)S(1)}, u32[]{:S(2)}, u32[]{:S(2)}) collective-permute-start(bf16[1,3,40,960]{3,2,1,0:T(8,128)(2,1)S(1)} %add.61), channel_id=1, source_target_pairs={{0,4},{1,5},{2,6},{3,7},{4,0},{5,1},{6,2},{7,3},{8,12},{9,13},{10,... | collective-permute-start | bytes 691208 | tf_op jit(solution)/shard_map/ppermute | solution.py:219
  51.9 1.3 %collective-permute-start.17 = (f32[3,8,960]{2,1,0:T(8,128)S(1)}, f32[3,8,960]{2,1,0:T(8,128)S(1)}, u32[]{:S(2)}, u32[]{:S(2)}) collective-permute-start(f32[3,8,960]{2,1,0:T(8,128)S(1)} %add.60), channel_id=1, source_target_pairs={{0,8},{1,9},{2,10},{3,11},{4,12},{5,13},{6,14},{7,15},{8,0},{9,1},... | collective-permute-start | bytes 276488 | tf_op jit(solution)/shard_map/ppermute | solution.py:219
  53.2 3.3 %collective-permute-done.17 = f32[3,8,960]{2,1,0:T(8,128)S(1)} collective-permute-done((f32[3,8,960]{2,1,0:T(8,128)S(1)}, f32[3,8,960]{2,1,0:T(8,128)S(1)}, u32[]{:S(2)}, u32[]{:S(2)}) %collective-permute-start.17) | collective-permute-done | bytes 92192 | tf_op jit(solution)/shard_map/ppermute | solution.py:219
  57.8 1.2 %collective-permute-start.24 = (bf16[1,3,40,960]{3,2,1,0:T(8,128)(2,1)S(1)}, bf16[1,3,40,960]{3,2,1,0:T(8,128)(2,1)S(1)}, u32[]{:S(2)}, u32[]{:S(2)}) collective-permute-start(bf16[1,3,40,960]{3,2,1,0:T(8,128)(2,1)S(1)} %collective-permute-done.16), channel_id=1, source_target_pairs={{0,4},{1,5},{2,6},{3,7},{4,0},{5,1},{6,2},{7,3},{8,12},{9,13},{10,... | collective-permute-start | bytes 691208 | tf_op jit(solution)/shard_map/ppermute | solution.py:219
  59.0 2.7 %collective-permute-start.19 = (f32[3,8,960]{2,1,0:T(8,128)S(1)}, f32[3,8,960]{2,1,0:T(8,128)S(1)}, u32[]{:S(2)}, u32[]{:S(2)}) collective-permute-start(f32[3,8,960]{2,1,0:T(8,128)S(1)} %add.62), channel_id=1, source_target_pairs={{0,16},{1,17},{2,18},{3,19},{4,20},{5,21},{6,22},{7,23},{8,24},{9,... | collective-permute-start | bytes 276488 | tf_op jit(solution)/shard_map/ppermute | solution.py:219
  61.7 2.3 %errors.1 = bf16[3,320,960]{2,1,0:T(8,128)(2,1)} custom-call(f32[3,320,960]{2,1,0:T(8,128)S(1)} %bitcast.9, bf16[3,320,960]{2,1,0:T(8,128)(2,1)S(1)} %bitcast.12, bf16[3,320,96]{2,1,0:T(8,128)(2,1)S(1)} %solve.1.w_ref, f32[3,32,960]{2,1,0:T(8,128)S(1)} %get-tuple-element.53.all_ref), custom_call_target="tpu_custom_call" | custom-call | bytes 12582912 | tf_op jit(solution)/shard_map/errors/pallas_call | solution.py:330
  64.0 2.9 %collective-permute-done.19 = f32[3,8,960]{2,1,0:T(8,128)S(1)} collective-permute-done((f32[3,8,960]{2,1,0:T(8,128)S(1)}, f32[3,8,960]{2,1,0:T(8,128)S(1)}, u32[]{:S(2)}, u32[]{:S(2)}) %collective-permute-start.19) | collective-permute-done | bytes 92192 | tf_op jit(solution)/shard_map/ppermute | solution.py:219
  67.1 0.8 %collective-permute-start.21 = (f32[3,8,960]{2,1,0:T(8,128)S(1)}, f32[3,8,960]{2,1,0:T(8,128)S(1)}, u32[]{:S(2)}, u32[]{:S(2)}) collective-permute-start(f32[3,8,960]{2,1,0:T(8,128)S(1)} %add.63.r0_ref), channel_id=1, source_target_pairs={{0,2},{1,3},{2,0},{3,1},{4,6},{5,7},{6,4},{7,5},{8,10},{9,11},{10,... | collective-permute-start | bytes 276488 | tf_op jit(solution)/shard_map/ppermute | solution.py:219
  68.1 4.2 %collective-permute-done.21.r2_ref = f32[3,8,960]{2,1,0:T(8,128)S(1)} collective-permute-done((f32[3,8,960]{2,1,0:T(8,128)S(1)}, f32[3,8,960]{2,1,0:T(8,128)S(1)}, u32[]{:S(2)}, u32[]{:S(2)}) %collective-permute-start.21) | collective-permute-done | bytes 92192 | tf_op jit(solution)/shard_map/ppermute | solution.py:219
  72.3 1.3 %collective-permute-done.22.r3_ref = f32[3,8,960]{2,1,0:T(8,128)S(1)} collective-permute-done((f32[3,8,960]{2,1,0:T(8,128)S(1)}, f32[3,8,960]{2,1,0:T(8,128)S(1)}, u32[]{:S(2)}, u32[]{:S(2)}) %collective-permute-start.22) | collective-permute-done | bytes 92192 | tf_op jit(solution)/shard_map/ppermute | solution.py:219
  73.6 4.0 %step.1 = (bf16[3,8,40,960]{3,2,1,0:T(8,128)(2,1)}, bf16[2,8,40,960]{3,2,1,0:T(8,128)(2,1)}) custom-call(s32[3]{0:T(128)S(1)} %copy-done.3, s32[3]{0:T(128)S(1)} %copy-done.4, f32[4]{0:T(128)S(1)} %copy-done.5, f32[4]{0:T(128)S(1)} %copy-done.6, f32[3,8,960]{2,1,0:T(8,128)S(1)} %add.63.r0_ref, f32[3,8,960]{2,1,0:T(8,128)S(1)} %collective-permute-done.20.r1_ref, ...), custom_call_target="tpu_custom_call" | custom-call | tf_op jit(solution)/shard_map/step/pallas_call | solution.py:350
  (55 shorter events, 5.5 us)
Async XLA Ops:
  0.6 8.0 %copy-start.2 = (bf16[2,320,960]{2,1,0:T(8,128)(2,1)S(1)}, bf16[2,320,960]{2,1,0:T(8,128)(2,1)}, u32[]{:S(2)}) copy-start(bf16[2,320,960]{2,1,0:T(8,128)(2,1)} %param.15) | copy-start | bytes 3686404
  0.7 34.6 %copy-start.1 = (bf16[1,3,320,960]{3,2,1,0:T(8,128)(2,1)S(1)}, bf16[1,3,320,960]{3,2,1,0:T(8,128)(2,1)}, u32[]{:S(2)}) copy-start(bf16[1,3,320,960]{3,2,1,0:T(8,128)(2,1)} %param.9) | copy-start | bytes 5529604
  5.8 2.8 %collective-permute-start.2 = (bf16[4,3,40,960]{3,2,1,0:T(8,128)(2,1)S(1)}, bf16[4,3,40,960]{3,2,1,0:T(8,128)(2,1)S(1)}, u32[]{:S(2)}, u32[]{:S(2)}) collective-permute-start(bf16[4,3,40,960]{3,2,1,0:T(8,128)(2,1)S(1)} %get-tuple-element.33), channel_id=1, source_target_pairs={{0,1},{1,0},{2,3},{3,2},{4,5},{5,4},{6,7},{7,6},{8,9},{9,8},{10,11... | collective-permute-start | bytes 2764808 | tf_op jit(solution)/shard_map/ppermute | solution.py:219
  6.3 2.3 %collective-permute-start = (f32[16,960]{1,0:T(8,128)S(1)}, f32[16,960]{1,0:T(8,128)S(1)}, u32[]{:S(2)}, u32[]{:S(2)}) collective-permute-start(f32[16,960]{1,0:T(8,128)S(1)} %get-tuple-element.32), channel_id=1, source_target_pairs={{0,1},{1,0},{2,3},{3,2},{4,5},{5,4},{6,7},{7,6},{8,9},{9,8},{10,11... | collective-permute-start | bytes 184328 | tf_op jit(solution)/shard_map/ppermute | solution.py:219
  8.6 26.7 %copy-start = (f32[1,3,320,960]{3,2,1,0:T(8,128)S(1)}, f32[1,3,320,960]{3,2,1,0:T(8,128)}, u32[]{:S(2)}) copy-start(f32[1,3,320,960]{3,2,1,0:T(8,128)} %param.8) | copy-start | bytes 11059204
  9.3 14.1 %collective-permute-start.4 = (bf16[1,3,40,960]{3,2,1,0:T(8,128)(2,1)S(1)}, bf16[1,3,40,960]{3,2,1,0:T(8,128)(2,1)S(1)}, u32[]{:S(2)}, u32[]{:S(2)}) collective-permute-start(bf16[1,3,40,960]{3,2,1,0:T(8,128)(2,1)S(1)} %get-tuple-element.36), channel_id=1, source_target_pairs={{0,2},{1,3},{2,0},{3,1},{4,6},{5,7},{6,4},{7,5},{8,10},{9,11},{10,... | collective-permute-start | bytes 691208 | tf_op jit(solution)/shard_map/ppermute | solution.py:219
  12.2 13.0 %collective-permute-start.5 = (bf16[1,3,40,960]{3,2,1,0:T(8,128)(2,1)S(1)}, bf16[1,3,40,960]{3,2,1,0:T(8,128)(2,1)S(1)}, u32[]{:S(2)}, u32[]{:S(2)}) collective-permute-start(bf16[1,3,40,960]{3,2,1,0:T(8,128)(2,1)S(1)} %get-tuple-element.37), channel_id=1, source_target_pairs={{0,4},{1,5},{2,6},{3,7},{4,0},{5,1},{6,2},{7,3},{8,12},{9,13},{10,... | collective-permute-start | bytes 691208 | tf_op jit(solution)/shard_map/ppermute | solution.py:219
  13.7 11.5 %collective-permute-start.6 = (bf16[1,3,40,960]{3,2,1,0:T(8,128)(2,1)S(1)}, bf16[1,3,40,960]{3,2,1,0:T(8,128)(2,1)S(1)}, u32[]{:S(2)}, u32[]{:S(2)}) collective-permute-start(bf16[1,3,40,960]{3,2,1,0:T(8,128)(2,1)S(1)} %get-tuple-element.38), channel_id=1, source_target_pairs={{0,6},{1,7},{2,4},{3,5},{4,2},{5,3},{6,0},{7,1},{8,14},{9,15},{10,... | collective-permute-start | bytes 691208 | tf_op jit(solution)/shard_map/ppermute | solution.py:219
  13.7 4.3 %collective-permute-start.1 = (f32[16,960]{1,0:T(8,128)S(1)}, f32[16,960]{1,0:T(8,128)S(1)}, u32[]{:S(2)}, u32[]{:S(2)}) collective-permute-start(f32[16,960]{1,0:T(8,128)S(1)} %add.48), channel_id=1, source_target_pairs={{0,8},{1,9},{2,10},{3,11},{4,12},{5,13},{6,14},{7,15},{8,0},{9,1},... | collective-permute-start | bytes 184328 | tf_op jit(solution)/shard_map/ppermute | solution.py:219
  18.0 5.3 %collective-permute-start.3 = (f32[16,960]{1,0:T(8,128)S(1)}, f32[16,960]{1,0:T(8,128)S(1)}, u32[]{:S(2)}, u32[]{:S(2)}) collective-permute-start(f32[16,960]{1,0:T(8,128)S(1)} %add.49), channel_id=1, source_target_pairs={{0,16},{1,17},{2,18},{3,19},{4,20},{5,21},{6,22},{7,23},{8,24},{9,... | collective-permute-start | bytes 184328 | tf_op jit(solution)/shard_map/ppermute | solution.py:219
  25.2 4.3 %collective-permute-start.7 = (f32[16,960]{1,0:T(8,128)S(1)}, f32[16,960]{1,0:T(8,128)S(1)}, u32[]{:S(2)}, u32[]{:S(2)}) collective-permute-start(f32[16,960]{1,0:T(8,128)S(1)} %add.50), channel_id=1, source_target_pairs={{0,2},{1,3},{2,0},{3,1},{4,6},{5,7},{6,4},{7,5},{8,10},{9,11},{10,... | collective-permute-start | bytes 184328 | tf_op jit(solution)/shard_map/ppermute | solution.py:219
  26.5 13.1 %collective-permute-start.12 = (bf16[1,3,40,960]{3,2,1,0:T(8,128)(2,1)S(1)}, bf16[1,3,40,960]{3,2,1,0:T(8,128)(2,1)S(1)}, u32[]{:S(2)}, u32[]{:S(2)}) collective-permute-start(bf16[1,3,40,960]{3,2,1,0:T(8,128)(2,1)S(1)} %add_add_fusion), channel_id=1, source_target_pairs={{0,16},{1,17},{2,18},{3,19},{4,20},{5,21},{6,22},{7,23},{8,24},{9,... | collective-permute-start | bytes 691208 | tf_op jit(solution)/shard_map/ppermute | solution.py:219
  29.6 4.3 %collective-permute-start.8 = (f32[16,960]{1,0:T(8,128)S(1)}, f32[16,960]{1,0:T(8,128)S(1)}, u32[]{:S(2)}, u32[]{:S(2)}) collective-permute-start(f32[16,960]{1,0:T(8,128)S(1)} %add.54), channel_id=1, source_target_pairs={{0,4},{1,5},{2,6},{3,7},{4,0},{5,1},{6,2},{7,3},{8,12},{9,13},{10,... | collective-permute-start | bytes 184328 | tf_op jit(solution)/shard_map/ppermute | solution.py:219
  33.9 1.3 %collective-permute-start.9 = (f32[16,960]{1,0:T(8,128)S(1)}, f32[16,960]{1,0:T(8,128)S(1)}, u32[]{:S(2)}, u32[]{:S(2)}) collective-permute-start(f32[16,960]{1,0:T(8,128)S(1)} %add.55.mine_ref), channel_id=1, source_target_pairs={{0,1},{1,0},{2,3},{3,2},{4,5},{5,4},{6,7},{7,6},{8,9},{9,8},{10,11... | collective-permute-start | bytes 184328 | tf_op jit(solution)/shard_map/ppermute | solution.py:219
  37.0 1.4 %collective-permute-start.10 = (f32[3,8,960]{2,1,0:T(8,128)S(1)}, f32[3,8,960]{2,1,0:T(8,128)S(1)}, u32[]{:S(2)}, u32[]{:S(2)}) collective-permute-start(f32[3,8,960]{2,1,0:T(8,128)S(1)} %get-tuple-element.43), channel_id=1, source_target_pairs={{0,1},{1,0},{2,3},{3,2},{4,5},{5,4},{6,7},{7,6},{8,9},{9,8},{10,11... | collective-permute-start | bytes 276488 | tf_op jit(solution)/shard_map/ppermute | solution.py:219
  37.2 1.3 %collective-permute-start.11 = (f32[3,8,960]{2,1,0:T(8,128)S(1)}, f32[3,8,960]{2,1,0:T(8,128)S(1)}, u32[]{:S(2)}, u32[]{:S(2)}) collective-permute-start(f32[3,8,960]{2,1,0:T(8,128)S(1)} %get-tuple-element.45), channel_id=1, source_target_pairs={{0,1},{1,0},{2,3},{3,2},{4,5},{5,4},{6,7},{7,6},{8,9},{9,8},{10,11... | collective-permute-start | bytes 276488 | tf_op jit(solution)/shard_map/ppermute | solution.py:219
  39.7 10.4 %collective-permute-start.15 = (bf16[1,3,40,960]{3,2,1,0:T(8,128)(2,1)S(1)}, bf16[1,3,40,960]{3,2,1,0:T(8,128)(2,1)S(1)}, u32[]{:S(2)}, u32[]{:S(2)}) collective-permute-start(bf16[1,3,40,960]{3,2,1,0:T(8,128)(2,1)S(1)} %add.58), channel_id=1, source_target_pairs={{0,8},{1,9},{2,10},{3,11},{4,12},{5,13},{6,14},{7,15},{8,0},{9,1},... | collective-permute-start | bytes 691208 | tf_op jit(solution)/shard_map/ppermute | solution.py:219
  40.4 4.6 %collective-permute-start.13 = (f32[3,8,960]{2,1,0:T(8,128)S(1)}, f32[3,8,960]{2,1,0:T(8,128)S(1)}, u32[]{:S(2)}, u32[]{:S(2)}) collective-permute-start(f32[3,8,960]{2,1,0:T(8,128)S(1)} %add.57), channel_id=1, source_target_pairs={{0,2},{1,3},{2,0},{3,1},{4,6},{5,7},{6,4},{7,5},{8,10},{9,11},{10,... | collective-permute-start | bytes 276488 | tf_op jit(solution)/shard_map/ppermute | solution.py:219
  45.0 5.0 %collective-permute-start.14 = (f32[3,8,960]{2,1,0:T(8,128)S(1)}, f32[3,8,960]{2,1,0:T(8,128)S(1)}, u32[]{:S(2)}, u32[]{:S(2)}) collective-permute-start(f32[3,8,960]{2,1,0:T(8,128)S(1)} %add.59), channel_id=1, source_target_pairs={{0,4},{1,5},{2,6},{3,7},{4,0},{5,1},{6,2},{7,3},{8,12},{9,13},{10,... | collective-permute-start | bytes 276488 | tf_op jit(solution)/shard_map/ppermute | solution.py:219
  50.1 6.9 %collective-permute-start.18 = (bf16[1,3,40,960]{3,2,1,0:T(8,128)(2,1)S(1)}, bf16[1,3,40,960]{3,2,1,0:T(8,128)(2,1)S(1)}, u32[]{:S(2)}, u32[]{:S(2)}) collective-permute-start(bf16[1,3,40,960]{3,2,1,0:T(8,128)(2,1)S(1)} %add.61), channel_id=1, source_target_pairs={{0,4},{1,5},{2,6},{3,7},{4,0},{5,1},{6,2},{7,3},{8,12},{9,13},{10,... | collective-permute-start | bytes 691208 | tf_op jit(solution)/shard_map/ppermute | solution.py:219
  51.4 6.2 %collective-permute-start.16 = (bf16[1,3,40,960]{3,2,1,0:T(8,128)(2,1)S(1)}, bf16[1,3,40,960]{3,2,1,0:T(8,128)(2,1)S(1)}, u32[]{:S(2)}, u32[]{:S(2)}) collective-permute-start(bf16[1,3,40,960]{3,2,1,0:T(8,128)(2,1)S(1)} %add.61), channel_id=1, source_target_pairs={{0,2},{1,3},{2,0},{3,1},{4,6},{5,7},{6,4},{7,5},{8,10},{9,11},{10,... | collective-permute-start | bytes 691208 | tf_op jit(solution)/shard_map/ppermute | solution.py:219
  51.9 4.6 %collective-permute-start.17 = (f32[3,8,960]{2,1,0:T(8,128)S(1)}, f32[3,8,960]{2,1,0:T(8,128)S(1)}, u32[]{:S(2)}, u32[]{:S(2)}) collective-permute-start(f32[3,8,960]{2,1,0:T(8,128)S(1)} %add.60), channel_id=1, source_target_pairs={{0,8},{1,9},{2,10},{3,11},{4,12},{5,13},{6,14},{7,15},{8,0},{9,1},... | collective-permute-start | bytes 276488 | tf_op jit(solution)/shard_map/ppermute | solution.py:219
  57.7 15.9 %collective-permute-start.23 = (bf16[3,3,40,960]{3,2,1,0:T(8,128)(2,1)S(1)}, bf16[3,3,40,960]{3,2,1,0:T(8,128)(2,1)S(1)}, u32[]{:S(2)}, u32[]{:S(2)}) collective-permute-start(bf16[3,3,40,960]{3,2,1,0:T(8,128)(2,1)S(1)} %pad_maximum_fusion.even_ref), channel_id=1, source_target_pairs={{0,1},{1,0},{2,3},{3,2},{4,5},{5,4},{6,7},{7,6},{8,9},{9,8},{10,11... | collective-permute-start | bytes 2073608 | tf_op jit(solution)/shard_map/ppermute | solution.py:219
  57.8 9.2 %collective-permute-start.24 = (bf16[1,3,40,960]{3,2,1,0:T(8,128)(2,1)S(1)}, bf16[1,3,40,960]{3,2,1,0:T(8,128)(2,1)S(1)}, u32[]{:S(2)}, u32[]{:S(2)}) collective-permute-start(bf16[1,3,40,960]{3,2,1,0:T(8,128)(2,1)S(1)} %collective-permute-done.16), channel_id=1, source_target_pairs={{0,4},{1,5},{2,6},{3,7},{4,0},{5,1},{6,2},{7,3},{8,12},{9,13},{10,... | collective-permute-start | bytes 691208 | tf_op jit(solution)/shard_map/ppermute | solution.py:219
  59.0 8.0 %collective-permute-start.19 = (f32[3,8,960]{2,1,0:T(8,128)S(1)}, f32[3,8,960]{2,1,0:T(8,128)S(1)}, u32[]{:S(2)}, u32[]{:S(2)}) collective-permute-start(f32[3,8,960]{2,1,0:T(8,128)S(1)} %add.62), channel_id=1, source_target_pairs={{0,16},{1,17},{2,18},{3,19},{4,20},{5,21},{6,22},{7,23},{8,24},{9,... | collective-permute-start | bytes 276488 | tf_op jit(solution)/shard_map/ppermute | solution.py:219
  61.7 11.9 %copy-start.4 = (s32[3]{0:T(128)S(1)}, s32[3]{0:T(128)}, u32[]{:S(2)}) copy-start(s32[3]{0:T(128)} %buckets_ref.1) | copy-start | bytes 40
  61.7 11.9 %copy-start.5 = (f32[4]{0:T(128)S(1)}, f32[4]{0:T(128)}, u32[]{:S(2)}) copy-start(f32[4]{0:T(128)} %rates_ref.1) | copy-start | bytes 52
  61.7 11.9 %copy-start.6 = (f32[4]{0:T(128)S(1)}, f32[4]{0:T(128)}, u32[]{:S(2)}) copy-start(f32[4]{0:T(128)} %betas_ref.1) | copy-start | bytes 52
  67.0 6.6 %collective-permute-start.25 = (bf16[1,3,40,960]{3,2,1,0:T(8,128)(2,1)S(1)}, bf16[1,3,40,960]{3,2,1,0:T(8,128)(2,1)S(1)}, u32[]{:S(2)}, u32[]{:S(2)}) collective-permute-start(bf16[1,3,40,960]{3,2,1,0:T(8,128)(2,1)S(1)} %collective-permute-done.24.far_ref), channel_id=1, source_target_pairs={{0,1},{1,0},{2,3},{3,2},{4,5},{5,4},{6,7},{7,6},{8,9},{9,8},{10,11... | collective-permute-start | bytes 691208 | tf_op jit(solution)/shard_map/ppermute | solution.py:219
  67.1 5.2 %collective-permute-start.21 = (f32[3,8,960]{2,1,0:T(8,128)S(1)}, f32[3,8,960]{2,1,0:T(8,128)S(1)}, u32[]{:S(2)}, u32[]{:S(2)}) collective-permute-start(f32[3,8,960]{2,1,0:T(8,128)S(1)} %add.63.r0_ref), channel_id=1, source_target_pairs={{0,2},{1,3},{2,0},{3,1},{4,6},{5,7},{6,4},{7,5},{8,10},{9,11},{10,... | collective-permute-start | bytes 276488 | tf_op jit(solution)/shard_map/ppermute | solution.py:219
  67.9 4.4 %collective-permute-start.20 = (f32[3,8,960]{2,1,0:T(8,128)S(1)}, f32[3,8,960]{2,1,0:T(8,128)S(1)}, u32[]{:S(2)}, u32[]{:S(2)}) collective-permute-start(f32[3,8,960]{2,1,0:T(8,128)S(1)} %add.63.r0_ref), channel_id=1, source_target_pairs={{0,1},{1,0},{2,3},{3,2},{4,5},{5,4},{6,7},{7,6},{8,9},{9,8},{10,11... | collective-permute-start | bytes 276488 | tf_op jit(solution)/shard_map/ppermute | solution.py:219
  72.3 1.3 %collective-permute-start.22 = (f32[3,8,960]{2,1,0:T(8,128)S(1)}, f32[3,8,960]{2,1,0:T(8,128)S(1)}, u32[]{:S(2)}, u32[]{:S(2)}) collective-permute-start(f32[3,8,960]{2,1,0:T(8,128)S(1)} %collective-permute-done.21.r2_ref), channel_id=1, source_target_pairs={{0,1},{1,0},{2,3},{3,2},{4,5},{5,4},{6,7},{7,6},{8,9},{9,8},{10,11... | collective-permute-start | bytes 276488 | tf_op jit(solution)/shard_map/ppermute | solution.py:219
  (1 other events, 8.0 us)

commit v10 on v9

--- a/solution.py
+++ b/solution.py
@@ -11,6 +11,8 @@
 F32 = jnp.float32
 BF16 = jnp.bfloat16
 SMEM = pl.BlockSpec(memory_space=pltpu.SMEM)
+VMEM = pl.BlockSpec(memory_space=pltpu.VMEM)
+ANY = pl.BlockSpec(memory_space=pl.ANY)
 
 
 def whole(shape):
@@ -49,28 +51,25 @@
         left_ref[m, 1 - bit] = other_ref[:, m * rows : (m + 1) * rows]
 
 
-def right_kernel(mine_ref, other_ref, grad_ref, error_ref, all_ref, k0_ref, k2_ref, s1_ref, s3_ref, left_ref, right_ref):
-    i = pl.program_id(0)
+def right_kernel(
+    mine_ref, other_ref, grad_ref, error_ref, all_ref, k0_ref, k2_ref, s1_ref, s3_ref, left_ref, right_ref
+):
     low_bits = lax.axis_index(AXES) & 3
-    rows = grad_ref.shape[1]
-
-    @pl.when(i == 0)
-    def _():
-        gather_left(mine_ref, other_ref, left_ref, rows)
-
-    merged = grad_ref[0] + error_ref[0].astype(F32)
-    high, low = split(merged)
-    left = left_ref[i].reshape(-1, rows)
-    rank = left.shape[0]
-    l_both = jnp.concatenate(split(left), 0)
-    both = dot(l_both, high, ((1,), (0,))) + dot(l_both, low, ((1,), (0,)))
-    total = both[:rank] + both[rank:]
-    all_ref[0] = total
-    right_ref[...] = total.reshape(right_ref.shape)
-    k0_ref[0] = right_ref[low_bits]
-    k2_ref[0] = right_ref[low_bits ^ 2]
-    s1_ref[0] = right_ref[low_bits ^ 1]
-    s3_ref[0] = right_ref[low_bits ^ 3]
+    mats, rows, _ = grad_ref.shape
+    gather_left(mine_ref, other_ref, left_ref, rows)
+    for m in range(mats):
+        high, low = split(grad_ref[m] + error_ref[m].astype(F32))
+        left = left_ref[m].reshape(-1, rows)
+        rank = left.shape[0]
+        l_both = jnp.concatenate(split(left), 0)
+        both = dot(l_both, high, ((1,), (0,))) + dot(l_both, low, ((1,), (0,)))
+        total = both[:rank] + both[rank:]
+        all_ref[m] = total
+        right_ref[...] = total.reshape(right_ref.shape)
+        k0_ref[m] = right_ref[low_bits]
+        k2_ref[m] = right_ref[low_bits ^ 2]
+        s1_ref[m] = right_ref[low_bits ^ 1]
+        s3_ref[m] = right_ref[low_bits ^ 3]
 
 
 def three(left):
@@ -185,34 +184,52 @@
 def step_kernel(
     owners_ref, buckets_ref, rates_ref, betas_ref,
     r0_ref, r1_ref, r2_ref, r3_ref, w_ref, even_ref, odd_ref, far_ref, odd_far_ref,
-    step_ref, mom_ref, right_ref, update_ref,
+    step_hbm, mom_hbm, step_ref, mom_ref, zero_ref, right_ref, update_ref, step_sems, mom_sems,
 ):
-    i = pl.program_id(0)
     me = lax.axis_index(AXES)
-    rate = rates_ref[buckets_ref[i]]
-    beta = betas_ref[buckets_ref[i]]
-    of_update, of_old = -rate * (1.0 + beta), -rate * beta * beta
-
-    @pl.when(i == 0)
-    def _():
-        mom_ref[...] = jnp.zeros_like(mom_ref)
-
-    for position, ref in enumerate((r0_ref, r1_ref, r2_ref, r3_ref)):
-        right_ref[position ^ (me & 3)] = ref[0]
-    right = three_right(right_ref[...].reshape(-1, right_ref.shape[2]))
-    update_ref[...] = dot(w_ref[0], right, ((1,), (0,))).reshape(update_ref.shape)
-    own = owners_ref[i] == me
-    slot = slot_of(owners_ref, i)
-    for position in range(8):
-        near, far = ((even_ref, far_ref), (odd_ref, odd_far_ref))[position % 2]
-        piece = position ^ (me & 7)
-        update = update_ref[piece]
-        old = (near[position // 2, 0] if position < 6 else far[0, 0]).astype(F32)
-        step_ref[0, piece] = (of_update * update + of_old * old).astype(BF16)
-
-        @pl.when(own)
+    mats, slots = step_ref.shape[0], mom_ref.shape[0]
+    own = [owners_ref[m] == me for m in range(mats)]
+    slot = [slot_of(owners_ref, m) for m in range(mats)]
+    zero_ref[...] = jnp.zeros_like(zero_ref)
+    for n in range(slots):
+        used = jnp.bool_(False)
+        for m in range(mats):
+            used |= own[m] & (slot[m] == n)
+
+        @pl.when(jnp.logical_not(used))
         def _():
-            mom_ref[slot, piece] = (beta * old + update).astype(BF16)
+            pltpu.make_async_copy(zero_ref, mom_hbm.at[n], mom_sems.at[n]).start()
+
+    for m in range(mats):
+        rate = rates_ref[buckets_ref[m]]
+        beta = betas_ref[buckets_ref[m]]
+        of_update, of_old = -rate * (1.0 + beta), -rate * beta * beta
+        for position, ref in enumerate((r0_ref, r1_ref, r2_ref, r3_ref)):
+            right_ref[position ^ (me & 3)] = ref[m]
+        right = three_right(right_ref[...].reshape(-1, right_ref.shape[2]))
+        update_ref[...] = dot(w_ref[m], right, ((1,), (0,))).reshape(update_ref.shape)
+        for position in range(8):
+            near, far = ((even_ref, far_ref), (odd_ref, odd_far_ref))[position % 2]
+            piece = position ^ (me & 7)
+            update = update_ref[piece]
+            old = (near[position // 2, m] if position < 6 else far[0, m]).astype(F32)
+            step_ref[m, piece] = (of_update * update + of_old * old).astype(BF16)
+
+            @pl.when(own[m])
+            def _():
+                mom_ref[slot[m], piece] = (beta * old + update).astype(BF16)
+
+        pltpu.make_async_copy(step_ref.at[m], step_hbm.at[m], step_sems.at[m]).start()
+
+        @pl.when(own[m])
+        def _():
+            n = slot[m]
+            pltpu.make_async_copy(mom_ref.at[n], mom_hbm.at[n], mom_sems.at[n]).start()
+
+    for n in range(slots):
+        pltpu.make_async_copy(zero_ref, mom_hbm.at[n], mom_sems.at[n]).wait()
+    for m in range(mats):
+        pltpu.make_async_copy(step_ref.at[m], step_hbm.at[m], step_sems.at[m]).wait()
 
 
 def exchange(value, mask, count):
@@ -267,11 +284,10 @@
     mine = mine + swap(other, 1)
     evens = pl.pallas_call(
         even_kernel,
-        grid=(1,),
-        in_specs=[SMEM, whole((slots, 8, piece, cols)), whole(old_shape(4))],
-        out_specs=[whole(old_shape(1))] * 4,
+        in_specs=[SMEM, VMEM, VMEM],
+        out_specs=[VMEM] * 4,
         out_shape=[sds(old_shape(1), BF16)] * 4,
-        compiler_params=params(),
+        compiler_params=pltpu.CompilerParams(vmem_limit_bytes=40 * 1024 * 1024),
         name="even",
     )(owners, momentum, after(got, mine))
     got = [swap(evens[n], 2 * n) for n in (1, 2, 3)]
@@ -288,12 +304,11 @@
 
     right_all, keep, send2, send1, send3 = pl.pallas_call(
         right_kernel,
-        grid=(mats,),
-        in_specs=[whole((half, mats * rows))] * 2 + [grad_spec, grad_spec],
-        out_specs=[per_matrix((rank, cols))] + [per_matrix((quarter, cols))] * 4,
+        in_specs=[VMEM] * 4,
+        out_specs=[VMEM] * 5,
         out_shape=[sds((mats, rank, cols), F32)] + [sds((mats, quarter, cols), F32)] * 4,
         scratch_shapes=[pltpu.VMEM((mats, 2, half, rows), F32), pltpu.VMEM((4, quarter, cols), F32)],
-        compiler_params=params(),
+        compiler_params=pltpu.CompilerParams(vmem_limit_bytes=40 * 1024 * 1024),
         name="right",
     )(mine, other, grads, errs)
 
@@ -343,18 +358,24 @@
     odds = swap(evens, 1)
     r3 = swap(r2, 1)
     far = after(far, r0)
-    odd_far = swap(far, 1)
-
-    quarter_spec = per_matrix((quarter, cols))
-    old_specs = [pl.BlockSpec((n, 1, piece, cols), lambda i: (0, i, 0, 0)) for n in (3, 3, 1, 1)]
+    odd_far = swap(after(far, r2), 1)
+
+    pieces = (8, piece, cols)
     steps, new_mom = pl.pallas_call(
         step_kernel,
-        grid=(mats,),
-        in_specs=[SMEM] * 4 + [quarter_spec] * 4 + [per_matrix((rows, 3 * rank))] + old_specs,
-        out_specs=[per_matrix((8, piece, cols)), whole((slots, 8, piece, cols))],
-        out_shape=[sds((mats, 8, piece, cols), BF16), sds((slots, 8, piece, cols), BF16)],
-        scratch_shapes=[pltpu.VMEM((4, quarter, cols), F32), pltpu.VMEM((8, piece, cols), F32)],
-        compiler_params=params(),
+        in_specs=[SMEM] * 4 + [VMEM] * 9,
+        out_specs=[ANY] * 2,
+        out_shape=[sds((mats,) + pieces, BF16), sds((slots,) + pieces, BF16)],
+        scratch_shapes=[
+            pltpu.VMEM((mats,) + pieces, BF16),
+            pltpu.VMEM((slots,) + pieces, BF16),
+            pltpu.VMEM(pieces, BF16),
+            pltpu.VMEM((4, quarter, cols), F32),
+            pltpu.VMEM(pieces, F32),
+            pltpu.SemaphoreType.DMA((mats,)),
+            pltpu.SemaphoreType.DMA((slots,)),
+        ],
+        compiler_params=pltpu.CompilerParams(vmem_limit_bytes=40 * 1024 * 1024),
         name="step",
     )(owners, buckets, learn_rates, beta_values, r0, r1, r2, r3, w, evens, odds, far, odd_far)
     return (new_errors[None], steps.reshape(1, mats, rows, cols), new_mom.reshape(slots, rows, cols))

time: 77.7 us -> 76.8 us (0.988)
  Pallas kernels: 17.1 us -> 15.8 us
    pallas_call x3, Pallas kernels: 6.32 us -> 4.94 us  [the longest x1 3.13 us: on_device(): pl.pallas_call(step_kernel, in_specs=[SMEM] * 4 + [VMEM] * 9, out_specs=[...]
  transfers between devices with their start and end apart: 26 -> 26, of which waited for: 17 -> 18; matrix products, arithmetic and copies ran while one was open for 0% -> 0% of each run, Pallas kernels for 10% -> 9%
where the time goes in v10:
time: 76.8 us; the launch traced here: 76.7 us
  waiting for transfers between devices  31.6 us (41%)
  starting transfers between devices  28 us (36%)
  Pallas kernels  15.8 us (21%)
  between operations  0.85 us (1%)
    ppermute x26, waiting for transfers between devices, exchange(): return lax.ppermute(value, AXES, [(d, d ^ mask) for d in range(count)])  31.6 us
    ppermute x26, starting transfers between devices, exchange(): return lax.ppermute(value, AXES, [(d, d ^ mask) for d in range(count)])  28 us
    pallas_call x1, Pallas kernels, on_device(): pl.pallas_call(first_kernel, in_specs=[pl.BlockSpec(memory_space=pltpu.HB...  5.11 us
    pallas_call x1, Pallas kernels, on_device(): pl.pallas_call(solve_kernel, grid=(1,), in_specs=[whole((half, mats * row...  3.38 us
    pallas_call x1, Pallas kernels, on_device(): pl.pallas_call(step_kernel, in_specs=[SMEM] * 4 + [VMEM] * 9, out_specs=[...  3.13 us
    pallas_call x1, Pallas kernels, on_device(): pl.pallas_call(error_kernel, grid=(mats,), in_specs=[grad_spec, grad_spec...  2.31 us
  transfers between devices with their start and end apart: 26, of which 18 were waited for; matrix products, arithmetic and copies ran while one was open for 0% of the time, Pallas kernels for 9%

profile of v10, /device:TPU:0, one launch (start us, length us, event | category | flops | bytes accessed | tf_op | source)
XLA Modules:
  0.0 76.7 jit_solution(3552715813779666189)
XLA Ops:
  0.7 5.1 %first.1 = (f32[16,960]{1,0:T(8,128)S(1)}, f32[16,960]{1,0:T(8,128)S(1)}, bf16[4,3,40,960]{3,2,1,0:T(8,128)(2,1)S(1)}) custom-call(s32[3]{0:T(128)} %owners_ref.3, f32[3,320,960]{2,1,0:T(8,128)} %bitcast.7, bf16[3,320,960]{2,1,0:T(8,128)(2,1)} %bitcast.10, f32[3,32,960]{2,1,0:T(8,128)} %bitcast.16, bf16[2,8,40,960]{3,2,1,0:T(8,128)(2,1)} %bitcast.13), custom_call_target="tpu_custom_call" | custom-call | tf_op jit(solution)/shard_map/first/pallas_call | solution.py:265
  6.4 2.2 %collective-permute-done = f32[16,960]{1,0:T(8,128)S(1)} collective-permute-done((f32[16,960]{1,0:T(8,128)S(1)}, f32[16,960]{1,0:T(8,128)S(1)}, u32[]{:S(2)}, u32[]{:S(2)}) %collective-permute-start) | collective-permute-done | bytes 61472 | tf_op jit(solution)/shard_map/ppermute | solution.py:236
  9.3 2.9 %collective-permute-start.4 = (bf16[1,3,40,960]{3,2,1,0:T(8,128)(2,1)S(1)}, bf16[1,3,40,960]{3,2,1,0:T(8,128)(2,1)S(1)}, u32[]{:S(2)}, u32[]{:S(2)}) collective-permute-start(bf16[1,3,40,960]{3,2,1,0:T(8,128)(2,1)S(1)} %get-tuple-element.37), channel_id=1, source_target_pairs={{0,2},{1,3},{2,0},{3,1},{4,6},{5,7},{6,4},{7,5},{8,10},{9,11},{10,... | collective-permute-start | bytes 691208 | tf_op jit(solution)/shard_map/ppermute | solution.py:236
  12.2 1.5 %collective-permute-start.5 = (bf16[1,3,40,960]{3,2,1,0:T(8,128)(2,1)S(1)}, bf16[1,3,40,960]{3,2,1,0:T(8,128)(2,1)S(1)}, u32[]{:S(2)}, u32[]{:S(2)}) collective-permute-start(bf16[1,3,40,960]{3,2,1,0:T(8,128)(2,1)S(1)} %get-tuple-element.38), channel_id=1, source_target_pairs={{0,4},{1,5},{2,6},{3,7},{4,0},{5,1},{6,2},{7,3},{8,12},{9,13},{10,... | collective-permute-start | bytes 691208 | tf_op jit(solution)/shard_map/ppermute | solution.py:236
  13.7 2.0 %collective-permute-start.1 = (f32[16,960]{1,0:T(8,128)S(1)}, f32[16,960]{1,0:T(8,128)S(1)}, u32[]{:S(2)}, u32[]{:S(2)}) collective-permute-start(f32[16,960]{1,0:T(8,128)S(1)} %add.48), channel_id=1, source_target_pairs={{0,8},{1,9},{2,10},{3,11},{4,12},{5,13},{6,14},{7,15},{8,0},{9,1},... | collective-permute-start | bytes 184328 | tf_op jit(solution)/shard_map/ppermute | solution.py:236
  15.8 2.2 %collective-permute-done.1 = f32[16,960]{1,0:T(8,128)S(1)} collective-permute-done((f32[16,960]{1,0:T(8,128)S(1)}, f32[16,960]{1,0:T(8,128)S(1)}, u32[]{:S(2)}, u32[]{:S(2)}) %collective-permute-start.1) | collective-permute-done | bytes 61472 | tf_op jit(solution)/shard_map/ppermute | solution.py:236
  18.0 3.1 %collective-permute-start.3 = (f32[16,960]{1,0:T(8,128)S(1)}, f32[16,960]{1,0:T(8,128)S(1)}, u32[]{:S(2)}, u32[]{:S(2)}) collective-permute-start(f32[16,960]{1,0:T(8,128)S(1)} %add.49), channel_id=1, source_target_pairs={{0,16},{1,17},{2,18},{3,19},{4,20},{5,21},{6,22},{7,23},{8,24},{9,... | collective-permute-start | bytes 184328 | tf_op jit(solution)/shard_map/ppermute | solution.py:236
  21.1 2.2 %collective-permute-done.3 = f32[16,960]{1,0:T(8,128)S(1)} collective-permute-done((f32[16,960]{1,0:T(8,128)S(1)}, f32[16,960]{1,0:T(8,128)S(1)}, u32[]{:S(2)}, u32[]{:S(2)}) %collective-permute-start.3) | collective-permute-done | bytes 61472 | tf_op jit(solution)/shard_map/ppermute | solution.py:236
  23.4 1.8 %collective-permute-done.5 = bf16[1,3,40,960]{3,2,1,0:T(8,128)(2,1)S(1)} collective-permute-done((bf16[1,3,40,960]{3,2,1,0:T(8,128)(2,1)S(1)}, bf16[1,3,40,960]{3,2,1,0:T(8,128)(2,1)S(1)}, u32[]{:S(2)}, u32[]{:S(2)}) %collective-permute-start.5) | collective-permute-done | bytes 230432 | tf_op jit(solution)/shard_map/ppermute | solution.py:236
  25.2 1.3 %collective-permute-start.7 = (f32[16,960]{1,0:T(8,128)S(1)}, f32[16,960]{1,0:T(8,128)S(1)}, u32[]{:S(2)}, u32[]{:S(2)}) collective-permute-start(f32[16,960]{1,0:T(8,128)S(1)} %add.50), channel_id=1, source_target_pairs={{0,2},{1,3},{2,0},{3,1},{4,6},{5,7},{6,4},{7,5},{8,10},{9,11},{10,... | collective-permute-start | bytes 184328 | tf_op jit(solution)/shard_map/ppermute | solution.py:236
  26.5 2.6 %collective-permute-start.12 = (bf16[1,3,40,960]{3,2,1,0:T(8,128)(2,1)S(1)}, bf16[1,3,40,960]{3,2,1,0:T(8,128)(2,1)S(1)}, u32[]{:S(2)}, u32[]{:S(2)}) collective-permute-start(bf16[1,3,40,960]{3,2,1,0:T(8,128)(2,1)S(1)} %add_add_fusion), channel_id=1, source_target_pairs={{0,16},{1,17},{2,18},{3,19},{4,20},{5,21},{6,22},{7,23},{8,24},{9,... | collective-permute-start | bytes 691208 | tf_op jit(solution)/shard_map/ppermute | solution.py:236
  29.6 1.6 %collective-permute-start.8 = (f32[16,960]{1,0:T(8,128)S(1)}, f32[16,960]{1,0:T(8,128)S(1)}, u32[]{:S(2)}, u32[]{:S(2)}) collective-permute-start(f32[16,960]{1,0:T(8,128)S(1)} %add.54), channel_id=1, source_target_pairs={{0,4},{1,5},{2,6},{3,7},{4,0},{5,1},{6,2},{7,3},{8,12},{9,13},{10,... | collective-permute-start | bytes 184328 | tf_op jit(solution)/shard_map/ppermute | solution.py:236
  31.2 2.7 %collective-permute-done.8 = f32[16,960]{1,0:T(8,128)S(1)} collective-permute-done((f32[16,960]{1,0:T(8,128)S(1)}, f32[16,960]{1,0:T(8,128)S(1)}, u32[]{:S(2)}, u32[]{:S(2)}) %collective-permute-start.8) | collective-permute-done | bytes 61472 | tf_op jit(solution)/shard_map/ppermute | solution.py:236
  34.0 1.2 %collective-permute-done.9.other_ref = f32[16,960]{1,0:T(8,128)S(1)} collective-permute-done((f32[16,960]{1,0:T(8,128)S(1)}, f32[16,960]{1,0:T(8,128)S(1)}, u32[]{:S(2)}, u32[]{:S(2)}) %collective-permute-start.9) | collective-permute-done | bytes 61472 | tf_op jit(solution)/shard_map/ppermute | solution.py:236
  35.3 1.2 %right.1 = (f32[3,32,960]{2,1,0:T(8,128)S(1)}, f32[3,8,960]{2,1,0:T(8,128)S(1)}, f32[3,8,960]{2,1,0:T(8,128)S(1)}, f32[3,8,960]{2,1,0:T(8,128)S(1)}, f32[3,8,960]{2,1,0:T(8,128)S(1)}) custom-call(f32[16,960]{1,0:T(8,128)S(1)} %add.55.mine_ref, f32[16,960]{1,0:T(8,128)S(1)} %collective-permute-done.9.other_ref, f32[3,320,960]{2,1,0:T(8,128)S(1)} %bitcast.8, ...), custom_call_target="tpu_custom_call" | custom-call | tf_op jit(solution)/shard_map/right/pallas_call | solution.py:305
  37.0 0.8 %collective-permute-done.10 = f32[3,8,960]{2,1,0:T(8,128)S(1)} collective-permute-done((f32[3,8,960]{2,1,0:T(8,128)S(1)}, f32[3,8,960]{2,1,0:T(8,128)S(1)}, u32[]{:S(2)}, u32[]{:S(2)}) %collective-permute-start.10) | collective-permute-done | bytes 92192 | tf_op jit(solution)/shard_map/ppermute | solution.py:236
  38.0 1.6 %collective-permute-done.12 = bf16[1,3,40,960]{3,2,1,0:T(8,128)(2,1)S(1)} collective-permute-done((bf16[1,3,40,960]{3,2,1,0:T(8,128)(2,1)S(1)}, bf16[1,3,40,960]{3,2,1,0:T(8,128)(2,1)S(1)}, u32[]{:S(2)}, u32[]{:S(2)}) %collective-permute-start.12) | collective-permute-done | bytes 230432 | tf_op jit(solution)/shard_map/ppermute | solution.py:236
  41.0 4.1 %collective-permute-done.13 = f32[3,8,960]{2,1,0:T(8,128)S(1)} collective-permute-done((f32[3,8,960]{2,1,0:T(8,128)S(1)}, f32[3,8,960]{2,1,0:T(8,128)S(1)}, u32[]{:S(2)}, u32[]{:S(2)}) %collective-permute-start.13) | collective-permute-done | bytes 92192 | tf_op jit(solution)/shard_map/ppermute | solution.py:236
  45.0 1.1 %collective-permute-start.14 = (f32[3,8,960]{2,1,0:T(8,128)S(1)}, f32[3,8,960]{2,1,0:T(8,128)S(1)}, u32[]{:S(2)}, u32[]{:S(2)}) collective-permute-start(f32[3,8,960]{2,1,0:T(8,128)S(1)} %add.59), channel_id=1, source_target_pairs={{0,4},{1,5},{2,6},{3,7},{4,0},{5,1},{6,2},{7,3},{8,12},{9,13},{10,... | collective-permute-start | bytes 276488 | tf_op jit(solution)/shard_map/ppermute | solution.py:236
  46.1 3.4 %solve.1.w_ref = bf16[3,320,96]{2,1,0:T(8,128)(2,1)S(1)} custom-call(f32[16,960]{1,0:T(8,128)S(1)} %add.55.mine_ref, f32[16,960]{1,0:T(8,128)S(1)} %collective-permute-done.9.other_ref), custom_call_target="tpu_custom_call" | custom-call | bytes 1048576 | tf_op jit(solution)/shard_map/solve/pallas_call | solution.py:315
  49.8 1.1 %collective-permute-start.18 = (bf16[1,3,40,960]{3,2,1,0:T(8,128)(2,1)S(1)}, bf16[1,3,40,960]{3,2,1,0:T(8,128)(2,1)S(1)}, u32[]{:S(2)}, u32[]{:S(2)}) collective-permute-start(bf16[1,3,40,960]{3,2,1,0:T(8,128)(2,1)S(1)} %add.61), channel_id=1, source_target_pairs={{0,4},{1,5},{2,6},{3,7},{4,0},{5,1},{6,2},{7,3},{8,12},{9,13},{10,... | collective-permute-start | bytes 691208 | tf_op jit(solution)/shard_map/ppermute | solution.py:236
  50.9 1.0 %collective-permute-start.16 = (bf16[1,3,40,960]{3,2,1,0:T(8,128)(2,1)S(1)}, bf16[1,3,40,960]{3,2,1,0:T(8,128)(2,1)S(1)}, u32[]{:S(2)}, u32[]{:S(2)}) collective-permute-start(bf16[1,3,40,960]{3,2,1,0:T(8,128)(2,1)S(1)} %add.61), channel_id=1, source_target_pairs={{0,2},{1,3},{2,0},{3,1},{4,6},{5,7},{6,4},{7,5},{8,10},{9,11},{10,... | collective-permute-start | bytes 691208 | tf_op jit(solution)/shard_map/ppermute | solution.py:236
  51.9 1.4 %collective-permute-start.17 = (f32[3,8,960]{2,1,0:T(8,128)S(1)}, f32[3,8,960]{2,1,0:T(8,128)S(1)}, u32[]{:S(2)}, u32[]{:S(2)}) collective-permute-start(f32[3,8,960]{2,1,0:T(8,128)S(1)} %add.60), channel_id=1, source_target_pairs={{0,8},{1,9},{2,10},{3,11},{4,12},{5,13},{6,14},{7,15},{8,0},{9,1},... | collective-permute-start | bytes 276488 | tf_op jit(solution)/shard_map/ppermute | solution.py:236
  53.2 3.3 %collective-permute-done.17 = f32[3,8,960]{2,1,0:T(8,128)S(1)} collective-permute-done((f32[3,8,960]{2,1,0:T(8,128)S(1)}, f32[3,8,960]{2,1,0:T(8,128)S(1)}, u32[]{:S(2)}, u32[]{:S(2)}) %collective-permute-start.17) | collective-permute-done | bytes 92192 | tf_op jit(solution)/shard_map/ppermute | solution.py:236
  57.2 1.2 %collective-permute-start.24 = (bf16[1,3,40,960]{3,2,1,0:T(8,128)(2,1)S(1)}, bf16[1,3,40,960]{3,2,1,0:T(8,128)(2,1)S(1)}, u32[]{:S(2)}, u32[]{:S(2)}) collective-permute-start(bf16[1,3,40,960]{3,2,1,0:T(8,128)(2,1)S(1)} %collective-permute-done.16), channel_id=1, source_target_pairs={{0,4},{1,5},{2,6},{3,7},{4,0},{5,1},{6,2},{7,3},{8,12},{9,13},{10,... | collective-permute-start | bytes 691208 | tf_op jit(solution)/shard_map/ppermute | solution.py:236
  58.5 3.3 %collective-permute-start.19 = (f32[3,8,960]{2,1,0:T(8,128)S(1)}, f32[3,8,960]{2,1,0:T(8,128)S(1)}, u32[]{:S(2)}, u32[]{:S(2)}) collective-permute-start(f32[3,8,960]{2,1,0:T(8,128)S(1)} %add.62), channel_id=1, source_target_pairs={{0,16},{1,17},{2,18},{3,19},{4,20},{5,21},{6,22},{7,23},{8,24},{9,... | collective-permute-start | bytes 276488 | tf_op jit(solution)/shard_map/ppermute | solution.py:236
  61.7 2.3 %errors.1 = bf16[3,320,960]{2,1,0:T(8,128)(2,1)} custom-call(f32[3,320,960]{2,1,0:T(8,128)S(1)} %bitcast.9, bf16[3,320,960]{2,1,0:T(8,128)(2,1)S(1)} %bitcast.12, bf16[3,320,96]{2,1,0:T(8,128)(2,1)S(1)} %solve.1.w_ref, f32[3,32,960]{2,1,0:T(8,128)S(1)} %get-tuple-element.54.all_ref), custom_call_target="tpu_custom_call" | custom-call | bytes 12582912 | tf_op jit(solution)/shard_map/errors/pallas_call | solution.py:345
  64.0 2.9 %collective-permute-done.19 = f32[3,8,960]{2,1,0:T(8,128)S(1)} collective-permute-done((f32[3,8,960]{2,1,0:T(8,128)S(1)}, f32[3,8,960]{2,1,0:T(8,128)S(1)}, u32[]{:S(2)}, u32[]{:S(2)}) %collective-permute-start.19) | collective-permute-done | bytes 92192 | tf_op jit(solution)/shard_map/ppermute | solution.py:236
  67.0 0.8 %collective-permute-start.21 = (f32[3,8,960]{2,1,0:T(8,128)S(1)}, f32[3,8,960]{2,1,0:T(8,128)S(1)}, u32[]{:S(2)}, u32[]{:S(2)}) collective-permute-start(f32[3,8,960]{2,1,0:T(8,128)S(1)} %add.63.r0_ref), channel_id=1, source_target_pairs={{0,2},{1,3},{2,0},{3,1},{4,6},{5,7},{6,4},{7,5},{8,10},{9,11},{10,... | collective-permute-start | bytes 276488 | tf_op jit(solution)/shard_map/ppermute | solution.py:236
  67.8 3.9 %collective-permute-done.21.r2_ref = f32[3,8,960]{2,1,0:T(8,128)S(1)} collective-permute-done((f32[3,8,960]{2,1,0:T(8,128)S(1)}, f32[3,8,960]{2,1,0:T(8,128)S(1)}, u32[]{:S(2)}, u32[]{:S(2)}) %collective-permute-start.21) | collective-permute-done | bytes 92192 | tf_op jit(solution)/shard_map/ppermute | solution.py:236
  72.2 1.1 %collective-permute-done.20.r1_ref = f32[3,8,960]{2,1,0:T(8,128)S(1)} collective-permute-done((f32[3,8,960]{2,1,0:T(8,128)S(1)}, f32[3,8,960]{2,1,0:T(8,128)S(1)}, u32[]{:S(2)}, u32[]{:S(2)}) %collective-permute-start.20) | collective-permute-done | bytes 92192 | tf_op jit(solution)/shard_map/ppermute | solution.py:236
  73.5 3.1 %step.1 = (bf16[3,8,40,960]{3,2,1,0:T(8,128)(2,1)}, bf16[2,8,40,960]{3,2,1,0:T(8,128)(2,1)}) custom-call(s32[3]{0:T(128)S(1)} %copy-done.3, s32[3]{0:T(128)S(1)} %copy-done.4, f32[4]{0:T(128)S(1)} %copy-done.5, f32[4]{0:T(128)S(1)} %copy-done.6, f32[3,8,960]{2,1,0:T(8,128)S(1)} %add.63.r0_ref, f32[3,8,960]{2,1,0:T(8,128)S(1)} %collective-permute-done.20.r1_ref, ...), custom_call_target="tpu_custom_call" | custom-call | tf_op jit(solution)/shard_map/step/pallas_call | solution.py:364
  (55 shorter events, 5.8 us)
Async XLA Ops:
  0.6 8.0 %copy-start.2 = (bf16[2,320,960]{2,1,0:T(8,128)(2,1)S(1)}, bf16[2,320,960]{2,1,0:T(8,128)(2,1)}, u32[]{:S(2)}) copy-start(bf16[2,320,960]{2,1,0:T(8,128)(2,1)} %param.15) | copy-start | bytes 3686404
  0.7 34.6 %copy-start.1 = (bf16[1,3,320,960]{3,2,1,0:T(8,128)(2,1)S(1)}, bf16[1,3,320,960]{3,2,1,0:T(8,128)(2,1)}, u32[]{:S(2)}) copy-start(bf16[1,3,320,960]{3,2,1,0:T(8,128)(2,1)} %param.9) | copy-start | bytes 5529604
  5.8 2.8 %collective-permute-start.2 = (bf16[4,3,40,960]{3,2,1,0:T(8,128)(2,1)S(1)}, bf16[4,3,40,960]{3,2,1,0:T(8,128)(2,1)S(1)}, u32[]{:S(2)}, u32[]{:S(2)}) collective-permute-start(bf16[4,3,40,960]{3,2,1,0:T(8,128)(2,1)S(1)} %get-tuple-element.34), channel_id=1, source_target_pairs={{0,1},{1,0},{2,3},{3,2},{4,5},{5,4},{6,7},{7,6},{8,9},{9,8},{10,11... | collective-permute-start | bytes 2764808 | tf_op jit(solution)/shard_map/ppermute | solution.py:236
  6.3 2.3 %collective-permute-start = (f32[16,960]{1,0:T(8,128)S(1)}, f32[16,960]{1,0:T(8,128)S(1)}, u32[]{:S(2)}, u32[]{:S(2)}) collective-permute-start(f32[16,960]{1,0:T(8,128)S(1)} %get-tuple-element.33), channel_id=1, source_target_pairs={{0,1},{1,0},{2,3},{3,2},{4,5},{5,4},{6,7},{7,6},{8,9},{9,8},{10,11... | collective-permute-start | bytes 184328 | tf_op jit(solution)/shard_map/ppermute | solution.py:236
  8.6 26.7 %copy-start = (f32[1,3,320,960]{3,2,1,0:T(8,128)S(1)}, f32[1,3,320,960]{3,2,1,0:T(8,128)}, u32[]{:S(2)}) copy-start(f32[1,3,320,960]{3,2,1,0:T(8,128)} %param.8) | copy-start | bytes 11059204
  9.3 14.1 %collective-permute-start.4 = (bf16[1,3,40,960]{3,2,1,0:T(8,128)(2,1)S(1)}, bf16[1,3,40,960]{3,2,1,0:T(8,128)(2,1)S(1)}, u32[]{:S(2)}, u32[]{:S(2)}) collective-permute-start(bf16[1,3,40,960]{3,2,1,0:T(8,128)(2,1)S(1)} %get-tuple-element.37), channel_id=1, source_target_pairs={{0,2},{1,3},{2,0},{3,1},{4,6},{5,7},{6,4},{7,5},{8,10},{9,11},{10,... | collective-permute-start | bytes 691208 | tf_op jit(solution)/shard_map/ppermute | solution.py:236
  12.2 13.0 %collective-permute-start.5 = (bf16[1,3,40,960]{3,2,1,0:T(8,128)(2,1)S(1)}, bf16[1,3,40,960]{3,2,1,0:T(8,128)(2,1)S(1)}, u32[]{:S(2)}, u32[]{:S(2)}) collective-permute-start(bf16[1,3,40,960]{3,2,1,0:T(8,128)(2,1)S(1)} %get-tuple-element.38), channel_id=1, source_target_pairs={{0,4},{1,5},{2,6},{3,7},{4,0},{5,1},{6,2},{7,3},{8,12},{9,13},{10,... | collective-permute-start | bytes 691208 | tf_op jit(solution)/shard_map/ppermute | solution.py:236
  13.7 11.5 %collective-permute-start.6 = (bf16[1,3,40,960]{3,2,1,0:T(8,128)(2,1)S(1)}, bf16[1,3,40,960]{3,2,1,0:T(8,128)(2,1)S(1)}, u32[]{:S(2)}, u32[]{:S(2)}) collective-permute-start(bf16[1,3,40,960]{3,2,1,0:T(8,128)(2,1)S(1)} %get-tuple-element.39), channel_id=1, source_target_pairs={{0,6},{1,7},{2,4},{3,5},{4,2},{5,3},{6,0},{7,1},{8,14},{9,15},{10,... | collective-permute-start | bytes 691208 | tf_op jit(solution)/shard_map/ppermute | solution.py:236
  13.7 4.3 %collective-permute-start.1 = (f32[16,960]{1,0:T(8,128)S(1)}, f32[16,960]{1,0:T(8,128)S(1)}, u32[]{:S(2)}, u32[]{:S(2)}) collective-permute-start(f32[16,960]{1,0:T(8,128)S(1)} %add.48), channel_id=1, source_target_pairs={{0,8},{1,9},{2,10},{3,11},{4,12},{5,13},{6,14},{7,15},{8,0},{9,1},... | collective-permute-start | bytes 184328 | tf_op jit(solution)/shard_map/ppermute | solution.py:236
  18.0 5.3 %collective-permute-start.3 = (f32[16,960]{1,0:T(8,128)S(1)}, f32[16,960]{1,0:T(8,128)S(1)}, u32[]{:S(2)}, u32[]{:S(2)}) collective-permute-start(f32[16,960]{1,0:T(8,128)S(1)} %add.49), channel_id=1, source_target_pairs={{0,16},{1,17},{2,18},{3,19},{4,20},{5,21},{6,22},{7,23},{8,24},{9,... | collective-permute-start | bytes 184328 | tf_op jit(solution)/shard_map/ppermute | solution.py:236
  25.2 4.3 %collective-permute-start.7 = (f32[16,960]{1,0:T(8,128)S(1)}, f32[16,960]{1,0:T(8,128)S(1)}, u32[]{:S(2)}, u32[]{:S(2)}) collective-permute-start(f32[16,960]{1,0:T(8,128)S(1)} %add.50), channel_id=1, source_target_pairs={{0,2},{1,3},{2,0},{3,1},{4,6},{5,7},{6,4},{7,5},{8,10},{9,11},{10,... | collective-permute-start | bytes 184328 | tf_op jit(solution)/shard_map/ppermute | solution.py:236
  26.5 13.1 %collective-permute-start.12 = (bf16[1,3,40,960]{3,2,1,0:T(8,128)(2,1)S(1)}, bf16[1,3,40,960]{3,2,1,0:T(8,128)(2,1)S(1)}, u32[]{:S(2)}, u32[]{:S(2)}) collective-permute-start(bf16[1,3,40,960]{3,2,1,0:T(8,128)(2,1)S(1)} %add_add_fusion), channel_id=1, source_target_pairs={{0,16},{1,17},{2,18},{3,19},{4,20},{5,21},{6,22},{7,23},{8,24},{9,... | collective-permute-start | bytes 691208 | tf_op jit(solution)/shard_map/ppermute | solution.py:236
  29.6 4.3 %collective-permute-start.8 = (f32[16,960]{1,0:T(8,128)S(1)}, f32[16,960]{1,0:T(8,128)S(1)}, u32[]{:S(2)}, u32[]{:S(2)}) collective-permute-start(f32[16,960]{1,0:T(8,128)S(1)} %add.54), channel_id=1, source_target_pairs={{0,4},{1,5},{2,6},{3,7},{4,0},{5,1},{6,2},{7,3},{8,12},{9,13},{10,... | collective-permute-start | bytes 184328 | tf_op jit(solution)/shard_map/ppermute | solution.py:236
  33.9 1.3 %collective-permute-start.9 = (f32[16,960]{1,0:T(8,128)S(1)}, f32[16,960]{1,0:T(8,128)S(1)}, u32[]{:S(2)}, u32[]{:S(2)}) collective-permute-start(f32[16,960]{1,0:T(8,128)S(1)} %add.55.mine_ref), channel_id=1, source_target_pairs={{0,1},{1,0},{2,3},{3,2},{4,5},{5,4},{6,7},{7,6},{8,9},{9,8},{10,11... | collective-permute-start | bytes 184328 | tf_op jit(solution)/shard_map/ppermute | solution.py:236
  36.5 1.4 %collective-permute-start.10 = (f32[3,8,960]{2,1,0:T(8,128)S(1)}, f32[3,8,960]{2,1,0:T(8,128)S(1)}, u32[]{:S(2)}, u32[]{:S(2)}) collective-permute-start(f32[3,8,960]{2,1,0:T(8,128)S(1)} %get-tuple-element.44), channel_id=1, source_target_pairs={{0,1},{1,0},{2,3},{3,2},{4,5},{5,4},{6,7},{7,6},{8,9},{9,8},{10,11... | collective-permute-start | bytes 276488 | tf_op jit(solution)/shard_map/ppermute | solution.py:236
  36.7 1.3 %collective-permute-start.11 = (f32[3,8,960]{2,1,0:T(8,128)S(1)}, f32[3,8,960]{2,1,0:T(8,128)S(1)}, u32[]{:S(2)}, u32[]{:S(2)}) collective-permute-start(f32[3,8,960]{2,1,0:T(8,128)S(1)} %get-tuple-element.46), channel_id=1, source_target_pairs={{0,1},{1,0},{2,3},{3,2},{4,5},{5,4},{6,7},{7,6},{8,9},{9,8},{10,11... | collective-permute-start | bytes 276488 | tf_op jit(solution)/shard_map/ppermute | solution.py:236
  39.7 10.1 %collective-permute-start.15 = (bf16[1,3,40,960]{3,2,1,0:T(8,128)(2,1)S(1)}, bf16[1,3,40,960]{3,2,1,0:T(8,128)(2,1)S(1)}, u32[]{:S(2)}, u32[]{:S(2)}) collective-permute-start(bf16[1,3,40,960]{3,2,1,0:T(8,128)(2,1)S(1)} %add.58), channel_id=1, source_target_pairs={{0,8},{1,9},{2,10},{3,11},{4,12},{5,13},{6,14},{7,15},{8,0},{9,1},... | collective-permute-start | bytes 691208 | tf_op jit(solution)/shard_map/ppermute | solution.py:236
  40.4 4.6 %collective-permute-start.13 = (f32[3,8,960]{2,1,0:T(8,128)S(1)}, f32[3,8,960]{2,1,0:T(8,128)S(1)}, u32[]{:S(2)}, u32[]{:S(2)}) collective-permute-start(f32[3,8,960]{2,1,0:T(8,128)S(1)} %add.57), channel_id=1, source_target_pairs={{0,2},{1,3},{2,0},{3,1},{4,6},{5,7},{6,4},{7,5},{8,10},{9,11},{10,... | collective-permute-start | bytes 276488 | tf_op jit(solution)/shard_map/ppermute | solution.py:236
  45.0 4.7 %collective-permute-start.14 = (f32[3,8,960]{2,1,0:T(8,128)S(1)}, f32[3,8,960]{2,1,0:T(8,128)S(1)}, u32[]{:S(2)}, u32[]{:S(2)}) collective-permute-start(f32[3,8,960]{2,1,0:T(8,128)S(1)} %add.59), channel_id=1, source_target_pairs={{0,4},{1,5},{2,6},{3,7},{4,0},{5,1},{6,2},{7,3},{8,12},{9,13},{10,... | collective-permute-start | bytes 276488 | tf_op jit(solution)/shard_map/ppermute | solution.py:236
  49.8 6.7 %collective-permute-start.18 = (bf16[1,3,40,960]{3,2,1,0:T(8,128)(2,1)S(1)}, bf16[1,3,40,960]{3,2,1,0:T(8,128)(2,1)S(1)}, u32[]{:S(2)}, u32[]{:S(2)}) collective-permute-start(bf16[1,3,40,960]{3,2,1,0:T(8,128)(2,1)S(1)} %add.61), channel_id=1, source_target_pairs={{0,4},{1,5},{2,6},{3,7},{4,0},{5,1},{6,2},{7,3},{8,12},{9,13},{10,... | collective-permute-start | bytes 691208 | tf_op jit(solution)/shard_map/ppermute | solution.py:236
  50.9 6.2 %collective-permute-start.16 = (bf16[1,3,40,960]{3,2,1,0:T(8,128)(2,1)S(1)}, bf16[1,3,40,960]{3,2,1,0:T(8,128)(2,1)S(1)}, u32[]{:S(2)}, u32[]{:S(2)}) collective-permute-start(bf16[1,3,40,960]{3,2,1,0:T(8,128)(2,1)S(1)} %add.61), channel_id=1, source_target_pairs={{0,2},{1,3},{2,0},{3,1},{4,6},{5,7},{6,4},{7,5},{8,10},{9,11},{10,... | collective-permute-start | bytes 691208 | tf_op jit(solution)/shard_map/ppermute | solution.py:236
  51.9 4.6 %collective-permute-start.17 = (f32[3,8,960]{2,1,0:T(8,128)S(1)}, f32[3,8,960]{2,1,0:T(8,128)S(1)}, u32[]{:S(2)}, u32[]{:S(2)}) collective-permute-start(f32[3,8,960]{2,1,0:T(8,128)S(1)} %add.60), channel_id=1, source_target_pairs={{0,8},{1,9},{2,10},{3,11},{4,12},{5,13},{6,14},{7,15},{8,0},{9,1},... | collective-permute-start | bytes 276488 | tf_op jit(solution)/shard_map/ppermute | solution.py:236
  57.2 16.3 %collective-permute-start.23 = (bf16[3,3,40,960]{3,2,1,0:T(8,128)(2,1)S(1)}, bf16[3,3,40,960]{3,2,1,0:T(8,128)(2,1)S(1)}, u32[]{:S(2)}, u32[]{:S(2)}) collective-permute-start(bf16[3,3,40,960]{3,2,1,0:T(8,128)(2,1)S(1)} %pad_maximum_fusion.even_ref), channel_id=1, source_target_pairs={{0,1},{1,0},{2,3},{3,2},{4,5},{5,4},{6,7},{7,6},{8,9},{9,8},{10,11... | collective-permute-start | bytes 2073608 | tf_op jit(solution)/shard_map/ppermute | solution.py:236
  57.2 10.6 %collective-permute-start.24 = (bf16[1,3,40,960]{3,2,1,0:T(8,128)(2,1)S(1)}, bf16[1,3,40,960]{3,2,1,0:T(8,128)(2,1)S(1)}, u32[]{:S(2)}, u32[]{:S(2)}) collective-permute-start(bf16[1,3,40,960]{3,2,1,0:T(8,128)(2,1)S(1)} %collective-permute-done.16), channel_id=1, source_target_pairs={{0,4},{1,5},{2,6},{3,7},{4,0},{5,1},{6,2},{7,3},{8,12},{9,13},{10,... | collective-permute-start | bytes 691208 | tf_op jit(solution)/shard_map/ppermute | solution.py:236
  58.5 8.5 %collective-permute-start.19 = (f32[3,8,960]{2,1,0:T(8,128)S(1)}, f32[3,8,960]{2,1,0:T(8,128)S(1)}, u32[]{:S(2)}, u32[]{:S(2)}) collective-permute-start(f32[3,8,960]{2,1,0:T(8,128)S(1)} %add.62), channel_id=1, source_target_pairs={{0,16},{1,17},{2,18},{3,19},{4,20},{5,21},{6,22},{7,23},{8,24},{9,... | collective-permute-start | bytes 276488 | tf_op jit(solution)/shard_map/ppermute | solution.py:236
  61.7 11.8 %copy-start.4 = (s32[3]{0:T(128)S(1)}, s32[3]{0:T(128)}, u32[]{:S(2)}) copy-start(s32[3]{0:T(128)} %buckets_ref.1) | copy-start | bytes 40
  61.7 11.8 %copy-start.5 = (f32[4]{0:T(128)S(1)}, f32[4]{0:T(128)}, u32[]{:S(2)}) copy-start(f32[4]{0:T(128)} %rates_ref.1) | copy-start | bytes 52
  61.7 11.8 %copy-start.6 = (f32[4]{0:T(128)S(1)}, f32[4]{0:T(128)}, u32[]{:S(2)}) copy-start(f32[4]{0:T(128)} %betas_ref.1) | copy-start | bytes 52
  67.0 4.7 %collective-permute-start.21 = (f32[3,8,960]{2,1,0:T(8,128)S(1)}, f32[3,8,960]{2,1,0:T(8,128)S(1)}, u32[]{:S(2)}, u32[]{:S(2)}) collective-permute-start(f32[3,8,960]{2,1,0:T(8,128)S(1)} %add.63.r0_ref), channel_id=1, source_target_pairs={{0,2},{1,3},{2,0},{3,1},{4,6},{5,7},{6,4},{7,5},{8,10},{9,11},{10,... | collective-permute-start | bytes 276488 | tf_op jit(solution)/shard_map/ppermute | solution.py:236
  71.7 1.8 %collective-permute-start.25 = (bf16[1,3,40,960]{3,2,1,0:T(8,128)(2,1)S(1)}, bf16[1,3,40,960]{3,2,1,0:T(8,128)(2,1)S(1)}, u32[]{:S(2)}, u32[]{:S(2)}) collective-permute-start(bf16[1,3,40,960]{3,2,1,0:T(8,128)(2,1)S(1)} %collective-permute-done.24.far_ref), channel_id=1, source_target_pairs={{0,1},{1,0},{2,3},{3,2},{4,5},{5,4},{6,7},{7,6},{8,9},{9,8},{10,11... | collective-permute-start | bytes 691208 | tf_op jit(solution)/shard_map/ppermute | solution.py:236
  71.7 1.6 %collective-permute-start.20 = (f32[3,8,960]{2,1,0:T(8,128)S(1)}, f32[3,8,960]{2,1,0:T(8,128)S(1)}, u32[]{:S(2)}, u32[]{:S(2)}) collective-permute-start(f32[3,8,960]{2,1,0:T(8,128)S(1)} %add.63.r0_ref), channel_id=1, source_target_pairs={{0,1},{1,0},{2,3},{3,2},{4,5},{5,4},{6,7},{7,6},{8,9},{9,8},{10,11... | collective-permute-start | bytes 276488 | tf_op jit(solution)/shard_map/ppermute | solution.py:236
  72.2 1.3 %collective-permute-start.22 = (f32[3,8,960]{2,1,0:T(8,128)S(1)}, f32[3,8,960]{2,1,0:T(8,128)S(1)}, u32[]{:S(2)}, u32[]{:S(2)}) collective-permute-start(f32[3,8,960]{2,1,0:T(8,128)S(1)} %collective-permute-done.21.r2_ref), channel_id=1, source_target_pairs={{0,1},{1,0},{2,3},{3,2},{4,5},{5,4},{6,7},{7,6},{8,9},{9,8},{10,11... | collective-permute-start | bytes 276488 | tf_op jit(solution)/shard_map/ppermute | solution.py:236
  (1 other events, 8.0 us)

commit v11 on v10

--- a/solution.py
+++ b/solution.py
@@ -124,9 +124,8 @@
 
 
 def first_kernel(
-    owners_hbm, grad_hbm, error_hbm, q_hbm, mom_hbm,
-    mine_ref, other_ref, odd_ref,
-    owners_ref, grad_ref, error_ref, q_ref, mom_ref, left_ref, sems, mom_sems,
+    grad_hbm, error_hbm, q_hbm, mom_hbm, mine_ref, other_ref, odd_ref,
+    grad_ref, error_ref, q_ref, left_ref, sems, mom_sems,
 ):
     mats, rows, _ = grad_ref.shape
     rank = q_ref.shape[1]
@@ -137,48 +136,49 @@
         for m in range(mats)
     ]
     mom_copies = [
-        pltpu.make_async_copy(mom_hbm, mom_ref, mom_sems.at[0]),
-        pltpu.make_async_copy(owners_hbm, owners_ref, mom_sems.at[1]),
+        pltpu.make_async_copy(mom_hbm.at[slot, (2 * n + 1) ^ (me & 7)], odd_ref.at[n, slot], mom_sems.at[n, slot])
+        for n in range(4)
+        for slot in range(odd_ref.shape[1])
     ]
-    for copy in copies[0] + mom_copies:
+    for copy in copies[0] + copies[1] + mom_copies:
         copy.start()
-
-    odd_ref[...] = jnp.zeros(odd_ref.shape, BF16)
-    for m in range(mats):
-        if m + 1 < mats:
-            for copy in copies[m + 1]:
-                copy.start()
+    for m in range(mats):
         for copy in copies[m]:
             copy.wait()
+        if m == 0:
+            for copies_of in copies[2:]:
+                for copy in copies_of:
+                    copy.start()
         high, low = split(grad_ref[m] + error_ref[m].astype(F32))
         q_both = jnp.concatenate(split(q_ref[m]), 0)
         both = dot(q_both, high, ((1,), (1,))) + dot(q_both, low, ((1,), (1,)))
         left_ref[...] = (both[:rank] + both[rank:]).reshape(left_ref.shape)
         mine_ref[:, m * rows : (m + 1) * rows] = left_ref[me & 1]
         other_ref[:, m * rows : (m + 1) * rows] = left_ref[1 - (me & 1)]
-        if m == 0:
-            for copy in mom_copies:
-                copy.wait()
-            for i in range(mats):
-                slot = slot_of(owners_ref, i)
-
-                @pl.when(owners_ref[i] == me)
-                def _():
-                    for n in range(4):
-                        odd_ref[n, i] = mom_ref[slot, (2 * n + 1) ^ (me & 7)]
+    for copy in mom_copies:
+        copy.wait()
 
 
 def even_kernel(owners_ref, mom_ref, got_ref, *outs):
     me = lax.axis_index(AXES)
-    for n, out in enumerate(outs):
-        out[0] = got_ref[n]
     for i in range(owners_ref.shape[0]):
         slot = slot_of(owners_ref, i)
-
-        @pl.when(owners_ref[i] == me)
+        here, there = owners_ref[i] == me, owners_ref[i] == (me ^ 1)
+
+        @pl.when(here)
         def _():
             for n, out in enumerate(outs):
                 out[0, i] = mom_ref[slot, (2 * n) ^ (me & 7)]
+
+        @pl.when(there)
+        def _():
+            for n, out in enumerate(outs):
+                out[0, i] = got_ref[n, slot]
+
+        @pl.when(jnp.logical_not(here | there))
+        def _():
+            for out in outs:
+                out[0, i] = jnp.zeros(out.shape[2:], BF16)
 
 
 def step_kernel(
@@ -264,21 +264,19 @@
     momentum = momentum.reshape(slots, 8, piece, cols)
     mine, other, odd = pl.pallas_call(
         first_kernel,
-        in_specs=[pl.BlockSpec(memory_space=pltpu.HBM)] * 5,
-        out_shape=[sds((half, mats * rows), F32)] * 2 + [sds(old_shape(4), BF16)],
+        in_specs=[pl.BlockSpec(memory_space=pltpu.HBM)] * 4,
+        out_shape=[sds((half, mats * rows), F32)] * 2 + [sds((4, slots, piece, cols), BF16)],
         scratch_shapes=[
-            pltpu.SMEM((mats,), jnp.int32),
             pltpu.VMEM((mats, rows, cols), F32),
             pltpu.VMEM((mats, rows, cols), BF16),
             pltpu.VMEM((mats, rank, cols), F32),
-            pltpu.VMEM((slots, 8, piece, cols), BF16),
             pltpu.VMEM((2, half, rows), F32),
             pltpu.SemaphoreType.DMA((mats, 3)),
-            pltpu.SemaphoreType.DMA((2,)),
+            pltpu.SemaphoreType.DMA((4, slots)),
         ],
         compiler_params=pltpu.CompilerParams(vmem_limit_bytes=40 * 1024 * 1024),
         name="first",
-    )(*(pltpu.with_memory_space_constraint(v, pltpu.HBM) for v in (owners, grads, errs, q_t, momentum)))
+    )(*(pltpu.with_memory_space_constraint(v, pltpu.HBM) for v in (grads, errs, q_t, momentum)))
 
     got = swap(odd, 1)
     mine = mine + swap(other, 1)

time: 76.8 us -> 76.4 us (level)
  no operation moved by 1% of the time
where the time goes in v11:
time: 76.4 us; the launch traced here: 76.2 us
  waiting for transfers between devices  31.2 us (41%)
  starting transfers between devices  28 us (37%)
  Pallas kernels  15.8 us (21%)
  between operations  0.86 us (1%)
    ppermute x26, waiting for transfers between devices, exchange(): return lax.ppermute(value, AXES, [(d, d ^ mask) for d in range(count)])  31.2 us
    ppermute x26, starting transfers between devices, exchange(): return lax.ppermute(value, AXES, [(d, d ^ mask) for d in range(count)])  28 us
    pallas_call x1, Pallas kernels, on_device(): pl.pallas_call(first_kernel, in_specs=[pl.BlockSpec(memory_space=pltpu.HB...  5.12 us
    pallas_call x1, Pallas kernels, on_device(): pl.pallas_call(solve_kernel, grid=(1,), in_specs=[whole((half, mats * row...  3.38 us
    pallas_call x1, Pallas kernels, on_device(): pl.pallas_call(step_kernel, in_specs=[SMEM] * 4 + [VMEM] * 9, out_specs=[...  3.13 us
    pallas_call x1, Pallas kernels, on_device(): pl.pallas_call(error_kernel, grid=(mats,), in_specs=[grad_spec, grad_spec...  2.31 us
  transfers between devices with their start and end apart: 26, of which 18 were waited for; matrix products, arithmetic and copies ran while one was open for 0% of the time, Pallas kernels for 9%

profile of v11, /device:TPU:0, one launch (start us, length us, event | category | flops | bytes accessed | tf_op | source)
XLA Modules:
  0.0 76.2 jit_solution(2590233190576194761)
XLA Ops:
  0.7 5.1 %first.1 = (f32[16,960]{1,0:T(8,128)S(1)}, f32[16,960]{1,0:T(8,128)S(1)}, bf16[4,2,40,960]{3,2,1,0:T(8,128)(2,1)S(1)}) custom-call(f32[3,320,960]{2,1,0:T(8,128)} %bitcast.7, bf16[3,320,960]{2,1,0:T(8,128)(2,1)} %bitcast.10, f32[3,32,960]{2,1,0:T(8,128)} %bitcast.16, bf16[2,8,40,960]{3,2,1,0:T(8,128)(2,1)} %bitcast.13), custom_call_target="tpu_custom_call" | custom-call | tf_op jit(solution)/shard_map/first/pallas_call | solution.py:265
  6.4 1.7 %collective-permute-done = f32[16,960]{1,0:T(8,128)S(1)} collective-permute-done((f32[16,960]{1,0:T(8,128)S(1)}, f32[16,960]{1,0:T(8,128)S(1)}, u32[]{:S(2)}, u32[]{:S(2)}) %collective-permute-start) | collective-permute-done | bytes 61472 | tf_op jit(solution)/shard_map/ppermute | solution.py:236
  8.9 2.9 %collective-permute-start.4 = (bf16[1,3,40,960]{3,2,1,0:T(8,128)(2,1)S(1)}, bf16[1,3,40,960]{3,2,1,0:T(8,128)(2,1)S(1)}, u32[]{:S(2)}, u32[]{:S(2)}) collective-permute-start(bf16[1,3,40,960]{3,2,1,0:T(8,128)(2,1)S(1)} %get-tuple-element.37), channel_id=1, source_target_pairs={{0,2},{1,3},{2,0},{3,1},{4,6},{5,7},{6,4},{7,5},{8,10},{9,11},{10,... | collective-permute-start | bytes 691208 | tf_op jit(solution)/shard_map/ppermute | solution.py:236
  11.8 1.5 %collective-permute-start.5 = (bf16[1,3,40,960]{3,2,1,0:T(8,128)(2,1)S(1)}, bf16[1,3,40,960]{3,2,1,0:T(8,128)(2,1)S(1)}, u32[]{:S(2)}, u32[]{:S(2)}) collective-permute-start(bf16[1,3,40,960]{3,2,1,0:T(8,128)(2,1)S(1)} %get-tuple-element.38), channel_id=1, source_target_pairs={{0,4},{1,5},{2,6},{3,7},{4,0},{5,1},{6,2},{7,3},{8,12},{9,13},{10,... | collective-permute-start | bytes 691208 | tf_op jit(solution)/shard_map/ppermute | solution.py:236
  13.3 2.0 %collective-permute-start.1 = (f32[16,960]{1,0:T(8,128)S(1)}, f32[16,960]{1,0:T(8,128)S(1)}, u32[]{:S(2)}, u32[]{:S(2)}) collective-permute-start(f32[16,960]{1,0:T(8,128)S(1)} %add.48), channel_id=1, source_target_pairs={{0,8},{1,9},{2,10},{3,11},{4,12},{5,13},{6,14},{7,15},{8,0},{9,1},... | collective-permute-start | bytes 184328 | tf_op jit(solution)/shard_map/ppermute | solution.py:236
  15.4 2.2 %collective-permute-done.1 = f32[16,960]{1,0:T(8,128)S(1)} collective-permute-done((f32[16,960]{1,0:T(8,128)S(1)}, f32[16,960]{1,0:T(8,128)S(1)}, u32[]{:S(2)}, u32[]{:S(2)}) %collective-permute-start.1) | collective-permute-done | bytes 61472 | tf_op jit(solution)/shard_map/ppermute | solution.py:236
  17.6 3.1 %collective-permute-start.3 = (f32[16,960]{1,0:T(8,128)S(1)}, f32[16,960]{1,0:T(8,128)S(1)}, u32[]{:S(2)}, u32[]{:S(2)}) collective-permute-start(f32[16,960]{1,0:T(8,128)S(1)} %add.49), channel_id=1, source_target_pairs={{0,16},{1,17},{2,18},{3,19},{4,20},{5,21},{6,22},{7,23},{8,24},{9,... | collective-permute-start | bytes 184328 | tf_op jit(solution)/shard_map/ppermute | solution.py:236
  20.7 2.2 %collective-permute-done.3 = f32[16,960]{1,0:T(8,128)S(1)} collective-permute-done((f32[16,960]{1,0:T(8,128)S(1)}, f32[16,960]{1,0:T(8,128)S(1)}, u32[]{:S(2)}, u32[]{:S(2)}) %collective-permute-start.3) | collective-permute-done | bytes 61472 | tf_op jit(solution)/shard_map/ppermute | solution.py:236
  23.0 1.8 %collective-permute-done.5 = bf16[1,3,40,960]{3,2,1,0:T(8,128)(2,1)S(1)} collective-permute-done((bf16[1,3,40,960]{3,2,1,0:T(8,128)(2,1)S(1)}, bf16[1,3,40,960]{3,2,1,0:T(8,128)(2,1)S(1)}, u32[]{:S(2)}, u32[]{:S(2)}) %collective-permute-start.5) | collective-permute-done | bytes 230432 | tf_op jit(solution)/shard_map/ppermute | solution.py:236
  24.8 1.3 %collective-permute-start.7 = (f32[16,960]{1,0:T(8,128)S(1)}, f32[16,960]{1,0:T(8,128)S(1)}, u32[]{:S(2)}, u32[]{:S(2)}) collective-permute-start(f32[16,960]{1,0:T(8,128)S(1)} %add.50), channel_id=1, source_target_pairs={{0,2},{1,3},{2,0},{3,1},{4,6},{5,7},{6,4},{7,5},{8,10},{9,11},{10,... | collective-permute-start | bytes 184328 | tf_op jit(solution)/shard_map/ppermute | solution.py:236
  26.1 2.6 %collective-permute-start.12 = (bf16[1,3,40,960]{3,2,1,0:T(8,128)(2,1)S(1)}, bf16[1,3,40,960]{3,2,1,0:T(8,128)(2,1)S(1)}, u32[]{:S(2)}, u32[]{:S(2)}) collective-permute-start(bf16[1,3,40,960]{3,2,1,0:T(8,128)(2,1)S(1)} %add_add_fusion), channel_id=1, source_target_pairs={{0,16},{1,17},{2,18},{3,19},{4,20},{5,21},{6,22},{7,23},{8,24},{9,... | collective-permute-start | bytes 691208 | tf_op jit(solution)/shard_map/ppermute | solution.py:236
  29.2 1.6 %collective-permute-start.8 = (f32[16,960]{1,0:T(8,128)S(1)}, f32[16,960]{1,0:T(8,128)S(1)}, u32[]{:S(2)}, u32[]{:S(2)}) collective-permute-start(f32[16,960]{1,0:T(8,128)S(1)} %add.54), channel_id=1, source_target_pairs={{0,4},{1,5},{2,6},{3,7},{4,0},{5,1},{6,2},{7,3},{8,12},{9,13},{10,... | collective-permute-start | bytes 184328 | tf_op jit(solution)/shard_map/ppermute | solution.py:236
  30.8 2.7 %collective-permute-done.8 = f32[16,960]{1,0:T(8,128)S(1)} collective-permute-done((f32[16,960]{1,0:T(8,128)S(1)}, f32[16,960]{1,0:T(8,128)S(1)}, u32[]{:S(2)}, u32[]{:S(2)}) %collective-permute-start.8) | collective-permute-done | bytes 61472 | tf_op jit(solution)/shard_map/ppermute | solution.py:236
  33.6 1.2 %collective-permute-done.9.other_ref = f32[16,960]{1,0:T(8,128)S(1)} collective-permute-done((f32[16,960]{1,0:T(8,128)S(1)}, f32[16,960]{1,0:T(8,128)S(1)}, u32[]{:S(2)}, u32[]{:S(2)}) %collective-permute-start.9) | collective-permute-done | bytes 61472 | tf_op jit(solution)/shard_map/ppermute | solution.py:236
  34.8 1.2 %right.1 = (f32[3,32,960]{2,1,0:T(8,128)S(1)}, f32[3,8,960]{2,1,0:T(8,128)S(1)}, f32[3,8,960]{2,1,0:T(8,128)S(1)}, f32[3,8,960]{2,1,0:T(8,128)S(1)}, f32[3,8,960]{2,1,0:T(8,128)S(1)}) custom-call(f32[16,960]{1,0:T(8,128)S(1)} %add.55.mine_ref, f32[16,960]{1,0:T(8,128)S(1)} %collective-permute-done.9.other_ref, f32[3,320,960]{2,1,0:T(8,128)S(1)} %bitcast.8, ...), custom_call_target="tpu_custom_call" | custom-call | tf_op jit(solution)/shard_map/right/pallas_call | solution.py:303
  36.6 0.8 %collective-permute-done.10 = f32[3,8,960]{2,1,0:T(8,128)S(1)} collective-permute-done((f32[3,8,960]{2,1,0:T(8,128)S(1)}, f32[3,8,960]{2,1,0:T(8,128)S(1)}, u32[]{:S(2)}, u32[]{:S(2)}) %collective-permute-start.10) | collective-permute-done | bytes 92192 | tf_op jit(solution)/shard_map/ppermute | solution.py:236
  37.6 1.6 %collective-permute-done.12 = bf16[1,3,40,960]{3,2,1,0:T(8,128)(2,1)S(1)} collective-permute-done((bf16[1,3,40,960]{3,2,1,0:T(8,128)(2,1)S(1)}, bf16[1,3,40,960]{3,2,1,0:T(8,128)(2,1)S(1)}, u32[]{:S(2)}, u32[]{:S(2)}) %collective-permute-start.12) | collective-permute-done | bytes 230432 | tf_op jit(solution)/shard_map/ppermute | solution.py:236
  40.6 4.0 %collective-permute-done.13 = f32[3,8,960]{2,1,0:T(8,128)S(1)} collective-permute-done((f32[3,8,960]{2,1,0:T(8,128)S(1)}, f32[3,8,960]{2,1,0:T(8,128)S(1)}, u32[]{:S(2)}, u32[]{:S(2)}) %collective-permute-start.13) | collective-permute-done | bytes 92192 | tf_op jit(solution)/shard_map/ppermute | solution.py:236
  44.6 1.1 %collective-permute-start.14 = (f32[3,8,960]{2,1,0:T(8,128)S(1)}, f32[3,8,960]{2,1,0:T(8,128)S(1)}, u32[]{:S(2)}, u32[]{:S(2)}) collective-permute-start(f32[3,8,960]{2,1,0:T(8,128)S(1)} %add.59), channel_id=1, source_target_pairs={{0,4},{1,5},{2,6},{3,7},{4,0},{5,1},{6,2},{7,3},{8,12},{9,13},{10,... | collective-permute-start | bytes 276488 | tf_op jit(solution)/shard_map/ppermute | solution.py:236
  45.7 3.4 %solve.1.w_ref = bf16[3,320,96]{2,1,0:T(8,128)(2,1)S(1)} custom-call(f32[16,960]{1,0:T(8,128)S(1)} %add.55.mine_ref, f32[16,960]{1,0:T(8,128)S(1)} %collective-permute-done.9.other_ref), custom_call_target="tpu_custom_call" | custom-call | bytes 1048576 | tf_op jit(solution)/shard_map/solve/pallas_call | solution.py:313
  49.4 1.1 %collective-permute-start.18 = (bf16[1,3,40,960]{3,2,1,0:T(8,128)(2,1)S(1)}, bf16[1,3,40,960]{3,2,1,0:T(8,128)(2,1)S(1)}, u32[]{:S(2)}, u32[]{:S(2)}) collective-permute-start(bf16[1,3,40,960]{3,2,1,0:T(8,128)(2,1)S(1)} %add.61), channel_id=1, source_target_pairs={{0,4},{1,5},{2,6},{3,7},{4,0},{5,1},{6,2},{7,3},{8,12},{9,13},{10,... | collective-permute-start | bytes 691208 | tf_op jit(solution)/shard_map/ppermute | solution.py:236
  50.5 1.0 %collective-permute-start.16 = (bf16[1,3,40,960]{3,2,1,0:T(8,128)(2,1)S(1)}, bf16[1,3,40,960]{3,2,1,0:T(8,128)(2,1)S(1)}, u32[]{:S(2)}, u32[]{:S(2)}) collective-permute-start(bf16[1,3,40,960]{3,2,1,0:T(8,128)(2,1)S(1)} %add.61), channel_id=1, source_target_pairs={{0,2},{1,3},{2,0},{3,1},{4,6},{5,7},{6,4},{7,5},{8,10},{9,11},{10,... | collective-permute-start | bytes 691208 | tf_op jit(solution)/shard_map/ppermute | solution.py:236
  51.4 1.4 %collective-permute-start.17 = (f32[3,8,960]{2,1,0:T(8,128)S(1)}, f32[3,8,960]{2,1,0:T(8,128)S(1)}, u32[]{:S(2)}, u32[]{:S(2)}) collective-permute-start(f32[3,8,960]{2,1,0:T(8,128)S(1)} %add.60), channel_id=1, source_target_pairs={{0,8},{1,9},{2,10},{3,11},{4,12},{5,13},{6,14},{7,15},{8,0},{9,1},... | collective-permute-start | bytes 276488 | tf_op jit(solution)/shard_map/ppermute | solution.py:236
  52.8 3.3 %collective-permute-done.17 = f32[3,8,960]{2,1,0:T(8,128)S(1)} collective-permute-done((f32[3,8,960]{2,1,0:T(8,128)S(1)}, f32[3,8,960]{2,1,0:T(8,128)S(1)}, u32[]{:S(2)}, u32[]{:S(2)}) %collective-permute-start.17) | collective-permute-done | bytes 92192 | tf_op jit(solution)/shard_map/ppermute | solution.py:236
  56.8 1.2 %collective-permute-start.24 = (bf16[1,3,40,960]{3,2,1,0:T(8,128)(2,1)S(1)}, bf16[1,3,40,960]{3,2,1,0:T(8,128)(2,1)S(1)}, u32[]{:S(2)}, u32[]{:S(2)}) collective-permute-start(bf16[1,3,40,960]{3,2,1,0:T(8,128)(2,1)S(1)} %collective-permute-done.16), channel_id=1, source_target_pairs={{0,4},{1,5},{2,6},{3,7},{4,0},{5,1},{6,2},{7,3},{8,12},{9,13},{10,... | collective-permute-start | bytes 691208 | tf_op jit(solution)/shard_map/ppermute | solution.py:236
  58.1 3.2 %collective-permute-start.19 = (f32[3,8,960]{2,1,0:T(8,128)S(1)}, f32[3,8,960]{2,1,0:T(8,128)S(1)}, u32[]{:S(2)}, u32[]{:S(2)}) collective-permute-start(f32[3,8,960]{2,1,0:T(8,128)S(1)} %add.62), channel_id=1, source_target_pairs={{0,16},{1,17},{2,18},{3,19},{4,20},{5,21},{6,22},{7,23},{8,24},{9,... | collective-permute-start | bytes 276488 | tf_op jit(solution)/shard_map/ppermute | solution.py:236
  61.3 2.3 %errors.1 = bf16[3,320,960]{2,1,0:T(8,128)(2,1)} custom-call(f32[3,320,960]{2,1,0:T(8,128)S(1)} %bitcast.9, bf16[3,320,960]{2,1,0:T(8,128)(2,1)S(1)} %bitcast.12, bf16[3,320,96]{2,1,0:T(8,128)(2,1)S(1)} %solve.1.w_ref, f32[3,32,960]{2,1,0:T(8,128)S(1)} %get-tuple-element.54.all_ref), custom_call_target="tpu_custom_call" | custom-call | bytes 12582912 | tf_op jit(solution)/shard_map/errors/pallas_call | solution.py:343
  63.6 2.9 %collective-permute-done.19 = f32[3,8,960]{2,1,0:T(8,128)S(1)} collective-permute-done((f32[3,8,960]{2,1,0:T(8,128)S(1)}, f32[3,8,960]{2,1,0:T(8,128)S(1)}, u32[]{:S(2)}, u32[]{:S(2)}) %collective-permute-start.19) | collective-permute-done | bytes 92192 | tf_op jit(solution)/shard_map/ppermute | solution.py:236
  66.5 0.8 %collective-permute-start.21 = (f32[3,8,960]{2,1,0:T(8,128)S(1)}, f32[3,8,960]{2,1,0:T(8,128)S(1)}, u32[]{:S(2)}, u32[]{:S(2)}) collective-permute-start(f32[3,8,960]{2,1,0:T(8,128)S(1)} %add.63.r0_ref), channel_id=1, source_target_pairs={{0,2},{1,3},{2,0},{3,1},{4,6},{5,7},{6,4},{7,5},{8,10},{9,11},{10,... | collective-permute-start | bytes 276488 | tf_op jit(solution)/shard_map/ppermute | solution.py:236
  67.4 3.9 %collective-permute-done.21.r2_ref = f32[3,8,960]{2,1,0:T(8,128)S(1)} collective-permute-done((f32[3,8,960]{2,1,0:T(8,128)S(1)}, f32[3,8,960]{2,1,0:T(8,128)S(1)}, u32[]{:S(2)}, u32[]{:S(2)}) %collective-permute-start.21) | collective-permute-done | bytes 92192 | tf_op jit(solution)/shard_map/ppermute | solution.py:236
  71.8 1.1 %collective-permute-done.20.r1_ref = f32[3,8,960]{2,1,0:T(8,128)S(1)} collective-permute-done((f32[3,8,960]{2,1,0:T(8,128)S(1)}, f32[3,8,960]{2,1,0:T(8,128)S(1)}, u32[]{:S(2)}, u32[]{:S(2)}) %collective-permute-start.20) | collective-permute-done | bytes 92192 | tf_op jit(solution)/shard_map/ppermute | solution.py:236
  73.1 3.1 %step.1 = (bf16[3,8,40,960]{3,2,1,0:T(8,128)(2,1)}, bf16[2,8,40,960]{3,2,1,0:T(8,128)(2,1)}) custom-call(s32[3]{0:T(128)S(1)} %copy-done.3, s32[3]{0:T(128)S(1)} %copy-done.4, f32[4]{0:T(128)S(1)} %copy-done.5, f32[4]{0:T(128)S(1)} %copy-done.6, f32[3,8,960]{2,1,0:T(8,128)S(1)} %add.63.r0_ref, f32[3,8,960]{2,1,0:T(8,128)S(1)} %collective-permute-done.20.r1_ref, ...), custom_call_target="tpu_custom_call" | custom-call | tf_op jit(solution)/shard_map/step/pallas_call | solution.py:362
  (55 shorter events, 5.8 us)
Async XLA Ops:
  0.6 7.5 %copy-start.2 = (bf16[2,320,960]{2,1,0:T(8,128)(2,1)S(1)}, bf16[2,320,960]{2,1,0:T(8,128)(2,1)}, u32[]{:S(2)}) copy-start(bf16[2,320,960]{2,1,0:T(8,128)(2,1)} %param.15) | copy-start | bytes 3686404
  0.7 34.2 %copy-start.1 = (bf16[1,3,320,960]{3,2,1,0:T(8,128)(2,1)S(1)}, bf16[1,3,320,960]{3,2,1,0:T(8,128)(2,1)}, u32[]{:S(2)}) copy-start(bf16[1,3,320,960]{3,2,1,0:T(8,128)(2,1)} %param.9) | copy-start | bytes 5529604
  5.8 2.4 %collective-permute-start.2 = (bf16[4,2,40,960]{3,2,1,0:T(8,128)(2,1)S(1)}, bf16[4,2,40,960]{3,2,1,0:T(8,128)(2,1)S(1)}, u32[]{:S(2)}, u32[]{:S(2)}) collective-permute-start(bf16[4,2,40,960]{3,2,1,0:T(8,128)(2,1)S(1)} %get-tuple-element.34), channel_id=1, source_target_pairs={{0,1},{1,0},{2,3},{3,2},{4,5},{5,4},{6,7},{7,6},{8,9},{9,8},{10,11... | collective-permute-start | bytes 1843208 | tf_op jit(solution)/shard_map/ppermute | solution.py:236
  6.3 1.8 %collective-permute-start = (f32[16,960]{1,0:T(8,128)S(1)}, f32[16,960]{1,0:T(8,128)S(1)}, u32[]{:S(2)}, u32[]{:S(2)}) collective-permute-start(f32[16,960]{1,0:T(8,128)S(1)} %get-tuple-element.33), channel_id=1, source_target_pairs={{0,1},{1,0},{2,3},{3,2},{4,5},{5,4},{6,7},{7,6},{8,9},{9,8},{10,11... | collective-permute-start | bytes 184328 | tf_op jit(solution)/shard_map/ppermute | solution.py:236
  8.1 26.7 %copy-start = (f32[1,3,320,960]{3,2,1,0:T(8,128)S(1)}, f32[1,3,320,960]{3,2,1,0:T(8,128)}, u32[]{:S(2)}) copy-start(f32[1,3,320,960]{3,2,1,0:T(8,128)} %param.8) | copy-start | bytes 11059204
  8.9 14.1 %collective-permute-start.4 = (bf16[1,3,40,960]{3,2,1,0:T(8,128)(2,1)S(1)}, bf16[1,3,40,960]{3,2,1,0:T(8,128)(2,1)S(1)}, u32[]{:S(2)}, u32[]{:S(2)}) collective-permute-start(bf16[1,3,40,960]{3,2,1,0:T(8,128)(2,1)S(1)} %get-tuple-element.37), channel_id=1, source_target_pairs={{0,2},{1,3},{2,0},{3,1},{4,6},{5,7},{6,4},{7,5},{8,10},{9,11},{10,... | collective-permute-start | bytes 691208 | tf_op jit(solution)/shard_map/ppermute | solution.py:236
  11.8 13.0 %collective-permute-start.5 = (bf16[1,3,40,960]{3,2,1,0:T(8,128)(2,1)S(1)}, bf16[1,3,40,960]{3,2,1,0:T(8,128)(2,1)S(1)}, u32[]{:S(2)}, u32[]{:S(2)}) collective-permute-start(bf16[1,3,40,960]{3,2,1,0:T(8,128)(2,1)S(1)} %get-tuple-element.38), channel_id=1, source_target_pairs={{0,4},{1,5},{2,6},{3,7},{4,0},{5,1},{6,2},{7,3},{8,12},{9,13},{10,... | collective-permute-start | bytes 691208 | tf_op jit(solution)/shard_map/ppermute | solution.py:236
  13.3 11.5 %collective-permute-start.6 = (bf16[1,3,40,960]{3,2,1,0:T(8,128)(2,1)S(1)}, bf16[1,3,40,960]{3,2,1,0:T(8,128)(2,1)S(1)}, u32[]{:S(2)}, u32[]{:S(2)}) collective-permute-start(bf16[1,3,40,960]{3,2,1,0:T(8,128)(2,1)S(1)} %get-tuple-element.39), channel_id=1, source_target_pairs={{0,6},{1,7},{2,4},{3,5},{4,2},{5,3},{6,0},{7,1},{8,14},{9,15},{10,... | collective-permute-start | bytes 691208 | tf_op jit(solution)/shard_map/ppermute | solution.py:236
  13.3 4.3 %collective-permute-start.1 = (f32[16,960]{1,0:T(8,128)S(1)}, f32[16,960]{1,0:T(8,128)S(1)}, u32[]{:S(2)}, u32[]{:S(2)}) collective-permute-start(f32[16,960]{1,0:T(8,128)S(1)} %add.48), channel_id=1, source_target_pairs={{0,8},{1,9},{2,10},{3,11},{4,12},{5,13},{6,14},{7,15},{8,0},{9,1},... | collective-permute-start | bytes 184328 | tf_op jit(solution)/shard_map/ppermute | solution.py:236
  17.6 5.3 %collective-permute-start.3 = (f32[16,960]{1,0:T(8,128)S(1)}, f32[16,960]{1,0:T(8,128)S(1)}, u32[]{:S(2)}, u32[]{:S(2)}) collective-permute-start(f32[16,960]{1,0:T(8,128)S(1)} %add.49), channel_id=1, source_target_pairs={{0,16},{1,17},{2,18},{3,19},{4,20},{5,21},{6,22},{7,23},{8,24},{9,... | collective-permute-start | bytes 184328 | tf_op jit(solution)/shard_map/ppermute | solution.py:236
  24.8 4.3 %collective-permute-start.7 = (f32[16,960]{1,0:T(8,128)S(1)}, f32[16,960]{1,0:T(8,128)S(1)}, u32[]{:S(2)}, u32[]{:S(2)}) collective-permute-start(f32[16,960]{1,0:T(8,128)S(1)} %add.50), channel_id=1, source_target_pairs={{0,2},{1,3},{2,0},{3,1},{4,6},{5,7},{6,4},{7,5},{8,10},{9,11},{10,... | collective-permute-start | bytes 184328 | tf_op jit(solution)/shard_map/ppermute | solution.py:236
  26.1 13.1 %collective-permute-start.12 = (bf16[1,3,40,960]{3,2,1,0:T(8,128)(2,1)S(1)}, bf16[1,3,40,960]{3,2,1,0:T(8,128)(2,1)S(1)}, u32[]{:S(2)}, u32[]{:S(2)}) collective-permute-start(bf16[1,3,40,960]{3,2,1,0:T(8,128)(2,1)S(1)} %add_add_fusion), channel_id=1, source_target_pairs={{0,16},{1,17},{2,18},{3,19},{4,20},{5,21},{6,22},{7,23},{8,24},{9,... | collective-permute-start | bytes 691208 | tf_op jit(solution)/shard_map/ppermute | solution.py:236
  29.2 4.3 %collective-permute-start.8 = (f32[16,960]{1,0:T(8,128)S(1)}, f32[16,960]{1,0:T(8,128)S(1)}, u32[]{:S(2)}, u32[]{:S(2)}) collective-permute-start(f32[16,960]{1,0:T(8,128)S(1)} %add.54), channel_id=1, source_target_pairs={{0,4},{1,5},{2,6},{3,7},{4,0},{5,1},{6,2},{7,3},{8,12},{9,13},{10,... | collective-permute-start | bytes 184328 | tf_op jit(solution)/shard_map/ppermute | solution.py:236
  33.5 1.3 %collective-permute-start.9 = (f32[16,960]{1,0:T(8,128)S(1)}, f32[16,960]{1,0:T(8,128)S(1)}, u32[]{:S(2)}, u32[]{:S(2)}) collective-permute-start(f32[16,960]{1,0:T(8,128)S(1)} %add.55.mine_ref), channel_id=1, source_target_pairs={{0,1},{1,0},{2,3},{3,2},{4,5},{5,4},{6,7},{7,6},{8,9},{9,8},{10,11... | collective-permute-start | bytes 184328 | tf_op jit(solution)/shard_map/ppermute | solution.py:236
  36.0 1.4 %collective-permute-start.10 = (f32[3,8,960]{2,1,0:T(8,128)S(1)}, f32[3,8,960]{2,1,0:T(8,128)S(1)}, u32[]{:S(2)}, u32[]{:S(2)}) collective-permute-start(f32[3,8,960]{2,1,0:T(8,128)S(1)} %get-tuple-element.44), channel_id=1, source_target_pairs={{0,1},{1,0},{2,3},{3,2},{4,5},{5,4},{6,7},{7,6},{8,9},{9,8},{10,11... | collective-permute-start | bytes 276488 | tf_op jit(solution)/shard_map/ppermute | solution.py:236
  36.3 1.3 %collective-permute-start.11 = (f32[3,8,960]{2,1,0:T(8,128)S(1)}, f32[3,8,960]{2,1,0:T(8,128)S(1)}, u32[]{:S(2)}, u32[]{:S(2)}) collective-permute-start(f32[3,8,960]{2,1,0:T(8,128)S(1)} %get-tuple-element.46), channel_id=1, source_target_pairs={{0,1},{1,0},{2,3},{3,2},{4,5},{5,4},{6,7},{7,6},{8,9},{9,8},{10,11... | collective-permute-start | bytes 276488 | tf_op jit(solution)/shard_map/ppermute | solution.py:236
  39.2 10.1 %collective-permute-start.15 = (bf16[1,3,40,960]{3,2,1,0:T(8,128)(2,1)S(1)}, bf16[1,3,40,960]{3,2,1,0:T(8,128)(2,1)S(1)}, u32[]{:S(2)}, u32[]{:S(2)}) collective-permute-start(bf16[1,3,40,960]{3,2,1,0:T(8,128)(2,1)S(1)} %add.58), channel_id=1, source_target_pairs={{0,8},{1,9},{2,10},{3,11},{4,12},{5,13},{6,14},{7,15},{8,0},{9,1},... | collective-permute-start | bytes 691208 | tf_op jit(solution)/shard_map/ppermute | solution.py:236
  40.0 4.6 %collective-permute-start.13 = (f32[3,8,960]{2,1,0:T(8,128)S(1)}, f32[3,8,960]{2,1,0:T(8,128)S(1)}, u32[]{:S(2)}, u32[]{:S(2)}) collective-permute-start(f32[3,8,960]{2,1,0:T(8,128)S(1)} %add.57), channel_id=1, source_target_pairs={{0,2},{1,3},{2,0},{3,1},{4,6},{5,7},{6,4},{7,5},{8,10},{9,11},{10,... | collective-permute-start | bytes 276488 | tf_op jit(solution)/shard_map/ppermute | solution.py:236
  44.6 4.7 %collective-permute-start.14 = (f32[3,8,960]{2,1,0:T(8,128)S(1)}, f32[3,8,960]{2,1,0:T(8,128)S(1)}, u32[]{:S(2)}, u32[]{:S(2)}) collective-permute-start(f32[3,8,960]{2,1,0:T(8,128)S(1)} %add.59), channel_id=1, source_target_pairs={{0,4},{1,5},{2,6},{3,7},{4,0},{5,1},{6,2},{7,3},{8,12},{9,13},{10,... | collective-permute-start | bytes 276488 | tf_op jit(solution)/shard_map/ppermute | solution.py:236
  49.4 6.7 %collective-permute-start.18 = (bf16[1,3,40,960]{3,2,1,0:T(8,128)(2,1)S(1)}, bf16[1,3,40,960]{3,2,1,0:T(8,128)(2,1)S(1)}, u32[]{:S(2)}, u32[]{:S(2)}) collective-permute-start(bf16[1,3,40,960]{3,2,1,0:T(8,128)(2,1)S(1)} %add.61), channel_id=1, source_target_pairs={{0,4},{1,5},{2,6},{3,7},{4,0},{5,1},{6,2},{7,3},{8,12},{9,13},{10,... | collective-permute-start | bytes 691208 | tf_op jit(solution)/shard_map/ppermute | solution.py:236
  50.5 6.2 %collective-permute-start.16 = (bf16[1,3,40,960]{3,2,1,0:T(8,128)(2,1)S(1)}, bf16[1,3,40,960]{3,2,1,0:T(8,128)(2,1)S(1)}, u32[]{:S(2)}, u32[]{:S(2)}) collective-permute-start(bf16[1,3,40,960]{3,2,1,0:T(8,128)(2,1)S(1)} %add.61), channel_id=1, source_target_pairs={{0,2},{1,3},{2,0},{3,1},{4,6},{5,7},{6,4},{7,5},{8,10},{9,11},{10,... | collective-permute-start | bytes 691208 | tf_op jit(solution)/shard_map/ppermute | solution.py:236
  51.4 4.6 %collective-permute-start.17 = (f32[3,8,960]{2,1,0:T(8,128)S(1)}, f32[3,8,960]{2,1,0:T(8,128)S(1)}, u32[]{:S(2)}, u32[]{:S(2)}) collective-permute-start(f32[3,8,960]{2,1,0:T(8,128)S(1)} %add.60), channel_id=1, source_target_pairs={{0,8},{1,9},{2,10},{3,11},{4,12},{5,13},{6,14},{7,15},{8,0},{9,1},... | collective-permute-start | bytes 276488 | tf_op jit(solution)/shard_map/ppermute | solution.py:236
  56.8 16.3 %collective-permute-start.23 = (bf16[3,3,40,960]{3,2,1,0:T(8,128)(2,1)S(1)}, bf16[3,3,40,960]{3,2,1,0:T(8,128)(2,1)S(1)}, u32[]{:S(2)}, u32[]{:S(2)}) collective-permute-start(bf16[3,3,40,960]{3,2,1,0:T(8,128)(2,1)S(1)} %pad_maximum_fusion.even_ref), channel_id=1, source_target_pairs={{0,1},{1,0},{2,3},{3,2},{4,5},{5,4},{6,7},{7,6},{8,9},{9,8},{10,11... | collective-permute-start | bytes 2073608 | tf_op jit(solution)/shard_map/ppermute | solution.py:236
  56.8 10.6 %collective-permute-start.24 = (bf16[1,3,40,960]{3,2,1,0:T(8,128)(2,1)S(1)}, bf16[1,3,40,960]{3,2,1,0:T(8,128)(2,1)S(1)}, u32[]{:S(2)}, u32[]{:S(2)}) collective-permute-start(bf16[1,3,40,960]{3,2,1,0:T(8,128)(2,1)S(1)} %collective-permute-done.16), channel_id=1, source_target_pairs={{0,4},{1,5},{2,6},{3,7},{4,0},{5,1},{6,2},{7,3},{8,12},{9,13},{10,... | collective-permute-start | bytes 691208 | tf_op jit(solution)/shard_map/ppermute | solution.py:236
  58.1 8.5 %collective-permute-start.19 = (f32[3,8,960]{2,1,0:T(8,128)S(1)}, f32[3,8,960]{2,1,0:T(8,128)S(1)}, u32[]{:S(2)}, u32[]{:S(2)}) collective-permute-start(f32[3,8,960]{2,1,0:T(8,128)S(1)} %add.62), channel_id=1, source_target_pairs={{0,16},{1,17},{2,18},{3,19},{4,20},{5,21},{6,22},{7,23},{8,24},{9,... | collective-permute-start | bytes 276488 | tf_op jit(solution)/shard_map/ppermute | solution.py:236
  61.3 11.8 %copy-start.4 = (s32[3]{0:T(128)S(1)}, s32[3]{0:T(128)}, u32[]{:S(2)}) copy-start(s32[3]{0:T(128)} %buckets_ref.1) | copy-start | bytes 40
  61.3 11.8 %copy-start.5 = (f32[4]{0:T(128)S(1)}, f32[4]{0:T(128)}, u32[]{:S(2)}) copy-start(f32[4]{0:T(128)} %rates_ref.1) | copy-start | bytes 52
  61.3 11.8 %copy-start.6 = (f32[4]{0:T(128)S(1)}, f32[4]{0:T(128)}, u32[]{:S(2)}) copy-start(f32[4]{0:T(128)} %betas_ref.1) | copy-start | bytes 52
  66.5 4.7 %collective-permute-start.21 = (f32[3,8,960]{2,1,0:T(8,128)S(1)}, f32[3,8,960]{2,1,0:T(8,128)S(1)}, u32[]{:S(2)}, u32[]{:S(2)}) collective-permute-start(f32[3,8,960]{2,1,0:T(8,128)S(1)} %add.63.r0_ref), channel_id=1, source_target_pairs={{0,2},{1,3},{2,0},{3,1},{4,6},{5,7},{6,4},{7,5},{8,10},{9,11},{10,... | collective-permute-start | bytes 276488 | tf_op jit(solution)/shard_map/ppermute | solution.py:236
  71.3 1.8 %collective-permute-start.25 = (bf16[1,3,40,960]{3,2,1,0:T(8,128)(2,1)S(1)}, bf16[1,3,40,960]{3,2,1,0:T(8,128)(2,1)S(1)}, u32[]{:S(2)}, u32[]{:S(2)}) collective-permute-start(bf16[1,3,40,960]{3,2,1,0:T(8,128)(2,1)S(1)} %collective-permute-done.24.far_ref), channel_id=1, source_target_pairs={{0,1},{1,0},{2,3},{3,2},{4,5},{5,4},{6,7},{7,6},{8,9},{9,8},{10,11... | collective-permute-start | bytes 691208 | tf_op jit(solution)/shard_map/ppermute | solution.py:236
  71.3 1.6 %collective-permute-start.20 = (f32[3,8,960]{2,1,0:T(8,128)S(1)}, f32[3,8,960]{2,1,0:T(8,128)S(1)}, u32[]{:S(2)}, u32[]{:S(2)}) collective-permute-start(f32[3,8,960]{2,1,0:T(8,128)S(1)} %add.63.r0_ref), channel_id=1, source_target_pairs={{0,1},{1,0},{2,3},{3,2},{4,5},{5,4},{6,7},{7,6},{8,9},{9,8},{10,11... | collective-permute-start | bytes 276488 | tf_op jit(solution)/shard_map/ppermute | solution.py:236
  71.8 1.3 %collective-permute-start.22 = (f32[3,8,960]{2,1,0:T(8,128)S(1)}, f32[3,8,960]{2,1,0:T(8,128)S(1)}, u32[]{:S(2)}, u32[]{:S(2)}) collective-permute-start(f32[3,8,960]{2,1,0:T(8,128)S(1)} %collective-permute-done.21.r2_ref), channel_id=1, source_target_pairs={{0,1},{1,0},{2,3},{3,2},{4,5},{5,4},{6,7},{7,6},{8,9},{9,8},{10,11... | collective-permute-start | bytes 276488 | tf_op jit(solution)/shard_map/ppermute | solution.py:236
  (1 other events, 7.5 us)

commit v12 on v11

--- a/solution.py
+++ b/solution.py
@@ -124,8 +124,8 @@
 
 
 def first_kernel(
-    grad_hbm, error_hbm, q_hbm, mom_hbm, mine_ref, other_ref, odd_ref,
-    grad_ref, error_ref, q_ref, left_ref, sems, mom_sems,
+    grad_hbm, error_hbm, q_hbm, mom_hbm, mine_ref, other_ref, odd_ref, grad_ref, error_ref,
+    q_ref, left_ref, sems, mom_sems,
 ):
     mats, rows, _ = grad_ref.shape
     rank = q_ref.shape[1]
@@ -262,13 +262,13 @@
         return exchange(value, mask, count)
 
     momentum = momentum.reshape(slots, 8, piece, cols)
-    mine, other, odd = pl.pallas_call(
+    mine, other, odd, grads, errs = pl.pallas_call(
         first_kernel,
         in_specs=[pl.BlockSpec(memory_space=pltpu.HBM)] * 4,
-        out_shape=[sds((half, mats * rows), F32)] * 2 + [sds((4, slots, piece, cols), BF16)],
+        out_specs=[VMEM] * 5,
+        out_shape=[sds((half, mats * rows), F32)] * 2
+        + [sds((4, slots, piece, cols), BF16), sds((mats, rows, cols), F32), sds((mats, rows, cols), BF16)],
         scratch_shapes=[
-            pltpu.VMEM((mats, rows, cols), F32),
-            pltpu.VMEM((mats, rows, cols), BF16),
             pltpu.VMEM((mats, rank, cols), F32),
             pltpu.VMEM((2, half, rows), F32),
             pltpu.SemaphoreType.DMA((mats, 3)),

time: 76.4 us -> 75.9 us (level)
  no operation moved by 1% of the time
where the time goes in v12:
time: 75.9 us; the launch traced here: 75.6 us
  waiting for transfers between devices  31.2 us (41%)
  starting transfers between devices  28 us (37%)
  Pallas kernels  15.2 us (20%)
  between operations  0.84 us (1%)
    ppermute x26, waiting for transfers between devices, exchange(): return lax.ppermute(value, AXES, [(d, d ^ mask) for d in range(count)])  31.2 us
    ppermute x26, starting transfers between devices, exchange(): return lax.ppermute(value, AXES, [(d, d ^ mask) for d in range(count)])  28 us
    pallas_call x1, Pallas kernels, on_device(): pl.pallas_call(first_kernel, in_specs=[pl.BlockSpec(memory_space=pltpu.HB...  4.54 us
    pallas_call x1, Pallas kernels, on_device(): pl.pallas_call(solve_kernel, grid=(1,), in_specs=[whole((half, mats * row...  3.38 us
    pallas_call x1, Pallas kernels, on_device(): pl.pallas_call(step_kernel, in_specs=[SMEM] * 4 + [VMEM] * 9, out_specs=[...  3.13 us
    pallas_call x1, Pallas kernels, on_device(): pl.pallas_call(error_kernel, grid=(mats,), in_specs=[grad_spec, grad_spec...  2.31 us
  transfers between devices with their start and end apart: 26, of which 18 were waited for; matrix products, arithmetic and copies ran while one was open for 0% of the time, Pallas kernels for 9%

profile of v12, /device:TPU:0, one launch (start us, length us, event | category | flops | bytes accessed | tf_op | source)
XLA Modules:
  0.0 75.6 jit_solution(6875565387775122903)
XLA Ops:
  0.7 4.5 %first.1 = (f32[16,960]{1,0:T(8,128)S(1)}, f32[16,960]{1,0:T(8,128)S(1)}, bf16[4,2,40,960]{3,2,1,0:T(8,128)(2,1)S(1)}, f32[3,320,960]{2,1,0:T(8,128)S(1)}, bf16[3,320,960]{2,1,0:T(8,128)(2,1)S(1)}) custom-call(f32[3,320,960]{2,1,0:T(8,128)} %bitcast.9, bf16[3,320,960]{2,1,0:T(8,128)(2,1)} %bitcast.11, f32[3,32,960]{2,1,0:T(8,128)} %bitcast.12, ...), custom_call_target="tpu_custom_call" | custom-call | tf_op jit(solution)/shard_map/first/pallas_call | solution.py:265
  5.8 1.7 %collective-permute-done = f32[16,960]{1,0:T(8,128)S(1)} collective-permute-done((f32[16,960]{1,0:T(8,128)S(1)}, f32[16,960]{1,0:T(8,128)S(1)}, u32[]{:S(2)}, u32[]{:S(2)}) %collective-permute-start) | collective-permute-done | bytes 61472 | tf_op jit(solution)/shard_map/ppermute | solution.py:236
  8.3 2.9 %collective-permute-start.4 = (bf16[1,3,40,960]{3,2,1,0:T(8,128)(2,1)S(1)}, bf16[1,3,40,960]{3,2,1,0:T(8,128)(2,1)S(1)}, u32[]{:S(2)}, u32[]{:S(2)}) collective-permute-start(bf16[1,3,40,960]{3,2,1,0:T(8,128)(2,1)S(1)} %get-tuple-element.41), channel_id=1, source_target_pairs={{0,2},{1,3},{2,0},{3,1},{4,6},{5,7},{6,4},{7,5},{8,10},{9,11},{10,... | collective-permute-start | bytes 691208 | tf_op jit(solution)/shard_map/ppermute | solution.py:236
  11.2 1.5 %collective-permute-start.5 = (bf16[1,3,40,960]{3,2,1,0:T(8,128)(2,1)S(1)}, bf16[1,3,40,960]{3,2,1,0:T(8,128)(2,1)S(1)}, u32[]{:S(2)}, u32[]{:S(2)}) collective-permute-start(bf16[1,3,40,960]{3,2,1,0:T(8,128)(2,1)S(1)} %get-tuple-element.42), channel_id=1, source_target_pairs={{0,4},{1,5},{2,6},{3,7},{4,0},{5,1},{6,2},{7,3},{8,12},{9,13},{10,... | collective-permute-start | bytes 691208 | tf_op jit(solution)/shard_map/ppermute | solution.py:236
  12.7 2.0 %collective-permute-start.1 = (f32[16,960]{1,0:T(8,128)S(1)}, f32[16,960]{1,0:T(8,128)S(1)}, u32[]{:S(2)}, u32[]{:S(2)}) collective-permute-start(f32[16,960]{1,0:T(8,128)S(1)} %add.48), channel_id=1, source_target_pairs={{0,8},{1,9},{2,10},{3,11},{4,12},{5,13},{6,14},{7,15},{8,0},{9,1},... | collective-permute-start | bytes 184328 | tf_op jit(solution)/shard_map/ppermute | solution.py:236
  14.7 2.2 %collective-permute-done.1 = f32[16,960]{1,0:T(8,128)S(1)} collective-permute-done((f32[16,960]{1,0:T(8,128)S(1)}, f32[16,960]{1,0:T(8,128)S(1)}, u32[]{:S(2)}, u32[]{:S(2)}) %collective-permute-start.1) | collective-permute-done | bytes 61472 | tf_op jit(solution)/shard_map/ppermute | solution.py:236
  17.0 3.1 %collective-permute-start.3 = (f32[16,960]{1,0:T(8,128)S(1)}, f32[16,960]{1,0:T(8,128)S(1)}, u32[]{:S(2)}, u32[]{:S(2)}) collective-permute-start(f32[16,960]{1,0:T(8,128)S(1)} %add.49), channel_id=1, source_target_pairs={{0,16},{1,17},{2,18},{3,19},{4,20},{5,21},{6,22},{7,23},{8,24},{9,... | collective-permute-start | bytes 184328 | tf_op jit(solution)/shard_map/ppermute | solution.py:236
  20.1 2.2 %collective-permute-done.3 = f32[16,960]{1,0:T(8,128)S(1)} collective-permute-done((f32[16,960]{1,0:T(8,128)S(1)}, f32[16,960]{1,0:T(8,128)S(1)}, u32[]{:S(2)}, u32[]{:S(2)}) %collective-permute-start.3) | collective-permute-done | bytes 61472 | tf_op jit(solution)/shard_map/ppermute | solution.py:236
  22.4 1.8 %collective-permute-done.5 = bf16[1,3,40,960]{3,2,1,0:T(8,128)(2,1)S(1)} collective-permute-done((bf16[1,3,40,960]{3,2,1,0:T(8,128)(2,1)S(1)}, bf16[1,3,40,960]{3,2,1,0:T(8,128)(2,1)S(1)}, u32[]{:S(2)}, u32[]{:S(2)}) %collective-permute-start.5) | collective-permute-done | bytes 230432 | tf_op jit(solution)/shard_map/ppermute | solution.py:236
  24.2 1.3 %collective-permute-start.7 = (f32[16,960]{1,0:T(8,128)S(1)}, f32[16,960]{1,0:T(8,128)S(1)}, u32[]{:S(2)}, u32[]{:S(2)}) collective-permute-start(f32[16,960]{1,0:T(8,128)S(1)} %add.50), channel_id=1, source_target_pairs={{0,2},{1,3},{2,0},{3,1},{4,6},{5,7},{6,4},{7,5},{8,10},{9,11},{10,... | collective-permute-start | bytes 184328 | tf_op jit(solution)/shard_map/ppermute | solution.py:236
  25.5 2.6 %collective-permute-start.12 = (bf16[1,3,40,960]{3,2,1,0:T(8,128)(2,1)S(1)}, bf16[1,3,40,960]{3,2,1,0:T(8,128)(2,1)S(1)}, u32[]{:S(2)}, u32[]{:S(2)}) collective-permute-start(bf16[1,3,40,960]{3,2,1,0:T(8,128)(2,1)S(1)} %add_add_fusion), channel_id=1, source_target_pairs={{0,16},{1,17},{2,18},{3,19},{4,20},{5,21},{6,22},{7,23},{8,24},{9,... | collective-permute-start | bytes 691208 | tf_op jit(solution)/shard_map/ppermute | solution.py:236
  28.6 1.6 %collective-permute-start.8 = (f32[16,960]{1,0:T(8,128)S(1)}, f32[16,960]{1,0:T(8,128)S(1)}, u32[]{:S(2)}, u32[]{:S(2)}) collective-permute-start(f32[16,960]{1,0:T(8,128)S(1)} %add.54), channel_id=1, source_target_pairs={{0,4},{1,5},{2,6},{3,7},{4,0},{5,1},{6,2},{7,3},{8,12},{9,13},{10,... | collective-permute-start | bytes 184328 | tf_op jit(solution)/shard_map/ppermute | solution.py:236
  30.1 2.7 %collective-permute-done.8 = f32[16,960]{1,0:T(8,128)S(1)} collective-permute-done((f32[16,960]{1,0:T(8,128)S(1)}, f32[16,960]{1,0:T(8,128)S(1)}, u32[]{:S(2)}, u32[]{:S(2)}) %collective-permute-start.8) | collective-permute-done | bytes 61472 | tf_op jit(solution)/shard_map/ppermute | solution.py:236
  33.0 1.2 %collective-permute-done.9.other_ref = f32[16,960]{1,0:T(8,128)S(1)} collective-permute-done((f32[16,960]{1,0:T(8,128)S(1)}, f32[16,960]{1,0:T(8,128)S(1)}, u32[]{:S(2)}, u32[]{:S(2)}) %collective-permute-start.9) | collective-permute-done | bytes 61472 | tf_op jit(solution)/shard_map/ppermute | solution.py:236
  34.2 1.2 %right.1 = (f32[3,32,960]{2,1,0:T(8,128)S(1)}, f32[3,8,960]{2,1,0:T(8,128)S(1)}, f32[3,8,960]{2,1,0:T(8,128)S(1)}, f32[3,8,960]{2,1,0:T(8,128)S(1)}, f32[3,8,960]{2,1,0:T(8,128)S(1)}) custom-call(f32[16,960]{1,0:T(8,128)S(1)} %add.55.mine_ref, f32[16,960]{1,0:T(8,128)S(1)} %collective-permute-done.9.other_ref, ...), custom_call_target="tpu_custom_call" | custom-call | tf_op jit(solution)/shard_map/right/pallas_call | solution.py:303
  36.0 0.8 %collective-permute-done.10 = f32[3,8,960]{2,1,0:T(8,128)S(1)} collective-permute-done((f32[3,8,960]{2,1,0:T(8,128)S(1)}, f32[3,8,960]{2,1,0:T(8,128)S(1)}, u32[]{:S(2)}, u32[]{:S(2)}) %collective-permute-start.10) | collective-permute-done | bytes 92192 | tf_op jit(solution)/shard_map/ppermute | solution.py:236
  37.0 1.6 %collective-permute-done.12 = bf16[1,3,40,960]{3,2,1,0:T(8,128)(2,1)S(1)} collective-permute-done((bf16[1,3,40,960]{3,2,1,0:T(8,128)(2,1)S(1)}, bf16[1,3,40,960]{3,2,1,0:T(8,128)(2,1)S(1)}, u32[]{:S(2)}, u32[]{:S(2)}) %collective-permute-start.12) | collective-permute-done | bytes 230432 | tf_op jit(solution)/shard_map/ppermute | solution.py:236
  40.0 4.0 %collective-permute-done.13 = f32[3,8,960]{2,1,0:T(8,128)S(1)} collective-permute-done((f32[3,8,960]{2,1,0:T(8,128)S(1)}, f32[3,8,960]{2,1,0:T(8,128)S(1)}, u32[]{:S(2)}, u32[]{:S(2)}) %collective-permute-start.13) | collective-permute-done | bytes 92192 | tf_op jit(solution)/shard_map/ppermute | solution.py:236
  44.0 1.1 %collective-permute-start.14 = (f32[3,8,960]{2,1,0:T(8,128)S(1)}, f32[3,8,960]{2,1,0:T(8,128)S(1)}, u32[]{:S(2)}, u32[]{:S(2)}) collective-permute-start(f32[3,8,960]{2,1,0:T(8,128)S(1)} %add.59), channel_id=1, source_target_pairs={{0,4},{1,5},{2,6},{3,7},{4,0},{5,1},{6,2},{7,3},{8,12},{9,13},{10,... | collective-permute-start | bytes 276488 | tf_op jit(solution)/shard_map/ppermute | solution.py:236
  45.1 3.4 %solve.1.w_ref = bf16[3,320,96]{2,1,0:T(8,128)(2,1)S(1)} custom-call(f32[16,960]{1,0:T(8,128)S(1)} %add.55.mine_ref, f32[16,960]{1,0:T(8,128)S(1)} %collective-permute-done.9.other_ref), custom_call_target="tpu_custom_call" | custom-call | bytes 1048576 | tf_op jit(solution)/shard_map/solve/pallas_call | solution.py:313
  48.8 1.1 %collective-permute-start.18 = (bf16[1,3,40,960]{3,2,1,0:T(8,128)(2,1)S(1)}, bf16[1,3,40,960]{3,2,1,0:T(8,128)(2,1)S(1)}, u32[]{:S(2)}, u32[]{:S(2)}) collective-permute-start(bf16[1,3,40,960]{3,2,1,0:T(8,128)(2,1)S(1)} %add.61), channel_id=1, source_target_pairs={{0,4},{1,5},{2,6},{3,7},{4,0},{5,1},{6,2},{7,3},{8,12},{9,13},{10,... | collective-permute-start | bytes 691208 | tf_op jit(solution)/shard_map/ppermute | solution.py:236
  49.8 1.0 %collective-permute-start.16 = (bf16[1,3,40,960]{3,2,1,0:T(8,128)(2,1)S(1)}, bf16[1,3,40,960]{3,2,1,0:T(8,128)(2,1)S(1)}, u32[]{:S(2)}, u32[]{:S(2)}) collective-permute-start(bf16[1,3,40,960]{3,2,1,0:T(8,128)(2,1)S(1)} %add.61), channel_id=1, source_target_pairs={{0,2},{1,3},{2,0},{3,1},{4,6},{5,7},{6,4},{7,5},{8,10},{9,11},{10,... | collective-permute-start | bytes 691208 | tf_op jit(solution)/shard_map/ppermute | solution.py:236
  50.8 1.4 %collective-permute-start.17 = (f32[3,8,960]{2,1,0:T(8,128)S(1)}, f32[3,8,960]{2,1,0:T(8,128)S(1)}, u32[]{:S(2)}, u32[]{:S(2)}) collective-permute-start(f32[3,8,960]{2,1,0:T(8,128)S(1)} %add.60), channel_id=1, source_target_pairs={{0,8},{1,9},{2,10},{3,11},{4,12},{5,13},{6,14},{7,15},{8,0},{9,1},... | collective-permute-start | bytes 276488 | tf_op jit(solution)/shard_map/ppermute | solution.py:236
  52.2 3.3 %collective-permute-done.17 = f32[3,8,960]{2,1,0:T(8,128)S(1)} collective-permute-done((f32[3,8,960]{2,1,0:T(8,128)S(1)}, f32[3,8,960]{2,1,0:T(8,128)S(1)}, u32[]{:S(2)}, u32[]{:S(2)}) %collective-permute-start.17) | collective-permute-done | bytes 92192 | tf_op jit(solution)/shard_map/ppermute | solution.py:236
  56.2 1.2 %collective-permute-start.24 = (bf16[1,3,40,960]{3,2,1,0:T(8,128)(2,1)S(1)}, bf16[1,3,40,960]{3,2,1,0:T(8,128)(2,1)S(1)}, u32[]{:S(2)}, u32[]{:S(2)}) collective-permute-start(bf16[1,3,40,960]{3,2,1,0:T(8,128)(2,1)S(1)} %collective-permute-done.16), channel_id=1, source_target_pairs={{0,4},{1,5},{2,6},{3,7},{4,0},{5,1},{6,2},{7,3},{8,12},{9,13},{10,... | collective-permute-start | bytes 691208 | tf_op jit(solution)/shard_map/ppermute | solution.py:236
  57.4 3.3 %collective-permute-start.19 = (f32[3,8,960]{2,1,0:T(8,128)S(1)}, f32[3,8,960]{2,1,0:T(8,128)S(1)}, u32[]{:S(2)}, u32[]{:S(2)}) collective-permute-start(f32[3,8,960]{2,1,0:T(8,128)S(1)} %add.62), channel_id=1, source_target_pairs={{0,16},{1,17},{2,18},{3,19},{4,20},{5,21},{6,22},{7,23},{8,24},{9,... | collective-permute-start | bytes 276488 | tf_op jit(solution)/shard_map/ppermute | solution.py:236
  60.7 2.3 %errors.1 = bf16[3,320,960]{2,1,0:T(8,128)(2,1)} custom-call(f32[3,320,960]{2,1,0:T(8,128)S(1)} %get-tuple-element.34.grad_ref, bf16[3,320,960]{2,1,0:T(8,128)(2,1)S(1)} %get-tuple-element.35.error_ref, bf16[3,320,96]{2,1,0:T(8,128)(2,1)S(1)} %solve.1.w_ref, f32[3,32,960]{2,1,0:T(8,128)S(1)} %get-tuple-element.58.all_ref), custom_call_target="tpu_custom_call" | custom-call | bytes 12582912 | tf_op jit(solution)/shard_map/errors/pallas_call | solution.py:343
  63.0 2.9 %collective-permute-done.19 = f32[3,8,960]{2,1,0:T(8,128)S(1)} collective-permute-done((f32[3,8,960]{2,1,0:T(8,128)S(1)}, f32[3,8,960]{2,1,0:T(8,128)S(1)}, u32[]{:S(2)}, u32[]{:S(2)}) %collective-permute-start.19) | collective-permute-done | bytes 92192 | tf_op jit(solution)/shard_map/ppermute | solution.py:236
  65.9 0.8 %collective-permute-start.21 = (f32[3,8,960]{2,1,0:T(8,128)S(1)}, f32[3,8,960]{2,1,0:T(8,128)S(1)}, u32[]{:S(2)}, u32[]{:S(2)}) collective-permute-start(f32[3,8,960]{2,1,0:T(8,128)S(1)} %add.63.r0_ref), channel_id=1, source_target_pairs={{0,2},{1,3},{2,0},{3,1},{4,6},{5,7},{6,4},{7,5},{8,10},{9,11},{10,... | collective-permute-start | bytes 276488 | tf_op jit(solution)/shard_map/ppermute | solution.py:236
  66.8 3.9 %collective-permute-done.21.r2_ref = f32[3,8,960]{2,1,0:T(8,128)S(1)} collective-permute-done((f32[3,8,960]{2,1,0:T(8,128)S(1)}, f32[3,8,960]{2,1,0:T(8,128)S(1)}, u32[]{:S(2)}, u32[]{:S(2)}) %collective-permute-start.21) | collective-permute-done | bytes 92192 | tf_op jit(solution)/shard_map/ppermute | solution.py:236
  71.2 1.1 %collective-permute-done.20.r1_ref = f32[3,8,960]{2,1,0:T(8,128)S(1)} collective-permute-done((f32[3,8,960]{2,1,0:T(8,128)S(1)}, f32[3,8,960]{2,1,0:T(8,128)S(1)}, u32[]{:S(2)}, u32[]{:S(2)}) %collective-permute-start.20) | collective-permute-done | bytes 92192 | tf_op jit(solution)/shard_map/ppermute | solution.py:236
  72.5 3.1 %step.1 = (bf16[3,8,40,960]{3,2,1,0:T(8,128)(2,1)}, bf16[2,8,40,960]{3,2,1,0:T(8,128)(2,1)}) custom-call(s32[3]{0:T(128)S(1)} %copy-done.1, s32[3]{0:T(128)S(1)} %copy-done.2, f32[4]{0:T(128)S(1)} %copy-done.3, f32[4]{0:T(128)S(1)} %copy-done.4, f32[3,8,960]{2,1,0:T(8,128)S(1)} %add.63.r0_ref, f32[3,8,960]{2,1,0:T(8,128)S(1)} %collective-permute-done.20.r1_ref, ...), custom_call_target="tpu_custom_call" | custom-call | tf_op jit(solution)/shard_map/step/pallas_call | solution.py:362
  (51 shorter events, 5.8 us)
Async XLA Ops:
  0.6 6.9 %copy-start = (bf16[2,320,960]{2,1,0:T(8,128)(2,1)S(1)}, bf16[2,320,960]{2,1,0:T(8,128)(2,1)}, u32[]{:S(2)}) copy-start(bf16[2,320,960]{2,1,0:T(8,128)(2,1)} %param.15) | copy-start | bytes 3686404
  0.6 6.9 %copy-start.1 = (s32[3]{0:T(128)S(1)}, s32[3]{0:T(128)}, u32[]{:S(2)}) copy-start(s32[3]{0:T(128)} %owners_ref.3) | copy-start | bytes 40
  5.2 2.4 %collective-permute-start.2 = (bf16[4,2,40,960]{3,2,1,0:T(8,128)(2,1)S(1)}, bf16[4,2,40,960]{3,2,1,0:T(8,128)(2,1)S(1)}, u32[]{:S(2)}, u32[]{:S(2)}) collective-permute-start(bf16[4,2,40,960]{3,2,1,0:T(8,128)(2,1)S(1)} %get-tuple-element.38), channel_id=1, source_target_pairs={{0,1},{1,0},{2,3},{3,2},{4,5},{5,4},{6,7},{7,6},{8,9},{9,8},{10,11... | collective-permute-start | bytes 1843208 | tf_op jit(solution)/shard_map/ppermute | solution.py:236
  5.7 1.8 %collective-permute-start = (f32[16,960]{1,0:T(8,128)S(1)}, f32[16,960]{1,0:T(8,128)S(1)}, u32[]{:S(2)}, u32[]{:S(2)}) collective-permute-start(f32[16,960]{1,0:T(8,128)S(1)} %get-tuple-element.37), channel_id=1, source_target_pairs={{0,1},{1,0},{2,3},{3,2},{4,5},{5,4},{6,7},{7,6},{8,9},{9,8},{10,11... | collective-permute-start | bytes 184328 | tf_op jit(solution)/shard_map/ppermute | solution.py:236
  8.3 14.1 %collective-permute-start.4 = (bf16[1,3,40,960]{3,2,1,0:T(8,128)(2,1)S(1)}, bf16[1,3,40,960]{3,2,1,0:T(8,128)(2,1)S(1)}, u32[]{:S(2)}, u32[]{:S(2)}) collective-permute-start(bf16[1,3,40,960]{3,2,1,0:T(8,128)(2,1)S(1)} %get-tuple-element.41), channel_id=1, source_target_pairs={{0,2},{1,3},{2,0},{3,1},{4,6},{5,7},{6,4},{7,5},{8,10},{9,11},{10,... | collective-permute-start | bytes 691208 | tf_op jit(solution)/shard_map/ppermute | solution.py:236
  11.2 13.0 %collective-permute-start.5 = (bf16[1,3,40,960]{3,2,1,0:T(8,128)(2,1)S(1)}, bf16[1,3,40,960]{3,2,1,0:T(8,128)(2,1)S(1)}, u32[]{:S(2)}, u32[]{:S(2)}) collective-permute-start(bf16[1,3,40,960]{3,2,1,0:T(8,128)(2,1)S(1)} %get-tuple-element.42), channel_id=1, source_target_pairs={{0,4},{1,5},{2,6},{3,7},{4,0},{5,1},{6,2},{7,3},{8,12},{9,13},{10,... | collective-permute-start | bytes 691208 | tf_op jit(solution)/shard_map/ppermute | solution.py:236
  12.7 11.5 %collective-permute-start.6 = (bf16[1,3,40,960]{3,2,1,0:T(8,128)(2,1)S(1)}, bf16[1,3,40,960]{3,2,1,0:T(8,128)(2,1)S(1)}, u32[]{:S(2)}, u32[]{:S(2)}) collective-permute-start(bf16[1,3,40,960]{3,2,1,0:T(8,128)(2,1)S(1)} %get-tuple-element.43), channel_id=1, source_target_pairs={{0,6},{1,7},{2,4},{3,5},{4,2},{5,3},{6,0},{7,1},{8,14},{9,15},{10,... | collective-permute-start | bytes 691208 | tf_op jit(solution)/shard_map/ppermute | solution.py:236
  12.7 4.3 %collective-permute-start.1 = (f32[16,960]{1,0:T(8,128)S(1)}, f32[16,960]{1,0:T(8,128)S(1)}, u32[]{:S(2)}, u32[]{:S(2)}) collective-permute-start(f32[16,960]{1,0:T(8,128)S(1)} %add.48), channel_id=1, source_target_pairs={{0,8},{1,9},{2,10},{3,11},{4,12},{5,13},{6,14},{7,15},{8,0},{9,1},... | collective-permute-start | bytes 184328 | tf_op jit(solution)/shard_map/ppermute | solution.py:236
  17.0 5.3 %collective-permute-start.3 = (f32[16,960]{1,0:T(8,128)S(1)}, f32[16,960]{1,0:T(8,128)S(1)}, u32[]{:S(2)}, u32[]{:S(2)}) collective-permute-start(f32[16,960]{1,0:T(8,128)S(1)} %add.49), channel_id=1, source_target_pairs={{0,16},{1,17},{2,18},{3,19},{4,20},{5,21},{6,22},{7,23},{8,24},{9,... | collective-permute-start | bytes 184328 | tf_op jit(solution)/shard_map/ppermute | solution.py:236
  24.2 4.3 %collective-permute-start.7 = (f32[16,960]{1,0:T(8,128)S(1)}, f32[16,960]{1,0:T(8,128)S(1)}, u32[]{:S(2)}, u32[]{:S(2)}) collective-permute-start(f32[16,960]{1,0:T(8,128)S(1)} %add.50), channel_id=1, source_target_pairs={{0,2},{1,3},{2,0},{3,1},{4,6},{5,7},{6,4},{7,5},{8,10},{9,11},{10,... | collective-permute-start | bytes 184328 | tf_op jit(solution)/shard_map/ppermute | solution.py:236
  25.5 13.1 %collective-permute-start.12 = (bf16[1,3,40,960]{3,2,1,0:T(8,128)(2,1)S(1)}, bf16[1,3,40,960]{3,2,1,0:T(8,128)(2,1)S(1)}, u32[]{:S(2)}, u32[]{:S(2)}) collective-permute-start(bf16[1,3,40,960]{3,2,1,0:T(8,128)(2,1)S(1)} %add_add_fusion), channel_id=1, source_target_pairs={{0,16},{1,17},{2,18},{3,19},{4,20},{5,21},{6,22},{7,23},{8,24},{9,... | collective-permute-start | bytes 691208 | tf_op jit(solution)/shard_map/ppermute | solution.py:236
  28.6 4.3 %collective-permute-start.8 = (f32[16,960]{1,0:T(8,128)S(1)}, f32[16,960]{1,0:T(8,128)S(1)}, u32[]{:S(2)}, u32[]{:S(2)}) collective-permute-start(f32[16,960]{1,0:T(8,128)S(1)} %add.54), channel_id=1, source_target_pairs={{0,4},{1,5},{2,6},{3,7},{4,0},{5,1},{6,2},{7,3},{8,12},{9,13},{10,... | collective-permute-start | bytes 184328 | tf_op jit(solution)/shard_map/ppermute | solution.py:236
  32.9 1.3 %collective-permute-start.9 = (f32[16,960]{1,0:T(8,128)S(1)}, f32[16,960]{1,0:T(8,128)S(1)}, u32[]{:S(2)}, u32[]{:S(2)}) collective-permute-start(f32[16,960]{1,0:T(8,128)S(1)} %add.55.mine_ref), channel_id=1, source_target_pairs={{0,1},{1,0},{2,3},{3,2},{4,5},{5,4},{6,7},{7,6},{8,9},{9,8},{10,11... | collective-permute-start | bytes 184328 | tf_op jit(solution)/shard_map/ppermute | solution.py:236
  35.4 1.4 %collective-permute-start.10 = (f32[3,8,960]{2,1,0:T(8,128)S(1)}, f32[3,8,960]{2,1,0:T(8,128)S(1)}, u32[]{:S(2)}, u32[]{:S(2)}) collective-permute-start(f32[3,8,960]{2,1,0:T(8,128)S(1)} %get-tuple-element.48), channel_id=1, source_target_pairs={{0,1},{1,0},{2,3},{3,2},{4,5},{5,4},{6,7},{7,6},{8,9},{9,8},{10,11... | collective-permute-start | bytes 276488 | tf_op jit(solution)/shard_map/ppermute | solution.py:236
  35.7 1.3 %collective-permute-start.11 = (f32[3,8,960]{2,1,0:T(8,128)S(1)}, f32[3,8,960]{2,1,0:T(8,128)S(1)}, u32[]{:S(2)}, u32[]{:S(2)}) collective-permute-start(f32[3,8,960]{2,1,0:T(8,128)S(1)} %get-tuple-element.50), channel_id=1, source_target_pairs={{0,1},{1,0},{2,3},{3,2},{4,5},{5,4},{6,7},{7,6},{8,9},{9,8},{10,11... | collective-permute-start | bytes 276488 | tf_op jit(solution)/shard_map/ppermute | solution.py:236
  38.6 10.1 %collective-permute-start.15 = (bf16[1,3,40,960]{3,2,1,0:T(8,128)(2,1)S(1)}, bf16[1,3,40,960]{3,2,1,0:T(8,128)(2,1)S(1)}, u32[]{:S(2)}, u32[]{:S(2)}) collective-permute-start(bf16[1,3,40,960]{3,2,1,0:T(8,128)(2,1)S(1)} %add.58), channel_id=1, source_target_pairs={{0,8},{1,9},{2,10},{3,11},{4,12},{5,13},{6,14},{7,15},{8,0},{9,1},... | collective-permute-start | bytes 691208 | tf_op jit(solution)/shard_map/ppermute | solution.py:236
  39.4 4.6 %collective-permute-start.13 = (f32[3,8,960]{2,1,0:T(8,128)S(1)}, f32[3,8,960]{2,1,0:T(8,128)S(1)}, u32[]{:S(2)}, u32[]{:S(2)}) collective-permute-start(f32[3,8,960]{2,1,0:T(8,128)S(1)} %add.57), channel_id=1, source_target_pairs={{0,2},{1,3},{2,0},{3,1},{4,6},{5,7},{6,4},{7,5},{8,10},{9,11},{10,... | collective-permute-start | bytes 276488 | tf_op jit(solution)/shard_map/ppermute | solution.py:236
  44.0 4.7 %collective-permute-start.14 = (f32[3,8,960]{2,1,0:T(8,128)S(1)}, f32[3,8,960]{2,1,0:T(8,128)S(1)}, u32[]{:S(2)}, u32[]{:S(2)}) collective-permute-start(f32[3,8,960]{2,1,0:T(8,128)S(1)} %add.59), channel_id=1, source_target_pairs={{0,4},{1,5},{2,6},{3,7},{4,0},{5,1},{6,2},{7,3},{8,12},{9,13},{10,... | collective-permute-start | bytes 276488 | tf_op jit(solution)/shard_map/ppermute | solution.py:236
  48.8 6.7 %collective-permute-start.18 = (bf16[1,3,40,960]{3,2,1,0:T(8,128)(2,1)S(1)}, bf16[1,3,40,960]{3,2,1,0:T(8,128)(2,1)S(1)}, u32[]{:S(2)}, u32[]{:S(2)}) collective-permute-start(bf16[1,3,40,960]{3,2,1,0:T(8,128)(2,1)S(1)} %add.61), channel_id=1, source_target_pairs={{0,4},{1,5},{2,6},{3,7},{4,0},{5,1},{6,2},{7,3},{8,12},{9,13},{10,... | collective-permute-start | bytes 691208 | tf_op jit(solution)/shard_map/ppermute | solution.py:236
  49.8 6.2 %collective-permute-start.16 = (bf16[1,3,40,960]{3,2,1,0:T(8,128)(2,1)S(1)}, bf16[1,3,40,960]{3,2,1,0:T(8,128)(2,1)S(1)}, u32[]{:S(2)}, u32[]{:S(2)}) collective-permute-start(bf16[1,3,40,960]{3,2,1,0:T(8,128)(2,1)S(1)} %add.61), channel_id=1, source_target_pairs={{0,2},{1,3},{2,0},{3,1},{4,6},{5,7},{6,4},{7,5},{8,10},{9,11},{10,... | collective-permute-start | bytes 691208 | tf_op jit(solution)/shard_map/ppermute | solution.py:236
  50.8 4.6 %collective-permute-start.17 = (f32[3,8,960]{2,1,0:T(8,128)S(1)}, f32[3,8,960]{2,1,0:T(8,128)S(1)}, u32[]{:S(2)}, u32[]{:S(2)}) collective-permute-start(f32[3,8,960]{2,1,0:T(8,128)S(1)} %add.60), channel_id=1, source_target_pairs={{0,8},{1,9},{2,10},{3,11},{4,12},{5,13},{6,14},{7,15},{8,0},{9,1},... | collective-permute-start | bytes 276488 | tf_op jit(solution)/shard_map/ppermute | solution.py:236
  56.1 16.3 %collective-permute-start.23 = (bf16[3,3,40,960]{3,2,1,0:T(8,128)(2,1)S(1)}, bf16[3,3,40,960]{3,2,1,0:T(8,128)(2,1)S(1)}, u32[]{:S(2)}, u32[]{:S(2)}) collective-permute-start(bf16[3,3,40,960]{3,2,1,0:T(8,128)(2,1)S(1)} %pad_maximum_fusion.even_ref), channel_id=1, source_target_pairs={{0,1},{1,0},{2,3},{3,2},{4,5},{5,4},{6,7},{7,6},{8,9},{9,8},{10,11... | collective-permute-start | bytes 2073608 | tf_op jit(solution)/shard_map/ppermute | solution.py:236
  56.2 10.6 %collective-permute-start.24 = (bf16[1,3,40,960]{3,2,1,0:T(8,128)(2,1)S(1)}, bf16[1,3,40,960]{3,2,1,0:T(8,128)(2,1)S(1)}, u32[]{:S(2)}, u32[]{:S(2)}) collective-permute-start(bf16[1,3,40,960]{3,2,1,0:T(8,128)(2,1)S(1)} %collective-permute-done.16), channel_id=1, source_target_pairs={{0,4},{1,5},{2,6},{3,7},{4,0},{5,1},{6,2},{7,3},{8,12},{9,13},{10,... | collective-permute-start | bytes 691208 | tf_op jit(solution)/shard_map/ppermute | solution.py:236
  57.4 8.5 %collective-permute-start.19 = (f32[3,8,960]{2,1,0:T(8,128)S(1)}, f32[3,8,960]{2,1,0:T(8,128)S(1)}, u32[]{:S(2)}, u32[]{:S(2)}) collective-permute-start(f32[3,8,960]{2,1,0:T(8,128)S(1)} %add.62), channel_id=1, source_target_pairs={{0,16},{1,17},{2,18},{3,19},{4,20},{5,21},{6,22},{7,23},{8,24},{9,... | collective-permute-start | bytes 276488 | tf_op jit(solution)/shard_map/ppermute | solution.py:236
  60.7 11.8 %copy-start.2 = (s32[3]{0:T(128)S(1)}, s32[3]{0:T(128)}, u32[]{:S(2)}) copy-start(s32[3]{0:T(128)} %buckets_ref.1) | copy-start | bytes 40
  60.7 11.8 %copy-start.3 = (f32[4]{0:T(128)S(1)}, f32[4]{0:T(128)}, u32[]{:S(2)}) copy-start(f32[4]{0:T(128)} %rates_ref.1) | copy-start | bytes 52
  60.7 11.8 %copy-start.4 = (f32[4]{0:T(128)S(1)}, f32[4]{0:T(128)}, u32[]{:S(2)}) copy-start(f32[4]{0:T(128)} %betas_ref.1) | copy-start | bytes 52
  65.9 4.7 %collective-permute-start.21 = (f32[3,8,960]{2,1,0:T(8,128)S(1)}, f32[3,8,960]{2,1,0:T(8,128)S(1)}, u32[]{:S(2)}, u32[]{:S(2)}) collective-permute-start(f32[3,8,960]{2,1,0:T(8,128)S(1)} %add.63.r0_ref), channel_id=1, source_target_pairs={{0,2},{1,3},{2,0},{3,1},{4,6},{5,7},{6,4},{7,5},{8,10},{9,11},{10,... | collective-permute-start | bytes 276488 | tf_op jit(solution)/shard_map/ppermute | solution.py:236
  70.7 1.8 %collective-permute-start.25 = (bf16[1,3,40,960]{3,2,1,0:T(8,128)(2,1)S(1)}, bf16[1,3,40,960]{3,2,1,0:T(8,128)(2,1)S(1)}, u32[]{:S(2)}, u32[]{:S(2)}) collective-permute-start(bf16[1,3,40,960]{3,2,1,0:T(8,128)(2,1)S(1)} %collective-permute-done.24.far_ref), channel_id=1, source_target_pairs={{0,1},{1,0},{2,3},{3,2},{4,5},{5,4},{6,7},{7,6},{8,9},{9,8},{10,11... | collective-permute-start | bytes 691208 | tf_op jit(solution)/shard_map/ppermute | solution.py:236
  70.7 1.6 %collective-permute-start.20 = (f32[3,8,960]{2,1,0:T(8,128)S(1)}, f32[3,8,960]{2,1,0:T(8,128)S(1)}, u32[]{:S(2)}, u32[]{:S(2)}) collective-permute-start(f32[3,8,960]{2,1,0:T(8,128)S(1)} %add.63.r0_ref), channel_id=1, source_target_pairs={{0,1},{1,0},{2,3},{3,2},{4,5},{5,4},{6,7},{7,6},{8,9},{9,8},{10,11... | collective-permute-start | bytes 276488 | tf_op jit(solution)/shard_map/ppermute | solution.py:236
  71.2 1.3 %collective-permute-start.22 = (f32[3,8,960]{2,1,0:T(8,128)S(1)}, f32[3,8,960]{2,1,0:T(8,128)S(1)}, u32[]{:S(2)}, u32[]{:S(2)}) collective-permute-start(f32[3,8,960]{2,1,0:T(8,128)S(1)} %collective-permute-done.21.r2_ref), channel_id=1, source_target_pairs={{0,1},{1,0},{2,3},{3,2},{4,5},{5,4},{6,7},{7,6},{8,9},{9,8},{10,11... | collective-permute-start | bytes 276488 | tf_op jit(solution)/shard_map/ppermute | solution.py:236
